TPU v7x, 128 devices: a whole 4x4x4 slice. The times are simulated.
128 devices in a mesh: section: 8 (over z_hi, x), dp: 16 (over z_lo, y, core).
Axes of the slice: x: 4, y: 4, z: 4 (z_hi: 2, z_lo: 2; z = z_hi * 2 + z_lo), core: 2. Of those that a mesh axis runs over, the one named last changes fastest.
Arguments:
- clean: bfloat16 [64, 16, 16, 384], P('dp'), may hold values from -12 to 12
- noise: bfloat16 [64, 16, 16, 384], P('dp'), may hold values from -6 to 6
- stamps: int32 [64], P('dp'), may hold values from 0 to 999
- enc_weight: bfloat16 [8, 3, 3, 384, 384], P('section'), may hold values from -0.109375 to 0.109375
- dec_weight: bfloat16 [8, 3, 3, 768, 384], P('section'), may hold values from -0.078125 to 0.078125
Outputs:
- enc_grad: float32 [8, 3, 3, 384, 384], P('section', None, None, 'dp')
- dec_grad: float32 [8, 3, 3, 768, 384], P('section', None, None, 'dp')
All inputs are finite; a program needn't handle non-finite values.
Results may differ from a plain program's by a relative error of at most 0.0035.
Values sent between devices are 32-bit elements; how exact they have to be, the bound alone decides.
A program may use at most 128 MiB of HBM per device.

v0:
```python
import math

import jax
import jax.numpy as jnp
from jax import lax
from jax.sharding import PartitionSpec as P

GROUPS = 32


def passed_along(value, axis, steps):
    count = lax.axis_size(axis)
    initial, last = (max(0, -steps), min(count, count - steps))
    return lax.ppermute(value, axis, [(source, source + steps) for source in range(initial, last)])


def embed(stamps_in, channels):
    half_width = channels // 2
    frequency = jnp.exp(-math.log(10000.0) * jnp.arange(half_width, dtype=jnp.float32) / half_width)
    angles = stamps_in.astype(jnp.float32)[:, None] * frequency[None, :]
    return jnp.concatenate([jnp.sin(angles), jnp.cos(angles)], axis=1)


def activate(inputs_f32, stamps_in):
    batch_rows, height, breadth, channels = inputs_f32.shape
    grouped = inputs_f32.reshape(batch_rows, height * breadth, GROUPS, channels // GROUPS)
    group_mean = jnp.mean(grouped, axis=(1, 3), keepdims=True)
    centered = grouped - group_mean
    group_var = jnp.mean(centered * centered, axis=(1, 3), keepdims=True)
    normed = (centered * lax.rsqrt(group_var + 1e-05)).reshape(inputs_f32.shape)
    modulate = 1.0 + 0.5 * embed(stamps_in, channels)[:, None, None, :]
    return jax.nn.silu(normed * modulate)


def conv_apply(activations, weight):
    batch_rows, height, breadth, channels = activations.shape
    padded = jnp.pad(activations, ((0, 0), (1, 1), (1, 1), (0, 0)))
    summed = jnp.zeros((batch_rows * height * breadth, weight.shape[3]), jnp.float32)
    for row_off in range(3):
        for col_off in range(3):
            window = padded[:, row_off : row_off + height, col_off : col_off + breadth, :].reshape(
                -1, channels
            )
            summed = summed + jnp.dot(
                window, weight[row_off, col_off], preferred_element_type=jnp.float32
            )
    return summed.reshape(batch_rows, height, breadth, weight.shape[3])


def conv_back(cotangent, weight):
    batch_rows, height, breadth, outputs = cotangent.shape
    padded = jnp.pad(cotangent.astype(jnp.bfloat16), ((0, 0), (1, 1), (1, 1), (0, 0)))
    summed = jnp.zeros((batch_rows * height * breadth, weight.shape[2]), jnp.float32)
    for row_off in range(3):
        for col_off in range(3):
            window = padded[
                :, 2 - row_off : 2 - row_off + height, 2 - col_off : 2 - col_off + breadth, :
            ].reshape(-1, outputs)
            summed = summed + lax.dot_general(
                window,
                weight[row_off, col_off],
                (((1,), (1,)), ((), ())),
                preferred_element_type=jnp.float32,
            )
    return summed.reshape(batch_rows, height, breadth, weight.shape[2])


def conv_weight_grad(activations, cotangent):
    batch_rows, height, breadth, channels = activations.shape
    padded = jnp.pad(activations, ((0, 0), (1, 1), (1, 1), (0, 0)))
    flat_cot = cotangent.astype(jnp.bfloat16).reshape(-1, cotangent.shape[3])
    kernel_rows = []
    for row_off in range(3):
        kernel_cols = []
        for col_off in range(3):
            window = padded[:, row_off : row_off + height, col_off : col_off + breadth, :].reshape(
                -1, channels
            )
            kernel_cols.append(
                lax.dot_general(
                    window, flat_cot, (((0,), (0,)), ((), ())), preferred_element_type=jnp.float32
                )
            )
        kernel_rows.append(jnp.stack(kernel_cols))
    return jnp.stack(kernel_rows)


def block_forward(inputs, residual, weight, stamps_in):
    activations = activate(inputs, stamps_in).astype(jnp.bfloat16)
    return residual + conv_apply(activations, weight)


def block_backward(inputs, weight, stamps_in, cotangent):
    activated, pullback = jax.vjp(lambda inner_field: activate(inner_field, stamps_in), inputs)
    activations = activated.astype(jnp.bfloat16)
    weight_grad = conv_weight_grad(activations, cotangent)
    input_grad = pullback(conv_back(cotangent, weight))[0]
    return (input_grad, weight_grad)


def noise_levels(stamps_in):
    phase = (stamps_in.astype(jnp.float32) / 1000.0 + 0.008) / 1.008 * (math.pi / 2.0)
    signal = jnp.cos(phase) ** 2
    return (jnp.sqrt(signal), jnp.sqrt(1.0 - signal))


def pick_row(buffer, slot_index):
    return lax.dynamic_slice_in_dim(buffer, slot_index, 1, 0)


def store_row(buffer, piece, slot_index, active):
    kept = pick_row(buffer, slot_index)
    return lax.dynamic_update_slice_in_dim(buffer, jnp.where(active, piece, kept), slot_index, 0)


def shards(clean, noise, stamps, enc_weight, dec_weight):
    sections = lax.axis_size("section")
    section_index = lax.axis_index("section")
    last_section = sections - 1
    samples = clean.shape[0]
    channels = clean.shape[3]
    enc_kernel = enc_weight[0]
    dec_kernel = dec_weight[0]
    keep_level, spread_level = noise_levels(stamps)
    noisy = keep_level[:, None, None, None] * clean.astype(jnp.float32) + spread_level[
        :, None, None, None
    ] * noise.astype(jnp.float32)
    factor = 1.0 / math.sqrt(samples * lax.axis_size("dp") * clean.shape[1] * clean.shape[2])
    ticks_total = samples + sections - 1
    blank_piece = jnp.zeros((1,) + clean.shape[1:], jnp.float32)
    blank_buffer = jnp.zeros(clean.shape, jnp.float32)

    def locate(tick_now, offset):
        sample_id = tick_now - offset
        active = (sample_id >= 0) & (sample_id < samples)
        slot_index = jnp.clip(sample_id, 0, samples - 1)
        return (active, slot_index)

    def encoder_tick(tick_now, carried):
        incoming, enc_inputs, skips = carried
        active, slot_index = locate(tick_now, section_index)
        source = jnp.where(section_index == 0, pick_row(noisy, slot_index), incoming)
        stamp_one = pick_row(stamps, slot_index)
        result = lax.cond(
            active,
            lambda: block_forward(source, source, enc_kernel, stamp_one),
            lambda: blank_piece,
        )
        enc_inputs = store_row(enc_inputs, source, slot_index, active)
        skips = store_row(skips, result, slot_index, active)
        incoming = passed_along(result, "section", 1)
        return (incoming, enc_inputs, skips)

    _, enc_inputs, skips = lax.fori_loop(
        0, ticks_total, encoder_tick, (blank_piece, blank_buffer, blank_buffer)
    )

    def decoder_tick(tick_now, carried):
        incoming, dec_inputs, outputs = carried
        active, slot_index = locate(tick_now, last_section - section_index)
        skip_piece = pick_row(skips, slot_index)
        source = jnp.where(section_index == last_section, skip_piece, incoming)
        joined = jnp.concatenate([source, skip_piece], axis=3)
        stamp_one = pick_row(stamps, slot_index)
        result = lax.cond(
            active,
            lambda: block_forward(joined, source, dec_kernel, stamp_one),
            lambda: blank_piece,
        )
        dec_inputs = store_row(dec_inputs, source, slot_index, active)
        outputs = store_row(outputs, result, slot_index, active)
        incoming = passed_along(result, "section", -1)
        return (incoming, dec_inputs, outputs)

    _, dec_inputs, outputs = lax.fori_loop(
        0, ticks_total, decoder_tick, (blank_piece, blank_buffer, blank_buffer)
    )

    def decoder_back_tick(tick_now, carried):
        incoming, dec_acc, skip_grads, up_grads = carried
        active, slot_index = locate(tick_now, section_index)
        top_grad = factor * (
            pick_row(outputs, slot_index) - pick_row(noise, slot_index).astype(jnp.float32)
        )
        flowing = jnp.where(section_index == 0, top_grad, incoming)
        joined = jnp.concatenate(
            [pick_row(dec_inputs, slot_index), pick_row(skips, slot_index)], axis=3
        )
        stamp_one = pick_row(stamps, slot_index)

        def decoder_working(accum):
            input_grad, weight_grad = block_backward(joined, dec_kernel, stamp_one, flowing)
            up_piece = input_grad[..., :channels] + flowing
            return (accum + weight_grad, up_piece, input_grad[..., channels:])

        def decoder_resting(accum):
            return (accum, blank_piece, blank_piece)

        dec_acc, up_piece, skip_grad = lax.cond(active, decoder_working, decoder_resting, dec_acc)
        skip_grads = store_row(skip_grads, skip_grad, slot_index, active)
        up_grads = store_row(up_grads, up_piece, slot_index, active)
        incoming = passed_along(up_piece, "section", 1)
        return (incoming, dec_acc, skip_grads, up_grads)

    dec_start = jnp.zeros(dec_kernel.shape, jnp.float32)
    _, dec_acc, skip_grads, up_grads = lax.fori_loop(
        0, ticks_total, decoder_back_tick, (blank_piece, dec_start, blank_buffer, blank_buffer)
    )

    def encoder_back_tick(tick_now, carried):
        incoming, enc_acc = carried
        active, slot_index = locate(tick_now, last_section - section_index)
        arriving = jnp.where(
            section_index == last_section, pick_row(up_grads, slot_index), incoming
        )
        merged = arriving + pick_row(skip_grads, slot_index)
        block_input = pick_row(enc_inputs, slot_index)
        stamp_one = pick_row(stamps, slot_index)

        def encoder_working(accum):
            input_grad, weight_grad = block_backward(block_input, enc_kernel, stamp_one, merged)
            return (accum + weight_grad, input_grad + merged)

        def encoder_resting(accum):
            return (accum, blank_piece)

        enc_acc, down_piece = lax.cond(active, encoder_working, encoder_resting, enc_acc)
        incoming = passed_along(down_piece, "section", -1)
        return (incoming, enc_acc)

    enc_start = jnp.zeros(enc_kernel.shape, jnp.float32)
    _, enc_acc = lax.fori_loop(0, ticks_total, encoder_back_tick, (blank_piece, enc_start))
    enc_share, dec_share = (
        lax.psum_scatter(enc_acc[None], "dp", scatter_dimension=3, tiled=True),
        lax.psum_scatter(dec_acc[None], "dp", scatter_dimension=3, tiled=True),
    )
    return (enc_share, dec_share)


def solution(mesh):
    placed = (
        P("dp", None, None, None),
        P("dp", None, None, None),
        P("dp"),
        P("section", None, None, None, None),
        P("section", None, None, None, None),
    )
    return jax.shard_map(
        shards,
        mesh=mesh,
        in_specs=placed,
        out_specs=(P("section", None, None, "dp", None), P("section", None, None, "dp", None)),
        check_vma=False,
    )
```

profile of v0, /device:TPU:0, one launch (start us, length us, event | category | flops | bytes accessed | tf_op | source)
XLA Modules:
  0.0 1415.7 jit_solution(2441908325496956105)
XLA Ops:
  14.3 182.2 %while.80 = (s32[]{:T(128)}, f32[1,16,16,384]{3,2,1,0:T(8,128)}, f32[4,16,16,384]{3,2,1,0:T(8,128)}, f32[4,16,16,384]{3,2,1,0:T(8,128)}, s32[]{:T(128)}, /*index...) while((s32[]{:T(128)}, f32[1,16,16,384]{3,2,1,0:T(8,128)}, ...), condition=%wide.region_7.8_spmd, body=%wide.region_0.7_spmd.sunk | while | flops 681838080 | bytes 20187440 | solution.py:154
  199.2 243.5 %while.81 = (s32[]{:T(128)}, f32[1,16,16,384]{3,2,1,0:T(8,128)S(1)}, f32[4,16,16,384]{3,2,1,0:T(8,128)}, f32[4,16,16,384]{3,2,1,0:T(8,128)}, s32[]{:T(128)}, /*i...) while((s32[]{:T(128)}, ...), condition=%wide.region_15.16_spmd, body=%wide.region_8.15_spmd.sunk | while | flops 1362693120 | bytes 50988884 | solution.py:175
  311.6 37.2 %collective-permute-done.1 = f32[1,16,16,384]{3,2,1,0:T(8,128)S(1)} collective-permute-done((f32[1,16,16,384]{3,2,1,0:T(8,128)S(1)}, f32[1,16,16,384]{3,2,1,0:T(8,128)S(1)}, u32[]{:S(2)}, u32[]{:S(2)}) %collective-permute-start.1) | collective-permute-done | bytes 393248 | tf_op jit(solution)/shard_map/while/body/eval_jaxpr/ppermute | solution.py:14
  450.2 360.2 %while.82 = (s32[]{:T(128)}, f32[1,16,16,384]{3,2,1,0:T(8,128)S(1)}, f32[3,3,768,384]{3,2,1,0:T(8,128)}, f32[4,16,16,384]{3,2,1,0:T(8,128)}, f32[4,16,16,384]{3,...) while((s32[]{:T(128)}, ...), condition=%wide.region_27.28_spmd, body=%wide.region_16.27_spmd.sunk | while | flops 2744945920 | bytes 206576816 | solution.py:206
  453.5 26.6 %conditional.10 = (f32[3,3,768,384]{3,2,1,0:T(8,128)}, f32[1,16,16,384]{3,2,1,0:T(8,128)S(1)}, f32[1,16,16,384]{3,2,1,0:T(8,128)}) conditional(s32[]{:T(128)} %convert_element_type.139, f32[3,3,768,384]{3,2,1,0:T(8,128)} %get-tuple-element.1624, (f32[1,16,16,768]{3,2,1,0:T(8,128)S(1)}, s32[4]{0:T(128)S(1)}, s32[]{:T(128)}, pred[]{:T(512)}, ...), branch_computations={%region_17.17_spmd, %region_18.26_spmd} | conditional | flops 2744454400 | bytes 198908256 | solution.py:199
  489.8 26.6 %conditional.10 = (f32[3,3,768,384]{3,2,1,0:T(8,128)}, f32[1,16,16,384]{3,2,1,0:T(8,128)S(1)}, f32[1,16,16,384]{3,2,1,0:T(8,128)}) conditional(s32[]{:T(128)} %convert_element_type.139, f32[3,3,768,384]{3,2,1,0:T(8,128)} %get-tuple-element.1624, (f32[1,16,16,768]{3,2,1,0:T(8,128)S(1)}, s32[4]{0:T(128)S(1)}, s32[]{:T(128)}, pred[]{:T(512)}, ...), branch_computations={%region_17.17_spmd, %region_18.26_spmd} | conditional | flops 2744454400 | bytes 198908256 | solution.py:199
  529.2 26.6 %conditional.10 = (f32[3,3,768,384]{3,2,1,0:T(8,128)}, f32[1,16,16,384]{3,2,1,0:T(8,128)S(1)}, f32[1,16,16,384]{3,2,1,0:T(8,128)}) conditional(s32[]{:T(128)} %convert_element_type.139, f32[3,3,768,384]{3,2,1,0:T(8,128)} %get-tuple-element.1624, (f32[1,16,16,768]{3,2,1,0:T(8,128)S(1)}, s32[4]{0:T(128)S(1)}, s32[]{:T(128)}, pred[]{:T(512)}, ...), branch_computations={%region_17.17_spmd, %region_18.26_spmd} | conditional | flops 2744454400 | bytes 198908256 | solution.py:199
  568.6 26.6 %conditional.10 = (f32[3,3,768,384]{3,2,1,0:T(8,128)}, f32[1,16,16,384]{3,2,1,0:T(8,128)S(1)}, f32[1,16,16,384]{3,2,1,0:T(8,128)}) conditional(s32[]{:T(128)} %convert_element_type.139, f32[3,3,768,384]{3,2,1,0:T(8,128)} %get-tuple-element.1624, (f32[1,16,16,768]{3,2,1,0:T(8,128)S(1)}, s32[4]{0:T(128)S(1)}, s32[]{:T(128)}, pred[]{:T(512)}, ...), branch_computations={%region_17.17_spmd, %region_18.26_spmd} | conditional | flops 2744454400 | bytes 198908256 | solution.py:199
  608.8 30.2 %collective-permute-start.2 = (f32[1,16,16,384]{3,2,1,0:T(8,128)S(1)}, f32[1,16,16,384]{3,2,1,0:T(8,128)S(1)}, u32[]{:S(2)}, u32[]{:S(2)}) collective-permute-start(f32[1,16,16,384]{3,2,1,0:T(8,128)S(1)} %get-tuple-element.1500), channel_id=1, source_target_pairs={{0,16},{16,32},{32,48},{48,64},{64,80},{80,96},{96,112},{1,17},{17... | collective-permute-start | bytes 1179656 | tf_op jit(solution)/shard_map/while/body/eval_jaxpr/ppermute | solution.py:14
  661.8 27.7 %collective-permute-start.2 = (f32[1,16,16,384]{3,2,1,0:T(8,128)S(1)}, f32[1,16,16,384]{3,2,1,0:T(8,128)S(1)}, u32[]{:S(2)}, u32[]{:S(2)}) collective-permute-start(f32[1,16,16,384]{3,2,1,0:T(8,128)S(1)} %get-tuple-element.1500), channel_id=1, source_target_pairs={{0,16},{16,32},{32,48},{48,64},{64,80},{80,96},{96,112},{1,17},{17... | collective-permute-start | bytes 1179656 | tf_op jit(solution)/shard_map/while/body/eval_jaxpr/ppermute | solution.py:14
  712.4 32.5 %collective-permute-start.2 = (f32[1,16,16,384]{3,2,1,0:T(8,128)S(1)}, f32[1,16,16,384]{3,2,1,0:T(8,128)S(1)}, u32[]{:S(2)}, u32[]{:S(2)}) collective-permute-start(f32[1,16,16,384]{3,2,1,0:T(8,128)S(1)} %get-tuple-element.1500), channel_id=1, source_target_pairs={{0,16},{16,32},{32,48},{48,64},{64,80},{80,96},{96,112},{1,17},{17... | collective-permute-start | bytes 1179656 | tf_op jit(solution)/shard_map/while/body/eval_jaxpr/ppermute | solution.py:14
  771.2 33.8 %collective-permute-start.2 = (f32[1,16,16,384]{3,2,1,0:T(8,128)S(1)}, f32[1,16,16,384]{3,2,1,0:T(8,128)S(1)}, u32[]{:S(2)}, u32[]{:S(2)}) collective-permute-start(f32[1,16,16,384]{3,2,1,0:T(8,128)S(1)} %get-tuple-element.1500), channel_id=1, source_target_pairs={{0,16},{16,32},{32,48},{48,64},{64,80},{80,96},{96,112},{1,17},{17... | collective-permute-start | bytes 1179656 | tf_op jit(solution)/shard_map/while/body/eval_jaxpr/ppermute | solution.py:14
  813.2 444.4 %while.83 = (s32[]{:T(128)}, f32[1,16,16,384]{3,2,1,0:T(8,128)S(1)}, f32[3,3,384,384]{3,2,1,0:T(8,128)}, s32[]{:T(128)}, f32[4,16,16,384]{3,2,1,0:T(8,128)}, /*i...) while((s32[]{:T(128)}, ...), condition=%wide.region_39.40_spmd, body=%wide.region_28.39_spmd.sunk | while | flops 1370015488 | bytes 93357616 | solution.py:232
  815.5 18.9 %collective-permute-done.3 = f32[1,16,16,384]{3,2,1,0:T(8,128)S(1)} collective-permute-done((f32[1,16,16,384]{3,2,1,0:T(8,128)}, f32[1,16,16,384]{3,2,1,0:T(8,128)S(1)}, u32[]{:S(2)}, u32[]{:S(2)}) %collective-permute-start.3) | collective-permute-done | bytes 393248 | tf_op jit(solution)/shard_map/while/body/eval_jaxpr/ppermute | solution.py:14
  836.5 22.5 %collective-permute-done.3 = f32[1,16,16,384]{3,2,1,0:T(8,128)S(1)} collective-permute-done((f32[1,16,16,384]{3,2,1,0:T(8,128)}, f32[1,16,16,384]{3,2,1,0:T(8,128)S(1)}, u32[]{:S(2)}, u32[]{:S(2)}) %collective-permute-start.3) | collective-permute-done | bytes 393248 | tf_op jit(solution)/shard_map/while/body/eval_jaxpr/ppermute | solution.py:14
  876.9 27.6 %collective-permute-done.3 = f32[1,16,16,384]{3,2,1,0:T(8,128)S(1)} collective-permute-done((f32[1,16,16,384]{3,2,1,0:T(8,128)}, f32[1,16,16,384]{3,2,1,0:T(8,128)S(1)}, u32[]{:S(2)}, u32[]{:S(2)}) %collective-permute-start.3) | collective-permute-done | bytes 393248 | tf_op jit(solution)/shard_map/while/body/eval_jaxpr/ppermute | solution.py:14
  922.0 28.1 %collective-permute-done.3 = f32[1,16,16,384]{3,2,1,0:T(8,128)S(1)} collective-permute-done((f32[1,16,16,384]{3,2,1,0:T(8,128)}, f32[1,16,16,384]{3,2,1,0:T(8,128)S(1)}, u32[]{:S(2)}, u32[]{:S(2)}) %collective-permute-start.3) | collective-permute-done | bytes 393248 | tf_op jit(solution)/shard_map/while/body/eval_jaxpr/ppermute | solution.py:14
  952.2 162.2 %collective-permute-done.3 = f32[1,16,16,384]{3,2,1,0:T(8,128)S(1)} collective-permute-done((f32[1,16,16,384]{3,2,1,0:T(8,128)}, f32[1,16,16,384]{3,2,1,0:T(8,128)S(1)}, u32[]{:S(2)}, u32[]{:S(2)}) %collective-permute-start.3) | collective-permute-done | bytes 393248 | tf_op jit(solution)/shard_map/while/body/eval_jaxpr/ppermute | solution.py:14
  1114.4 22.6 %conditional.11 = (f32[3,3,384,384]{3,2,1,0:T(8,128)}, f32[1,16,16,384]{3,2,1,0:T(8,128)}) conditional(s32[]{:T(128)} %convert_element_type.140, f32[3,3,384,384]{3,2,1,0:T(8,128)} %get-tuple-element.1671, (s32[]{:T(128)}, f32[4,16,16,384]{3,2,1,0:T(8,128)}, s32[4]{0:T(128)S(1)}, pred[]{:T(512)}, f32[4,16,16,384]{3,2,1,0:T(8,128)}, ...), branch_computations={%region_29.29_spmd, %region_30.38_spmd} | conditional | flops 1370015488 | bytes 91784480 | solution.py:227
  1150.3 22.6 %conditional.11 = (f32[3,3,384,384]{3,2,1,0:T(8,128)}, f32[1,16,16,384]{3,2,1,0:T(8,128)}) conditional(s32[]{:T(128)} %convert_element_type.140, f32[3,3,384,384]{3,2,1,0:T(8,128)} %get-tuple-element.1671, (s32[]{:T(128)}, f32[4,16,16,384]{3,2,1,0:T(8,128)}, s32[4]{0:T(128)S(1)}, pred[]{:T(512)}, f32[4,16,16,384]{3,2,1,0:T(8,128)}, ...), branch_computations={%region_29.29_spmd, %region_30.38_spmd} | conditional | flops 1370015488 | bytes 91784480 | solution.py:227
  1186.4 22.6 %conditional.11 = (f32[3,3,384,384]{3,2,1,0:T(8,128)}, f32[1,16,16,384]{3,2,1,0:T(8,128)}) conditional(s32[]{:T(128)} %convert_element_type.140, f32[3,3,384,384]{3,2,1,0:T(8,128)} %get-tuple-element.1671, (s32[]{:T(128)}, f32[4,16,16,384]{3,2,1,0:T(8,128)}, s32[4]{0:T(128)S(1)}, pred[]{:T(512)}, f32[4,16,16,384]{3,2,1,0:T(8,128)}, ...), branch_computations={%region_29.29_spmd, %region_30.38_spmd} | conditional | flops 1370015488 | bytes 91784480 | solution.py:227
  1225.1 22.6 %conditional.11 = (f32[3,3,384,384]{3,2,1,0:T(8,128)}, f32[1,16,16,384]{3,2,1,0:T(8,128)}) conditional(s32[]{:T(128)} %convert_element_type.140, f32[3,3,384,384]{3,2,1,0:T(8,128)} %get-tuple-element.1671, (s32[]{:T(128)}, f32[4,16,16,384]{3,2,1,0:T(8,128)}, s32[4]{0:T(128)S(1)}, pred[]{:T(512)}, f32[4,16,16,384]{3,2,1,0:T(8,128)}, ...), branch_computations={%region_29.29_spmd, %region_30.38_spmd} | conditional | flops 1370015488 | bytes 91784480 | solution.py:227
  1258.3 70.2 %reduce-scatter.3.cloned.1.call-done = f32[1,3,3,24,384]{4,3,2,1,0:T(8,128)} async-done(((f32[1,3,3,384,384]{4,3,2,1,0:T(8,128)}), f32[1,3,3,24,384]{4,3,2,1,0:T(8,128)}) %reduce-scatter.3.cloned.1.call-update) | async-done | bytes 331792 | tf_op jit(solution)/shard_map/reduce_scatter | solution.py:234
  1328.5 80.4 %reduce-scatter.5.cloned.1.call-done = f32[1,3,3,48,384]{4,3,2,1,0:T(8,128)} async-done(((f32[1,3,3,768,384]{4,3,2,1,0:T(8,128)}), f32[1,3,3,48,384]{4,3,2,1,0:T(8,128)}) %reduce-scatter.5.cloned.1.call-update) | async-done | bytes 663568 | tf_op jit(solution)/shard_map/reduce_scatter | solution.py:235
  (999 shorter events, 880.0 us)
Async XLA Ops:
  7.2 1321.3 %reduce-scatter.3.cloned.1.call-start = ((), (), s32[]{:S(2)}) async-start(), calls=%async_computation.2 | async-start | bytes 5640192 | tf_op jit(solution)/shard_map/reduce_scatter | solution.py:234
  86.3 15.1 %collective-permute-start = (f32[1,16,16,384]{3,2,1,0:T(8,128)S(1)}, f32[1,16,16,384]{3,2,1,0:T(8,128)}, u32[]{:S(2)}, u32[]{:S(2)}) collective-permute-start(f32[1,16,16,384]{3,2,1,0:T(8,128)S(1)} %get-tuple-element.1695), channel_id=1, source_target_pairs={{0,16},{16,32},{32,48},{48,64},{64,80},{80,96},{96,112},{1,17},{17... | collective-permute-start | bytes 1179656 | tf_op jit(solution)/shard_map/while/body/eval_jaxpr/ppermute | solution.py:14
  142.4 17.9 %collective-permute-start = (f32[1,16,16,384]{3,2,1,0:T(8,128)S(1)}, f32[1,16,16,384]{3,2,1,0:T(8,128)}, u32[]{:S(2)}, u32[]{:S(2)}) collective-permute-start(f32[1,16,16,384]{3,2,1,0:T(8,128)S(1)} %get-tuple-element.1695), channel_id=1, source_target_pairs={{0,16},{16,32},{32,48},{48,64},{64,80},{80,96},{96,112},{1,17},{17... | collective-permute-start | bytes 1179656 | tf_op jit(solution)/shard_map/while/body/eval_jaxpr/ppermute | solution.py:14
  177.8 18.7 %collective-permute-start = (f32[1,16,16,384]{3,2,1,0:T(8,128)S(1)}, f32[1,16,16,384]{3,2,1,0:T(8,128)}, u32[]{:S(2)}, u32[]{:S(2)}) collective-permute-start(f32[1,16,16,384]{3,2,1,0:T(8,128)S(1)} %get-tuple-element.1695), channel_id=1, source_target_pairs={{0,16},{16,32},{32,48},{48,64},{64,80},{80,96},{96,112},{1,17},{17... | collective-permute-start | bytes 1179656 | tf_op jit(solution)/shard_map/while/body/eval_jaxpr/ppermute | solution.py:14
  201.3 14.5 %collective-permute-start.1 = (f32[1,16,16,384]{3,2,1,0:T(8,128)S(1)}, f32[1,16,16,384]{3,2,1,0:T(8,128)S(1)}, u32[]{:S(2)}, u32[]{:S(2)}) collective-permute-start(f32[1,16,16,384]{3,2,1,0:T(8,128)S(1)} %get-tuple-element.1696), channel_id=1, source_target_pairs={{16,0},{32,16},{48,32},{64,48},{80,64},{96,80},{112,96},{17,1},{33... | collective-permute-start | bytes 1179656 | tf_op jit(solution)/shard_map/while/body/eval_jaxpr/ppermute | solution.py:14
  218.0 15.8 %collective-permute-start.1 = (f32[1,16,16,384]{3,2,1,0:T(8,128)S(1)}, f32[1,16,16,384]{3,2,1,0:T(8,128)S(1)}, u32[]{:S(2)}, u32[]{:S(2)}) collective-permute-start(f32[1,16,16,384]{3,2,1,0:T(8,128)S(1)} %get-tuple-element.1696), channel_id=1, source_target_pairs={{16,0},{32,16},{48,32},{64,48},{80,64},{96,80},{112,96},{17,1},{33... | collective-permute-start | bytes 1179656 | tf_op jit(solution)/shard_map/while/body/eval_jaxpr/ppermute | solution.py:14
  235.9 17.3 %collective-permute-start.1 = (f32[1,16,16,384]{3,2,1,0:T(8,128)S(1)}, f32[1,16,16,384]{3,2,1,0:T(8,128)S(1)}, u32[]{:S(2)}, u32[]{:S(2)}) collective-permute-start(f32[1,16,16,384]{3,2,1,0:T(8,128)S(1)} %get-tuple-element.1696), channel_id=1, source_target_pairs={{16,0},{32,16},{48,32},{64,48},{80,64},{96,80},{112,96},{17,1},{33... | collective-permute-start | bytes 1179656 | tf_op jit(solution)/shard_map/while/body/eval_jaxpr/ppermute | solution.py:14
  255.3 20.3 %collective-permute-start.1 = (f32[1,16,16,384]{3,2,1,0:T(8,128)S(1)}, f32[1,16,16,384]{3,2,1,0:T(8,128)S(1)}, u32[]{:S(2)}, u32[]{:S(2)}) collective-permute-start(f32[1,16,16,384]{3,2,1,0:T(8,128)S(1)} %get-tuple-element.1696), channel_id=1, source_target_pairs={{16,0},{32,16},{48,32},{64,48},{80,64},{96,80},{112,96},{17,1},{33... | collective-permute-start | bytes 1179656 | tf_op jit(solution)/shard_map/while/body/eval_jaxpr/ppermute | solution.py:14
  277.8 16.9 %collective-permute-start.1 = (f32[1,16,16,384]{3,2,1,0:T(8,128)S(1)}, f32[1,16,16,384]{3,2,1,0:T(8,128)S(1)}, u32[]{:S(2)}, u32[]{:S(2)}) collective-permute-start(f32[1,16,16,384]{3,2,1,0:T(8,128)S(1)} %get-tuple-element.1696), channel_id=1, source_target_pairs={{16,0},{32,16},{48,32},{64,48},{80,64},{96,80},{112,96},{17,1},{33... | collective-permute-start | bytes 1179656 | tf_op jit(solution)/shard_map/while/body/eval_jaxpr/ppermute | solution.py:14
  308.6 40.3 %collective-permute-start.1 = (f32[1,16,16,384]{3,2,1,0:T(8,128)S(1)}, f32[1,16,16,384]{3,2,1,0:T(8,128)S(1)}, u32[]{:S(2)}, u32[]{:S(2)}) collective-permute-start(f32[1,16,16,384]{3,2,1,0:T(8,128)S(1)} %get-tuple-element.1696), channel_id=1, source_target_pairs={{16,0},{32,16},{48,32},{64,48},{80,64},{96,80},{112,96},{17,1},{33... | collective-permute-start | bytes 1179656 | tf_op jit(solution)/shard_map/while/body/eval_jaxpr/ppermute | solution.py:14
  406.6 16.3 %collective-permute-start.1 = (f32[1,16,16,384]{3,2,1,0:T(8,128)S(1)}, f32[1,16,16,384]{3,2,1,0:T(8,128)S(1)}, u32[]{:S(2)}, u32[]{:S(2)}) collective-permute-start(f32[1,16,16,384]{3,2,1,0:T(8,128)S(1)} %get-tuple-element.1696), channel_id=1, source_target_pairs={{16,0},{32,16},{48,32},{64,48},{80,64},{96,80},{112,96},{17,1},{33... | collective-permute-start | bytes 1179656 | tf_op jit(solution)/shard_map/while/body/eval_jaxpr/ppermute | solution.py:14
  608.8 35.5 %collective-permute-start.2 = (f32[1,16,16,384]{3,2,1,0:T(8,128)S(1)}, f32[1,16,16,384]{3,2,1,0:T(8,128)S(1)}, u32[]{:S(2)}, u32[]{:S(2)}) collective-permute-start(f32[1,16,16,384]{3,2,1,0:T(8,128)S(1)} %get-tuple-element.1500), channel_id=1, source_target_pairs={{0,16},{16,32},{32,48},{48,64},{64,80},{80,96},{96,112},{1,17},{17... | collective-permute-start | bytes 1179656 | tf_op jit(solution)/shard_map/while/body/eval_jaxpr/ppermute | solution.py:14
  661.8 33.0 %collective-permute-start.2 = (f32[1,16,16,384]{3,2,1,0:T(8,128)S(1)}, f32[1,16,16,384]{3,2,1,0:T(8,128)S(1)}, u32[]{:S(2)}, u32[]{:S(2)}) collective-permute-start(f32[1,16,16,384]{3,2,1,0:T(8,128)S(1)} %get-tuple-element.1500), channel_id=1, source_target_pairs={{0,16},{16,32},{32,48},{48,64},{64,80},{80,96},{96,112},{1,17},{17... | collective-permute-start | bytes 1179656 | tf_op jit(solution)/shard_map/while/body/eval_jaxpr/ppermute | solution.py:14
  712.4 37.8 %collective-permute-start.2 = (f32[1,16,16,384]{3,2,1,0:T(8,128)S(1)}, f32[1,16,16,384]{3,2,1,0:T(8,128)S(1)}, u32[]{:S(2)}, u32[]{:S(2)}) collective-permute-start(f32[1,16,16,384]{3,2,1,0:T(8,128)S(1)} %get-tuple-element.1500), channel_id=1, source_target_pairs={{0,16},{16,32},{32,48},{48,64},{64,80},{80,96},{96,112},{1,17},{17... | collective-permute-start | bytes 1179656 | tf_op jit(solution)/shard_map/while/body/eval_jaxpr/ppermute | solution.py:14
  771.2 39.1 %collective-permute-start.2 = (f32[1,16,16,384]{3,2,1,0:T(8,128)S(1)}, f32[1,16,16,384]{3,2,1,0:T(8,128)S(1)}, u32[]{:S(2)}, u32[]{:S(2)}) collective-permute-start(f32[1,16,16,384]{3,2,1,0:T(8,128)S(1)} %get-tuple-element.1500), channel_id=1, source_target_pairs={{0,16},{16,32},{32,48},{48,64},{64,80},{80,96},{96,112},{1,17},{17... | collective-permute-start | bytes 1179656 | tf_op jit(solution)/shard_map/while/body/eval_jaxpr/ppermute | solution.py:14
  814.2 20.2 %collective-permute-start.3 = (f32[1,16,16,384]{3,2,1,0:T(8,128)}, f32[1,16,16,384]{3,2,1,0:T(8,128)S(1)}, u32[]{:S(2)}, u32[]{:S(2)}) collective-permute-start(f32[1,16,16,384]{3,2,1,0:T(8,128)} %get-tuple-element.1515), channel_id=1, source_target_pairs={{16,0},{32,16},{48,32},{64,48},{80,64},{96,80},{112,96},{17,1},{33... | collective-permute-start | bytes 1179656 | tf_op jit(solution)/shard_map/while/body/eval_jaxpr/ppermute | solution.py:14
  835.2 23.8 %collective-permute-start.3 = (f32[1,16,16,384]{3,2,1,0:T(8,128)}, f32[1,16,16,384]{3,2,1,0:T(8,128)S(1)}, u32[]{:S(2)}, u32[]{:S(2)}) collective-permute-start(f32[1,16,16,384]{3,2,1,0:T(8,128)} %get-tuple-element.1515), channel_id=1, source_target_pairs={{16,0},{32,16},{48,32},{64,48},{80,64},{96,80},{112,96},{17,1},{33... | collective-permute-start | bytes 1179656 | tf_op jit(solution)/shard_map/while/body/eval_jaxpr/ppermute | solution.py:14
  859.8 15.1 %collective-permute-start.3 = (f32[1,16,16,384]{3,2,1,0:T(8,128)}, f32[1,16,16,384]{3,2,1,0:T(8,128)S(1)}, u32[]{:S(2)}, u32[]{:S(2)}) collective-permute-start(f32[1,16,16,384]{3,2,1,0:T(8,128)} %get-tuple-element.1515), channel_id=1, source_target_pairs={{16,0},{32,16},{48,32},{64,48},{80,64},{96,80},{112,96},{17,1},{33... | collective-permute-start | bytes 1179656 | tf_op jit(solution)/shard_map/while/body/eval_jaxpr/ppermute | solution.py:14
  875.6 28.9 %collective-permute-start.3 = (f32[1,16,16,384]{3,2,1,0:T(8,128)}, f32[1,16,16,384]{3,2,1,0:T(8,128)S(1)}, u32[]{:S(2)}, u32[]{:S(2)}) collective-permute-start(f32[1,16,16,384]{3,2,1,0:T(8,128)} %get-tuple-element.1515), channel_id=1, source_target_pairs={{16,0},{32,16},{48,32},{64,48},{80,64},{96,80},{112,96},{17,1},{33... | collective-permute-start | bytes 1179656 | tf_op jit(solution)/shard_map/while/body/eval_jaxpr/ppermute | solution.py:14
  905.3 14.6 %collective-permute-start.3 = (f32[1,16,16,384]{3,2,1,0:T(8,128)}, f32[1,16,16,384]{3,2,1,0:T(8,128)S(1)}, u32[]{:S(2)}, u32[]{:S(2)}) collective-permute-start(f32[1,16,16,384]{3,2,1,0:T(8,128)} %get-tuple-element.1515), channel_id=1, source_target_pairs={{16,0},{32,16},{48,32},{64,48},{80,64},{96,80},{112,96},{17,1},{33... | collective-permute-start | bytes 1179656 | tf_op jit(solution)/shard_map/while/body/eval_jaxpr/ppermute | solution.py:14
  920.7 29.4 %collective-permute-start.3 = (f32[1,16,16,384]{3,2,1,0:T(8,128)}, f32[1,16,16,384]{3,2,1,0:T(8,128)S(1)}, u32[]{:S(2)}, u32[]{:S(2)}) collective-permute-start(f32[1,16,16,384]{3,2,1,0:T(8,128)} %get-tuple-element.1515), channel_id=1, source_target_pairs={{16,0},{32,16},{48,32},{64,48},{80,64},{96,80},{112,96},{17,1},{33... | collective-permute-start | bytes 1179656 | tf_op jit(solution)/shard_map/while/body/eval_jaxpr/ppermute | solution.py:14
  950.9 163.5 %collective-permute-start.3 = (f32[1,16,16,384]{3,2,1,0:T(8,128)}, f32[1,16,16,384]{3,2,1,0:T(8,128)S(1)}, u32[]{:S(2)}, u32[]{:S(2)}) collective-permute-start(f32[1,16,16,384]{3,2,1,0:T(8,128)} %get-tuple-element.1515), channel_id=1, source_target_pairs={{16,0},{32,16},{48,32},{64,48},{80,64},{96,80},{112,96},{17,1},{33... | collective-permute-start | bytes 1179656 | tf_op jit(solution)/shard_map/while/body/eval_jaxpr/ppermute | solution.py:14
  1209.0 16.0 %collective-permute-start.3 = (f32[1,16,16,384]{3,2,1,0:T(8,128)}, f32[1,16,16,384]{3,2,1,0:T(8,128)S(1)}, u32[]{:S(2)}, u32[]{:S(2)}) collective-permute-start(f32[1,16,16,384]{3,2,1,0:T(8,128)} %get-tuple-element.1515), channel_id=1, source_target_pairs={{16,0},{32,16},{48,32},{64,48},{80,64},{96,80},{112,96},{17,1},{33... | collective-permute-start | bytes 1179656 | tf_op jit(solution)/shard_map/while/body/eval_jaxpr/ppermute | solution.py:14
  1257.6 151.3 %reduce-scatter.5.cloned.1.call-start = ((), (), s32[]{:S(2)}) async-start(), calls=%async_computation.3 | async-start | bytes 11280384 | tf_op jit(solution)/shard_map/reduce_scatter | solution.py:235
  (65 other events, 367.4 us)
Sparse Core Ops, SparseCore 0:
  1257.7 70.7 reduce-scatter.2
  1331.5 77.3 reduce-scatter.4
where the time goes:
time: 1420 us
  waiting for transfers between devices  709 us (50%)
  starting transfers between devices  269 us (19%)
  other arithmetic  195 us (14%)
  local copies, waits for them, and re-layouts  120 us (8%)
  matrix products  94.4 us (7%)
  loops' own time  15.1 us (1%)
    ppermute x44, waiting for transfers between devices, passed_along(): lax.ppermute(value, axis, [(source, source + steps) for source in range(i...  558 us
    ppermute x44, starting transfers between devices, passed_along(): lax.ppermute(value, axis, [(source, source + steps) for source in range(i...  269 us
    dynamic_update_slice x55, other arithmetic, store_row(): lax.dynamic_update_slice_in_dim(buffer, jnp.where(active, piece, kept), s...  106 us
    reduce_scatter x1, waiting for transfers between devices, shards(): lax.psum_scatter(dec_acc[None], 'dp', scatter_dimension=3, tiled=True)  80.4 us
    reduce_scatter x1, waiting for transfers between devices, shards(): lax.psum_scatter(enc_acc[None], 'dp', scatter_dimension=3, tiled=True)  70.2 us
    cond x80, local copies, waits for them, and re-layouts  44.1 us
    dot_general x72, matrix products, conv_back(): lax.dot_general(window, weight[row_off, col_off], (((1,), (1,)), ((), ())...  41.6 us
    dynamic_slice x38, local copies, waits for them, and re-layouts, pick_row(): return lax.dynamic_slice_in_dim(buffer, slot_index, 1, 0)  32.3 us
  transfers between devices with their start and end apart: 46, of which 46 were waited for; matrix products, arithmetic and copies ran while one was open for 4% of the time, Pallas kernels for 0%

commit v1 on v0

v1 whole, which is shorter than its diff:
```python
import math

import jax
import jax.numpy as jnp
from jax import lax
from jax.sharding import PartitionSpec as P

GROUPS = 32


def passed_along(value, axis, steps):
    count = lax.axis_size(axis)
    initial, last = (max(0, -steps), min(count, count - steps))
    return lax.ppermute(value, axis, [(source, source + steps) for source in range(initial, last)])


def embed(stamps_in, channels):
    half_width = channels // 2
    frequency = jnp.exp(-math.log(10000.0) * jnp.arange(half_width, dtype=jnp.float32) / half_width)
    angles = stamps_in.astype(jnp.float32)[:, None] * frequency[None, :]
    return jnp.concatenate([jnp.sin(angles), jnp.cos(angles)], axis=1)


def activate(inputs_f32, stamps_in):
    batch_rows, height, breadth, channels = inputs_f32.shape
    grouped = inputs_f32.reshape(batch_rows, height * breadth, GROUPS, channels // GROUPS)
    group_mean = jnp.mean(grouped, axis=(1, 3), keepdims=True)
    centered = grouped - group_mean
    group_var = jnp.mean(centered * centered, axis=(1, 3), keepdims=True)
    normed = (centered * lax.rsqrt(group_var + 1e-05)).reshape(inputs_f32.shape)
    modulate = 1.0 + 0.5 * embed(stamps_in, channels)[:, None, None, :]
    return jax.nn.silu(normed * modulate)


def conv_apply(activations, weight):
    batch_rows, height, breadth, channels = activations.shape
    padded = jnp.pad(activations, ((0, 0), (1, 1), (1, 1), (0, 0)))
    summed = jnp.zeros((batch_rows * height * breadth, weight.shape[3]), jnp.float32)
    for row_off in range(3):
        for col_off in range(3):
            window = padded[:, row_off : row_off + height, col_off : col_off + breadth, :].reshape(
                -1, channels
            )
            summed = summed + jnp.dot(
                window, weight[row_off, col_off], preferred_element_type=jnp.float32
            )
    return summed.reshape(batch_rows, height, breadth, weight.shape[3])


def conv_back(cotangent, weight):
    batch_rows, height, breadth, outputs = cotangent.shape
    padded = jnp.pad(cotangent.astype(jnp.bfloat16), ((0, 0), (1, 1), (1, 1), (0, 0)))
    summed = jnp.zeros((batch_rows * height * breadth, weight.shape[2]), jnp.float32)
    for row_off in range(3):
        for col_off in range(3):
            window = padded[
                :, 2 - row_off : 2 - row_off + height, 2 - col_off : 2 - col_off + breadth, :
            ].reshape(-1, outputs)
            summed = summed + lax.dot_general(
                window,
                weight[row_off, col_off],
                (((1,), (1,)), ((), ())),
                preferred_element_type=jnp.float32,
            )
    return summed.reshape(batch_rows, height, breadth, weight.shape[2])


def conv_weight_grad(activations, cotangent):
    batch_rows, height, breadth, channels = activations.shape
    padded = jnp.pad(activations, ((0, 0), (1, 1), (1, 1), (0, 0)))
    flat_cot = cotangent.astype(jnp.bfloat16).reshape(-1, cotangent.shape[3])
    kernel_rows = []
    for row_off in range(3):
        kernel_cols = []
        for col_off in range(3):
            window = padded[:, row_off : row_off + height, col_off : col_off + breadth, :].reshape(
                -1, channels
            )
            kernel_cols.append(
                lax.dot_general(
                    window, flat_cot, (((0,), (0,)), ((), ())), preferred_element_type=jnp.float32
                )
            )
        kernel_rows.append(jnp.stack(kernel_cols))
    return jnp.stack(kernel_rows)


def block_forward(inputs, residual, weight, stamps_in):
    activations = activate(inputs, stamps_in).astype(jnp.bfloat16)
    return residual + conv_apply(activations, weight)


def block_backward(inputs, weight, stamps_in, cotangent):
    activated, pullback = jax.vjp(lambda inner_field: activate(inner_field, stamps_in), inputs)
    activations = activated.astype(jnp.bfloat16)
    weight_grad = conv_weight_grad(activations, cotangent)
    input_grad = pullback(conv_back(cotangent, weight))[0]
    return (input_grad, weight_grad)


def noise_levels(stamps_in):
    phase = (stamps_in.astype(jnp.float32) / 1000.0 + 0.008) / 1.008 * (math.pi / 2.0)
    signal = jnp.cos(phase) ** 2
    return (jnp.sqrt(signal), jnp.sqrt(1.0 - signal))


def pick_row(buffer, slot_index):
    return lax.dynamic_slice_in_dim(buffer, slot_index, 1, 0)


def put_row(buffer, piece, slot_index):
    return lax.dynamic_update_slice_in_dim(buffer, piece, slot_index, 0)


def shards(clean, noise, stamps, enc_weight, dec_weight):
    sections = lax.axis_size("section")
    section_index = lax.axis_index("section")
    last_section = sections - 1
    samples = clean.shape[0]
    channels = clean.shape[3]
    enc_kernel = enc_weight[0]
    dec_kernel = dec_weight[0]
    keep_level, spread_level = noise_levels(stamps)
    noisy = keep_level[:, None, None, None] * clean.astype(jnp.float32) + spread_level[
        :, None, None, None
    ] * noise.astype(jnp.float32)
    factor = 1.0 / math.sqrt(samples * lax.axis_size("dp") * clean.shape[1] * clean.shape[2])
    blank_piece = jnp.zeros((1,) + clean.shape[1:], jnp.float32)
    blank_buffer = jnp.zeros((samples + 2,) + clean.shape[1:], jnp.float32)

    enc_fwd_off = section_index
    dec_fwd_off = 2 * sections - 1 - section_index
    dec_back_off = 2 * sections + section_index
    enc_back_off = 4 * sections - 1 - section_index

    def locate(tick_now, offset):
        sample_id = tick_now - offset
        active = (sample_id >= 0) & (sample_id < samples)
        clipped = jnp.clip(sample_id, 0, samples - 1)
        slot_index = jnp.clip(sample_id, -1, samples) + 1
        return (active, clipped, slot_index)

    def make_tick(tasks):
        def tick(tick_now, carried):
            (fwd_in, bwd_in, enc_inputs, skips, dec_inputs, outputs, skip_grads, up_grads,
             enc_acc, dec_acc) = carried
            fwd_out = blank_piece
            bwd_out = blank_piece
            if "enc_fwd" in tasks:
                active, sample_at, slot_index = locate(tick_now, enc_fwd_off)
                source = jnp.where(section_index == 0, pick_row(noisy, sample_at), fwd_in)
                stamp_one = pick_row(stamps, sample_at)
                result = lax.cond(
                    active,
                    lambda: block_forward(source, source, enc_kernel, stamp_one),
                    lambda: blank_piece,
                )
                enc_inputs = put_row(enc_inputs, source, slot_index)
                skips = put_row(skips, result, slot_index)
                fwd_out = jnp.where(active, result, fwd_out)
            if "dec_fwd" in tasks:
                active, sample_at, slot_index = locate(tick_now, dec_fwd_off)
                skip_piece = pick_row(skips, slot_index)
                source = jnp.where(section_index == last_section, skip_piece, bwd_in)
                joined = jnp.concatenate([source, skip_piece], axis=3)
                stamp_one = pick_row(stamps, sample_at)
                result = lax.cond(
                    active,
                    lambda: block_forward(joined, source, dec_kernel, stamp_one),
                    lambda: blank_piece,
                )
                dec_inputs = put_row(dec_inputs, source, slot_index)
                outputs = put_row(outputs, result, slot_index)
                bwd_out = jnp.where(active, result, bwd_out)
            if "dec_back" in tasks:
                active, sample_at, slot_index = locate(tick_now, dec_back_off)
                top_grad = factor * (
                    pick_row(outputs, slot_index) - pick_row(noise, sample_at).astype(jnp.float32)
                )
                flowing = jnp.where(section_index == 0, top_grad, fwd_in)
                joined = jnp.concatenate(
                    [pick_row(dec_inputs, slot_index), pick_row(skips, slot_index)], axis=3
                )
                stamp_one = pick_row(stamps, sample_at)

                def decoder_working(accum):
                    input_grad, weight_grad = block_backward(joined, dec_kernel, stamp_one, flowing)
                    up_piece = input_grad[..., :channels] + flowing
                    return (accum + weight_grad, up_piece, input_grad[..., channels:])

                def decoder_resting(accum):
                    return (accum, blank_piece, blank_piece)

                dec_acc, up_piece, skip_grad = lax.cond(
                    active, decoder_working, decoder_resting, dec_acc
                )
                skip_grads = put_row(skip_grads, skip_grad, slot_index)
                up_grads = put_row(up_grads, up_piece, slot_index)
                fwd_out = jnp.where(active, up_piece, fwd_out)
            if "enc_back" in tasks:
                active, sample_at, slot_index = locate(tick_now, enc_back_off)
                arriving = jnp.where(
                    section_index == last_section, pick_row(up_grads, slot_index), bwd_in
                )
                merged = arriving + pick_row(skip_grads, slot_index)
                block_input = pick_row(enc_inputs, slot_index)
                stamp_one = pick_row(stamps, sample_at)

                def encoder_working(accum):
                    input_grad, weight_grad = block_backward(
                        block_input, enc_kernel, stamp_one, merged
                    )
                    return (accum + weight_grad, input_grad + merged)

                def encoder_resting(accum):
                    return (accum, blank_piece)

                enc_acc, down_piece = lax.cond(active, encoder_working, encoder_resting, enc_acc)
                bwd_out = jnp.where(active, down_piece, bwd_out)
            if "enc_fwd" in tasks or "dec_back" in tasks:
                fwd_in = passed_along(fwd_out, "section", 1)
            if "dec_fwd" in tasks or "enc_back" in tasks:
                bwd_in = passed_along(bwd_out, "section", -1)
            return (fwd_in, bwd_in, enc_inputs, skips, dec_inputs, outputs, skip_grads, up_grads,
                    enc_acc, dec_acc)

        return tick

    dec_fwd_begin = sections
    dec_back_begin = 2 * sections
    enc_back_begin = 3 * sections
    dec_back_end = dec_back_begin + last_section + samples
    ticks_total = 4 * sections - 1 + samples
    stages = [
        (0, dec_fwd_begin, ("enc_fwd",)),
        (dec_fwd_begin, dec_back_begin, ("enc_fwd", "dec_fwd")),
        (dec_back_begin, enc_back_begin, ("dec_fwd", "dec_back")),
        (enc_back_begin, dec_back_end, ("dec_back", "enc_back")),
    ]
    carried = (
        blank_piece, blank_piece, blank_buffer, blank_buffer, blank_buffer, blank_buffer,
        blank_buffer, blank_buffer,
        jnp.zeros(enc_kernel.shape, jnp.float32), jnp.zeros(dec_kernel.shape, jnp.float32),
    )
    for begin, end, tasks in stages:
        carried = lax.fori_loop(begin, end, make_tick(tasks), carried)
    dec_acc = carried[9]
    dec_share = lax.psum_scatter(dec_acc[None], "dp", scatter_dimension=3, tiled=True)
    carried = lax.fori_loop(dec_back_end, ticks_total, make_tick(("enc_back",)), carried)
    enc_acc = carried[8]
    enc_share = lax.psum_scatter(enc_acc[None], "dp", scatter_dimension=3, tiled=True)
    return (enc_share, dec_share)


def solution(mesh):
    placed = (
        P("dp", None, None, None),
        P("dp", None, None, None),
        P("dp"),
        P("section", None, None, None, None),
        P("section", None, None, None, None),
    )
    return jax.shard_map(
        shards,
        mesh=mesh,
        in_specs=placed,
        out_specs=(P("section", None, None, "dp", None), P("section", None, None, "dp", None)),
        check_vma=False,
    )
```

time: 1420 us -> 1510 us (1.063)
  starting transfers between devices: 269 us -> 373 us
  waiting for transfers between devices: 709 us -> 639 us
  other arithmetic: 195 us -> 227 us
  local copies, waits for them, and re-layouts: 120 us -> 136 us
    ppermute x44 -> x54, starting transfers between devices: 269 us -> 373 us  [passed_along(): lax.ppermute(value, axis, [(source, source + steps) for source in range(i...]
    ppermute x44 -> x54, waiting for transfers between devices: 558 us -> 488 us  [passed_along(): lax.ppermute(value, axis, [(source, source + steps) for source in range(i...]
    dynamic_slice x38 -> x27, local copies, waits for them, and re-layouts: 32.3 us -> 21.4 us  [pick_row(): return lax.dynamic_slice_in_dim(buffer, slot_index, 1, 0)]
    dynamic_update_slice x55 -> x67, other arithmetic: 106 us -> 111 us  [put_row(): return lax.dynamic_update_slice_in_dim(buffer, piece, slot_index, 0)]
    cond x80 -> x88, local copies, waits for them, and re-layouts: 44.1 us -> 48.3 us
  transfers between devices with their start and end apart: 46 -> 56, of which waited for: 46 -> 40; matrix products, arithmetic and copies ran while one was open for 4% -> 11% of each run, Pallas kernels for 0% -> 0%
where the time goes in v1:
time: 1510 us; the launch traced here: 1490 us
  waiting for transfers between devices  639 us (42%)
  starting transfers between devices  373 us (25%)
  other arithmetic  227 us (15%)
  local copies, waits for them, and re-layouts  136 us (9%)
  matrix products  87.6 us (6%)
  loops' own time  15.7 us (1%)
    ppermute x54, waiting for transfers between devices, passed_along(): lax.ppermute(value, axis, [(source, source + steps) for source in range(i...  488 us
    ppermute x54, starting transfers between devices, passed_along(): lax.ppermute(value, axis, [(source, source + steps) for source in range(i...  373 us
    dynamic_update_slice x67, other arithmetic, put_row(): return lax.dynamic_update_slice_in_dim(buffer, piece, slot_index, 0)  111 us
    reduce_scatter x1, waiting for transfers between devices, shards(): lax.psum_scatter(dec_acc[None], 'dp', scatter_dimension=3, tiled=True)  80.4 us
    reduce_scatter x1, waiting for transfers between devices, shards(): lax.psum_scatter(enc_acc[None], 'dp', scatter_dimension=3, tiled=True)  70.6 us
    cond x88, local copies, waits for them, and re-layouts  48.3 us
    dot_general x72, matrix products, conv_back(): lax.dot_general(window, weight[row_off, col_off], (((1,), (1,)), ((), ())...  34.5 us
  transfers between devices with their start and end apart: 56, of which 40 were waited for; matrix products, arithmetic and copies ran while one was open for 11% of the time, Pallas kernels for 0%

profile of v1, /device:TPU:0, one launch (start us, length us, event | category | flops | bytes accessed | tf_op | source)
XLA Modules:
  0.0 1492.6 jit_solution(13523138747076557864)
XLA Ops:
  14.8 130.9 %while.128 = (s32[]{:T(128)}, f32[1,16,16,384]{3,2,1,0:T(8,128)}, f32[6,16,16,384]{3,2,1,0:T(8,128)}, f32[6,16,16,384]{3,2,1,0:T(8,128)}, s32[]{:T(128)}, /*inde...) while((s32[]{:T(128)}, f32[1,16,16,384]{3,2,1,0:T(8,128)}, ...), condition=%wide.region_7.8_spmd, body=%wide.region_0.7_spmd.sunk | while | flops 681739776 | bytes 19793804 | solution.py:246
  149.0 277.1 %while.129 = (s32[]{:T(128)}, f32[1,16,16,384]{3,2,1,0:T(8,128)}, f32[1,16,16,384]{3,2,1,0:T(8,128)S(1)}, f32[6,16,16,384]{3,2,1,0:T(8,128)}, f32[6,16,16,384]{3...) while((s32[]{:T(128)}, f32[1,16,16,384]{3,2,1,0:T(8,128)}, ...), condition=%wide.region_21.22_spmd, body=%wide.region_8.21_spmd.sunk | while | flops 2044334592 | bytes 70388472 | solution.py:246
  434.4 336.9 %while.130 = (s32[]{:T(128)}, f32[1,16,16,384]{3,2,1,0:T(8,128)}, f32[1,16,16,384]{3,2,1,0:T(8,128)S(1)}, f32[6,16,16,384]{3,2,1,0:T(8,128)}, f32[6,16,16,384]{3...) while((s32[]{:T(128)}, f32[1,16,16,384]{3,2,1,0:T(8,128)}, ...), condition=%wide.region_39.40_spmd, body=%wide.region_22.39_spmd.sunk | while | flops 4107442432 | bytes 255209552 | solution.py:246
  449.1 27.6 %conditional.20 = (f32[3,3,768,384]{3,2,1,0:T(8,128)}, f32[1,16,16,384]{3,2,1,0:T(8,128)}, f32[1,16,16,384]{3,2,1,0:T(8,128)S(1)}) conditional(s32[]{:T(128)} %convert_element_type.285, f32[3,3,768,384]{3,2,1,0:T(8,128)} %get-tuple-element.3287, (f32[1,16,16,768]{3,2,1,0:T(8,128)S(1)}, s32[4]{0:T(128)S(1)}, s32[]{:T(128)}, pred[]{:T(512)}, ...), branch_computations={%region_29.29_spmd, %region_30.38_spmd} | conditional | flops 2744454400 | bytes 197338432 | solution.py:194
  499.5 27.6 %conditional.20 = (f32[3,3,768,384]{3,2,1,0:T(8,128)}, f32[1,16,16,384]{3,2,1,0:T(8,128)}, f32[1,16,16,384]{3,2,1,0:T(8,128)S(1)}) conditional(s32[]{:T(128)} %convert_element_type.285, f32[3,3,768,384]{3,2,1,0:T(8,128)} %get-tuple-element.3287, (f32[1,16,16,768]{3,2,1,0:T(8,128)S(1)}, s32[4]{0:T(128)S(1)}, s32[]{:T(128)}, pred[]{:T(512)}, ...), branch_computations={%region_29.29_spmd, %region_30.38_spmd} | conditional | flops 2744454400 | bytes 197338432 | solution.py:194
  553.9 27.6 %conditional.20 = (f32[3,3,768,384]{3,2,1,0:T(8,128)}, f32[1,16,16,384]{3,2,1,0:T(8,128)}, f32[1,16,16,384]{3,2,1,0:T(8,128)S(1)}) conditional(s32[]{:T(128)} %convert_element_type.285, f32[3,3,768,384]{3,2,1,0:T(8,128)} %get-tuple-element.3287, (f32[1,16,16,768]{3,2,1,0:T(8,128)S(1)}, s32[4]{0:T(128)S(1)}, s32[]{:T(128)}, pred[]{:T(512)}, ...), branch_computations={%region_29.29_spmd, %region_30.38_spmd} | conditional | flops 2744454400 | bytes 197338432 | solution.py:194
  599.7 27.6 %conditional.20 = (f32[3,3,768,384]{3,2,1,0:T(8,128)}, f32[1,16,16,384]{3,2,1,0:T(8,128)}, f32[1,16,16,384]{3,2,1,0:T(8,128)S(1)}) conditional(s32[]{:T(128)} %convert_element_type.285, f32[3,3,768,384]{3,2,1,0:T(8,128)} %get-tuple-element.3287, (f32[1,16,16,768]{3,2,1,0:T(8,128)S(1)}, s32[4]{0:T(128)S(1)}, s32[]{:T(128)}, pred[]{:T(512)}, ...), branch_computations={%region_29.29_spmd, %region_30.38_spmd} | conditional | flops 2744454400 | bytes 197338432 | solution.py:194
  648.7 32.8 %collective-permute-start.3 = (f32[1,16,16,384]{3,2,1,0:T(8,128)S(1)}, f32[1,16,16,384]{3,2,1,0:T(8,128)}, u32[]{:S(2)}, u32[]{:S(2)}) collective-permute-start(f32[1,16,16,384]{3,2,1,0:T(8,128)S(1)} %get-tuple-element.3081), channel_id=1, source_target_pairs={{0,16},{16,32},{32,48},{48,64},{64,80},{80,96},{96,112},{1,17},{17... | collective-permute-start | bytes 1179656 | tf_op jit(solution)/shard_map/while/body/eval_jaxpr/ppermute | solution.py:14
  714.7 32.2 %collective-permute-start.3 = (f32[1,16,16,384]{3,2,1,0:T(8,128)S(1)}, f32[1,16,16,384]{3,2,1,0:T(8,128)}, u32[]{:S(2)}, u32[]{:S(2)}) collective-permute-start(f32[1,16,16,384]{3,2,1,0:T(8,128)S(1)} %get-tuple-element.3081), channel_id=1, source_target_pairs={{0,16},{16,32},{32,48},{48,64},{64,80},{80,96},{96,112},{1,17},{17... | collective-permute-start | bytes 1179656 | tf_op jit(solution)/shard_map/while/body/eval_jaxpr/ppermute | solution.py:14
  774.2 167.7 %while.131 = (s32[]{:T(128)}, f32[1,16,16,384]{3,2,1,0:T(8,128)}, f32[1,16,16,384]{3,2,1,0:T(8,128)S(1)}, f32[6,16,16,384]{3,2,1,0:T(8,128)}, f32[6,16,16,384]{3...) while((s32[]{:T(128)}, f32[1,16,16,384]{3,2,1,0:T(8,128)}, ...), condition=%wide.region_61.62_spmd, body=%wide.region_40.61_spmd.sunk | while | flops 4114961408 | bytes 303477184 | solution.py:246
  781.2 37.9 %collective-permute-start.5 = (f32[1,16,16,384]{3,2,1,0:T(8,128)}, f32[1,16,16,384]{3,2,1,0:T(8,128)}, u32[]{:S(2)}, u32[]{:S(2)}) collective-permute-start(f32[1,16,16,384]{3,2,1,0:T(8,128)} %get-tuple-element.3108), channel_id=1, source_target_pairs={{0,16},{16,32},{32,48},{48,64},{64,80},{80,96},{96,112},{1,17},{17... | collective-permute-start | bytes 1179656 | tf_op jit(solution)/shard_map/while/body/eval_jaxpr/ppermute | solution.py:14
  839.3 36.0 %collective-permute-start.5 = (f32[1,16,16,384]{3,2,1,0:T(8,128)}, f32[1,16,16,384]{3,2,1,0:T(8,128)}, u32[]{:S(2)}, u32[]{:S(2)}) collective-permute-start(f32[1,16,16,384]{3,2,1,0:T(8,128)} %get-tuple-element.3108), channel_id=1, source_target_pairs={{0,16},{16,32},{32,48},{48,64},{64,80},{80,96},{96,112},{1,17},{17... | collective-permute-start | bytes 1179656 | tf_op jit(solution)/shard_map/while/body/eval_jaxpr/ppermute | solution.py:14
  897.7 31.8 %collective-permute-start.5 = (f32[1,16,16,384]{3,2,1,0:T(8,128)}, f32[1,16,16,384]{3,2,1,0:T(8,128)}, u32[]{:S(2)}, u32[]{:S(2)}) collective-permute-start(f32[1,16,16,384]{3,2,1,0:T(8,128)} %get-tuple-element.3108), channel_id=1, source_target_pairs={{0,16},{16,32},{32,48},{48,64},{64,80},{80,96},{96,112},{1,17},{17... | collective-permute-start | bytes 1179656 | tf_op jit(solution)/shard_map/while/body/eval_jaxpr/ppermute | solution.py:14
  941.9 391.9 %while.132 = (s32[]{:T(128)}, f32[1,16,16,384]{3,2,1,0:T(8,128)S(1)}, f32[3,3,384,384]{3,2,1,0:T(8,128)}, s32[]{:T(128)}, f32[6,16,16,384]{3,2,1,0:T(8,128)}, /*...) while((s32[]{:T(128)}, ...), condition=%wide.region_73.74_spmd, body=%wide.region_62.73_spmd.sunk | while | flops 1370113792 | bytes 95717064 | solution.py:249
  954.9 57.3 %collective-permute-done.7 = f32[1,16,16,384]{3,2,1,0:T(8,128)S(1)} collective-permute-done((f32[1,16,16,384]{3,2,1,0:T(8,128)S(1)}, f32[1,16,16,384]{3,2,1,0:T(8,128)S(1)}, u32[]{:S(2)}, u32[]{:S(2)}) %collective-permute-start.7) | collective-permute-done | bytes 393248 | tf_op jit(solution)/shard_map/while/body/eval_jaxpr/ppermute | solution.py:14
  1014.3 18.0 %collective-permute-done.7 = f32[1,16,16,384]{3,2,1,0:T(8,128)S(1)} collective-permute-done((f32[1,16,16,384]{3,2,1,0:T(8,128)S(1)}, f32[1,16,16,384]{3,2,1,0:T(8,128)S(1)}, u32[]{:S(2)}, u32[]{:S(2)}) %collective-permute-start.7) | collective-permute-done | bytes 393248 | tf_op jit(solution)/shard_map/while/body/eval_jaxpr/ppermute | solution.py:14
  1034.3 119.4 %collective-permute-done.7 = f32[1,16,16,384]{3,2,1,0:T(8,128)S(1)} collective-permute-done((f32[1,16,16,384]{3,2,1,0:T(8,128)S(1)}, f32[1,16,16,384]{3,2,1,0:T(8,128)S(1)}, u32[]{:S(2)}, u32[]{:S(2)}) %collective-permute-start.7) | collective-permute-done | bytes 393248 | tf_op jit(solution)/shard_map/while/body/eval_jaxpr/ppermute | solution.py:14
  1153.7 22.0 %conditional.23 = (f32[3,3,384,384]{3,2,1,0:T(8,128)}, f32[1,16,16,384]{3,2,1,0:T(8,128)}) conditional(s32[]{:T(128)} %convert_element_type.290, f32[3,3,384,384]{3,2,1,0:T(8,128)} %get-tuple-element.3420, (s32[]{:T(128)}, f32[6,16,16,384]{3,2,1,0:T(8,128)}, s32[4]{0:T(128)S(1)}, pred[]{:T(512)}, f32[6,16,16,384]{3,2,1,0:T(8,128)}, ...), branch_computations={%region_63.63_spmd, %region_64.72_spmd} | conditional | flops 1370015488 | bytes 93357472 | solution.py:218
  1178.0 52.6 %collective-permute-done.7 = f32[1,16,16,384]{3,2,1,0:T(8,128)S(1)} collective-permute-done((f32[1,16,16,384]{3,2,1,0:T(8,128)S(1)}, f32[1,16,16,384]{3,2,1,0:T(8,128)S(1)}, u32[]{:S(2)}, u32[]{:S(2)}) %collective-permute-start.7) | collective-permute-done | bytes 393248 | tf_op jit(solution)/shard_map/while/body/eval_jaxpr/ppermute | solution.py:14
  1230.6 22.0 %conditional.23 = (f32[3,3,384,384]{3,2,1,0:T(8,128)}, f32[1,16,16,384]{3,2,1,0:T(8,128)}) conditional(s32[]{:T(128)} %convert_element_type.290, f32[3,3,384,384]{3,2,1,0:T(8,128)} %get-tuple-element.3420, (s32[]{:T(128)}, f32[6,16,16,384]{3,2,1,0:T(8,128)}, s32[4]{0:T(128)S(1)}, pred[]{:T(512)}, f32[6,16,16,384]{3,2,1,0:T(8,128)}, ...), branch_computations={%region_63.63_spmd, %region_64.72_spmd} | conditional | flops 1370015488 | bytes 93357472 | solution.py:218
  1267.7 22.0 %conditional.23 = (f32[3,3,384,384]{3,2,1,0:T(8,128)}, f32[1,16,16,384]{3,2,1,0:T(8,128)}) conditional(s32[]{:T(128)} %convert_element_type.290, f32[3,3,384,384]{3,2,1,0:T(8,128)} %get-tuple-element.3420, (s32[]{:T(128)}, f32[6,16,16,384]{3,2,1,0:T(8,128)}, s32[4]{0:T(128)S(1)}, pred[]{:T(512)}, f32[6,16,16,384]{3,2,1,0:T(8,128)}, ...), branch_computations={%region_63.63_spmd, %region_64.72_spmd} | conditional | flops 1370015488 | bytes 93357472 | solution.py:218
  1301.2 22.0 %conditional.23 = (f32[3,3,384,384]{3,2,1,0:T(8,128)}, f32[1,16,16,384]{3,2,1,0:T(8,128)}) conditional(s32[]{:T(128)} %convert_element_type.290, f32[3,3,384,384]{3,2,1,0:T(8,128)} %get-tuple-element.3420, (s32[]{:T(128)}, f32[6,16,16,384]{3,2,1,0:T(8,128)}, s32[4]{0:T(128)S(1)}, pred[]{:T(512)}, f32[6,16,16,384]{3,2,1,0:T(8,128)}, ...), branch_computations={%region_63.63_spmd, %region_64.72_spmd} | conditional | flops 1370015488 | bytes 93357472 | solution.py:218
  1334.6 70.6 %reduce-scatter.3.cloned.1.call-done = f32[1,3,3,24,384]{4,3,2,1,0:T(8,128)} async-done(((f32[1,3,3,384,384]{4,3,2,1,0:T(8,128)}), f32[1,3,3,24,384]{4,3,2,1,0:T(8,128)}) %reduce-scatter.3.cloned.1.call-update) | async-done | bytes 331792 | tf_op jit(solution)/shard_map/reduce_scatter | solution.py:251
  1405.2 80.4 %reduce-scatter.5.cloned.1.call-done = f32[1,3,3,48,384]{4,3,2,1,0:T(8,128)} async-done(((f32[1,3,3,768,384]{4,3,2,1,0:T(8,128)}), f32[1,3,3,48,384]{4,3,2,1,0:T(8,128)}) %reduce-scatter.5.cloned.1.call-update) | async-done | bytes 663568 | tf_op jit(solution)/shard_map/reduce_scatter | solution.py:248
  (1082 shorter events, 967.7 us)
Async XLA Ops:
  7.2 1398.0 %reduce-scatter.3.cloned.1.call-start = ((), (), s32[]{:S(2)}) async-start(), calls=%async_computation.2 | async-start | bytes 5640192 | tf_op jit(solution)/shard_map/reduce_scatter | solution.py:251
  153.5 18.7 %collective-permute-start.1 = (f32[1,16,16,384]{3,2,1,0:T(8,128)}, f32[1,16,16,384]{3,2,1,0:T(8,128)}, u32[]{:S(2)}, u32[]{:S(2)}) collective-permute-start(f32[1,16,16,384]{3,2,1,0:T(8,128)} %get-tuple-element.3049), channel_id=1, source_target_pairs={{0,16},{16,32},{32,48},{48,64},{64,80},{80,96},{96,112},{1,17},{17... | collective-permute-start | bytes 1179656 | tf_op jit(solution)/shard_map/while/body/eval_jaxpr/ppermute | solution.py:14
  188.8 19.5 %collective-permute-start.1 = (f32[1,16,16,384]{3,2,1,0:T(8,128)}, f32[1,16,16,384]{3,2,1,0:T(8,128)}, u32[]{:S(2)}, u32[]{:S(2)}) collective-permute-start(f32[1,16,16,384]{3,2,1,0:T(8,128)} %get-tuple-element.3049), channel_id=1, source_target_pairs={{0,16},{16,32},{32,48},{48,64},{64,80},{80,96},{96,112},{1,17},{17... | collective-permute-start | bytes 1179656 | tf_op jit(solution)/shard_map/while/body/eval_jaxpr/ppermute | solution.py:14
  309.0 22.1 %collective-permute-start.1 = (f32[1,16,16,384]{3,2,1,0:T(8,128)}, f32[1,16,16,384]{3,2,1,0:T(8,128)}, u32[]{:S(2)}, u32[]{:S(2)}) collective-permute-start(f32[1,16,16,384]{3,2,1,0:T(8,128)} %get-tuple-element.3049), channel_id=1, source_target_pairs={{0,16},{16,32},{32,48},{48,64},{64,80},{80,96},{96,112},{1,17},{17... | collective-permute-start | bytes 1179656 | tf_op jit(solution)/shard_map/while/body/eval_jaxpr/ppermute | solution.py:14
  329.8 18.2 %collective-permute-start.2 = (f32[1,16,16,384]{3,2,1,0:T(8,128)}, f32[1,16,16,384]{3,2,1,0:T(8,128)S(1)}, u32[]{:S(2)}, u32[]{:S(2)}) collective-permute-start(f32[1,16,16,384]{3,2,1,0:T(8,128)} %get-tuple-element.3053), channel_id=1, source_target_pairs={{16,0},{32,16},{48,32},{64,48},{80,64},{96,80},{112,96},{17,1},{33... | collective-permute-start | bytes 1179656 | tf_op jit(solution)/shard_map/while/body/eval_jaxpr/ppermute | solution.py:14
  352.5 22.8 %collective-permute-start.1 = (f32[1,16,16,384]{3,2,1,0:T(8,128)}, f32[1,16,16,384]{3,2,1,0:T(8,128)}, u32[]{:S(2)}, u32[]{:S(2)}) collective-permute-start(f32[1,16,16,384]{3,2,1,0:T(8,128)} %get-tuple-element.3049), channel_id=1, source_target_pairs={{0,16},{16,32},{32,48},{48,64},{64,80},{80,96},{96,112},{1,17},{17... | collective-permute-start | bytes 1179656 | tf_op jit(solution)/shard_map/while/body/eval_jaxpr/ppermute | solution.py:14
  374.0 18.1 %collective-permute-start.2 = (f32[1,16,16,384]{3,2,1,0:T(8,128)}, f32[1,16,16,384]{3,2,1,0:T(8,128)S(1)}, u32[]{:S(2)}, u32[]{:S(2)}) collective-permute-start(f32[1,16,16,384]{3,2,1,0:T(8,128)} %get-tuple-element.3053), channel_id=1, source_target_pairs={{16,0},{32,16},{48,32},{64,48},{80,64},{96,80},{112,96},{17,1},{33... | collective-permute-start | bytes 1179656 | tf_op jit(solution)/shard_map/while/body/eval_jaxpr/ppermute | solution.py:14
  396.6 20.9 %collective-permute-start.1 = (f32[1,16,16,384]{3,2,1,0:T(8,128)}, f32[1,16,16,384]{3,2,1,0:T(8,128)}, u32[]{:S(2)}, u32[]{:S(2)}) collective-permute-start(f32[1,16,16,384]{3,2,1,0:T(8,128)} %get-tuple-element.3049), channel_id=1, source_target_pairs={{0,16},{16,32},{32,48},{48,64},{64,80},{80,96},{96,112},{1,17},{17... | collective-permute-start | bytes 1179656 | tf_op jit(solution)/shard_map/while/body/eval_jaxpr/ppermute | solution.py:14
  446.8 34.5 %collective-permute-start.4 = (f32[1,16,16,384]{3,2,1,0:T(8,128)}, f32[1,16,16,384]{3,2,1,0:T(8,128)S(1)}, u32[]{:S(2)}, u32[]{:S(2)}) collective-permute-start(f32[1,16,16,384]{3,2,1,0:T(8,128)} %get-tuple-element.3082), channel_id=1, source_target_pairs={{16,0},{32,16},{48,32},{64,48},{80,64},{96,80},{112,96},{17,1},{33... | collective-permute-start | bytes 1179656 | tf_op jit(solution)/shard_map/while/body/eval_jaxpr/ppermute | solution.py:14
  497.3 38.4 %collective-permute-start.4 = (f32[1,16,16,384]{3,2,1,0:T(8,128)}, f32[1,16,16,384]{3,2,1,0:T(8,128)S(1)}, u32[]{:S(2)}, u32[]{:S(2)}) collective-permute-start(f32[1,16,16,384]{3,2,1,0:T(8,128)} %get-tuple-element.3082), channel_id=1, source_target_pairs={{16,0},{32,16},{48,32},{64,48},{80,64},{96,80},{112,96},{17,1},{33... | collective-permute-start | bytes 1179656 | tf_op jit(solution)/shard_map/while/body/eval_jaxpr/ppermute | solution.py:14
  551.6 37.8 %collective-permute-start.4 = (f32[1,16,16,384]{3,2,1,0:T(8,128)}, f32[1,16,16,384]{3,2,1,0:T(8,128)S(1)}, u32[]{:S(2)}, u32[]{:S(2)}) collective-permute-start(f32[1,16,16,384]{3,2,1,0:T(8,128)} %get-tuple-element.3082), channel_id=1, source_target_pairs={{16,0},{32,16},{48,32},{64,48},{80,64},{96,80},{112,96},{17,1},{33... | collective-permute-start | bytes 1179656 | tf_op jit(solution)/shard_map/while/body/eval_jaxpr/ppermute | solution.py:14
  597.4 38.5 %collective-permute-start.4 = (f32[1,16,16,384]{3,2,1,0:T(8,128)}, f32[1,16,16,384]{3,2,1,0:T(8,128)S(1)}, u32[]{:S(2)}, u32[]{:S(2)}) collective-permute-start(f32[1,16,16,384]{3,2,1,0:T(8,128)} %get-tuple-element.3082), channel_id=1, source_target_pairs={{16,0},{32,16},{48,32},{64,48},{80,64},{96,80},{112,96},{17,1},{33... | collective-permute-start | bytes 1179656 | tf_op jit(solution)/shard_map/while/body/eval_jaxpr/ppermute | solution.py:14
  643.8 38.5 %collective-permute-start.4 = (f32[1,16,16,384]{3,2,1,0:T(8,128)}, f32[1,16,16,384]{3,2,1,0:T(8,128)S(1)}, u32[]{:S(2)}, u32[]{:S(2)}) collective-permute-start(f32[1,16,16,384]{3,2,1,0:T(8,128)} %get-tuple-element.3082), channel_id=1, source_target_pairs={{16,0},{32,16},{48,32},{64,48},{80,64},{96,80},{112,96},{17,1},{33... | collective-permute-start | bytes 1179656 | tf_op jit(solution)/shard_map/while/body/eval_jaxpr/ppermute | solution.py:14
  648.7 37.4 %collective-permute-start.3 = (f32[1,16,16,384]{3,2,1,0:T(8,128)S(1)}, f32[1,16,16,384]{3,2,1,0:T(8,128)}, u32[]{:S(2)}, u32[]{:S(2)}) collective-permute-start(f32[1,16,16,384]{3,2,1,0:T(8,128)S(1)} %get-tuple-element.3081), channel_id=1, source_target_pairs={{0,16},{16,32},{32,48},{48,64},{64,80},{80,96},{96,112},{1,17},{17... | collective-permute-start | bytes 1179656 | tf_op jit(solution)/shard_map/while/body/eval_jaxpr/ppermute | solution.py:14
  709.8 37.9 %collective-permute-start.4 = (f32[1,16,16,384]{3,2,1,0:T(8,128)}, f32[1,16,16,384]{3,2,1,0:T(8,128)S(1)}, u32[]{:S(2)}, u32[]{:S(2)}) collective-permute-start(f32[1,16,16,384]{3,2,1,0:T(8,128)} %get-tuple-element.3082), channel_id=1, source_target_pairs={{16,0},{32,16},{48,32},{64,48},{80,64},{96,80},{112,96},{17,1},{33... | collective-permute-start | bytes 1179656 | tf_op jit(solution)/shard_map/while/body/eval_jaxpr/ppermute | solution.py:14
  714.7 36.7 %collective-permute-start.3 = (f32[1,16,16,384]{3,2,1,0:T(8,128)S(1)}, f32[1,16,16,384]{3,2,1,0:T(8,128)}, u32[]{:S(2)}, u32[]{:S(2)}) collective-permute-start(f32[1,16,16,384]{3,2,1,0:T(8,128)S(1)} %get-tuple-element.3081), channel_id=1, source_target_pairs={{0,16},{16,32},{32,48},{48,64},{64,80},{80,96},{96,112},{1,17},{17... | collective-permute-start | bytes 1179656 | tf_op jit(solution)/shard_map/while/body/eval_jaxpr/ppermute | solution.py:14
  781.2 42.7 %collective-permute-start.5 = (f32[1,16,16,384]{3,2,1,0:T(8,128)}, f32[1,16,16,384]{3,2,1,0:T(8,128)}, u32[]{:S(2)}, u32[]{:S(2)}) collective-permute-start(f32[1,16,16,384]{3,2,1,0:T(8,128)} %get-tuple-element.3108), channel_id=1, source_target_pairs={{0,16},{16,32},{32,48},{48,64},{64,80},{80,96},{96,112},{1,17},{17... | collective-permute-start | bytes 1179656 | tf_op jit(solution)/shard_map/while/body/eval_jaxpr/ppermute | solution.py:14
  839.3 40.9 %collective-permute-start.5 = (f32[1,16,16,384]{3,2,1,0:T(8,128)}, f32[1,16,16,384]{3,2,1,0:T(8,128)}, u32[]{:S(2)}, u32[]{:S(2)}) collective-permute-start(f32[1,16,16,384]{3,2,1,0:T(8,128)} %get-tuple-element.3108), channel_id=1, source_target_pairs={{0,16},{16,32},{32,48},{48,64},{64,80},{80,96},{96,112},{1,17},{17... | collective-permute-start | bytes 1179656 | tf_op jit(solution)/shard_map/while/body/eval_jaxpr/ppermute | solution.py:14
  897.7 36.6 %collective-permute-start.5 = (f32[1,16,16,384]{3,2,1,0:T(8,128)}, f32[1,16,16,384]{3,2,1,0:T(8,128)}, u32[]{:S(2)}, u32[]{:S(2)}) collective-permute-start(f32[1,16,16,384]{3,2,1,0:T(8,128)} %get-tuple-element.3108), channel_id=1, source_target_pairs={{0,16},{16,32},{32,48},{48,64},{64,80},{80,96},{96,112},{1,17},{17... | collective-permute-start | bytes 1179656 | tf_op jit(solution)/shard_map/while/body/eval_jaxpr/ppermute | solution.py:14
  953.6 58.6 %collective-permute-start.7 = (f32[1,16,16,384]{3,2,1,0:T(8,128)S(1)}, f32[1,16,16,384]{3,2,1,0:T(8,128)S(1)}, u32[]{:S(2)}, u32[]{:S(2)}) collective-permute-start(f32[1,16,16,384]{3,2,1,0:T(8,128)S(1)} %broadcast_select_fusion.17), channel_id=1, source_target_pairs={{16,0},{32,16},{48,32},{64,48},{80,64},{96,80},{112,96},{17,1},{33... | collective-permute-start | bytes 1179656 | tf_op jit(solution)/shard_map/while/body/eval_jaxpr/ppermute | solution.py:14
  1013.0 19.3 %collective-permute-start.7 = (f32[1,16,16,384]{3,2,1,0:T(8,128)S(1)}, f32[1,16,16,384]{3,2,1,0:T(8,128)S(1)}, u32[]{:S(2)}, u32[]{:S(2)}) collective-permute-start(f32[1,16,16,384]{3,2,1,0:T(8,128)S(1)} %broadcast_select_fusion.17), channel_id=1, source_target_pairs={{16,0},{32,16},{48,32},{64,48},{80,64},{96,80},{112,96},{17,1},{33... | collective-permute-start | bytes 1179656 | tf_op jit(solution)/shard_map/while/body/eval_jaxpr/ppermute | solution.py:14
  1033.0 120.7 %collective-permute-start.7 = (f32[1,16,16,384]{3,2,1,0:T(8,128)S(1)}, f32[1,16,16,384]{3,2,1,0:T(8,128)S(1)}, u32[]{:S(2)}, u32[]{:S(2)}) collective-permute-start(f32[1,16,16,384]{3,2,1,0:T(8,128)S(1)} %broadcast_select_fusion.17), channel_id=1, source_target_pairs={{16,0},{32,16},{48,32},{64,48},{80,64},{96,80},{112,96},{17,1},{33... | collective-permute-start | bytes 1179656 | tf_op jit(solution)/shard_map/while/body/eval_jaxpr/ppermute | solution.py:14
  1176.7 53.9 %collective-permute-start.7 = (f32[1,16,16,384]{3,2,1,0:T(8,128)S(1)}, f32[1,16,16,384]{3,2,1,0:T(8,128)S(1)}, u32[]{:S(2)}, u32[]{:S(2)}) collective-permute-start(f32[1,16,16,384]{3,2,1,0:T(8,128)S(1)} %broadcast_select_fusion.17), channel_id=1, source_target_pairs={{16,0},{32,16},{48,32},{64,48},{80,64},{96,80},{112,96},{17,1},{33... | collective-permute-start | bytes 1179656 | tf_op jit(solution)/shard_map/while/body/eval_jaxpr/ppermute | solution.py:14
  1333.8 151.8 %reduce-scatter.5.cloned.1.call-start = ((), (), s32[]{:S(2)}) async-start(), calls=%async_computation.3 | async-start | bytes 11280384 | tf_op jit(solution)/shard_map/reduce_scatter | solution.py:248
  (83 other events, 522.9 us)
Sparse Core Ops, SparseCore 0:
  1334.0 71.1 reduce-scatter.2
  1408.2 77.3 reduce-scatter.4

commit v2 on v0

--- a/solution.py
+++ b/solution.py
@@ -23,11 +23,17 @@
 
 def activate(inputs_f32, stamps_in):
     batch_rows, height, breadth, channels = inputs_f32.shape
-    grouped = inputs_f32.reshape(batch_rows, height * breadth, GROUPS, channels // GROUPS)
-    group_mean = jnp.mean(grouped, axis=(1, 3), keepdims=True)
-    centered = grouped - group_mean
-    group_var = jnp.mean(centered * centered, axis=(1, 3), keepdims=True)
-    normed = (centered * lax.rsqrt(group_var + 1e-05)).reshape(inputs_f32.shape)
+    width = channels // GROUPS
+    count = height * breadth * width
+
+    def group_mean(values):
+        per_channel = jnp.sum(values, axis=(1, 2))
+        per_group = jnp.sum(per_channel.reshape(batch_rows, GROUPS, width), axis=2) / count
+        return jnp.repeat(per_group, width, axis=1)[:, None, None, :]
+
+    centered = inputs_f32 - group_mean(inputs_f32)
+    group_var = group_mean(centered * centered)
+    normed = centered * lax.rsqrt(group_var + 1e-05)
     modulate = 1.0 + 0.5 * embed(stamps_in, channels)[:, None, None, :]
     return jax.nn.silu(normed * modulate)
 

time: 1420 us -> 1420 us (level)
  no operation moved by 1% of the time
where the time goes in v2:
time: 1420 us
  waiting for transfers between devices  709 us (50%)
  starting transfers between devices  269 us (19%)
  other arithmetic  195 us (14%)
  local copies, waits for them, and re-layouts  120 us (8%)
  matrix products  94.4 us (7%)
  loops' own time  15.1 us (1%)
    ppermute x44, waiting for transfers between devices, passed_along(): lax.ppermute(value, axis, [(source, source + steps) for source in range(i...  558 us
    ppermute x44, starting transfers between devices, passed_along(): lax.ppermute(value, axis, [(source, source + steps) for source in range(i...  269 us
    dynamic_update_slice x55, other arithmetic, store_row(): lax.dynamic_update_slice_in_dim(buffer, jnp.where(active, piece, kept), s...  106 us
    reduce_scatter x1, waiting for transfers between devices, shards(): lax.psum_scatter(dec_acc[None], 'dp', scatter_dimension=3, tiled=True)  80 us
    reduce_scatter x1, waiting for transfers between devices, shards(): lax.psum_scatter(enc_acc[None], 'dp', scatter_dimension=3, tiled=True)  70.3 us
    cond x80, local copies, waits for them, and re-layouts  44.2 us
    dot_general x72, matrix products, conv_back(): lax.dot_general(window, weight[row_off, col_off], (((1,), (1,)), ((), ())...  41.6 us
    dynamic_slice x38, local copies, waits for them, and re-layouts, pick_row(): return lax.dynamic_slice_in_dim(buffer, slot_index, 1, 0)  32.3 us
  transfers between devices with their start and end apart: 46, of which 46 were waited for; matrix products, arithmetic and copies ran while one was open for 4% of the time, Pallas kernels for 0%

profile of v2, /device:TPU:0, one launch (start us, length us, event | category | flops | bytes accessed | tf_op | source)
XLA Modules:
  0.0 1416.9 jit_solution(16147008516701969693)
XLA Ops:
  14.3 182.2 %while.80 = (s32[]{:T(128)}, f32[1,16,16,384]{3,2,1,0:T(8,128)}, f32[4,16,16,384]{3,2,1,0:T(8,128)}, f32[4,16,16,384]{3,2,1,0:T(8,128)}, s32[]{:T(128)}, /*index...) while((s32[]{:T(128)}, f32[1,16,16,384]{3,2,1,0:T(8,128)}, ...), condition=%wide.region_7.8_spmd, body=%wide.region_0.7_spmd.sunk | while | flops 681838080 | bytes 20187440 | solution.py:160
  199.2 243.5 %while.81 = (s32[]{:T(128)}, f32[1,16,16,384]{3,2,1,0:T(8,128)S(1)}, f32[4,16,16,384]{3,2,1,0:T(8,128)}, f32[4,16,16,384]{3,2,1,0:T(8,128)}, s32[]{:T(128)}, /*i...) while((s32[]{:T(128)}, ...), condition=%wide.region_15.16_spmd, body=%wide.region_8.15_spmd.sunk | while | flops 1362693120 | bytes 50988884 | solution.py:181
  311.6 37.2 %collective-permute-done.1 = f32[1,16,16,384]{3,2,1,0:T(8,128)S(1)} collective-permute-done((f32[1,16,16,384]{3,2,1,0:T(8,128)S(1)}, f32[1,16,16,384]{3,2,1,0:T(8,128)S(1)}, u32[]{:S(2)}, u32[]{:S(2)}) %collective-permute-start.1) | collective-permute-done | bytes 393248 | tf_op jit(solution)/shard_map/while/body/eval_jaxpr/ppermute | solution.py:14
  450.2 360.7 %while.82 = (s32[]{:T(128)}, f32[1,16,16,384]{3,2,1,0:T(8,128)S(1)}, f32[3,3,768,384]{3,2,1,0:T(8,128)}, f32[4,16,16,384]{3,2,1,0:T(8,128)}, f32[4,16,16,384]{3,...) while((s32[]{:T(128)}, ...), condition=%wide.region_27.28_spmd, body=%wide.region_16.27_spmd.sunk | while | flops 2744946688 | bytes 206576944 | solution.py:212
  453.5 26.7 %conditional.10 = (f32[3,3,768,384]{3,2,1,0:T(8,128)}, f32[1,16,16,384]{3,2,1,0:T(8,128)S(1)}, f32[1,16,16,384]{3,2,1,0:T(8,128)}) conditional(s32[]{:T(128)} %convert_element_type.131, f32[3,3,768,384]{3,2,1,0:T(8,128)} %get-tuple-element.1628, (f32[1,16,16,768]{3,2,1,0:T(8,128)S(1)}, s32[4]{0:T(128)S(1)}, s32[]{:T(128)}, pred[]{:T(512)}, ...), branch_computations={%region_17.17_spmd, %region_18.26_spmd} | conditional | flops 2744455168 | bytes 198908384 | solution.py:205
  489.9 26.7 %conditional.10 = (f32[3,3,768,384]{3,2,1,0:T(8,128)}, f32[1,16,16,384]{3,2,1,0:T(8,128)S(1)}, f32[1,16,16,384]{3,2,1,0:T(8,128)}) conditional(s32[]{:T(128)} %convert_element_type.131, f32[3,3,768,384]{3,2,1,0:T(8,128)} %get-tuple-element.1628, (f32[1,16,16,768]{3,2,1,0:T(8,128)S(1)}, s32[4]{0:T(128)S(1)}, s32[]{:T(128)}, pred[]{:T(512)}, ...), branch_computations={%region_17.17_spmd, %region_18.26_spmd} | conditional | flops 2744455168 | bytes 198908384 | solution.py:205
  529.3 26.7 %conditional.10 = (f32[3,3,768,384]{3,2,1,0:T(8,128)}, f32[1,16,16,384]{3,2,1,0:T(8,128)S(1)}, f32[1,16,16,384]{3,2,1,0:T(8,128)}) conditional(s32[]{:T(128)} %convert_element_type.131, f32[3,3,768,384]{3,2,1,0:T(8,128)} %get-tuple-element.1628, (f32[1,16,16,768]{3,2,1,0:T(8,128)S(1)}, s32[4]{0:T(128)S(1)}, s32[]{:T(128)}, pred[]{:T(512)}, ...), branch_computations={%region_17.17_spmd, %region_18.26_spmd} | conditional | flops 2744455168 | bytes 198908384 | solution.py:205
  568.8 26.7 %conditional.10 = (f32[3,3,768,384]{3,2,1,0:T(8,128)}, f32[1,16,16,384]{3,2,1,0:T(8,128)S(1)}, f32[1,16,16,384]{3,2,1,0:T(8,128)}) conditional(s32[]{:T(128)} %convert_element_type.131, f32[3,3,768,384]{3,2,1,0:T(8,128)} %get-tuple-element.1628, (f32[1,16,16,768]{3,2,1,0:T(8,128)S(1)}, s32[4]{0:T(128)S(1)}, s32[]{:T(128)}, pred[]{:T(512)}, ...), branch_computations={%region_17.17_spmd, %region_18.26_spmd} | conditional | flops 2744455168 | bytes 198908384 | solution.py:205
  609.1 30.3 %collective-permute-start.2 = (f32[1,16,16,384]{3,2,1,0:T(8,128)S(1)}, f32[1,16,16,384]{3,2,1,0:T(8,128)S(1)}, u32[]{:S(2)}, u32[]{:S(2)}) collective-permute-start(f32[1,16,16,384]{3,2,1,0:T(8,128)S(1)} %get-tuple-element.1504), channel_id=1, source_target_pairs={{0,16},{16,32},{32,48},{48,64},{64,80},{80,96},{96,112},{1,17},{17... | collective-permute-start | bytes 1179656 | tf_op jit(solution)/shard_map/while/body/eval_jaxpr/ppermute | solution.py:14
  662.1 27.8 %collective-permute-start.2 = (f32[1,16,16,384]{3,2,1,0:T(8,128)S(1)}, f32[1,16,16,384]{3,2,1,0:T(8,128)S(1)}, u32[]{:S(2)}, u32[]{:S(2)}) collective-permute-start(f32[1,16,16,384]{3,2,1,0:T(8,128)S(1)} %get-tuple-element.1504), channel_id=1, source_target_pairs={{0,16},{16,32},{32,48},{48,64},{64,80},{80,96},{96,112},{1,17},{17... | collective-permute-start | bytes 1179656 | tf_op jit(solution)/shard_map/while/body/eval_jaxpr/ppermute | solution.py:14
  712.7 32.6 %collective-permute-start.2 = (f32[1,16,16,384]{3,2,1,0:T(8,128)S(1)}, f32[1,16,16,384]{3,2,1,0:T(8,128)S(1)}, u32[]{:S(2)}, u32[]{:S(2)}) collective-permute-start(f32[1,16,16,384]{3,2,1,0:T(8,128)S(1)} %get-tuple-element.1504), channel_id=1, source_target_pairs={{0,16},{16,32},{32,48},{48,64},{64,80},{80,96},{96,112},{1,17},{17... | collective-permute-start | bytes 1179656 | tf_op jit(solution)/shard_map/while/body/eval_jaxpr/ppermute | solution.py:14
  771.7 33.9 %collective-permute-start.2 = (f32[1,16,16,384]{3,2,1,0:T(8,128)S(1)}, f32[1,16,16,384]{3,2,1,0:T(8,128)S(1)}, u32[]{:S(2)}, u32[]{:S(2)}) collective-permute-start(f32[1,16,16,384]{3,2,1,0:T(8,128)S(1)} %get-tuple-element.1504), channel_id=1, source_target_pairs={{0,16},{16,32},{32,48},{48,64},{64,80},{80,96},{96,112},{1,17},{17... | collective-permute-start | bytes 1179656 | tf_op jit(solution)/shard_map/while/body/eval_jaxpr/ppermute | solution.py:14
  813.7 445.3 %while.83 = (s32[]{:T(128)}, f32[1,16,16,384]{3,2,1,0:T(8,128)S(1)}, f32[3,3,384,384]{3,2,1,0:T(8,128)}, s32[]{:T(128)}, f32[4,16,16,384]{3,2,1,0:T(8,128)}, /*i...) while((s32[]{:T(128)}, ...), condition=%wide.region_39.40_spmd, body=%wide.region_28.39_spmd.sunk | while | flops 1370015744 | bytes 93357744 | solution.py:238
  816.0 19.1 %collective-permute-done.3 = f32[1,16,16,384]{3,2,1,0:T(8,128)S(1)} collective-permute-done((f32[1,16,16,384]{3,2,1,0:T(8,128)}, f32[1,16,16,384]{3,2,1,0:T(8,128)S(1)}, u32[]{:S(2)}, u32[]{:S(2)}) %collective-permute-start.3) | collective-permute-done | bytes 393248 | tf_op jit(solution)/shard_map/while/body/eval_jaxpr/ppermute | solution.py:14
  837.1 22.4 %collective-permute-done.3 = f32[1,16,16,384]{3,2,1,0:T(8,128)S(1)} collective-permute-done((f32[1,16,16,384]{3,2,1,0:T(8,128)}, f32[1,16,16,384]{3,2,1,0:T(8,128)S(1)}, u32[]{:S(2)}, u32[]{:S(2)}) %collective-permute-start.3) | collective-permute-done | bytes 393248 | tf_op jit(solution)/shard_map/while/body/eval_jaxpr/ppermute | solution.py:14
  877.5 27.7 %collective-permute-done.3 = f32[1,16,16,384]{3,2,1,0:T(8,128)S(1)} collective-permute-done((f32[1,16,16,384]{3,2,1,0:T(8,128)}, f32[1,16,16,384]{3,2,1,0:T(8,128)S(1)}, u32[]{:S(2)}, u32[]{:S(2)}) %collective-permute-start.3) | collective-permute-done | bytes 393248 | tf_op jit(solution)/shard_map/while/body/eval_jaxpr/ppermute | solution.py:14
  922.9 27.9 %collective-permute-done.3 = f32[1,16,16,384]{3,2,1,0:T(8,128)S(1)} collective-permute-done((f32[1,16,16,384]{3,2,1,0:T(8,128)}, f32[1,16,16,384]{3,2,1,0:T(8,128)S(1)}, u32[]{:S(2)}, u32[]{:S(2)}) %collective-permute-start.3) | collective-permute-done | bytes 393248 | tf_op jit(solution)/shard_map/while/body/eval_jaxpr/ppermute | solution.py:14
  952.9 162.7 %collective-permute-done.3 = f32[1,16,16,384]{3,2,1,0:T(8,128)S(1)} collective-permute-done((f32[1,16,16,384]{3,2,1,0:T(8,128)}, f32[1,16,16,384]{3,2,1,0:T(8,128)S(1)}, u32[]{:S(2)}, u32[]{:S(2)}) %collective-permute-start.3) | collective-permute-done | bytes 393248 | tf_op jit(solution)/shard_map/while/body/eval_jaxpr/ppermute | solution.py:14
  1115.6 22.7 %conditional.11 = (f32[3,3,384,384]{3,2,1,0:T(8,128)}, f32[1,16,16,384]{3,2,1,0:T(8,128)}) conditional(s32[]{:T(128)} %convert_element_type.132, f32[3,3,384,384]{3,2,1,0:T(8,128)} %get-tuple-element.1675, (s32[]{:T(128)}, f32[4,16,16,384]{3,2,1,0:T(8,128)}, s32[4]{0:T(128)S(1)}, pred[]{:T(512)}, f32[4,16,16,384]{3,2,1,0:T(8,128)}, ...), branch_computations={%region_29.29_spmd, %region_30.38_spmd} | conditional | flops 1370015744 | bytes 91784608 | solution.py:233
  1151.5 22.7 %conditional.11 = (f32[3,3,384,384]{3,2,1,0:T(8,128)}, f32[1,16,16,384]{3,2,1,0:T(8,128)}) conditional(s32[]{:T(128)} %convert_element_type.132, f32[3,3,384,384]{3,2,1,0:T(8,128)} %get-tuple-element.1675, (s32[]{:T(128)}, f32[4,16,16,384]{3,2,1,0:T(8,128)}, s32[4]{0:T(128)S(1)}, pred[]{:T(512)}, f32[4,16,16,384]{3,2,1,0:T(8,128)}, ...), branch_computations={%region_29.29_spmd, %region_30.38_spmd} | conditional | flops 1370015744 | bytes 91784608 | solution.py:233
  1187.6 22.7 %conditional.11 = (f32[3,3,384,384]{3,2,1,0:T(8,128)}, f32[1,16,16,384]{3,2,1,0:T(8,128)}) conditional(s32[]{:T(128)} %convert_element_type.132, f32[3,3,384,384]{3,2,1,0:T(8,128)} %get-tuple-element.1675, (s32[]{:T(128)}, f32[4,16,16,384]{3,2,1,0:T(8,128)}, s32[4]{0:T(128)S(1)}, pred[]{:T(512)}, f32[4,16,16,384]{3,2,1,0:T(8,128)}, ...), branch_computations={%region_29.29_spmd, %region_30.38_spmd} | conditional | flops 1370015744 | bytes 91784608 | solution.py:233
  1226.5 22.7 %conditional.11 = (f32[3,3,384,384]{3,2,1,0:T(8,128)}, f32[1,16,16,384]{3,2,1,0:T(8,128)}) conditional(s32[]{:T(128)} %convert_element_type.132, f32[3,3,384,384]{3,2,1,0:T(8,128)} %get-tuple-element.1675, (s32[]{:T(128)}, f32[4,16,16,384]{3,2,1,0:T(8,128)}, s32[4]{0:T(128)S(1)}, pred[]{:T(512)}, f32[4,16,16,384]{3,2,1,0:T(8,128)}, ...), branch_computations={%region_29.29_spmd, %region_30.38_spmd} | conditional | flops 1370015744 | bytes 91784608 | solution.py:233
  1259.8 70.3 %reduce-scatter.3.cloned.1.call-done = f32[1,3,3,24,384]{4,3,2,1,0:T(8,128)} async-done(((f32[1,3,3,384,384]{4,3,2,1,0:T(8,128)}), f32[1,3,3,24,384]{4,3,2,1,0:T(8,128)}) %reduce-scatter.3.cloned.1.call-update) | async-done | bytes 331792 | tf_op jit(solution)/shard_map/reduce_scatter | solution.py:240
  1330.1 80.0 %reduce-scatter.5.cloned.1.call-done = f32[1,3,3,48,384]{4,3,2,1,0:T(8,128)} async-done(((f32[1,3,3,768,384]{4,3,2,1,0:T(8,128)}), f32[1,3,3,48,384]{4,3,2,1,0:T(8,128)}) %reduce-scatter.5.cloned.1.call-update) | async-done | bytes 663568 | tf_op jit(solution)/shard_map/reduce_scatter | solution.py:241
  (999 shorter events, 880.7 us)
Async XLA Ops:
  7.2 1322.9 %reduce-scatter.3.cloned.1.call-start = ((), (), s32[]{:S(2)}) async-start(), calls=%async_computation.2 | async-start | bytes 5640192 | tf_op jit(solution)/shard_map/reduce_scatter | solution.py:240
  86.3 15.1 %collective-permute-start = (f32[1,16,16,384]{3,2,1,0:T(8,128)S(1)}, f32[1,16,16,384]{3,2,1,0:T(8,128)}, u32[]{:S(2)}, u32[]{:S(2)}) collective-permute-start(f32[1,16,16,384]{3,2,1,0:T(8,128)S(1)} %get-tuple-element.1699), channel_id=1, source_target_pairs={{0,16},{16,32},{32,48},{48,64},{64,80},{80,96},{96,112},{1,17},{17... | collective-permute-start | bytes 1179656 | tf_op jit(solution)/shard_map/while/body/eval_jaxpr/ppermute | solution.py:14
  142.4 17.9 %collective-permute-start = (f32[1,16,16,384]{3,2,1,0:T(8,128)S(1)}, f32[1,16,16,384]{3,2,1,0:T(8,128)}, u32[]{:S(2)}, u32[]{:S(2)}) collective-permute-start(f32[1,16,16,384]{3,2,1,0:T(8,128)S(1)} %get-tuple-element.1699), channel_id=1, source_target_pairs={{0,16},{16,32},{32,48},{48,64},{64,80},{80,96},{96,112},{1,17},{17... | collective-permute-start | bytes 1179656 | tf_op jit(solution)/shard_map/while/body/eval_jaxpr/ppermute | solution.py:14
  177.8 18.7 %collective-permute-start = (f32[1,16,16,384]{3,2,1,0:T(8,128)S(1)}, f32[1,16,16,384]{3,2,1,0:T(8,128)}, u32[]{:S(2)}, u32[]{:S(2)}) collective-permute-start(f32[1,16,16,384]{3,2,1,0:T(8,128)S(1)} %get-tuple-element.1699), channel_id=1, source_target_pairs={{0,16},{16,32},{32,48},{48,64},{64,80},{80,96},{96,112},{1,17},{17... | collective-permute-start | bytes 1179656 | tf_op jit(solution)/shard_map/while/body/eval_jaxpr/ppermute | solution.py:14
  201.3 14.5 %collective-permute-start.1 = (f32[1,16,16,384]{3,2,1,0:T(8,128)S(1)}, f32[1,16,16,384]{3,2,1,0:T(8,128)S(1)}, u32[]{:S(2)}, u32[]{:S(2)}) collective-permute-start(f32[1,16,16,384]{3,2,1,0:T(8,128)S(1)} %get-tuple-element.1700), channel_id=1, source_target_pairs={{16,0},{32,16},{48,32},{64,48},{80,64},{96,80},{112,96},{17,1},{33... | collective-permute-start | bytes 1179656 | tf_op jit(solution)/shard_map/while/body/eval_jaxpr/ppermute | solution.py:14
  218.0 15.8 %collective-permute-start.1 = (f32[1,16,16,384]{3,2,1,0:T(8,128)S(1)}, f32[1,16,16,384]{3,2,1,0:T(8,128)S(1)}, u32[]{:S(2)}, u32[]{:S(2)}) collective-permute-start(f32[1,16,16,384]{3,2,1,0:T(8,128)S(1)} %get-tuple-element.1700), channel_id=1, source_target_pairs={{16,0},{32,16},{48,32},{64,48},{80,64},{96,80},{112,96},{17,1},{33... | collective-permute-start | bytes 1179656 | tf_op jit(solution)/shard_map/while/body/eval_jaxpr/ppermute | solution.py:14
  235.9 17.3 %collective-permute-start.1 = (f32[1,16,16,384]{3,2,1,0:T(8,128)S(1)}, f32[1,16,16,384]{3,2,1,0:T(8,128)S(1)}, u32[]{:S(2)}, u32[]{:S(2)}) collective-permute-start(f32[1,16,16,384]{3,2,1,0:T(8,128)S(1)} %get-tuple-element.1700), channel_id=1, source_target_pairs={{16,0},{32,16},{48,32},{64,48},{80,64},{96,80},{112,96},{17,1},{33... | collective-permute-start | bytes 1179656 | tf_op jit(solution)/shard_map/while/body/eval_jaxpr/ppermute | solution.py:14
  255.3 20.3 %collective-permute-start.1 = (f32[1,16,16,384]{3,2,1,0:T(8,128)S(1)}, f32[1,16,16,384]{3,2,1,0:T(8,128)S(1)}, u32[]{:S(2)}, u32[]{:S(2)}) collective-permute-start(f32[1,16,16,384]{3,2,1,0:T(8,128)S(1)} %get-tuple-element.1700), channel_id=1, source_target_pairs={{16,0},{32,16},{48,32},{64,48},{80,64},{96,80},{112,96},{17,1},{33... | collective-permute-start | bytes 1179656 | tf_op jit(solution)/shard_map/while/body/eval_jaxpr/ppermute | solution.py:14
  277.8 16.9 %collective-permute-start.1 = (f32[1,16,16,384]{3,2,1,0:T(8,128)S(1)}, f32[1,16,16,384]{3,2,1,0:T(8,128)S(1)}, u32[]{:S(2)}, u32[]{:S(2)}) collective-permute-start(f32[1,16,16,384]{3,2,1,0:T(8,128)S(1)} %get-tuple-element.1700), channel_id=1, source_target_pairs={{16,0},{32,16},{48,32},{64,48},{80,64},{96,80},{112,96},{17,1},{33... | collective-permute-start | bytes 1179656 | tf_op jit(solution)/shard_map/while/body/eval_jaxpr/ppermute | solution.py:14
  308.6 40.3 %collective-permute-start.1 = (f32[1,16,16,384]{3,2,1,0:T(8,128)S(1)}, f32[1,16,16,384]{3,2,1,0:T(8,128)S(1)}, u32[]{:S(2)}, u32[]{:S(2)}) collective-permute-start(f32[1,16,16,384]{3,2,1,0:T(8,128)S(1)} %get-tuple-element.1700), channel_id=1, source_target_pairs={{16,0},{32,16},{48,32},{64,48},{80,64},{96,80},{112,96},{17,1},{33... | collective-permute-start | bytes 1179656 | tf_op jit(solution)/shard_map/while/body/eval_jaxpr/ppermute | solution.py:14
  406.6 16.3 %collective-permute-start.1 = (f32[1,16,16,384]{3,2,1,0:T(8,128)S(1)}, f32[1,16,16,384]{3,2,1,0:T(8,128)S(1)}, u32[]{:S(2)}, u32[]{:S(2)}) collective-permute-start(f32[1,16,16,384]{3,2,1,0:T(8,128)S(1)} %get-tuple-element.1700), channel_id=1, source_target_pairs={{16,0},{32,16},{48,32},{64,48},{80,64},{96,80},{112,96},{17,1},{33... | collective-permute-start | bytes 1179656 | tf_op jit(solution)/shard_map/while/body/eval_jaxpr/ppermute | solution.py:14
  609.1 35.5 %collective-permute-start.2 = (f32[1,16,16,384]{3,2,1,0:T(8,128)S(1)}, f32[1,16,16,384]{3,2,1,0:T(8,128)S(1)}, u32[]{:S(2)}, u32[]{:S(2)}) collective-permute-start(f32[1,16,16,384]{3,2,1,0:T(8,128)S(1)} %get-tuple-element.1504), channel_id=1, source_target_pairs={{0,16},{16,32},{32,48},{48,64},{64,80},{80,96},{96,112},{1,17},{17... | collective-permute-start | bytes 1179656 | tf_op jit(solution)/shard_map/while/body/eval_jaxpr/ppermute | solution.py:14
  662.1 33.1 %collective-permute-start.2 = (f32[1,16,16,384]{3,2,1,0:T(8,128)S(1)}, f32[1,16,16,384]{3,2,1,0:T(8,128)S(1)}, u32[]{:S(2)}, u32[]{:S(2)}) collective-permute-start(f32[1,16,16,384]{3,2,1,0:T(8,128)S(1)} %get-tuple-element.1504), channel_id=1, source_target_pairs={{0,16},{16,32},{32,48},{48,64},{64,80},{80,96},{96,112},{1,17},{17... | collective-permute-start | bytes 1179656 | tf_op jit(solution)/shard_map/while/body/eval_jaxpr/ppermute | solution.py:14
  712.7 37.8 %collective-permute-start.2 = (f32[1,16,16,384]{3,2,1,0:T(8,128)S(1)}, f32[1,16,16,384]{3,2,1,0:T(8,128)S(1)}, u32[]{:S(2)}, u32[]{:S(2)}) collective-permute-start(f32[1,16,16,384]{3,2,1,0:T(8,128)S(1)} %get-tuple-element.1504), channel_id=1, source_target_pairs={{0,16},{16,32},{32,48},{48,64},{64,80},{80,96},{96,112},{1,17},{17... | collective-permute-start | bytes 1179656 | tf_op jit(solution)/shard_map/while/body/eval_jaxpr/ppermute | solution.py:14
  771.7 39.1 %collective-permute-start.2 = (f32[1,16,16,384]{3,2,1,0:T(8,128)S(1)}, f32[1,16,16,384]{3,2,1,0:T(8,128)S(1)}, u32[]{:S(2)}, u32[]{:S(2)}) collective-permute-start(f32[1,16,16,384]{3,2,1,0:T(8,128)S(1)} %get-tuple-element.1504), channel_id=1, source_target_pairs={{0,16},{16,32},{32,48},{48,64},{64,80},{80,96},{96,112},{1,17},{17... | collective-permute-start | bytes 1179656 | tf_op jit(solution)/shard_map/while/body/eval_jaxpr/ppermute | solution.py:14
  814.7 20.3 %collective-permute-start.3 = (f32[1,16,16,384]{3,2,1,0:T(8,128)}, f32[1,16,16,384]{3,2,1,0:T(8,128)S(1)}, u32[]{:S(2)}, u32[]{:S(2)}) collective-permute-start(f32[1,16,16,384]{3,2,1,0:T(8,128)} %get-tuple-element.1519), channel_id=1, source_target_pairs={{16,0},{32,16},{48,32},{64,48},{80,64},{96,80},{112,96},{17,1},{33... | collective-permute-start | bytes 1179656 | tf_op jit(solution)/shard_map/while/body/eval_jaxpr/ppermute | solution.py:14
  835.8 23.7 %collective-permute-start.3 = (f32[1,16,16,384]{3,2,1,0:T(8,128)}, f32[1,16,16,384]{3,2,1,0:T(8,128)S(1)}, u32[]{:S(2)}, u32[]{:S(2)}) collective-permute-start(f32[1,16,16,384]{3,2,1,0:T(8,128)} %get-tuple-element.1519), channel_id=1, source_target_pairs={{16,0},{32,16},{48,32},{64,48},{80,64},{96,80},{112,96},{17,1},{33... | collective-permute-start | bytes 1179656 | tf_op jit(solution)/shard_map/while/body/eval_jaxpr/ppermute | solution.py:14
  860.3 15.1 %collective-permute-start.3 = (f32[1,16,16,384]{3,2,1,0:T(8,128)}, f32[1,16,16,384]{3,2,1,0:T(8,128)S(1)}, u32[]{:S(2)}, u32[]{:S(2)}) collective-permute-start(f32[1,16,16,384]{3,2,1,0:T(8,128)} %get-tuple-element.1519), channel_id=1, source_target_pairs={{16,0},{32,16},{48,32},{64,48},{80,64},{96,80},{112,96},{17,1},{33... | collective-permute-start | bytes 1179656 | tf_op jit(solution)/shard_map/while/body/eval_jaxpr/ppermute | solution.py:14
  876.2 29.0 %collective-permute-start.3 = (f32[1,16,16,384]{3,2,1,0:T(8,128)}, f32[1,16,16,384]{3,2,1,0:T(8,128)S(1)}, u32[]{:S(2)}, u32[]{:S(2)}) collective-permute-start(f32[1,16,16,384]{3,2,1,0:T(8,128)} %get-tuple-element.1519), channel_id=1, source_target_pairs={{16,0},{32,16},{48,32},{64,48},{80,64},{96,80},{112,96},{17,1},{33... | collective-permute-start | bytes 1179656 | tf_op jit(solution)/shard_map/while/body/eval_jaxpr/ppermute | solution.py:14
  906.0 14.9 %collective-permute-start.3 = (f32[1,16,16,384]{3,2,1,0:T(8,128)}, f32[1,16,16,384]{3,2,1,0:T(8,128)S(1)}, u32[]{:S(2)}, u32[]{:S(2)}) collective-permute-start(f32[1,16,16,384]{3,2,1,0:T(8,128)} %get-tuple-element.1519), channel_id=1, source_target_pairs={{16,0},{32,16},{48,32},{64,48},{80,64},{96,80},{112,96},{17,1},{33... | collective-permute-start | bytes 1179656 | tf_op jit(solution)/shard_map/while/body/eval_jaxpr/ppermute | solution.py:14
  921.6 29.2 %collective-permute-start.3 = (f32[1,16,16,384]{3,2,1,0:T(8,128)}, f32[1,16,16,384]{3,2,1,0:T(8,128)S(1)}, u32[]{:S(2)}, u32[]{:S(2)}) collective-permute-start(f32[1,16,16,384]{3,2,1,0:T(8,128)} %get-tuple-element.1519), channel_id=1, source_target_pairs={{16,0},{32,16},{48,32},{64,48},{80,64},{96,80},{112,96},{17,1},{33... | collective-permute-start | bytes 1179656 | tf_op jit(solution)/shard_map/while/body/eval_jaxpr/ppermute | solution.py:14
  951.6 164.0 %collective-permute-start.3 = (f32[1,16,16,384]{3,2,1,0:T(8,128)}, f32[1,16,16,384]{3,2,1,0:T(8,128)S(1)}, u32[]{:S(2)}, u32[]{:S(2)}) collective-permute-start(f32[1,16,16,384]{3,2,1,0:T(8,128)} %get-tuple-element.1519), channel_id=1, source_target_pairs={{16,0},{32,16},{48,32},{64,48},{80,64},{96,80},{112,96},{17,1},{33... | collective-permute-start | bytes 1179656 | tf_op jit(solution)/shard_map/while/body/eval_jaxpr/ppermute | solution.py:14
  1210.3 16.2 %collective-permute-start.3 = (f32[1,16,16,384]{3,2,1,0:T(8,128)}, f32[1,16,16,384]{3,2,1,0:T(8,128)S(1)}, u32[]{:S(2)}, u32[]{:S(2)}) collective-permute-start(f32[1,16,16,384]{3,2,1,0:T(8,128)} %get-tuple-element.1519), channel_id=1, source_target_pairs={{16,0},{32,16},{48,32},{64,48},{80,64},{96,80},{112,96},{17,1},{33... | collective-permute-start | bytes 1179656 | tf_op jit(solution)/shard_map/while/body/eval_jaxpr/ppermute | solution.py:14
  1259.0 151.1 %reduce-scatter.5.cloned.1.call-start = ((), (), s32[]{:S(2)}) async-start(), calls=%async_computation.3 | async-start | bytes 11280384 | tf_op jit(solution)/shard_map/reduce_scatter | solution.py:241
  (65 other events, 367.3 us)
Sparse Core Ops, SparseCore 0:
  1259.1 70.8 reduce-scatter.2
  1333.0 77.0 reduce-scatter.4

commit v3 on v0

--- a/solution.py
+++ b/solution.py
@@ -108,9 +108,8 @@
     return lax.dynamic_slice_in_dim(buffer, slot_index, 1, 0)
 
 
-def store_row(buffer, piece, slot_index, active):
-    kept = pick_row(buffer, slot_index)
-    return lax.dynamic_update_slice_in_dim(buffer, jnp.where(active, piece, kept), slot_index, 0)
+def put_row(buffer, piece, slot_index):
+    return lax.dynamic_update_slice_in_dim(buffer, piece.astype(buffer.dtype), slot_index, 0)
 
 
 def shards(clean, noise, stamps, enc_weight, dec_weight):
@@ -128,108 +127,145 @@
     factor = 1.0 / math.sqrt(samples * lax.axis_size("dp") * clean.shape[1] * clean.shape[2])
     ticks_total = samples + sections - 1
     blank_piece = jnp.zeros((1,) + clean.shape[1:], jnp.float32)
-    blank_buffer = jnp.zeros(clean.shape, jnp.float32)
 
     def locate(tick_now, offset):
         sample_id = tick_now - offset
         active = (sample_id >= 0) & (sample_id < samples)
-        slot_index = jnp.clip(sample_id, 0, samples - 1)
-        return (active, slot_index)
+        slot_index = jnp.clip(sample_id, -1, samples) + 1
+        return (active, jnp.clip(sample_id, 0, samples - 1), slot_index)
+
+    def padded(inner_shape, dtype=jnp.float32):
+        return jnp.zeros((samples + 2,) + inner_shape, dtype)
+
+    def real_rows(buffer):
+        return buffer[1 : samples + 1]
+
+    row_shape = clean.shape[1:]
+    wide_shape = row_shape[:-1] + (2 * channels,)
 
     def encoder_tick(tick_now, carried):
         incoming, enc_inputs, skips = carried
-        active, slot_index = locate(tick_now, section_index)
-        source = jnp.where(section_index == 0, pick_row(noisy, slot_index), incoming)
-        stamp_one = pick_row(stamps, slot_index)
+        active, sample_at, slot_index = locate(tick_now, section_index)
+        source = jnp.where(section_index == 0, pick_row(noisy, sample_at), incoming)
+        stamp_one = pick_row(stamps, sample_at)
         result = lax.cond(
             active,
             lambda: block_forward(source, source, enc_kernel, stamp_one),
             lambda: blank_piece,
         )
-        enc_inputs = store_row(enc_inputs, source, slot_index, active)
-        skips = store_row(skips, result, slot_index, active)
+        enc_inputs = put_row(enc_inputs, source, slot_index)
+        skips = put_row(skips, result, slot_index)
         incoming = passed_along(result, "section", 1)
         return (incoming, enc_inputs, skips)
 
     _, enc_inputs, skips = lax.fori_loop(
-        0, ticks_total, encoder_tick, (blank_piece, blank_buffer, blank_buffer)
+        0, ticks_total, encoder_tick, (blank_piece, padded(row_shape), padded(row_shape))
     )
 
     def decoder_tick(tick_now, carried):
         incoming, dec_inputs, outputs = carried
-        active, slot_index = locate(tick_now, last_section - section_index)
+        active, sample_at, slot_index = locate(tick_now, last_section - section_index)
         skip_piece = pick_row(skips, slot_index)
         source = jnp.where(section_index == last_section, skip_piece, incoming)
         joined = jnp.concatenate([source, skip_piece], axis=3)
-        stamp_one = pick_row(stamps, slot_index)
+        stamp_one = pick_row(stamps, sample_at)
         result = lax.cond(
             active,
             lambda: block_forward(joined, source, dec_kernel, stamp_one),
             lambda: blank_piece,
         )
-        dec_inputs = store_row(dec_inputs, source, slot_index, active)
-        outputs = store_row(outputs, result, slot_index, active)
+        dec_inputs = put_row(dec_inputs, source, slot_index)
+        outputs = put_row(outputs, result, slot_index)
         incoming = passed_along(result, "section", -1)
         return (incoming, dec_inputs, outputs)
 
     _, dec_inputs, outputs = lax.fori_loop(
-        0, ticks_total, decoder_tick, (blank_piece, blank_buffer, blank_buffer)
-    )
+        0, ticks_total, decoder_tick, (blank_piece, padded(row_shape), padded(row_shape))
+    )
+
+    def input_backward(inputs, weight, stamp_one, cotangent):
+        activated, pullback = jax.vjp(lambda inner_field: activate(inner_field, stamp_one), inputs)
+        input_grad = pullback(conv_back(cotangent, weight))[0]
+        return (input_grad, activated.astype(jnp.bfloat16), cotangent.astype(jnp.bfloat16))
 
     def decoder_back_tick(tick_now, carried):
-        incoming, dec_acc, skip_grads, up_grads = carried
-        active, slot_index = locate(tick_now, section_index)
+        incoming, skip_grads, up_grads, dec_acts, dec_cots = carried
+        active, sample_at, slot_index = locate(tick_now, section_index)
         top_grad = factor * (
-            pick_row(outputs, slot_index) - pick_row(noise, slot_index).astype(jnp.float32)
+            pick_row(outputs, slot_index) - pick_row(noise, sample_at).astype(jnp.float32)
         )
         flowing = jnp.where(section_index == 0, top_grad, incoming)
         joined = jnp.concatenate(
             [pick_row(dec_inputs, slot_index), pick_row(skips, slot_index)], axis=3
         )
-        stamp_one = pick_row(stamps, slot_index)
-
-        def decoder_working(accum):
-            input_grad, weight_grad = block_backward(joined, dec_kernel, stamp_one, flowing)
+        stamp_one = pick_row(stamps, sample_at)
+
+        def decoder_working():
+            input_grad, acts, cots = input_backward(joined, dec_kernel, stamp_one, flowing)
             up_piece = input_grad[..., :channels] + flowing
-            return (accum + weight_grad, up_piece, input_grad[..., channels:])
-
-        def decoder_resting(accum):
-            return (accum, blank_piece, blank_piece)
-
-        dec_acc, up_piece, skip_grad = lax.cond(active, decoder_working, decoder_resting, dec_acc)
-        skip_grads = store_row(skip_grads, skip_grad, slot_index, active)
-        up_grads = store_row(up_grads, up_piece, slot_index, active)
+            return (up_piece, input_grad[..., channels:], acts, cots)
+
+        def decoder_resting():
+            return (
+                blank_piece,
+                blank_piece,
+                jnp.zeros((1,) + wide_shape, jnp.bfloat16),
+                jnp.zeros((1,) + row_shape, jnp.bfloat16),
+            )
+
+        up_piece, skip_grad, acts, cots = lax.cond(active, decoder_working, decoder_resting)
+        skip_grads = put_row(skip_grads, skip_grad, slot_index)
+        up_grads = put_row(up_grads, up_piece, slot_index)
+        dec_acts = put_row(dec_acts, acts, slot_index)
+        dec_cots = put_row(dec_cots, cots, slot_index)
         incoming = passed_along(up_piece, "section", 1)
-        return (incoming, dec_acc, skip_grads, up_grads)
-
-    dec_start = jnp.zeros(dec_kernel.shape, jnp.float32)
-    _, dec_acc, skip_grads, up_grads = lax.fori_loop(
-        0, ticks_total, decoder_back_tick, (blank_piece, dec_start, blank_buffer, blank_buffer)
-    )
+        return (incoming, skip_grads, up_grads, dec_acts, dec_cots)
+
+    _, skip_grads, up_grads, dec_acts, dec_cots = lax.fori_loop(
+        0,
+        ticks_total,
+        decoder_back_tick,
+        (
+            blank_piece,
+            padded(row_shape),
+            padded(row_shape),
+            padded(wide_shape, jnp.bfloat16),
+            padded(row_shape, jnp.bfloat16),
+        ),
+    )
+    dec_acc = conv_weight_grad(real_rows(dec_acts), real_rows(dec_cots))
 
     def encoder_back_tick(tick_now, carried):
-        incoming, enc_acc = carried
-        active, slot_index = locate(tick_now, last_section - section_index)
+        incoming, enc_acts, enc_cots = carried
+        active, sample_at, slot_index = locate(tick_now, last_section - section_index)
         arriving = jnp.where(
             section_index == last_section, pick_row(up_grads, slot_index), incoming
         )
         merged = arriving + pick_row(skip_grads, slot_index)
         block_input = pick_row(enc_inputs, slot_index)
-        stamp_one = pick_row(stamps, slot_index)
-
-        def encoder_working(accum):
-            input_grad, weight_grad = block_backward(block_input, enc_kernel, stamp_one, merged)
-            return (accum + weight_grad, input_grad + merged)
-
-        def encoder_resting(accum):
-            return (accum, blank_piece)
-
-        enc_acc, down_piece = lax.cond(active, encoder_working, encoder_resting, enc_acc)
+        stamp_one = pick_row(stamps, sample_at)
+
+        def encoder_working():
+            input_grad, acts, cots = input_backward(block_input, enc_kernel, stamp_one, merged)
+            return (input_grad + merged, acts, cots)
+
+        def encoder_resting():
+            blank_half = jnp.zeros((1,) + row_shape, jnp.bfloat16)
+            return (blank_piece, blank_half, blank_half)
+
+        down_piece, acts, cots = lax.cond(active, encoder_working, encoder_resting)
+        enc_acts = put_row(enc_acts, acts, slot_index)
+        enc_cots = put_row(enc_cots, cots, slot_index)
         incoming = passed_along(down_piece, "section", -1)
-        return (incoming, enc_acc)
-
-    enc_start = jnp.zeros(enc_kernel.shape, jnp.float32)
-    _, enc_acc = lax.fori_loop(0, ticks_total, encoder_back_tick, (blank_piece, enc_start))
+        return (incoming, enc_acts, enc_cots)
+
+    _, enc_acts, enc_cots = lax.fori_loop(
+        0,
+        ticks_total,
+        encoder_back_tick,
+        (blank_piece, padded(row_shape, jnp.bfloat16), padded(row_shape, jnp.bfloat16)),
+    )
+    enc_acc = conv_weight_grad(real_rows(enc_acts), real_rows(enc_cots))
     enc_share, dec_share = (
         lax.psum_scatter(enc_acc[None], "dp", scatter_dimension=3, tiled=True),
         lax.psum_scatter(dec_acc[None], "dp", scatter_dimension=3, tiled=True),

time: 1420 us -> 1360 us (0.958)
  local copies, waits for them, and re-layouts: 120 us -> 221 us
  waiting for transfers between devices: 709 us -> 608 us
  other arithmetic: 195 us -> 161 us
  starting transfers between devices: 269 us -> 242 us
    dynamic_update_slice x0 -> x66, local copies, waits for them, and re-layouts: none -> 86 us  [put_row(): lax.dynamic_update_slice_in_dim(buffer, piece.astype(buffer.dtype), slot_...]
    ppermute x44, waiting for transfers between devices: 558 us -> 481 us  [passed_along(): lax.ppermute(value, axis, [(source, source + steps) for source in range(i...]
    dynamic_update_slice x55 -> x22, other arithmetic: 106 us -> 42.8 us  [put_row(): lax.dynamic_update_slice_in_dim(buffer, piece.astype(buffer.dtype), slot_...]
    cond x80 -> x40, local copies, waits for them, and re-layouts: 44.1 us -> 1.84 us
    ppermute x44, starting transfers between devices: 269 us -> 242 us  [passed_along(): lax.ppermute(value, axis, [(source, source + steps) for source in range(i...]
    reduce_scatter x1, waiting for transfers between devices: 70.2 us -> 45.9 us  [shards(): lax.psum_scatter(enc_acc[None], 'dp', scatter_dimension=3, tiled=True)]
    another operation x0 -> x37, local copies, waits for them, and re-layouts: none -> 23.8 us
    dynamic_slice x38, local copies, waits for them, and re-layouts: 32.3 us -> 49.3 us  [pick_row(): return lax.dynamic_slice_in_dim(buffer, slot_index, 1, 0)]
  transfers between devices with their start and end apart: 46 -> 46, of which waited for: 46 -> 46; matrix products, arithmetic and copies ran while one was open for 4% -> 7% of each run, Pallas kernels for 0% -> 0%
where the time goes in v3:
time: 1360 us
  waiting for transfers between devices  608 us (45%)
  starting transfers between devices  242 us (18%)
  local copies, waits for them, and re-layouts  221 us (16%)
  other arithmetic  161 us (12%)
  matrix products  97.9 us (7%)
  between operations  14.2 us (1%)
  loops' own time  13.9 us (1%)
    ppermute x44, waiting for transfers between devices, passed_along(): lax.ppermute(value, axis, [(source, source + steps) for source in range(i...  481 us
    ppermute x44, starting transfers between devices, passed_along(): lax.ppermute(value, axis, [(source, source + steps) for source in range(i...  242 us
    dynamic_update_slice x66, local copies, waits for them, and re-layouts, put_row(): lax.dynamic_update_slice_in_dim(buffer, piece.astype(buffer.dtype), slot_...  86 us
    reduce_scatter x1, waiting for transfers between devices, shards(): lax.psum_scatter(dec_acc[None], 'dp', scatter_dimension=3, tiled=True)  80.5 us
    dot_general x72, matrix products, conv_back(): lax.dot_general(window, weight[row_off, col_off], (((1,), (1,)), ((), ())...  53.7 us
    dynamic_slice x38, local copies, waits for them, and re-layouts, pick_row(): return lax.dynamic_slice_in_dim(buffer, slot_index, 1, 0)  49.3 us
    reduce_scatter x1, waiting for transfers between devices, shards(): lax.psum_scatter(enc_acc[None], 'dp', scatter_dimension=3, tiled=True)  45.9 us
    dynamic_update_slice x22, other arithmetic, put_row(): lax.dynamic_update_slice_in_dim(buffer, piece.astype(buffer.dtype), slot_...  42.8 us
  transfers between devices with their start and end apart: 46, of which 46 were waited for; matrix products, arithmetic and copies ran while one was open for 7% of the time, Pallas kernels for 0%

profile of v3, /device:TPU:0, one launch (start us, length us, event | category | flops | bytes accessed | tf_op | source)
XLA Modules:
  0.0 1357.1 jit_solution(1991788094621111447)
XLA Ops:
  14.9 181.0 %while.80 = (s32[]{:T(128)}, f32[1,16,16,384]{3,2,1,0:T(8,128)}, f32[6,16,16,384]{3,2,1,0:T(8,128)}, f32[6,16,16,384]{3,2,1,0:T(8,128)}, s32[]{:T(128)}, /*index...) while((s32[]{:T(128)}, f32[1,16,16,384]{3,2,1,0:T(8,128)}, ...), condition=%wide.region_7.8_spmd, body=%wide.region_0.7_spmd.sunk | while | flops 681641472 | bytes 19400588 | solution.py:161
  199.9 269.8 %while.81 = (s32[]{:T(128)}, f32[1,16,16,384]{3,2,1,0:T(8,128)}, f32[6,16,16,384]{3,2,1,0:T(8,128)}, f32[6,16,16,384]{3,2,1,0:T(8,128)}, s32[]{:T(128)}, /*index...) while((s32[]{:T(128)}, f32[1,16,16,384]{3,2,1,0:T(8,128)}, ...), condition=%wide.region_15.16_spmd, body=%wide.region_8.15_spmd.sunk | while | flops 1362496512 | bytes 50201512 | solution.py:182
  259.3 17.7 %collective-permute-done.1 = f32[1,16,16,384]{3,2,1,0:T(8,128)} collective-permute-done((f32[1,16,16,384]{3,2,1,0:T(8,128)S(1)}, f32[1,16,16,384]{3,2,1,0:T(8,128)}, u32[]{:S(2)}, u32[]{:S(2)}) %collective-permute-start.1) | collective-permute-done | bytes 393248 | tf_op jit(solution)/shard_map/while/body/eval_jaxpr/ppermute | solution.py:14
  282.2 16.1 %collective-permute-done.1 = f32[1,16,16,384]{3,2,1,0:T(8,128)} collective-permute-done((f32[1,16,16,384]{3,2,1,0:T(8,128)S(1)}, f32[1,16,16,384]{3,2,1,0:T(8,128)}, u32[]{:S(2)}, u32[]{:S(2)}) %collective-permute-start.1) | collective-permute-done | bytes 393248 | tf_op jit(solution)/shard_map/while/body/eval_jaxpr/ppermute | solution.py:14
  316.6 48.4 %collective-permute-done.1 = f32[1,16,16,384]{3,2,1,0:T(8,128)} collective-permute-done((f32[1,16,16,384]{3,2,1,0:T(8,128)S(1)}, f32[1,16,16,384]{3,2,1,0:T(8,128)}, u32[]{:S(2)}, u32[]{:S(2)}) %collective-permute-start.1) | collective-permute-done | bytes 393248 | tf_op jit(solution)/shard_map/while/body/eval_jaxpr/ppermute | solution.py:14
  430.8 16.9 %collective-permute-done.1 = f32[1,16,16,384]{3,2,1,0:T(8,128)} collective-permute-done((f32[1,16,16,384]{3,2,1,0:T(8,128)S(1)}, f32[1,16,16,384]{3,2,1,0:T(8,128)}, u32[]{:S(2)}, u32[]{:S(2)}) %collective-permute-start.1) | collective-permute-done | bytes 393248 | tf_op jit(solution)/shard_map/while/body/eval_jaxpr/ppermute | solution.py:14
  476.4 374.0 %while.82 = (s32[]{:T(128)}, f32[1,16,16,384]{3,2,1,0:T(8,128)}, f32[6,16,16,384]{3,2,1,0:T(8,128)}, f32[6,16,16,384]{3,2,1,0:T(8,128)}, bf16[6,16,16,768]{3,2,1...) while((s32[]{:T(128)}, f32[1,16,16,384]{3,2,1,0:T(8,128)}, ...), condition=%wide.region_27.28_spmd, body=%wide.region_16.27_spmd.sunk | while | flops 1372523776 | bytes 65216728 | solution.py:224
  482.1 22.5 %conditional.10 = (f32[1,16,16,384]{3,2,1,0:T(8,128)}, f32[1,16,16,384]{3,2,1,0:T(8,128)}, bf16[1,16,16,768]{3,2,1,0:T(8,128)(2,1)}, bf16[1,16,16,384]{3,2,1,0:T(8,128)(2,1)}) conditional(s32[]{:T(128)} %convert_element_type.148, () %tuple.254, (pred[]{:T(512)}, f32[6,16,16,384]{3,2,1,0:T(8,128)}, s32[]{:T(128)}, ...), branch_computations={%region_17.17_spmd, %region_18.26_spmd} | conditional | flops 1372228864 | bytes 55580936 | solution.py:216
  518.0 22.5 %conditional.10 = (f32[1,16,16,384]{3,2,1,0:T(8,128)}, f32[1,16,16,384]{3,2,1,0:T(8,128)}, bf16[1,16,16,768]{3,2,1,0:T(8,128)(2,1)}, bf16[1,16,16,384]{3,2,1,0:T(8,128)(2,1)}) conditional(s32[]{:T(128)} %convert_element_type.148, () %tuple.254, (pred[]{:T(512)}, f32[6,16,16,384]{3,2,1,0:T(8,128)}, s32[]{:T(128)}, ...), branch_computations={%region_17.17_spmd, %region_18.26_spmd} | conditional | flops 1372228864 | bytes 55580936 | solution.py:216
  556.9 22.5 %conditional.10 = (f32[1,16,16,384]{3,2,1,0:T(8,128)}, f32[1,16,16,384]{3,2,1,0:T(8,128)}, bf16[1,16,16,768]{3,2,1,0:T(8,128)(2,1)}, bf16[1,16,16,384]{3,2,1,0:T(8,128)(2,1)}) conditional(s32[]{:T(128)} %convert_element_type.148, () %tuple.254, (pred[]{:T(512)}, f32[6,16,16,384]{3,2,1,0:T(8,128)}, s32[]{:T(128)}, ...), branch_computations={%region_17.17_spmd, %region_18.26_spmd} | conditional | flops 1372228864 | bytes 55580936 | solution.py:216
  595.9 22.5 %conditional.10 = (f32[1,16,16,384]{3,2,1,0:T(8,128)}, f32[1,16,16,384]{3,2,1,0:T(8,128)}, bf16[1,16,16,768]{3,2,1,0:T(8,128)(2,1)}, bf16[1,16,16,384]{3,2,1,0:T(8,128)(2,1)}) conditional(s32[]{:T(128)} %convert_element_type.148, () %tuple.254, (pred[]{:T(512)}, f32[6,16,16,384]{3,2,1,0:T(8,128)}, s32[]{:T(128)}, ...), branch_computations={%region_17.17_spmd, %region_18.26_spmd} | conditional | flops 1372228864 | bytes 55580936 | solution.py:216
  637.9 23.8 %collective-permute-start.2 = (f32[1,16,16,384]{3,2,1,0:T(8,128)}, f32[1,16,16,384]{3,2,1,0:T(8,128)S(1)}, u32[]{:S(2)}, u32[]{:S(2)}) collective-permute-start(f32[1,16,16,384]{3,2,1,0:T(8,128)} %get-tuple-element.1653), channel_id=1, source_target_pairs={{0,16},{16,32},{32,48},{48,64},{64,80},{80,96},{96,112},{1,17},{17... | collective-permute-start | bytes 1179656 | tf_op jit(solution)/shard_map/while/body/eval_jaxpr/ppermute | solution.py:14
  697.4 20.3 %collective-permute-start.2 = (f32[1,16,16,384]{3,2,1,0:T(8,128)}, f32[1,16,16,384]{3,2,1,0:T(8,128)S(1)}, u32[]{:S(2)}, u32[]{:S(2)}) collective-permute-start(f32[1,16,16,384]{3,2,1,0:T(8,128)} %get-tuple-element.1653), channel_id=1, source_target_pairs={{0,16},{16,32},{32,48},{48,64},{64,80},{80,96},{96,112},{1,17},{17... | collective-permute-start | bytes 1179656 | tf_op jit(solution)/shard_map/while/body/eval_jaxpr/ppermute | solution.py:14
  752.2 26.4 %collective-permute-start.2 = (f32[1,16,16,384]{3,2,1,0:T(8,128)}, f32[1,16,16,384]{3,2,1,0:T(8,128)S(1)}, u32[]{:S(2)}, u32[]{:S(2)}) collective-permute-start(f32[1,16,16,384]{3,2,1,0:T(8,128)} %get-tuple-element.1653), channel_id=1, source_target_pairs={{0,16},{16,32},{32,48},{48,64},{64,80},{80,96},{96,112},{1,17},{17... | collective-permute-start | bytes 1179656 | tf_op jit(solution)/shard_map/while/body/eval_jaxpr/ppermute | solution.py:14
  816.7 27.5 %collective-permute-start.2 = (f32[1,16,16,384]{3,2,1,0:T(8,128)}, f32[1,16,16,384]{3,2,1,0:T(8,128)S(1)}, u32[]{:S(2)}, u32[]{:S(2)}) collective-permute-start(f32[1,16,16,384]{3,2,1,0:T(8,128)} %get-tuple-element.1653), channel_id=1, source_target_pairs={{0,16},{16,32},{32,48},{48,64},{64,80},{80,96},{96,112},{1,17},{17... | collective-permute-start | bytes 1179656 | tf_op jit(solution)/shard_map/while/body/eval_jaxpr/ppermute | solution.py:14
  852.7 343.0 %while.83 = (s32[]{:T(128)}, f32[1,16,16,384]{3,2,1,0:T(8,128)S(1)}, bf16[6,16,16,384]{3,2,1,0:T(8,128)(2,1)}, bf16[6,16,16,384]{3,2,1,0:T(8,128)(2,1)}, s32[]{:...) while((s32[]{:T(128)}, ...), condition=%wide.region_39.40_spmd, body=%wide.region_28.39_spmd.sunk | while | flops 683902656 | bytes 23169172 | solution.py:262
  855.7 17.9 %collective-permute-done.3 = f32[1,16,16,384]{3,2,1,0:T(8,128)S(1)} collective-permute-done((f32[1,16,16,384]{3,2,1,0:T(8,128)}, f32[1,16,16,384]{3,2,1,0:T(8,128)S(1)}, u32[]{:S(2)}, u32[]{:S(2)}) %collective-permute-start.3) | collective-permute-done | bytes 393248 | tf_op jit(solution)/shard_map/while/body/eval_jaxpr/ppermute | solution.py:14
  876.6 16.6 %collective-permute-done.3 = f32[1,16,16,384]{3,2,1,0:T(8,128)S(1)} collective-permute-done((f32[1,16,16,384]{3,2,1,0:T(8,128)}, f32[1,16,16,384]{3,2,1,0:T(8,128)S(1)}, u32[]{:S(2)}, u32[]{:S(2)}) %collective-permute-start.3) | collective-permute-done | bytes 393248 | tf_op jit(solution)/shard_map/while/body/eval_jaxpr/ppermute | solution.py:14
  896.1 16.3 %collective-permute-done.3 = f32[1,16,16,384]{3,2,1,0:T(8,128)S(1)} collective-permute-done((f32[1,16,16,384]{3,2,1,0:T(8,128)}, f32[1,16,16,384]{3,2,1,0:T(8,128)S(1)}, u32[]{:S(2)}, u32[]{:S(2)}) %collective-permute-start.3) | collective-permute-done | bytes 393248 | tf_op jit(solution)/shard_map/while/body/eval_jaxpr/ppermute | solution.py:14
  915.3 22.0 %collective-permute-done.3 = f32[1,16,16,384]{3,2,1,0:T(8,128)S(1)} collective-permute-done((f32[1,16,16,384]{3,2,1,0:T(8,128)}, f32[1,16,16,384]{3,2,1,0:T(8,128)S(1)}, u32[]{:S(2)}, u32[]{:S(2)}) %collective-permute-start.3) | collective-permute-done | bytes 393248 | tf_op jit(solution)/shard_map/while/body/eval_jaxpr/ppermute | solution.py:14
  954.0 22.5 %collective-permute-done.3 = f32[1,16,16,384]{3,2,1,0:T(8,128)S(1)} collective-permute-done((f32[1,16,16,384]{3,2,1,0:T(8,128)}, f32[1,16,16,384]{3,2,1,0:T(8,128)S(1)}, u32[]{:S(2)}, u32[]{:S(2)}) %collective-permute-start.3) | collective-permute-done | bytes 393248 | tf_op jit(solution)/shard_map/while/body/eval_jaxpr/ppermute | solution.py:14
  979.4 107.1 %collective-permute-done.3 = f32[1,16,16,384]{3,2,1,0:T(8,128)S(1)} collective-permute-done((f32[1,16,16,384]{3,2,1,0:T(8,128)}, f32[1,16,16,384]{3,2,1,0:T(8,128)S(1)}, u32[]{:S(2)}, u32[]{:S(2)}) %collective-permute-start.3) | collective-permute-done | bytes 393248 | tf_op jit(solution)/shard_map/while/body/eval_jaxpr/ppermute | solution.py:14
  1223.8 45.9 %reduce-scatter.3.cloned.1.call-done = f32[1,3,3,24,384]{4,3,2,1,0:T(8,128)} async-done(((f32[1,3,3,384,384]{4,3,2,1,0:T(8,128)}), f32[1,3,3,24,384]{4,3,2,1,0:T(8,128)}) %reduce-scatter.3.cloned.1.call-update) | async-done | bytes 331792 | tf_op jit(solution)/shard_map/reduce_scatter | solution.py:270
  1269.7 80.5 %reduce-scatter.5.cloned.1.call-done = f32[1,3,3,48,384]{4,3,2,1,0:T(8,128)} async-done(((f32[1,3,3,768,384]{4,3,2,1,0:T(8,128)}), f32[1,3,3,48,384]{4,3,2,1,0:T(8,128)}) %reduce-scatter.5.cloned.1.call-update) | async-done | bytes 663568 | tf_op jit(solution)/shard_map/reduce_scatter | solution.py:271
  (962 shorter events, 945.6 us)
Async XLA Ops:
  7.2 1262.5 %reduce-scatter.3.cloned.1.call-start = ((), (), s32[]{:S(2)}) async-start(), calls=%async_computation.2 | async-start | bytes 5640192 | tf_op jit(solution)/shard_map/reduce_scatter | solution.py:270
  86.4 15.2 %collective-permute-start = (f32[1,16,16,384]{3,2,1,0:T(8,128)S(1)}, f32[1,16,16,384]{3,2,1,0:T(8,128)}, u32[]{:S(2)}, u32[]{:S(2)}) collective-permute-start(f32[1,16,16,384]{3,2,1,0:T(8,128)S(1)} %get-tuple-element.1884), channel_id=1, source_target_pairs={{0,16},{16,32},{32,48},{48,64},{64,80},{80,96},{96,112},{1,17},{17... | collective-permute-start | bytes 1179656 | tf_op jit(solution)/shard_map/while/body/eval_jaxpr/ppermute | solution.py:14
  142.0 17.9 %collective-permute-start = (f32[1,16,16,384]{3,2,1,0:T(8,128)S(1)}, f32[1,16,16,384]{3,2,1,0:T(8,128)}, u32[]{:S(2)}, u32[]{:S(2)}) collective-permute-start(f32[1,16,16,384]{3,2,1,0:T(8,128)S(1)} %get-tuple-element.1884), channel_id=1, source_target_pairs={{0,16},{16,32},{32,48},{48,64},{64,80},{80,96},{96,112},{1,17},{17... | collective-permute-start | bytes 1179656 | tf_op jit(solution)/shard_map/while/body/eval_jaxpr/ppermute | solution.py:14
  177.1 18.8 %collective-permute-start = (f32[1,16,16,384]{3,2,1,0:T(8,128)S(1)}, f32[1,16,16,384]{3,2,1,0:T(8,128)}, u32[]{:S(2)}, u32[]{:S(2)}) collective-permute-start(f32[1,16,16,384]{3,2,1,0:T(8,128)S(1)} %get-tuple-element.1884), channel_id=1, source_target_pairs={{0,16},{16,32},{32,48},{48,64},{64,80},{80,96},{96,112},{1,17},{17... | collective-permute-start | bytes 1179656 | tf_op jit(solution)/shard_map/while/body/eval_jaxpr/ppermute | solution.py:14
  203.1 14.0 %collective-permute-start.1 = (f32[1,16,16,384]{3,2,1,0:T(8,128)S(1)}, f32[1,16,16,384]{3,2,1,0:T(8,128)}, u32[]{:S(2)}, u32[]{:S(2)}) collective-permute-start(f32[1,16,16,384]{3,2,1,0:T(8,128)S(1)} %get-tuple-element.1885), channel_id=1, source_target_pairs={{16,0},{32,16},{48,32},{64,48},{80,64},{96,80},{112,96},{17,1},{33... | collective-permute-start | bytes 1179656 | tf_op jit(solution)/shard_map/while/body/eval_jaxpr/ppermute | solution.py:14
  220.3 14.7 %collective-permute-start.1 = (f32[1,16,16,384]{3,2,1,0:T(8,128)S(1)}, f32[1,16,16,384]{3,2,1,0:T(8,128)}, u32[]{:S(2)}, u32[]{:S(2)}) collective-permute-start(f32[1,16,16,384]{3,2,1,0:T(8,128)S(1)} %get-tuple-element.1885), channel_id=1, source_target_pairs={{16,0},{32,16},{48,32},{64,48},{80,64},{96,80},{112,96},{17,1},{33... | collective-permute-start | bytes 1179656 | tf_op jit(solution)/shard_map/while/body/eval_jaxpr/ppermute | solution.py:14
  238.1 15.8 %collective-permute-start.1 = (f32[1,16,16,384]{3,2,1,0:T(8,128)S(1)}, f32[1,16,16,384]{3,2,1,0:T(8,128)}, u32[]{:S(2)}, u32[]{:S(2)}) collective-permute-start(f32[1,16,16,384]{3,2,1,0:T(8,128)S(1)} %get-tuple-element.1885), channel_id=1, source_target_pairs={{16,0},{32,16},{48,32},{64,48},{80,64},{96,80},{112,96},{17,1},{33... | collective-permute-start | bytes 1179656 | tf_op jit(solution)/shard_map/while/body/eval_jaxpr/ppermute | solution.py:14
  257.2 19.8 %collective-permute-start.1 = (f32[1,16,16,384]{3,2,1,0:T(8,128)S(1)}, f32[1,16,16,384]{3,2,1,0:T(8,128)}, u32[]{:S(2)}, u32[]{:S(2)}) collective-permute-start(f32[1,16,16,384]{3,2,1,0:T(8,128)S(1)} %get-tuple-element.1885), channel_id=1, source_target_pairs={{16,0},{32,16},{48,32},{64,48},{80,64},{96,80},{112,96},{17,1},{33... | collective-permute-start | bytes 1179656 | tf_op jit(solution)/shard_map/while/body/eval_jaxpr/ppermute | solution.py:14
  280.2 18.2 %collective-permute-start.1 = (f32[1,16,16,384]{3,2,1,0:T(8,128)S(1)}, f32[1,16,16,384]{3,2,1,0:T(8,128)}, u32[]{:S(2)}, u32[]{:S(2)}) collective-permute-start(f32[1,16,16,384]{3,2,1,0:T(8,128)S(1)} %get-tuple-element.1885), channel_id=1, source_target_pairs={{16,0},{32,16},{48,32},{64,48},{80,64},{96,80},{112,96},{17,1},{33... | collective-permute-start | bytes 1179656 | tf_op jit(solution)/shard_map/while/body/eval_jaxpr/ppermute | solution.py:14
  314.6 50.5 %collective-permute-start.1 = (f32[1,16,16,384]{3,2,1,0:T(8,128)S(1)}, f32[1,16,16,384]{3,2,1,0:T(8,128)}, u32[]{:S(2)}, u32[]{:S(2)}) collective-permute-start(f32[1,16,16,384]{3,2,1,0:T(8,128)S(1)} %get-tuple-element.1885), channel_id=1, source_target_pairs={{16,0},{32,16},{48,32},{64,48},{80,64},{96,80},{112,96},{17,1},{33... | collective-permute-start | bytes 1179656 | tf_op jit(solution)/shard_map/while/body/eval_jaxpr/ppermute | solution.py:14
  428.7 19.0 %collective-permute-start.1 = (f32[1,16,16,384]{3,2,1,0:T(8,128)S(1)}, f32[1,16,16,384]{3,2,1,0:T(8,128)}, u32[]{:S(2)}, u32[]{:S(2)}) collective-permute-start(f32[1,16,16,384]{3,2,1,0:T(8,128)S(1)} %get-tuple-element.1885), channel_id=1, source_target_pairs={{16,0},{32,16},{48,32},{64,48},{80,64},{96,80},{112,96},{17,1},{33... | collective-permute-start | bytes 1179656 | tf_op jit(solution)/shard_map/while/body/eval_jaxpr/ppermute | solution.py:14
  637.9 29.4 %collective-permute-start.2 = (f32[1,16,16,384]{3,2,1,0:T(8,128)}, f32[1,16,16,384]{3,2,1,0:T(8,128)S(1)}, u32[]{:S(2)}, u32[]{:S(2)}) collective-permute-start(f32[1,16,16,384]{3,2,1,0:T(8,128)} %get-tuple-element.1653), channel_id=1, source_target_pairs={{0,16},{16,32},{32,48},{48,64},{64,80},{80,96},{96,112},{1,17},{17... | collective-permute-start | bytes 1179656 | tf_op jit(solution)/shard_map/while/body/eval_jaxpr/ppermute | solution.py:14
  697.4 25.9 %collective-permute-start.2 = (f32[1,16,16,384]{3,2,1,0:T(8,128)}, f32[1,16,16,384]{3,2,1,0:T(8,128)S(1)}, u32[]{:S(2)}, u32[]{:S(2)}) collective-permute-start(f32[1,16,16,384]{3,2,1,0:T(8,128)} %get-tuple-element.1653), channel_id=1, source_target_pairs={{0,16},{16,32},{32,48},{48,64},{64,80},{80,96},{96,112},{1,17},{17... | collective-permute-start | bytes 1179656 | tf_op jit(solution)/shard_map/while/body/eval_jaxpr/ppermute | solution.py:14
  752.2 31.9 %collective-permute-start.2 = (f32[1,16,16,384]{3,2,1,0:T(8,128)}, f32[1,16,16,384]{3,2,1,0:T(8,128)S(1)}, u32[]{:S(2)}, u32[]{:S(2)}) collective-permute-start(f32[1,16,16,384]{3,2,1,0:T(8,128)} %get-tuple-element.1653), channel_id=1, source_target_pairs={{0,16},{16,32},{32,48},{48,64},{64,80},{80,96},{96,112},{1,17},{17... | collective-permute-start | bytes 1179656 | tf_op jit(solution)/shard_map/while/body/eval_jaxpr/ppermute | solution.py:14
  816.7 33.0 %collective-permute-start.2 = (f32[1,16,16,384]{3,2,1,0:T(8,128)}, f32[1,16,16,384]{3,2,1,0:T(8,128)S(1)}, u32[]{:S(2)}, u32[]{:S(2)}) collective-permute-start(f32[1,16,16,384]{3,2,1,0:T(8,128)} %get-tuple-element.1653), channel_id=1, source_target_pairs={{0,16},{16,32},{32,48},{48,64},{64,80},{80,96},{96,112},{1,17},{17... | collective-permute-start | bytes 1179656 | tf_op jit(solution)/shard_map/while/body/eval_jaxpr/ppermute | solution.py:14
  853.6 20.0 %collective-permute-start.3 = (f32[1,16,16,384]{3,2,1,0:T(8,128)}, f32[1,16,16,384]{3,2,1,0:T(8,128)S(1)}, u32[]{:S(2)}, u32[]{:S(2)}) collective-permute-start(f32[1,16,16,384]{3,2,1,0:T(8,128)} %get-tuple-element.1670), channel_id=1, source_target_pairs={{16,0},{32,16},{48,32},{64,48},{80,64},{96,80},{112,96},{17,1},{33... | collective-permute-start | bytes 1179656 | tf_op jit(solution)/shard_map/while/body/eval_jaxpr/ppermute | solution.py:14
  874.5 18.7 %collective-permute-start.3 = (f32[1,16,16,384]{3,2,1,0:T(8,128)}, f32[1,16,16,384]{3,2,1,0:T(8,128)S(1)}, u32[]{:S(2)}, u32[]{:S(2)}) collective-permute-start(f32[1,16,16,384]{3,2,1,0:T(8,128)} %get-tuple-element.1670), channel_id=1, source_target_pairs={{16,0},{32,16},{48,32},{64,48},{80,64},{96,80},{112,96},{17,1},{33... | collective-permute-start | bytes 1179656 | tf_op jit(solution)/shard_map/while/body/eval_jaxpr/ppermute | solution.py:14
  894.0 18.4 %collective-permute-start.3 = (f32[1,16,16,384]{3,2,1,0:T(8,128)}, f32[1,16,16,384]{3,2,1,0:T(8,128)S(1)}, u32[]{:S(2)}, u32[]{:S(2)}) collective-permute-start(f32[1,16,16,384]{3,2,1,0:T(8,128)} %get-tuple-element.1670), channel_id=1, source_target_pairs={{16,0},{32,16},{48,32},{64,48},{80,64},{96,80},{112,96},{17,1},{33... | collective-permute-start | bytes 1179656 | tf_op jit(solution)/shard_map/while/body/eval_jaxpr/ppermute | solution.py:14
  913.2 24.1 %collective-permute-start.3 = (f32[1,16,16,384]{3,2,1,0:T(8,128)}, f32[1,16,16,384]{3,2,1,0:T(8,128)S(1)}, u32[]{:S(2)}, u32[]{:S(2)}) collective-permute-start(f32[1,16,16,384]{3,2,1,0:T(8,128)} %get-tuple-element.1670), channel_id=1, source_target_pairs={{16,0},{32,16},{48,32},{64,48},{80,64},{96,80},{112,96},{17,1},{33... | collective-permute-start | bytes 1179656 | tf_op jit(solution)/shard_map/while/body/eval_jaxpr/ppermute | solution.py:14
  951.9 24.6 %collective-permute-start.3 = (f32[1,16,16,384]{3,2,1,0:T(8,128)}, f32[1,16,16,384]{3,2,1,0:T(8,128)S(1)}, u32[]{:S(2)}, u32[]{:S(2)}) collective-permute-start(f32[1,16,16,384]{3,2,1,0:T(8,128)} %get-tuple-element.1670), channel_id=1, source_target_pairs={{16,0},{32,16},{48,32},{64,48},{80,64},{96,80},{112,96},{17,1},{33... | collective-permute-start | bytes 1179656 | tf_op jit(solution)/shard_map/while/body/eval_jaxpr/ppermute | solution.py:14
  977.3 109.2 %collective-permute-start.3 = (f32[1,16,16,384]{3,2,1,0:T(8,128)}, f32[1,16,16,384]{3,2,1,0:T(8,128)S(1)}, u32[]{:S(2)}, u32[]{:S(2)}) collective-permute-start(f32[1,16,16,384]{3,2,1,0:T(8,128)} %get-tuple-element.1670), channel_id=1, source_target_pairs={{16,0},{32,16},{48,32},{64,48},{80,64},{96,80},{112,96},{17,1},{33... | collective-permute-start | bytes 1179656 | tf_op jit(solution)/shard_map/while/body/eval_jaxpr/ppermute | solution.py:14
  1100.8 16.3 %collective-permute-start.3 = (f32[1,16,16,384]{3,2,1,0:T(8,128)}, f32[1,16,16,384]{3,2,1,0:T(8,128)S(1)}, u32[]{:S(2)}, u32[]{:S(2)}) collective-permute-start(f32[1,16,16,384]{3,2,1,0:T(8,128)} %get-tuple-element.1670), channel_id=1, source_target_pairs={{16,0},{32,16},{48,32},{64,48},{80,64},{96,80},{112,96},{17,1},{33... | collective-permute-start | bytes 1179656 | tf_op jit(solution)/shard_map/while/body/eval_jaxpr/ppermute | solution.py:14
  1131.4 14.8 %collective-permute-start.3 = (f32[1,16,16,384]{3,2,1,0:T(8,128)}, f32[1,16,16,384]{3,2,1,0:T(8,128)S(1)}, u32[]{:S(2)}, u32[]{:S(2)}) collective-permute-start(f32[1,16,16,384]{3,2,1,0:T(8,128)} %get-tuple-element.1670), channel_id=1, source_target_pairs={{16,0},{32,16},{48,32},{64,48},{80,64},{96,80},{112,96},{17,1},{33... | collective-permute-start | bytes 1179656 | tf_op jit(solution)/shard_map/while/body/eval_jaxpr/ppermute | solution.py:14
  1207.2 143.1 %reduce-scatter.5.cloned.1.call-start = ((), (), s32[]{:S(2)}) async-start(), calls=%async_computation.3 | async-start | bytes 11280384 | tf_op jit(solution)/shard_map/reduce_scatter | solution.py:271
  (58 other events, 341.6 us)
Sparse Core Ops, SparseCore 0:
  1207.3 62.3 reduce-scatter.2
  1272.7 77.5 reduce-scatter.4

commit v4 on v3

--- a/solution.py
+++ b/solution.py
@@ -33,36 +33,22 @@
 
 
 def conv_apply(activations, weight):
-    batch_rows, height, breadth, channels = activations.shape
-    padded = jnp.pad(activations, ((0, 0), (1, 1), (1, 1), (0, 0)))
-    summed = jnp.zeros((batch_rows * height * breadth, weight.shape[3]), jnp.float32)
-    for row_off in range(3):
-        for col_off in range(3):
-            window = padded[:, row_off : row_off + height, col_off : col_off + breadth, :].reshape(
-                -1, channels
-            )
-            summed = summed + jnp.dot(
-                window, weight[row_off, col_off], preferred_element_type=jnp.float32
-            )
-    return summed.reshape(batch_rows, height, breadth, weight.shape[3])
-
-
-def conv_back(cotangent, weight):
-    batch_rows, height, breadth, outputs = cotangent.shape
-    padded = jnp.pad(cotangent.astype(jnp.bfloat16), ((0, 0), (1, 1), (1, 1), (0, 0)))
-    summed = jnp.zeros((batch_rows * height * breadth, weight.shape[2]), jnp.float32)
-    for row_off in range(3):
-        for col_off in range(3):
-            window = padded[
-                :, 2 - row_off : 2 - row_off + height, 2 - col_off : 2 - col_off + breadth, :
-            ].reshape(-1, outputs)
-            summed = summed + lax.dot_general(
-                window,
-                weight[row_off, col_off],
-                (((1,), (1,)), ((), ())),
-                preferred_element_type=jnp.float32,
-            )
-    return summed.reshape(batch_rows, height, breadth, weight.shape[2])
+    return lax.conv_general_dilated(
+        activations,
+        weight,
+        window_strides=(1, 1),
+        padding=((1, 1), (1, 1)),
+        dimension_numbers=("NHWC", "HWIO", "NHWC"),
+        preferred_element_type=jnp.float32,
+    )
+
+
+def flipped(weight):
+    return jnp.flip(weight, (0, 1)).swapaxes(2, 3)
+
+
+def conv_back(cotangent, flipped_weight):
+    return conv_apply(cotangent.astype(jnp.bfloat16), flipped_weight)
 
 
 def conv_weight_grad(activations, cotangent):
@@ -90,14 +76,6 @@
     return residual + conv_apply(activations, weight)
 
 
-def block_backward(inputs, weight, stamps_in, cotangent):
-    activated, pullback = jax.vjp(lambda inner_field: activate(inner_field, stamps_in), inputs)
-    activations = activated.astype(jnp.bfloat16)
-    weight_grad = conv_weight_grad(activations, cotangent)
-    input_grad = pullback(conv_back(cotangent, weight))[0]
-    return (input_grad, weight_grad)
-
-
 def noise_levels(stamps_in):
     phase = (stamps_in.astype(jnp.float32) / 1000.0 + 0.008) / 1.008 * (math.pi / 2.0)
     signal = jnp.cos(phase) ** 2
@@ -120,6 +98,8 @@
     channels = clean.shape[3]
     enc_kernel = enc_weight[0]
     dec_kernel = dec_weight[0]
+    enc_back_kernel = flipped(enc_kernel)
+    dec_back_kernel = flipped(dec_kernel)
     keep_level, spread_level = noise_levels(stamps)
     noisy = keep_level[:, None, None, None] * clean.astype(jnp.float32) + spread_level[
         :, None, None, None
@@ -201,7 +181,7 @@
         stamp_one = pick_row(stamps, sample_at)
 
         def decoder_working():
-            input_grad, acts, cots = input_backward(joined, dec_kernel, stamp_one, flowing)
+            input_grad, acts, cots = input_backward(joined, dec_back_kernel, stamp_one, flowing)
             up_piece = input_grad[..., :channels] + flowing
             return (up_piece, input_grad[..., channels:], acts, cots)
 
@@ -246,7 +226,7 @@
         stamp_one = pick_row(stamps, sample_at)
 
         def encoder_working():
-            input_grad, acts, cots = input_backward(block_input, enc_kernel, stamp_one, merged)
+            input_grad, acts, cots = input_backward(block_input, enc_back_kernel, stamp_one, merged)
             return (input_grad + merged, acts, cots)
 
         def encoder_resting():

time: 1360 us -> 1200 us (0.88)
  other arithmetic: 161 us -> 97 us
  local copies, waits for them, and re-layouts: 221 us -> 180 us
  starting transfers between devices: 242 us -> 212 us
  matrix products: 97.9 us -> 76.6 us
    dot_general x144 -> x0, matrix products: 81.8 us -> none  [the longest x72 53.7 us: conv_back(): lax.dot_general(window, weight[row_off, col_off], (((1,), (1,)), ((), ())...]
    conv_general_dilated x0 -> x16, matrix products: none -> 60.5 us  [conv_apply(): lax.conv_general_dilated(activations, weight, window_strides=(1, 1), padd...]
    ppermute x44, starting transfers between devices: 242 us -> 212 us  [passed_along(): lax.ppermute(value, axis, [(source, source + steps) for source in range(i...]
    dynamic_update_slice x66, local copies, waits for them, and re-layouts: 86 us -> 64.6 us  [put_row(): lax.dynamic_update_slice_in_dim(buffer, piece.astype(buffer.dtype), slot_...]
    ppermute x44, waiting for transfers between devices: 481 us -> 462 us  [passed_along(): lax.ppermute(value, axis, [(source, source + steps) for source in range(i...]
    unnamed x10 -> x17, local copies, waits for them, and re-layouts: 1.81 us -> 17.4 us
    slice x16 -> x0, local copies, waits for them, and re-layouts: 14.9 us -> none  [the longest x8 13.1 us: conv_back(): padded[:, 2 - row_off:2 - row_off + height, 2 - col_off:2 - col_off + bre...]
where the time goes in v4:
time: 1200 us; the launch traced here: 1190 us
  waiting for transfers between devices  597 us (50%)
  starting transfers between devices  212 us (18%)
  local copies, waits for them, and re-layouts  180 us (15%)
  other arithmetic  97 us (8%)
  matrix products  76.6 us (6%)
  loops' own time  14.7 us (1%)
  between operations  14.3 us (1%)
    ppermute x44, waiting for transfers between devices, passed_along(): lax.ppermute(value, axis, [(source, source + steps) for source in range(i...  462 us
    ppermute x44, starting transfers between devices, passed_along(): lax.ppermute(value, axis, [(source, source + steps) for source in range(i...  212 us
    reduce_scatter x1, waiting for transfers between devices, shards(): lax.psum_scatter(dec_acc[None], 'dp', scatter_dimension=3, tiled=True)  80.1 us
    dynamic_update_slice x66, local copies, waits for them, and re-layouts, put_row(): lax.dynamic_update_slice_in_dim(buffer, piece.astype(buffer.dtype), slot_...  64.6 us
    conv_general_dilated x16, matrix products, conv_apply(): lax.conv_general_dilated(activations, weight, window_strides=(1, 1), padd...  60.5 us
    reduce_scatter x1, waiting for transfers between devices, shards(): lax.psum_scatter(enc_acc[None], 'dp', scatter_dimension=3, tiled=True)  55.2 us
    dynamic_slice x38, local copies, waits for them, and re-layouts, pick_row(): return lax.dynamic_slice_in_dim(buffer, slot_index, 1, 0)  42.8 us
    dynamic_update_slice x22, other arithmetic, put_row(): lax.dynamic_update_slice_in_dim(buffer, piece.astype(buffer.dtype), slot_...  31.8 us
  transfers between devices with their start and end apart: 46, of which 46 were waited for; matrix products, arithmetic and copies ran while one was open for 7% of the time, Pallas kernels for 0%

profile of v4, /device:TPU:0, one launch (start us, length us, event | category | flops | bytes accessed | tf_op | source)
XLA Modules:
  0.0 1191.0 jit_solution(1726388333590905149)
XLA Ops:
  34.1 185.1 %while.80 = (s32[]{:T(128)}, f32[1,16,16,384]{3,1,2,0:T(8,128)S(1)}, f32[6,16,16,384]{3,1,2,0:T(8,128)S(1)}, f32[6,16,16,384]{3,1,2,0:T(8,128)}, s32[]{:T(128)},...) while((s32[]{:T(128)}, ...), condition=%wide.region_7.8_spmd, body=%wide.region_0.7_spmd.sunk | while | flops 979748416 | bytes 12837928 | solution.py:141
  164.1 13.7 %collective-permute-start = (f32[1,16,16,384]{3,1,2,0:T(8,128)S(1)}, f32[1,16,16,384]{3,1,2,0:T(8,128)S(1)}, u32[]{:S(2)}, u32[]{:S(2)}) collective-permute-start(f32[1,16,16,384]{3,1,2,0:T(8,128)S(1)} %get-tuple-element.1901), channel_id=1, source_target_pairs={{0,16},{16,32},{32,48},{48,64},{64,80},{80,96},{96,112},{1,17},{17... | collective-permute-start | bytes 1179656 | tf_op jit(solution)/shard_map/while/body/eval_jaxpr/ppermute | solution.py:14
  198.5 15.4 %collective-permute-start = (f32[1,16,16,384]{3,1,2,0:T(8,128)S(1)}, f32[1,16,16,384]{3,1,2,0:T(8,128)S(1)}, u32[]{:S(2)}, u32[]{:S(2)}) collective-permute-start(f32[1,16,16,384]{3,1,2,0:T(8,128)S(1)} %get-tuple-element.1901), channel_id=1, source_target_pairs={{0,16},{16,32},{32,48},{48,64},{64,80},{80,96},{96,112},{1,17},{17... | collective-permute-start | bytes 1179656 | tf_op jit(solution)/shard_map/while/body/eval_jaxpr/ppermute | solution.py:14
  222.8 262.0 %while.81 = (s32[]{:T(128)}, f32[1,16,16,384]{3,1,2,0:T(8,128)S(1)}, f32[6,16,16,384]{3,1,2,0:T(8,128)}, f32[6,16,16,384]{3,1,2,0:T(8,128)}, s32[]{:T(128)}, /*i...) while((s32[]{:T(128)}, ...), condition=%wide.region_15.16_spmd, body=%wide.region_8.15_spmd.sunk | while | flops 1959349248 | bytes 20759588 | solution.py:162
  226.9 12.8 %collective-permute-done.1 = f32[1,16,16,384]{3,1,2,0:T(8,128)S(1)} collective-permute-done((f32[1,16,16,384]{3,1,2,0:T(8,128)S(1)}, f32[1,16,16,384]{3,1,2,0:T(8,128)S(1)}, u32[]{:S(2)}, u32[]{:S(2)}) %collective-permute-start.1) | collective-permute-done | bytes 393248 | tf_op jit(solution)/shard_map/while/body/eval_jaxpr/ppermute | solution.py:14
  243.7 15.1 %collective-permute-done.1 = f32[1,16,16,384]{3,1,2,0:T(8,128)S(1)} collective-permute-done((f32[1,16,16,384]{3,1,2,0:T(8,128)S(1)}, f32[1,16,16,384]{3,1,2,0:T(8,128)S(1)}, u32[]{:S(2)}, u32[]{:S(2)}) %collective-permute-start.1) | collective-permute-done | bytes 393248 | tf_op jit(solution)/shard_map/while/body/eval_jaxpr/ppermute | solution.py:14
  262.9 15.6 %collective-permute-done.1 = f32[1,16,16,384]{3,1,2,0:T(8,128)S(1)} collective-permute-done((f32[1,16,16,384]{3,1,2,0:T(8,128)S(1)}, f32[1,16,16,384]{3,1,2,0:T(8,128)S(1)}, u32[]{:S(2)}, u32[]{:S(2)}) %collective-permute-start.1) | collective-permute-done | bytes 393248 | tf_op jit(solution)/shard_map/while/body/eval_jaxpr/ppermute | solution.py:14
  282.5 17.7 %collective-permute-done.1 = f32[1,16,16,384]{3,1,2,0:T(8,128)S(1)} collective-permute-done((f32[1,16,16,384]{3,1,2,0:T(8,128)S(1)}, f32[1,16,16,384]{3,1,2,0:T(8,128)S(1)}, u32[]{:S(2)}, u32[]{:S(2)}) %collective-permute-start.1) | collective-permute-done | bytes 393248 | tf_op jit(solution)/shard_map/while/body/eval_jaxpr/ppermute | solution.py:14
  304.3 13.9 %collective-permute-done.1 = f32[1,16,16,384]{3,1,2,0:T(8,128)S(1)} collective-permute-done((f32[1,16,16,384]{3,1,2,0:T(8,128)S(1)}, f32[1,16,16,384]{3,1,2,0:T(8,128)S(1)}, u32[]{:S(2)}, u32[]{:S(2)}) %collective-permute-start.1) | collective-permute-done | bytes 393248 | tf_op jit(solution)/shard_map/while/body/eval_jaxpr/ppermute | solution.py:14
  333.8 51.3 %collective-permute-done.1 = f32[1,16,16,384]{3,1,2,0:T(8,128)S(1)} collective-permute-done((f32[1,16,16,384]{3,1,2,0:T(8,128)S(1)}, f32[1,16,16,384]{3,1,2,0:T(8,128)S(1)}, u32[]{:S(2)}, u32[]{:S(2)}) %collective-permute-start.1) | collective-permute-done | bytes 393248 | tf_op jit(solution)/shard_map/while/body/eval_jaxpr/ppermute | solution.py:14
  447.8 16.1 %collective-permute-done.1 = f32[1,16,16,384]{3,1,2,0:T(8,128)S(1)} collective-permute-done((f32[1,16,16,384]{3,1,2,0:T(8,128)S(1)}, f32[1,16,16,384]{3,1,2,0:T(8,128)S(1)}, u32[]{:S(2)}, u32[]{:S(2)}) %collective-permute-start.1) | collective-permute-done | bytes 393248 | tf_op jit(solution)/shard_map/while/body/eval_jaxpr/ppermute | solution.py:14
  490.9 248.9 %while.82 = (s32[]{:T(128)}, f32[1,16,16,384]{3,1,2,0:T(8,128)S(1)}, f32[6,16,16,384]{3,1,2,0:T(8,128)}, f32[6,16,16,384]{3,1,2,0:T(8,128)}, bf16[6,16,16,768]{3...) while((s32[]{:T(128)}, ...), condition=%wide.region_27.28_spmd, body=%wide.region_16.27_spmd.sunk | while | flops 1967262976 | bytes 31719764 | solution.py:204
  542.3 12.2 %conditional.10 = (f32[1,16,16,384]{3,1,2,0:T(8,128)S(1)}, f32[1,16,16,384]{3,1,2,0:T(8,128)S(1)}, bf16[1,16,16,768]{3,1,2,0:T(8,128)(2,1)S(1)}, bf16[1,16,16,384]{3,1,2,0:T(8,128)(2,1)S(1)}) conditional(s32[]{:T(128)} %convert_element_type.146, () %tuple.230, (pred[]{:T(512)}, f32[6,16,16,384]{3,1,2,0:T(8,128)}, s32[]{:T(128)}, ...), branch_computations={%region_17.17_spmd, %region_18.26_spmd} | conditional | flops 1966968064 | bytes 23656864 | solution.py:196
  592.4 16.4 %collective-permute-start.2 = (f32[1,16,16,384]{3,1,2,0:T(8,128)S(1)}, f32[1,16,16,384]{3,1,2,0:T(8,128)S(1)}, u32[]{:S(2)}, u32[]{:S(2)}) collective-permute-start(f32[1,16,16,384]{3,1,2,0:T(8,128)S(1)} %get-tuple-element.1670), channel_id=1, source_target_pairs={{0,16},{16,32},{32,48},{48,64},{64,80},{80,96},{96,112},{1,17},{17... | collective-permute-start | bytes 1179656 | tf_op jit(solution)/shard_map/while/body/eval_jaxpr/ppermute | solution.py:14
  666.1 19.3 %collective-permute-start.2 = (f32[1,16,16,384]{3,1,2,0:T(8,128)S(1)}, f32[1,16,16,384]{3,1,2,0:T(8,128)S(1)}, u32[]{:S(2)}, u32[]{:S(2)}) collective-permute-start(f32[1,16,16,384]{3,1,2,0:T(8,128)S(1)} %get-tuple-element.1670), channel_id=1, source_target_pairs={{0,16},{16,32},{32,48},{48,64},{64,80},{80,96},{96,112},{1,17},{17... | collective-permute-start | bytes 1179656 | tf_op jit(solution)/shard_map/while/body/eval_jaxpr/ppermute | solution.py:14
  710.4 24.1 %collective-permute-start.2 = (f32[1,16,16,384]{3,1,2,0:T(8,128)S(1)}, f32[1,16,16,384]{3,1,2,0:T(8,128)S(1)}, u32[]{:S(2)}, u32[]{:S(2)}) collective-permute-start(f32[1,16,16,384]{3,1,2,0:T(8,128)S(1)} %get-tuple-element.1670), channel_id=1, source_target_pairs={{0,16},{16,32},{32,48},{48,64},{64,80},{80,96},{96,112},{1,17},{17... | collective-permute-start | bytes 1179656 | tf_op jit(solution)/shard_map/while/body/eval_jaxpr/ppermute | solution.py:14
  742.1 278.8 %while.83 = (s32[]{:T(128)}, f32[1,16,16,384]{3,1,2,0:T(8,128)S(1)}, bf16[6,16,16,384]{3,2,1,0:T(8,128)(2,1)}, bf16[6,16,16,384]{3,2,1,0:T(8,128)(2,1)}, s32[]{:...) while((s32[]{:T(128)}, ...), condition=%wide.region_39.40_spmd, body=%wide.region_28.39_spmd.sunk | while | flops 982009536 | bytes 27224392 | solution.py:242
  762.1 13.6 %collective-permute-done.3 = f32[1,16,16,384]{3,1,2,0:T(8,128)S(1)} collective-permute-done((f32[1,16,16,384]{3,1,2,0:T(8,128)}, f32[1,16,16,384]{3,1,2,0:T(8,128)S(1)}, u32[]{:S(2)}, u32[]{:S(2)}) %collective-permute-start.3) | collective-permute-done | bytes 393248 | tf_op jit(solution)/shard_map/while/body/eval_jaxpr/ppermute | solution.py:14
  795.3 13.2 %collective-permute-done.3 = f32[1,16,16,384]{3,1,2,0:T(8,128)S(1)} collective-permute-done((f32[1,16,16,384]{3,1,2,0:T(8,128)}, f32[1,16,16,384]{3,1,2,0:T(8,128)S(1)}, u32[]{:S(2)}, u32[]{:S(2)}) %collective-permute-start.3) | collective-permute-done | bytes 393248 | tf_op jit(solution)/shard_map/while/body/eval_jaxpr/ppermute | solution.py:14
  828.1 15.4 %collective-permute-done.3 = f32[1,16,16,384]{3,1,2,0:T(8,128)S(1)} collective-permute-done((f32[1,16,16,384]{3,1,2,0:T(8,128)}, f32[1,16,16,384]{3,1,2,0:T(8,128)S(1)}, u32[]{:S(2)}, u32[]{:S(2)}) %collective-permute-start.3) | collective-permute-done | bytes 393248 | tf_op jit(solution)/shard_map/while/body/eval_jaxpr/ppermute | solution.py:14
  848.0 81.4 %collective-permute-done.3 = f32[1,16,16,384]{3,1,2,0:T(8,128)S(1)} collective-permute-done((f32[1,16,16,384]{3,1,2,0:T(8,128)}, f32[1,16,16,384]{3,1,2,0:T(8,128)S(1)}, u32[]{:S(2)}, u32[]{:S(2)}) %collective-permute-start.3) | collective-permute-done | bytes 393248 | tf_op jit(solution)/shard_map/while/body/eval_jaxpr/ppermute | solution.py:14
  943.2 13.9 %collective-permute-done.3 = f32[1,16,16,384]{3,1,2,0:T(8,128)S(1)} collective-permute-done((f32[1,16,16,384]{3,1,2,0:T(8,128)}, f32[1,16,16,384]{3,1,2,0:T(8,128)S(1)}, u32[]{:S(2)}, u32[]{:S(2)}) %collective-permute-start.3) | collective-permute-done | bytes 393248 | tf_op jit(solution)/shard_map/while/body/eval_jaxpr/ppermute | solution.py:14
  1048.9 55.2 %reduce-scatter.3.cloned.1.call-done = f32[1,3,3,24,384]{4,3,2,1,0:T(8,128)} async-done(((f32[1,3,3,384,384]{4,3,2,1,0:T(8,128)}), f32[1,3,3,24,384]{4,3,2,1,0:T(8,128)}) %reduce-scatter.3.cloned.1.call-update) | async-done | bytes 331792 | tf_op jit(solution)/shard_map/reduce_scatter | solution.py:250
  1104.1 80.1 %reduce-scatter.5.cloned.1.call-done = f32[1,3,3,48,384]{4,3,2,1,0:T(8,128)} async-done(((f32[1,3,3,768,384]{4,3,2,1,0:T(8,128)}), f32[1,3,3,48,384]{4,3,2,1,0:T(8,128)}) %reduce-scatter.5.cloned.1.call-update) | async-done | bytes 663568 | tf_op jit(solution)/shard_map/reduce_scatter | solution.py:251
  (905 shorter events, 814.6 us)
Async XLA Ops:
  7.2 1096.9 %reduce-scatter.3.cloned.1.call-start = ((), (), s32[]{:S(2)}) async-start(), calls=%async_computation.2 | async-start | bytes 5640192 | tf_op jit(solution)/shard_map/reduce_scatter | solution.py:250
  108.1 16.6 %collective-permute-start = (f32[1,16,16,384]{3,1,2,0:T(8,128)S(1)}, f32[1,16,16,384]{3,1,2,0:T(8,128)S(1)}, u32[]{:S(2)}, u32[]{:S(2)}) collective-permute-start(f32[1,16,16,384]{3,1,2,0:T(8,128)S(1)} %get-tuple-element.1901), channel_id=1, source_target_pairs={{0,16},{16,32},{32,48},{48,64},{64,80},{80,96},{96,112},{1,17},{17... | collective-permute-start | bytes 1179656 | tf_op jit(solution)/shard_map/while/body/eval_jaxpr/ppermute | solution.py:14
  136.6 15.6 %collective-permute-start = (f32[1,16,16,384]{3,1,2,0:T(8,128)S(1)}, f32[1,16,16,384]{3,1,2,0:T(8,128)S(1)}, u32[]{:S(2)}, u32[]{:S(2)}) collective-permute-start(f32[1,16,16,384]{3,1,2,0:T(8,128)S(1)} %get-tuple-element.1901), channel_id=1, source_target_pairs={{0,16},{16,32},{32,48},{48,64},{64,80},{80,96},{96,112},{1,17},{17... | collective-permute-start | bytes 1179656 | tf_op jit(solution)/shard_map/while/body/eval_jaxpr/ppermute | solution.py:14
  164.1 18.9 %collective-permute-start = (f32[1,16,16,384]{3,1,2,0:T(8,128)S(1)}, f32[1,16,16,384]{3,1,2,0:T(8,128)S(1)}, u32[]{:S(2)}, u32[]{:S(2)}) collective-permute-start(f32[1,16,16,384]{3,1,2,0:T(8,128)S(1)} %get-tuple-element.1901), channel_id=1, source_target_pairs={{0,16},{16,32},{32,48},{48,64},{64,80},{80,96},{96,112},{1,17},{17... | collective-permute-start | bytes 1179656 | tf_op jit(solution)/shard_map/while/body/eval_jaxpr/ppermute | solution.py:14
  198.5 20.7 %collective-permute-start = (f32[1,16,16,384]{3,1,2,0:T(8,128)S(1)}, f32[1,16,16,384]{3,1,2,0:T(8,128)S(1)}, u32[]{:S(2)}, u32[]{:S(2)}) collective-permute-start(f32[1,16,16,384]{3,1,2,0:T(8,128)S(1)} %get-tuple-element.1901), channel_id=1, source_target_pairs={{0,16},{16,32},{32,48},{48,64},{64,80},{80,96},{96,112},{1,17},{17... | collective-permute-start | bytes 1179656 | tf_op jit(solution)/shard_map/while/body/eval_jaxpr/ppermute | solution.py:14
  224.8 14.9 %collective-permute-start.1 = (f32[1,16,16,384]{3,1,2,0:T(8,128)S(1)}, f32[1,16,16,384]{3,1,2,0:T(8,128)S(1)}, u32[]{:S(2)}, u32[]{:S(2)}) collective-permute-start(f32[1,16,16,384]{3,1,2,0:T(8,128)S(1)} %get-tuple-element.1902), channel_id=1, source_target_pairs={{16,0},{32,16},{48,32},{64,48},{80,64},{96,80},{112,96},{17,1},{33... | collective-permute-start | bytes 1179656 | tf_op jit(solution)/shard_map/while/body/eval_jaxpr/ppermute | solution.py:14
  241.6 17.2 %collective-permute-start.1 = (f32[1,16,16,384]{3,1,2,0:T(8,128)S(1)}, f32[1,16,16,384]{3,1,2,0:T(8,128)S(1)}, u32[]{:S(2)}, u32[]{:S(2)}) collective-permute-start(f32[1,16,16,384]{3,1,2,0:T(8,128)S(1)} %get-tuple-element.1902), channel_id=1, source_target_pairs={{16,0},{32,16},{48,32},{64,48},{80,64},{96,80},{112,96},{17,1},{33... | collective-permute-start | bytes 1179656 | tf_op jit(solution)/shard_map/while/body/eval_jaxpr/ppermute | solution.py:14
  260.8 17.7 %collective-permute-start.1 = (f32[1,16,16,384]{3,1,2,0:T(8,128)S(1)}, f32[1,16,16,384]{3,1,2,0:T(8,128)S(1)}, u32[]{:S(2)}, u32[]{:S(2)}) collective-permute-start(f32[1,16,16,384]{3,1,2,0:T(8,128)S(1)} %get-tuple-element.1902), channel_id=1, source_target_pairs={{16,0},{32,16},{48,32},{64,48},{80,64},{96,80},{112,96},{17,1},{33... | collective-permute-start | bytes 1179656 | tf_op jit(solution)/shard_map/while/body/eval_jaxpr/ppermute | solution.py:14
  280.4 19.8 %collective-permute-start.1 = (f32[1,16,16,384]{3,1,2,0:T(8,128)S(1)}, f32[1,16,16,384]{3,1,2,0:T(8,128)S(1)}, u32[]{:S(2)}, u32[]{:S(2)}) collective-permute-start(f32[1,16,16,384]{3,1,2,0:T(8,128)S(1)} %get-tuple-element.1902), channel_id=1, source_target_pairs={{16,0},{32,16},{48,32},{64,48},{80,64},{96,80},{112,96},{17,1},{33... | collective-permute-start | bytes 1179656 | tf_op jit(solution)/shard_map/while/body/eval_jaxpr/ppermute | solution.py:14
  302.2 16.0 %collective-permute-start.1 = (f32[1,16,16,384]{3,1,2,0:T(8,128)S(1)}, f32[1,16,16,384]{3,1,2,0:T(8,128)S(1)}, u32[]{:S(2)}, u32[]{:S(2)}) collective-permute-start(f32[1,16,16,384]{3,1,2,0:T(8,128)S(1)} %get-tuple-element.1902), channel_id=1, source_target_pairs={{16,0},{32,16},{48,32},{64,48},{80,64},{96,80},{112,96},{17,1},{33... | collective-permute-start | bytes 1179656 | tf_op jit(solution)/shard_map/while/body/eval_jaxpr/ppermute | solution.py:14
  331.8 53.4 %collective-permute-start.1 = (f32[1,16,16,384]{3,1,2,0:T(8,128)S(1)}, f32[1,16,16,384]{3,1,2,0:T(8,128)S(1)}, u32[]{:S(2)}, u32[]{:S(2)}) collective-permute-start(f32[1,16,16,384]{3,1,2,0:T(8,128)S(1)} %get-tuple-element.1902), channel_id=1, source_target_pairs={{16,0},{32,16},{48,32},{64,48},{80,64},{96,80},{112,96},{17,1},{33... | collective-permute-start | bytes 1179656 | tf_op jit(solution)/shard_map/while/body/eval_jaxpr/ppermute | solution.py:14
  445.7 18.1 %collective-permute-start.1 = (f32[1,16,16,384]{3,1,2,0:T(8,128)S(1)}, f32[1,16,16,384]{3,1,2,0:T(8,128)S(1)}, u32[]{:S(2)}, u32[]{:S(2)}) collective-permute-start(f32[1,16,16,384]{3,1,2,0:T(8,128)S(1)} %get-tuple-element.1902), channel_id=1, source_target_pairs={{16,0},{32,16},{48,32},{64,48},{80,64},{96,80},{112,96},{17,1},{33... | collective-permute-start | bytes 1179656 | tf_op jit(solution)/shard_map/while/body/eval_jaxpr/ppermute | solution.py:14
  592.4 23.0 %collective-permute-start.2 = (f32[1,16,16,384]{3,1,2,0:T(8,128)S(1)}, f32[1,16,16,384]{3,1,2,0:T(8,128)S(1)}, u32[]{:S(2)}, u32[]{:S(2)}) collective-permute-start(f32[1,16,16,384]{3,1,2,0:T(8,128)S(1)} %get-tuple-element.1670), channel_id=1, source_target_pairs={{0,16},{16,32},{32,48},{48,64},{64,80},{80,96},{96,112},{1,17},{17... | collective-permute-start | bytes 1179656 | tf_op jit(solution)/shard_map/while/body/eval_jaxpr/ppermute | solution.py:14
  633.9 15.9 %collective-permute-start.2 = (f32[1,16,16,384]{3,1,2,0:T(8,128)S(1)}, f32[1,16,16,384]{3,1,2,0:T(8,128)S(1)}, u32[]{:S(2)}, u32[]{:S(2)}) collective-permute-start(f32[1,16,16,384]{3,1,2,0:T(8,128)S(1)} %get-tuple-element.1670), channel_id=1, source_target_pairs={{0,16},{16,32},{32,48},{48,64},{64,80},{80,96},{96,112},{1,17},{17... | collective-permute-start | bytes 1179656 | tf_op jit(solution)/shard_map/while/body/eval_jaxpr/ppermute | solution.py:14
  666.1 24.6 %collective-permute-start.2 = (f32[1,16,16,384]{3,1,2,0:T(8,128)S(1)}, f32[1,16,16,384]{3,1,2,0:T(8,128)S(1)}, u32[]{:S(2)}, u32[]{:S(2)}) collective-permute-start(f32[1,16,16,384]{3,1,2,0:T(8,128)S(1)} %get-tuple-element.1670), channel_id=1, source_target_pairs={{0,16},{16,32},{32,48},{48,64},{64,80},{80,96},{96,112},{1,17},{17... | collective-permute-start | bytes 1179656 | tf_op jit(solution)/shard_map/while/body/eval_jaxpr/ppermute | solution.py:14
  710.4 29.3 %collective-permute-start.2 = (f32[1,16,16,384]{3,1,2,0:T(8,128)S(1)}, f32[1,16,16,384]{3,1,2,0:T(8,128)S(1)}, u32[]{:S(2)}, u32[]{:S(2)}) collective-permute-start(f32[1,16,16,384]{3,1,2,0:T(8,128)S(1)} %get-tuple-element.1670), channel_id=1, source_target_pairs={{0,16},{16,32},{32,48},{48,64},{64,80},{80,96},{96,112},{1,17},{17... | collective-permute-start | bytes 1179656 | tf_op jit(solution)/shard_map/while/body/eval_jaxpr/ppermute | solution.py:14
  743.6 14.0 %collective-permute-start.3 = (f32[1,16,16,384]{3,1,2,0:T(8,128)}, f32[1,16,16,384]{3,1,2,0:T(8,128)S(1)}, u32[]{:S(2)}, u32[]{:S(2)}) collective-permute-start(f32[1,16,16,384]{3,1,2,0:T(8,128)} %get-tuple-element.1687), channel_id=1, source_target_pairs={{16,0},{32,16},{48,32},{64,48},{80,64},{96,80},{112,96},{17,1},{33... | collective-permute-start | bytes 1179656 | tf_op jit(solution)/shard_map/while/body/eval_jaxpr/ppermute | solution.py:14
  759.1 16.7 %collective-permute-start.3 = (f32[1,16,16,384]{3,1,2,0:T(8,128)}, f32[1,16,16,384]{3,1,2,0:T(8,128)S(1)}, u32[]{:S(2)}, u32[]{:S(2)}) collective-permute-start(f32[1,16,16,384]{3,1,2,0:T(8,128)} %get-tuple-element.1687), channel_id=1, source_target_pairs={{16,0},{32,16},{48,32},{64,48},{80,64},{96,80},{112,96},{17,1},{33... | collective-permute-start | bytes 1179656 | tf_op jit(solution)/shard_map/while/body/eval_jaxpr/ppermute | solution.py:14
  792.2 16.3 %collective-permute-start.3 = (f32[1,16,16,384]{3,1,2,0:T(8,128)}, f32[1,16,16,384]{3,1,2,0:T(8,128)S(1)}, u32[]{:S(2)}, u32[]{:S(2)}) collective-permute-start(f32[1,16,16,384]{3,1,2,0:T(8,128)} %get-tuple-element.1687), channel_id=1, source_target_pairs={{16,0},{32,16},{48,32},{64,48},{80,64},{96,80},{112,96},{17,1},{33... | collective-permute-start | bytes 1179656 | tf_op jit(solution)/shard_map/while/body/eval_jaxpr/ppermute | solution.py:14
  810.0 13.5 %collective-permute-start.3 = (f32[1,16,16,384]{3,1,2,0:T(8,128)}, f32[1,16,16,384]{3,1,2,0:T(8,128)S(1)}, u32[]{:S(2)}, u32[]{:S(2)}) collective-permute-start(f32[1,16,16,384]{3,1,2,0:T(8,128)} %get-tuple-element.1687), channel_id=1, source_target_pairs={{16,0},{32,16},{48,32},{64,48},{80,64},{96,80},{112,96},{17,1},{33... | collective-permute-start | bytes 1179656 | tf_op jit(solution)/shard_map/while/body/eval_jaxpr/ppermute | solution.py:14
  825.0 18.5 %collective-permute-start.3 = (f32[1,16,16,384]{3,1,2,0:T(8,128)}, f32[1,16,16,384]{3,1,2,0:T(8,128)S(1)}, u32[]{:S(2)}, u32[]{:S(2)}) collective-permute-start(f32[1,16,16,384]{3,1,2,0:T(8,128)} %get-tuple-element.1687), channel_id=1, source_target_pairs={{16,0},{32,16},{48,32},{64,48},{80,64},{96,80},{112,96},{17,1},{33... | collective-permute-start | bytes 1179656 | tf_op jit(solution)/shard_map/while/body/eval_jaxpr/ppermute | solution.py:14
  845.0 84.5 %collective-permute-start.3 = (f32[1,16,16,384]{3,1,2,0:T(8,128)}, f32[1,16,16,384]{3,1,2,0:T(8,128)S(1)}, u32[]{:S(2)}, u32[]{:S(2)}) collective-permute-start(f32[1,16,16,384]{3,1,2,0:T(8,128)} %get-tuple-element.1687), channel_id=1, source_target_pairs={{16,0},{32,16},{48,32},{64,48},{80,64},{96,80},{112,96},{17,1},{33... | collective-permute-start | bytes 1179656 | tf_op jit(solution)/shard_map/while/body/eval_jaxpr/ppermute | solution.py:14
  940.1 16.9 %collective-permute-start.3 = (f32[1,16,16,384]{3,1,2,0:T(8,128)}, f32[1,16,16,384]{3,1,2,0:T(8,128)S(1)}, u32[]{:S(2)}, u32[]{:S(2)}) collective-permute-start(f32[1,16,16,384]{3,1,2,0:T(8,128)} %get-tuple-element.1687), channel_id=1, source_target_pairs={{16,0},{32,16},{48,32},{64,48},{80,64},{96,80},{112,96},{17,1},{33... | collective-permute-start | bytes 1179656 | tf_op jit(solution)/shard_map/while/body/eval_jaxpr/ppermute | solution.py:14
  1032.2 151.9 %reduce-scatter.5.cloned.1.call-start = ((), (), s32[]{:S(2)}) async-start(), calls=%async_computation.3 | async-start | bytes 11280384 | tf_op jit(solution)/shard_map/reduce_scatter | solution.py:251
  (65 other events, 342.1 us)
Sparse Core Ops, SparseCore 0:
  1032.3 71.6 reduce-scatter.2
  1107.1 77.0 reduce-scatter.4

commit v5 on v4

--- a/solution.py
+++ b/solution.py
@@ -246,10 +246,19 @@
         (blank_piece, padded(row_shape, jnp.bfloat16), padded(row_shape, jnp.bfloat16)),
     )
     enc_acc = conv_weight_grad(real_rows(enc_acts), real_rows(enc_cots))
-    enc_share, dec_share = (
-        lax.psum_scatter(enc_acc[None], "dp", scatter_dimension=3, tiled=True),
-        lax.psum_scatter(dec_acc[None], "dp", scatter_dimension=3, tiled=True),
-    )
+    replicas = lax.axis_size("dp")
+    enc_rows = enc_acc.shape[2] // replicas
+    dec_rows = dec_acc.shape[2] // replicas
+    both = jnp.concatenate(
+        [
+            enc_acc.reshape(3, 3, replicas, enc_rows, -1),
+            dec_acc.reshape(3, 3, replicas, dec_rows, -1),
+        ],
+        axis=3,
+    ).reshape(1, 3, 3, replicas * (enc_rows + dec_rows), -1)
+    share = lax.psum_scatter(both, "dp", scatter_dimension=3, tiled=True)
+    enc_share = share[:, :, :, :enc_rows]
+    dec_share = share[:, :, :, enc_rows:]
     return (enc_share, dec_share)
 
 

time: 1200 us -> 1160 us (0.967)
  waiting for transfers between devices: 597 us -> 575 us
    reduce_scatter x2 -> x1, waiting for transfers between devices: 135 us -> 98.1 us  [shards(): share = lax.psum_scatter(both, 'dp', scatter_dimension=3, tiled=True)]
    ppermute x44, waiting for transfers between devices: 462 us -> 477 us  [passed_along(): lax.ppermute(value, axis, [(source, source + steps) for source in range(i...]
  transfers between devices with their start and end apart: 46 -> 45, of which waited for: 46 -> 45; matrix products, arithmetic and copies ran while one was open for 7% -> 5% of each run, Pallas kernels for 0% -> 0%
where the time goes in v5:
time: 1160 us
  waiting for transfers between devices  575 us (50%)
  starting transfers between devices  212 us (18%)
  local copies, waits for them, and re-layouts  172 us (15%)
  other arithmetic  91.6 us (8%)
  matrix products  75.1 us (6%)
  loops' own time  14.9 us (1%)
  between operations  14.2 us (1%)
    ppermute x44, waiting for transfers between devices, passed_along(): lax.ppermute(value, axis, [(source, source + steps) for source in range(i...  477 us
    ppermute x44, starting transfers between devices, passed_along(): lax.ppermute(value, axis, [(source, source + steps) for source in range(i...  212 us
    reduce_scatter x1, waiting for transfers between devices, shards(): share = lax.psum_scatter(both, 'dp', scatter_dimension=3, tiled=True)  98.1 us
    conv_general_dilated x16, matrix products, conv_apply(): lax.conv_general_dilated(activations, weight, window_strides=(1, 1), padd...  60.5 us
    dynamic_update_slice x66, local copies, waits for them, and re-layouts, put_row(): lax.dynamic_update_slice_in_dim(buffer, piece.astype(buffer.dtype), slot_...  54.4 us
    dynamic_slice x38, local copies, waits for them, and re-layouts, pick_row(): return lax.dynamic_slice_in_dim(buffer, slot_index, 1, 0)  43.1 us
    dynamic_update_slice x22, other arithmetic, put_row(): lax.dynamic_update_slice_in_dim(buffer, piece.astype(buffer.dtype), slot_...  31.8 us
  transfers between devices with their start and end apart: 45, of which 45 were waited for; matrix products, arithmetic and copies ran while one was open for 5% of the time, Pallas kernels for 0%

profile of v5, /device:TPU:0, one launch (start us, length us, event | category | flops | bytes accessed | tf_op | source)
XLA Modules:
  0.0 1155.4 jit_solution(4940184652315606854)
XLA Ops:
  34.2 184.9 %while.80 = (s32[]{:T(128)}, f32[1,16,16,384]{3,1,2,0:T(8,128)S(1)}, f32[6,16,16,384]{3,1,2,0:T(8,128)S(1)}, f32[6,16,16,384]{3,1,2,0:T(8,128)}, s32[]{:T(128)},...) while((s32[]{:T(128)}, ...), condition=%wide.region_7.8_spmd, body=%wide.region_0.7_spmd.sunk | while | flops 979748416 | bytes 12837928 | solution.py:141
  164.0 13.6 %collective-permute-start = (f32[1,16,16,384]{3,1,2,0:T(8,128)S(1)}, f32[1,16,16,384]{3,1,2,0:T(8,128)S(1)}, u32[]{:S(2)}, u32[]{:S(2)}) collective-permute-start(f32[1,16,16,384]{3,1,2,0:T(8,128)S(1)} %get-tuple-element.1897), channel_id=1, source_target_pairs={{0,16},{16,32},{32,48},{48,64},{64,80},{80,96},{96,112},{1,17},{17... | collective-permute-start | bytes 1179656 | tf_op jit(solution)/shard_map/while/body/eval_jaxpr/ppermute | solution.py:14
  198.5 15.4 %collective-permute-start = (f32[1,16,16,384]{3,1,2,0:T(8,128)S(1)}, f32[1,16,16,384]{3,1,2,0:T(8,128)S(1)}, u32[]{:S(2)}, u32[]{:S(2)}) collective-permute-start(f32[1,16,16,384]{3,1,2,0:T(8,128)S(1)} %get-tuple-element.1897), channel_id=1, source_target_pairs={{0,16},{16,32},{32,48},{48,64},{64,80},{80,96},{96,112},{1,17},{17... | collective-permute-start | bytes 1179656 | tf_op jit(solution)/shard_map/while/body/eval_jaxpr/ppermute | solution.py:14
  222.6 263.0 %while.81 = (s32[]{:T(128)}, f32[1,16,16,384]{3,1,2,0:T(8,128)S(1)}, f32[6,16,16,384]{3,1,2,0:T(8,128)}, f32[6,16,16,384]{3,1,2,0:T(8,128)}, s32[]{:T(128)}, /*i...) while((s32[]{:T(128)}, ...), condition=%wide.region_15.16_spmd, body=%wide.region_8.15_spmd.sunk | while | flops 1959349248 | bytes 20759588 | solution.py:162
  226.8 12.8 %collective-permute-done.1 = f32[1,16,16,384]{3,1,2,0:T(8,128)S(1)} collective-permute-done((f32[1,16,16,384]{3,1,2,0:T(8,128)S(1)}, f32[1,16,16,384]{3,1,2,0:T(8,128)S(1)}, u32[]{:S(2)}, u32[]{:S(2)}) %collective-permute-start.1) | collective-permute-done | bytes 393248 | tf_op jit(solution)/shard_map/while/body/eval_jaxpr/ppermute | solution.py:14
  243.6 14.9 %collective-permute-done.1 = f32[1,16,16,384]{3,1,2,0:T(8,128)S(1)} collective-permute-done((f32[1,16,16,384]{3,1,2,0:T(8,128)S(1)}, f32[1,16,16,384]{3,1,2,0:T(8,128)S(1)}, u32[]{:S(2)}, u32[]{:S(2)}) %collective-permute-start.1) | collective-permute-done | bytes 393248 | tf_op jit(solution)/shard_map/while/body/eval_jaxpr/ppermute | solution.py:14
  262.5 15.5 %collective-permute-done.1 = f32[1,16,16,384]{3,1,2,0:T(8,128)S(1)} collective-permute-done((f32[1,16,16,384]{3,1,2,0:T(8,128)S(1)}, f32[1,16,16,384]{3,1,2,0:T(8,128)S(1)}, u32[]{:S(2)}, u32[]{:S(2)}) %collective-permute-start.1) | collective-permute-done | bytes 393248 | tf_op jit(solution)/shard_map/while/body/eval_jaxpr/ppermute | solution.py:14
  282.1 17.7 %collective-permute-done.1 = f32[1,16,16,384]{3,1,2,0:T(8,128)S(1)} collective-permute-done((f32[1,16,16,384]{3,1,2,0:T(8,128)S(1)}, f32[1,16,16,384]{3,1,2,0:T(8,128)S(1)}, u32[]{:S(2)}, u32[]{:S(2)}) %collective-permute-start.1) | collective-permute-done | bytes 393248 | tf_op jit(solution)/shard_map/while/body/eval_jaxpr/ppermute | solution.py:14
  303.9 14.1 %collective-permute-done.1 = f32[1,16,16,384]{3,1,2,0:T(8,128)S(1)} collective-permute-done((f32[1,16,16,384]{3,1,2,0:T(8,128)S(1)}, f32[1,16,16,384]{3,1,2,0:T(8,128)S(1)}, u32[]{:S(2)}, u32[]{:S(2)}) %collective-permute-start.1) | collective-permute-done | bytes 393248 | tf_op jit(solution)/shard_map/while/body/eval_jaxpr/ppermute | solution.py:14
  333.7 51.9 %collective-permute-done.1 = f32[1,16,16,384]{3,1,2,0:T(8,128)S(1)} collective-permute-done((f32[1,16,16,384]{3,1,2,0:T(8,128)S(1)}, f32[1,16,16,384]{3,1,2,0:T(8,128)S(1)}, u32[]{:S(2)}, u32[]{:S(2)}) %collective-permute-start.1) | collective-permute-done | bytes 393248 | tf_op jit(solution)/shard_map/while/body/eval_jaxpr/ppermute | solution.py:14
  448.5 16.1 %collective-permute-done.1 = f32[1,16,16,384]{3,1,2,0:T(8,128)S(1)} collective-permute-done((f32[1,16,16,384]{3,1,2,0:T(8,128)S(1)}, f32[1,16,16,384]{3,1,2,0:T(8,128)S(1)}, u32[]{:S(2)}, u32[]{:S(2)}) %collective-permute-start.1) | collective-permute-done | bytes 393248 | tf_op jit(solution)/shard_map/while/body/eval_jaxpr/ppermute | solution.py:14
  491.8 251.7 %while.82 = (s32[]{:T(128)}, f32[1,16,16,384]{3,1,2,0:T(8,128)S(1)}, f32[6,16,16,384]{3,1,2,0:T(8,128)}, f32[6,16,16,384]{3,1,2,0:T(8,128)}, bf16[6,16,16,768]{3...) while((s32[]{:T(128)}, ...), condition=%wide.region_27.28_spmd, body=%wide.region_16.27_spmd.sunk | while | flops 1967262976 | bytes 31719764 | solution.py:204
  495.1 12.7 %conditional.10 = (f32[1,16,16,384]{3,1,2,0:T(8,128)S(1)}, f32[1,16,16,384]{3,1,2,0:T(8,128)S(1)}, bf16[1,16,16,768]{3,1,2,0:T(8,128)(2,1)S(1)}, bf16[1,16,16,384]{3,1,2,0:T(8,128)(2,1)S(1)}) conditional(s32[]{:T(128)} %convert_element_type.146, () %tuple.228, (pred[]{:T(512)}, f32[6,16,16,384]{3,1,2,0:T(8,128)}, s32[]{:T(128)}, ...), branch_computations={%region_17.17_spmd, %region_18.26_spmd} | conditional | flops 1966968064 | bytes 23656864 | solution.py:196
  519.0 12.7 %conditional.10 = (f32[1,16,16,384]{3,1,2,0:T(8,128)S(1)}, f32[1,16,16,384]{3,1,2,0:T(8,128)S(1)}, bf16[1,16,16,768]{3,1,2,0:T(8,128)(2,1)S(1)}, bf16[1,16,16,384]{3,1,2,0:T(8,128)(2,1)S(1)}) conditional(s32[]{:T(128)} %convert_element_type.146, () %tuple.228, (pred[]{:T(512)}, f32[6,16,16,384]{3,1,2,0:T(8,128)}, s32[]{:T(128)}, ...), branch_computations={%region_17.17_spmd, %region_18.26_spmd} | conditional | flops 1966968064 | bytes 23656864 | solution.py:196
  570.6 12.7 %conditional.10 = (f32[1,16,16,384]{3,1,2,0:T(8,128)S(1)}, f32[1,16,16,384]{3,1,2,0:T(8,128)S(1)}, bf16[1,16,16,768]{3,1,2,0:T(8,128)(2,1)S(1)}, bf16[1,16,16,384]{3,1,2,0:T(8,128)(2,1)S(1)}) conditional(s32[]{:T(128)} %convert_element_type.146, () %tuple.228, (pred[]{:T(512)}, f32[6,16,16,384]{3,1,2,0:T(8,128)}, s32[]{:T(128)}, ...), branch_computations={%region_17.17_spmd, %region_18.26_spmd} | conditional | flops 1966968064 | bytes 23656864 | solution.py:196
  596.2 17.0 %collective-permute-start.2 = (f32[1,16,16,384]{3,1,2,0:T(8,128)S(1)}, f32[1,16,16,384]{3,1,2,0:T(8,128)S(1)}, u32[]{:S(2)}, u32[]{:S(2)}) collective-permute-start(f32[1,16,16,384]{3,1,2,0:T(8,128)S(1)} %get-tuple-element.1666), channel_id=1, source_target_pairs={{0,16},{16,32},{32,48},{48,64},{64,80},{80,96},{96,112},{1,17},{17... | collective-permute-start | bytes 1179656 | tf_op jit(solution)/shard_map/while/body/eval_jaxpr/ppermute | solution.py:14
  671.2 19.2 %collective-permute-start.2 = (f32[1,16,16,384]{3,1,2,0:T(8,128)S(1)}, f32[1,16,16,384]{3,1,2,0:T(8,128)S(1)}, u32[]{:S(2)}, u32[]{:S(2)}) collective-permute-start(f32[1,16,16,384]{3,1,2,0:T(8,128)S(1)} %get-tuple-element.1666), channel_id=1, source_target_pairs={{0,16},{16,32},{32,48},{48,64},{64,80},{80,96},{96,112},{1,17},{17... | collective-permute-start | bytes 1179656 | tf_op jit(solution)/shard_map/while/body/eval_jaxpr/ppermute | solution.py:14
  715.5 22.7 %collective-permute-start.2 = (f32[1,16,16,384]{3,1,2,0:T(8,128)S(1)}, f32[1,16,16,384]{3,1,2,0:T(8,128)S(1)}, u32[]{:S(2)}, u32[]{:S(2)}) collective-permute-start(f32[1,16,16,384]{3,1,2,0:T(8,128)S(1)} %get-tuple-element.1666), channel_id=1, source_target_pairs={{0,16},{16,32},{32,48},{48,64},{64,80},{80,96},{96,112},{1,17},{17... | collective-permute-start | bytes 1179656 | tf_op jit(solution)/shard_map/while/body/eval_jaxpr/ppermute | solution.py:14
  745.8 276.0 %while.83 = (s32[]{:T(128)}, f32[1,16,16,384]{3,1,2,0:T(8,128)S(1)}, bf16[6,16,16,384]{3,2,1,0:T(8,128)(2,1)}, bf16[6,16,16,384]{3,2,1,0:T(8,128)(2,1)}, s32[]{:...) while((s32[]{:T(128)}, ...), condition=%wide.region_39.40_spmd, body=%wide.region_28.39_spmd.sunk | while | flops 982009536 | bytes 27224392 | solution.py:242
  763.6 24.0 %collective-permute-done.3 = f32[1,16,16,384]{3,1,2,0:T(8,128)S(1)} collective-permute-done((f32[1,16,16,384]{3,1,2,0:T(8,128)}, f32[1,16,16,384]{3,1,2,0:T(8,128)S(1)}, u32[]{:S(2)}, u32[]{:S(2)}) %collective-permute-start.3) | collective-permute-done | bytes 393248 | tf_op jit(solution)/shard_map/while/body/eval_jaxpr/ppermute | solution.py:14
  829.5 19.9 %collective-permute-done.3 = f32[1,16,16,384]{3,1,2,0:T(8,128)S(1)} collective-permute-done((f32[1,16,16,384]{3,1,2,0:T(8,128)}, f32[1,16,16,384]{3,1,2,0:T(8,128)S(1)}, u32[]{:S(2)}, u32[]{:S(2)}) %collective-permute-start.3) | collective-permute-done | bytes 393248 | tf_op jit(solution)/shard_map/while/body/eval_jaxpr/ppermute | solution.py:14
  852.4 80.7 %collective-permute-done.3 = f32[1,16,16,384]{3,1,2,0:T(8,128)S(1)} collective-permute-done((f32[1,16,16,384]{3,1,2,0:T(8,128)}, f32[1,16,16,384]{3,1,2,0:T(8,128)S(1)}, u32[]{:S(2)}, u32[]{:S(2)}) %collective-permute-start.3) | collective-permute-done | bytes 393248 | tf_op jit(solution)/shard_map/while/body/eval_jaxpr/ppermute | solution.py:14
  945.3 13.8 %collective-permute-done.3 = f32[1,16,16,384]{3,1,2,0:T(8,128)S(1)} collective-permute-done((f32[1,16,16,384]{3,1,2,0:T(8,128)}, f32[1,16,16,384]{3,1,2,0:T(8,128)S(1)}, u32[]{:S(2)}, u32[]{:S(2)}) %collective-permute-start.3) | collective-permute-done | bytes 393248 | tf_op jit(solution)/shard_map/while/body/eval_jaxpr/ppermute | solution.py:14
  1046.8 98.1 %reduce-scatter.2.cloned.1.call-done = f32[1,3,3,72,384]{4,3,2,1,0:T(8,128)} async-done(((f32[1,3,3,1152,384]{4,3,2,1,0:T(8,128)}), f32[1,3,3,72,384]{4,3,2,1,0:T(8,128)}) %reduce-scatter.2.cloned.1.call-update) | async-done | bytes 995344 | tf_op jit(solution)/shard_map/reduce_scatter | solution.py:259
  (901 shorter events, 784.9 us)
Async XLA Ops:
  7.2 1137.7 %reduce-scatter.2.cloned.1.call-start = ((), (), s32[]{:S(2)}) async-start(), calls=%async_computation.1 | async-start | bytes 16920576 | tf_op jit(solution)/shard_map/reduce_scatter | solution.py:259
  108.1 16.6 %collective-permute-start = (f32[1,16,16,384]{3,1,2,0:T(8,128)S(1)}, f32[1,16,16,384]{3,1,2,0:T(8,128)S(1)}, u32[]{:S(2)}, u32[]{:S(2)}) collective-permute-start(f32[1,16,16,384]{3,1,2,0:T(8,128)S(1)} %get-tuple-element.1897), channel_id=1, source_target_pairs={{0,16},{16,32},{32,48},{48,64},{64,80},{80,96},{96,112},{1,17},{17... | collective-permute-start | bytes 1179656 | tf_op jit(solution)/shard_map/while/body/eval_jaxpr/ppermute | solution.py:14
  136.6 15.6 %collective-permute-start = (f32[1,16,16,384]{3,1,2,0:T(8,128)S(1)}, f32[1,16,16,384]{3,1,2,0:T(8,128)S(1)}, u32[]{:S(2)}, u32[]{:S(2)}) collective-permute-start(f32[1,16,16,384]{3,1,2,0:T(8,128)S(1)} %get-tuple-element.1897), channel_id=1, source_target_pairs={{0,16},{16,32},{32,48},{48,64},{64,80},{80,96},{96,112},{1,17},{17... | collective-permute-start | bytes 1179656 | tf_op jit(solution)/shard_map/while/body/eval_jaxpr/ppermute | solution.py:14
  164.0 18.9 %collective-permute-start = (f32[1,16,16,384]{3,1,2,0:T(8,128)S(1)}, f32[1,16,16,384]{3,1,2,0:T(8,128)S(1)}, u32[]{:S(2)}, u32[]{:S(2)}) collective-permute-start(f32[1,16,16,384]{3,1,2,0:T(8,128)S(1)} %get-tuple-element.1897), channel_id=1, source_target_pairs={{0,16},{16,32},{32,48},{48,64},{64,80},{80,96},{96,112},{1,17},{17... | collective-permute-start | bytes 1179656 | tf_op jit(solution)/shard_map/while/body/eval_jaxpr/ppermute | solution.py:14
  184.1 13.3 %collective-permute-start = (f32[1,16,16,384]{3,1,2,0:T(8,128)S(1)}, f32[1,16,16,384]{3,1,2,0:T(8,128)S(1)}, u32[]{:S(2)}, u32[]{:S(2)}) collective-permute-start(f32[1,16,16,384]{3,1,2,0:T(8,128)S(1)} %get-tuple-element.1897), channel_id=1, source_target_pairs={{0,16},{16,32},{32,48},{48,64},{64,80},{80,96},{96,112},{1,17},{17... | collective-permute-start | bytes 1179656 | tf_op jit(solution)/shard_map/while/body/eval_jaxpr/ppermute | solution.py:14
  198.5 20.7 %collective-permute-start = (f32[1,16,16,384]{3,1,2,0:T(8,128)S(1)}, f32[1,16,16,384]{3,1,2,0:T(8,128)S(1)}, u32[]{:S(2)}, u32[]{:S(2)}) collective-permute-start(f32[1,16,16,384]{3,1,2,0:T(8,128)S(1)} %get-tuple-element.1897), channel_id=1, source_target_pairs={{0,16},{16,32},{32,48},{48,64},{64,80},{80,96},{96,112},{1,17},{17... | collective-permute-start | bytes 1179656 | tf_op jit(solution)/shard_map/while/body/eval_jaxpr/ppermute | solution.py:14
  224.7 14.9 %collective-permute-start.1 = (f32[1,16,16,384]{3,1,2,0:T(8,128)S(1)}, f32[1,16,16,384]{3,1,2,0:T(8,128)S(1)}, u32[]{:S(2)}, u32[]{:S(2)}) collective-permute-start(f32[1,16,16,384]{3,1,2,0:T(8,128)S(1)} %get-tuple-element.1898), channel_id=1, source_target_pairs={{16,0},{32,16},{48,32},{64,48},{80,64},{96,80},{112,96},{17,1},{33... | collective-permute-start | bytes 1179656 | tf_op jit(solution)/shard_map/while/body/eval_jaxpr/ppermute | solution.py:14
  241.5 17.0 %collective-permute-start.1 = (f32[1,16,16,384]{3,1,2,0:T(8,128)S(1)}, f32[1,16,16,384]{3,1,2,0:T(8,128)S(1)}, u32[]{:S(2)}, u32[]{:S(2)}) collective-permute-start(f32[1,16,16,384]{3,1,2,0:T(8,128)S(1)} %get-tuple-element.1898), channel_id=1, source_target_pairs={{16,0},{32,16},{48,32},{64,48},{80,64},{96,80},{112,96},{17,1},{33... | collective-permute-start | bytes 1179656 | tf_op jit(solution)/shard_map/while/body/eval_jaxpr/ppermute | solution.py:14
  260.4 17.6 %collective-permute-start.1 = (f32[1,16,16,384]{3,1,2,0:T(8,128)S(1)}, f32[1,16,16,384]{3,1,2,0:T(8,128)S(1)}, u32[]{:S(2)}, u32[]{:S(2)}) collective-permute-start(f32[1,16,16,384]{3,1,2,0:T(8,128)S(1)} %get-tuple-element.1898), channel_id=1, source_target_pairs={{16,0},{32,16},{48,32},{64,48},{80,64},{96,80},{112,96},{17,1},{33... | collective-permute-start | bytes 1179656 | tf_op jit(solution)/shard_map/while/body/eval_jaxpr/ppermute | solution.py:14
  280.0 19.8 %collective-permute-start.1 = (f32[1,16,16,384]{3,1,2,0:T(8,128)S(1)}, f32[1,16,16,384]{3,1,2,0:T(8,128)S(1)}, u32[]{:S(2)}, u32[]{:S(2)}) collective-permute-start(f32[1,16,16,384]{3,1,2,0:T(8,128)S(1)} %get-tuple-element.1898), channel_id=1, source_target_pairs={{16,0},{32,16},{48,32},{64,48},{80,64},{96,80},{112,96},{17,1},{33... | collective-permute-start | bytes 1179656 | tf_op jit(solution)/shard_map/while/body/eval_jaxpr/ppermute | solution.py:14
  301.8 16.2 %collective-permute-start.1 = (f32[1,16,16,384]{3,1,2,0:T(8,128)S(1)}, f32[1,16,16,384]{3,1,2,0:T(8,128)S(1)}, u32[]{:S(2)}, u32[]{:S(2)}) collective-permute-start(f32[1,16,16,384]{3,1,2,0:T(8,128)S(1)} %get-tuple-element.1898), channel_id=1, source_target_pairs={{16,0},{32,16},{48,32},{64,48},{80,64},{96,80},{112,96},{17,1},{33... | collective-permute-start | bytes 1179656 | tf_op jit(solution)/shard_map/while/body/eval_jaxpr/ppermute | solution.py:14
  331.6 54.0 %collective-permute-start.1 = (f32[1,16,16,384]{3,1,2,0:T(8,128)S(1)}, f32[1,16,16,384]{3,1,2,0:T(8,128)S(1)}, u32[]{:S(2)}, u32[]{:S(2)}) collective-permute-start(f32[1,16,16,384]{3,1,2,0:T(8,128)S(1)} %get-tuple-element.1898), channel_id=1, source_target_pairs={{16,0},{32,16},{48,32},{64,48},{80,64},{96,80},{112,96},{17,1},{33... | collective-permute-start | bytes 1179656 | tf_op jit(solution)/shard_map/while/body/eval_jaxpr/ppermute | solution.py:14
  397.0 13.3 %collective-permute-start.1 = (f32[1,16,16,384]{3,1,2,0:T(8,128)S(1)}, f32[1,16,16,384]{3,1,2,0:T(8,128)S(1)}, u32[]{:S(2)}, u32[]{:S(2)}) collective-permute-start(f32[1,16,16,384]{3,1,2,0:T(8,128)S(1)} %get-tuple-element.1898), channel_id=1, source_target_pairs={{16,0},{32,16},{48,32},{64,48},{80,64},{96,80},{112,96},{17,1},{33... | collective-permute-start | bytes 1179656 | tf_op jit(solution)/shard_map/while/body/eval_jaxpr/ppermute | solution.py:14
  446.4 18.2 %collective-permute-start.1 = (f32[1,16,16,384]{3,1,2,0:T(8,128)S(1)}, f32[1,16,16,384]{3,1,2,0:T(8,128)S(1)}, u32[]{:S(2)}, u32[]{:S(2)}) collective-permute-start(f32[1,16,16,384]{3,1,2,0:T(8,128)S(1)} %get-tuple-element.1898), channel_id=1, source_target_pairs={{16,0},{32,16},{48,32},{64,48},{80,64},{96,80},{112,96},{17,1},{33... | collective-permute-start | bytes 1179656 | tf_op jit(solution)/shard_map/while/body/eval_jaxpr/ppermute | solution.py:14
  596.2 23.0 %collective-permute-start.2 = (f32[1,16,16,384]{3,1,2,0:T(8,128)S(1)}, f32[1,16,16,384]{3,1,2,0:T(8,128)S(1)}, u32[]{:S(2)}, u32[]{:S(2)}) collective-permute-start(f32[1,16,16,384]{3,1,2,0:T(8,128)S(1)} %get-tuple-element.1666), channel_id=1, source_target_pairs={{0,16},{16,32},{32,48},{48,64},{64,80},{80,96},{96,112},{1,17},{17... | collective-permute-start | bytes 1179656 | tf_op jit(solution)/shard_map/while/body/eval_jaxpr/ppermute | solution.py:14
  637.3 17.7 %collective-permute-start.2 = (f32[1,16,16,384]{3,1,2,0:T(8,128)S(1)}, f32[1,16,16,384]{3,1,2,0:T(8,128)S(1)}, u32[]{:S(2)}, u32[]{:S(2)}) collective-permute-start(f32[1,16,16,384]{3,1,2,0:T(8,128)S(1)} %get-tuple-element.1666), channel_id=1, source_target_pairs={{0,16},{16,32},{32,48},{48,64},{64,80},{80,96},{96,112},{1,17},{17... | collective-permute-start | bytes 1179656 | tf_op jit(solution)/shard_map/while/body/eval_jaxpr/ppermute | solution.py:14
  671.2 24.4 %collective-permute-start.2 = (f32[1,16,16,384]{3,1,2,0:T(8,128)S(1)}, f32[1,16,16,384]{3,1,2,0:T(8,128)S(1)}, u32[]{:S(2)}, u32[]{:S(2)}) collective-permute-start(f32[1,16,16,384]{3,1,2,0:T(8,128)S(1)} %get-tuple-element.1666), channel_id=1, source_target_pairs={{0,16},{16,32},{32,48},{48,64},{64,80},{80,96},{96,112},{1,17},{17... | collective-permute-start | bytes 1179656 | tf_op jit(solution)/shard_map/while/body/eval_jaxpr/ppermute | solution.py:14
  715.5 28.0 %collective-permute-start.2 = (f32[1,16,16,384]{3,1,2,0:T(8,128)S(1)}, f32[1,16,16,384]{3,1,2,0:T(8,128)S(1)}, u32[]{:S(2)}, u32[]{:S(2)}) collective-permute-start(f32[1,16,16,384]{3,1,2,0:T(8,128)S(1)} %get-tuple-element.1666), channel_id=1, source_target_pairs={{0,16},{16,32},{32,48},{48,64},{64,80},{80,96},{96,112},{1,17},{17... | collective-permute-start | bytes 1179656 | tf_op jit(solution)/shard_map/while/body/eval_jaxpr/ppermute | solution.py:14
  746.6 14.0 %collective-permute-start.3 = (f32[1,16,16,384]{3,1,2,0:T(8,128)}, f32[1,16,16,384]{3,1,2,0:T(8,128)S(1)}, u32[]{:S(2)}, u32[]{:S(2)}) collective-permute-start(f32[1,16,16,384]{3,1,2,0:T(8,128)} %get-tuple-element.1683), channel_id=1, source_target_pairs={{16,0},{32,16},{48,32},{64,48},{80,64},{96,80},{112,96},{17,1},{33... | collective-permute-start | bytes 1179656 | tf_op jit(solution)/shard_map/while/body/eval_jaxpr/ppermute | solution.py:14
  761.4 26.1 %collective-permute-start.3 = (f32[1,16,16,384]{3,1,2,0:T(8,128)}, f32[1,16,16,384]{3,1,2,0:T(8,128)S(1)}, u32[]{:S(2)}, u32[]{:S(2)}) collective-permute-start(f32[1,16,16,384]{3,1,2,0:T(8,128)} %get-tuple-element.1683), channel_id=1, source_target_pairs={{16,0},{32,16},{48,32},{64,48},{80,64},{96,80},{112,96},{17,1},{33... | collective-permute-start | bytes 1179656 | tf_op jit(solution)/shard_map/while/body/eval_jaxpr/ppermute | solution.py:14
  788.4 14.0 %collective-permute-start.3 = (f32[1,16,16,384]{3,1,2,0:T(8,128)}, f32[1,16,16,384]{3,1,2,0:T(8,128)S(1)}, u32[]{:S(2)}, u32[]{:S(2)}) collective-permute-start(f32[1,16,16,384]{3,1,2,0:T(8,128)} %get-tuple-element.1683), channel_id=1, source_target_pairs={{16,0},{32,16},{48,32},{64,48},{80,64},{96,80},{112,96},{17,1},{33... | collective-permute-start | bytes 1179656 | tf_op jit(solution)/shard_map/while/body/eval_jaxpr/ppermute | solution.py:14
  827.4 22.1 %collective-permute-start.3 = (f32[1,16,16,384]{3,1,2,0:T(8,128)}, f32[1,16,16,384]{3,1,2,0:T(8,128)S(1)}, u32[]{:S(2)}, u32[]{:S(2)}) collective-permute-start(f32[1,16,16,384]{3,1,2,0:T(8,128)} %get-tuple-element.1683), channel_id=1, source_target_pairs={{16,0},{32,16},{48,32},{64,48},{80,64},{96,80},{112,96},{17,1},{33... | collective-permute-start | bytes 1179656 | tf_op jit(solution)/shard_map/while/body/eval_jaxpr/ppermute | solution.py:14
  850.3 82.8 %collective-permute-start.3 = (f32[1,16,16,384]{3,1,2,0:T(8,128)}, f32[1,16,16,384]{3,1,2,0:T(8,128)S(1)}, u32[]{:S(2)}, u32[]{:S(2)}) collective-permute-start(f32[1,16,16,384]{3,1,2,0:T(8,128)} %get-tuple-element.1683), channel_id=1, source_target_pairs={{16,0},{32,16},{48,32},{64,48},{80,64},{96,80},{112,96},{17,1},{33... | collective-permute-start | bytes 1179656 | tf_op jit(solution)/shard_map/while/body/eval_jaxpr/ppermute | solution.py:14
  943.2 15.9 %collective-permute-start.3 = (f32[1,16,16,384]{3,1,2,0:T(8,128)}, f32[1,16,16,384]{3,1,2,0:T(8,128)S(1)}, u32[]{:S(2)}, u32[]{:S(2)}) collective-permute-start(f32[1,16,16,384]{3,1,2,0:T(8,128)} %get-tuple-element.1683), channel_id=1, source_target_pairs={{16,0},{32,16},{48,32},{64,48},{80,64},{96,80},{112,96},{17,1},{33... | collective-permute-start | bytes 1179656 | tf_op jit(solution)/shard_map/while/body/eval_jaxpr/ppermute | solution.py:14
  (65 other events, 320.5 us)
Sparse Core Ops, SparseCore 0:
  1046.9 97.9 reduce-scatter.1

commit v6 on v5

--- a/solution.py
+++ b/solution.py
@@ -21,15 +21,14 @@
     return jnp.concatenate([jnp.sin(angles), jnp.cos(angles)], axis=1)
 
 
-def activate(inputs_f32, stamps_in):
+def activate(inputs_f32, modulate_row):
     batch_rows, height, breadth, channels = inputs_f32.shape
     grouped = inputs_f32.reshape(batch_rows, height * breadth, GROUPS, channels // GROUPS)
     group_mean = jnp.mean(grouped, axis=(1, 3), keepdims=True)
     centered = grouped - group_mean
     group_var = jnp.mean(centered * centered, axis=(1, 3), keepdims=True)
     normed = (centered * lax.rsqrt(group_var + 1e-05)).reshape(inputs_f32.shape)
-    modulate = 1.0 + 0.5 * embed(stamps_in, channels)[:, None, None, :]
-    return jax.nn.silu(normed * modulate)
+    return jax.nn.silu(normed * modulate_row[:, None, None, :])
 
 
 def conv_apply(activations, weight):
@@ -71,8 +70,17 @@
     return jnp.stack(kernel_rows)
 
 
-def block_forward(inputs, residual, weight, stamps_in):
-    activations = activate(inputs, stamps_in).astype(jnp.bfloat16)
+def modulation(stamps_in, channels):
+    return 1.0 + 0.5 * embed(stamps_in, channels)
+
+
+def chosen_row(table, sample_at):
+    hit = (jnp.arange(table.shape[0]) == sample_at)[:, None]
+    return jnp.sum(jnp.where(hit, table, 0.0), axis=0, keepdims=True)
+
+
+def block_forward(inputs, residual, weight, modulate_row):
+    activations = activate(inputs, modulate_row).astype(jnp.bfloat16)
     return residual + conv_apply(activations, weight)
 
 
@@ -98,6 +106,8 @@
     channels = clean.shape[3]
     enc_kernel = enc_weight[0]
     dec_kernel = dec_weight[0]
+    narrow_table = modulation(stamps, channels)
+    wide_table = modulation(stamps, 2 * channels)
     enc_back_kernel = flipped(enc_kernel)
     dec_back_kernel = flipped(dec_kernel)
     keep_level, spread_level = noise_levels(stamps)
@@ -127,7 +137,7 @@
         incoming, enc_inputs, skips = carried
         active, sample_at, slot_index = locate(tick_now, section_index)
         source = jnp.where(section_index == 0, pick_row(noisy, sample_at), incoming)
-        stamp_one = pick_row(stamps, sample_at)
+        stamp_one = chosen_row(narrow_table, sample_at)
         result = lax.cond(
             active,
             lambda: block_forward(source, source, enc_kernel, stamp_one),
@@ -148,7 +158,7 @@
         skip_piece = pick_row(skips, slot_index)
         source = jnp.where(section_index == last_section, skip_piece, incoming)
         joined = jnp.concatenate([source, skip_piece], axis=3)
-        stamp_one = pick_row(stamps, sample_at)
+        stamp_one = chosen_row(wide_table, sample_at)
         result = lax.cond(
             active,
             lambda: block_forward(joined, source, dec_kernel, stamp_one),
@@ -178,7 +188,7 @@
         joined = jnp.concatenate(
             [pick_row(dec_inputs, slot_index), pick_row(skips, slot_index)], axis=3
         )
-        stamp_one = pick_row(stamps, sample_at)
+        stamp_one = chosen_row(wide_table, sample_at)
 
         def decoder_working():
             input_grad, acts, cots = input_backward(joined, dec_back_kernel, stamp_one, flowing)
@@ -223,7 +233,7 @@
         )
         merged = arriving + pick_row(skip_grads, slot_index)
         block_input = pick_row(enc_inputs, slot_index)
-        stamp_one = pick_row(stamps, sample_at)
+        stamp_one = chosen_row(narrow_table, sample_at)
 
         def encoder_working():
             input_grad, acts, cots = input_backward(block_input, enc_back_kernel, stamp_one, merged)

time: 1160 us -> 1120 us (0.966)
  waiting for transfers between devices: 575 us -> 550 us
    dynamic_slice x38 -> x22, local copies, waits for them, and re-layouts: 43.1 us -> 22.5 us  [pick_row(): return lax.dynamic_slice_in_dim(buffer, slot_index, 1, 0)]
    ppermute x44, waiting for transfers between devices: 477 us -> 458 us  [passed_along(): lax.ppermute(value, axis, [(source, source + steps) for source in range(i...]
where the time goes in v6:
time: 1120 us; the launch traced here: 1110 us
  waiting for transfers between devices  550 us (49%)
  starting transfers between devices  207 us (18%)
  local copies, waits for them, and re-layouts  163 us (15%)
  other arithmetic  100 us (9%)
  matrix products  75.1 us (7%)
  between operations  14.2 us (1%)
    ppermute x44, waiting for transfers between devices, passed_along(): lax.ppermute(value, axis, [(source, source + steps) for source in range(i...  458 us
    ppermute x44, starting transfers between devices, passed_along(): lax.ppermute(value, axis, [(source, source + steps) for source in range(i...  207 us
    reduce_scatter x1, waiting for transfers between devices, shards(): share = lax.psum_scatter(both, 'dp', scatter_dimension=3, tiled=True)  91.8 us
    conv_general_dilated x16, matrix products, conv_apply(): lax.conv_general_dilated(activations, weight, window_strides=(1, 1), padd...  60.5 us
    dynamic_update_slice x66, local copies, waits for them, and re-layouts, put_row(): lax.dynamic_update_slice_in_dim(buffer, piece.astype(buffer.dtype), slot_...  54.4 us
    dynamic_update_slice x22, other arithmetic, put_row(): lax.dynamic_update_slice_in_dim(buffer, piece.astype(buffer.dtype), slot_...  31.8 us
    dynamic_slice x22, local copies, waits for them, and re-layouts, pick_row(): return lax.dynamic_slice_in_dim(buffer, slot_index, 1, 0)  22.5 us
  transfers between devices with their start and end apart: 45, of which 45 were waited for; matrix products, arithmetic and copies ran while one was open for 5% of the time, Pallas kernels for 0%

profile of v6, /device:TPU:0, one launch (start us, length us, event | category | flops | bytes accessed | tf_op | source)
XLA Modules:
  0.0 1113.4 jit_solution(21802962932101176)
XLA Ops:
  35.8 174.1 %while.80 = (s32[]{:T(128)}, f32[1,16,16,384]{3,1,2,0:T(8,128)S(1)}, f32[6,16,16,384]{3,1,2,0:T(8,128)S(1)}, f32[6,16,16,384]{3,1,2,0:T(8,128)}, s32[]{:T(128)},...) while((s32[]{:T(128)}, ...), condition=%wide.region_8.9_spmd, body=%wide.region_0.8_spmd.sunk | while | flops 979749568 | bytes 12841028 | solution.py:151
  157.6 12.3 %collective-permute-start = (f32[1,16,16,384]{3,1,2,0:T(8,128)S(1)}, f32[1,16,16,384]{3,1,2,0:T(8,128)S(1)}, u32[]{:S(2)}, u32[]{:S(2)}) collective-permute-start(f32[1,16,16,384]{3,1,2,0:T(8,128)S(1)} %get-tuple-element.2033), channel_id=1, source_target_pairs={{0,16},{16,32},{32,48},{48,64},{64,80},{80,96},{96,112},{1,17},{17... | collective-permute-start | bytes 1179656 | tf_op jit(solution)/shard_map/while/body/eval_jaxpr/ppermute | solution.py:14
  190.7 14.0 %collective-permute-start = (f32[1,16,16,384]{3,1,2,0:T(8,128)S(1)}, f32[1,16,16,384]{3,1,2,0:T(8,128)S(1)}, u32[]{:S(2)}, u32[]{:S(2)}) collective-permute-start(f32[1,16,16,384]{3,1,2,0:T(8,128)S(1)} %get-tuple-element.2033), channel_id=1, source_target_pairs={{0,16},{16,32},{32,48},{48,64},{64,80},{80,96},{96,112},{1,17},{17... | collective-permute-start | bytes 1179656 | tf_op jit(solution)/shard_map/while/body/eval_jaxpr/ppermute | solution.py:14
  213.5 237.2 %while.81 = (s32[]{:T(128)}, f32[1,16,16,384]{3,1,2,0:T(8,128)S(1)}, f32[6,16,16,384]{3,1,2,0:T(8,128)}, f32[6,16,16,384]{3,1,2,0:T(8,128)}, s32[]{:T(128)}, /*i...) while((s32[]{:T(128)}, ...), condition=%wide.region_17.18_spmd, body=%wide.region_9.17_spmd.sunk | while | flops 1959351552 | bytes 20765760 | solution.py:172
  217.6 12.8 %collective-permute-done.1 = f32[1,16,16,384]{3,1,2,0:T(8,128)S(1)} collective-permute-done((f32[1,16,16,384]{3,1,2,0:T(8,128)S(1)}, f32[1,16,16,384]{3,1,2,0:T(8,128)S(1)}, u32[]{:S(2)}, u32[]{:S(2)}) %collective-permute-start.1) | collective-permute-done | bytes 393248 | tf_op jit(solution)/shard_map/while/body/eval_jaxpr/ppermute | solution.py:14
  234.4 14.2 %collective-permute-done.1 = f32[1,16,16,384]{3,1,2,0:T(8,128)S(1)} collective-permute-done((f32[1,16,16,384]{3,1,2,0:T(8,128)S(1)}, f32[1,16,16,384]{3,1,2,0:T(8,128)S(1)}, u32[]{:S(2)}, u32[]{:S(2)}) %collective-permute-start.1) | collective-permute-done | bytes 393248 | tf_op jit(solution)/shard_map/while/body/eval_jaxpr/ppermute | solution.py:14
  252.7 15.3 %collective-permute-done.1 = f32[1,16,16,384]{3,1,2,0:T(8,128)S(1)} collective-permute-done((f32[1,16,16,384]{3,1,2,0:T(8,128)S(1)}, f32[1,16,16,384]{3,1,2,0:T(8,128)S(1)}, u32[]{:S(2)}, u32[]{:S(2)}) %collective-permute-start.1) | collective-permute-done | bytes 393248 | tf_op jit(solution)/shard_map/while/body/eval_jaxpr/ppermute | solution.py:14
  272.1 17.7 %collective-permute-done.1 = f32[1,16,16,384]{3,1,2,0:T(8,128)S(1)} collective-permute-done((f32[1,16,16,384]{3,1,2,0:T(8,128)S(1)}, f32[1,16,16,384]{3,1,2,0:T(8,128)S(1)}, u32[]{:S(2)}, u32[]{:S(2)}) %collective-permute-start.1) | collective-permute-done | bytes 393248 | tf_op jit(solution)/shard_map/while/body/eval_jaxpr/ppermute | solution.py:14
  293.9 14.9 %collective-permute-done.1 = f32[1,16,16,384]{3,1,2,0:T(8,128)S(1)} collective-permute-done((f32[1,16,16,384]{3,1,2,0:T(8,128)S(1)}, f32[1,16,16,384]{3,1,2,0:T(8,128)S(1)}, u32[]{:S(2)}, u32[]{:S(2)}) %collective-permute-start.1) | collective-permute-done | bytes 393248 | tf_op jit(solution)/shard_map/while/body/eval_jaxpr/ppermute | solution.py:14
  324.5 34.5 %collective-permute-done.1 = f32[1,16,16,384]{3,1,2,0:T(8,128)S(1)} collective-permute-done((f32[1,16,16,384]{3,1,2,0:T(8,128)S(1)}, f32[1,16,16,384]{3,1,2,0:T(8,128)S(1)}, u32[]{:S(2)}, u32[]{:S(2)}) %collective-permute-start.1) | collective-permute-done | bytes 393248 | tf_op jit(solution)/shard_map/while/body/eval_jaxpr/ppermute | solution.py:14
  393.7 12.8 %collective-permute-done.1 = f32[1,16,16,384]{3,1,2,0:T(8,128)S(1)} collective-permute-done((f32[1,16,16,384]{3,1,2,0:T(8,128)S(1)}, f32[1,16,16,384]{3,1,2,0:T(8,128)S(1)}, u32[]{:S(2)}, u32[]{:S(2)}) %collective-permute-start.1) | collective-permute-done | bytes 393248 | tf_op jit(solution)/shard_map/while/body/eval_jaxpr/ppermute | solution.py:14
  418.0 13.5 %collective-permute-done.1 = f32[1,16,16,384]{3,1,2,0:T(8,128)S(1)} collective-permute-done((f32[1,16,16,384]{3,1,2,0:T(8,128)S(1)}, f32[1,16,16,384]{3,1,2,0:T(8,128)S(1)}, u32[]{:S(2)}, u32[]{:S(2)}) %collective-permute-start.1) | collective-permute-done | bytes 393248 | tf_op jit(solution)/shard_map/while/body/eval_jaxpr/ppermute | solution.py:14
  456.8 246.3 %while.82 = (s32[]{:T(128)}, f32[1,16,16,384]{3,1,2,0:T(8,128)S(1)}, f32[6,16,16,384]{3,1,2,0:T(8,128)}, f32[6,16,16,384]{3,1,2,0:T(8,128)}, bf16[6,16,16,768]{3...) while((s32[]{:T(128)}, ...), condition=%wide.region_30.31_spmd, body=%wide.region_18.30_spmd.sunk | while | flops 1967265280 | bytes 31725936 | solution.py:214
  558.4 15.1 %collective-permute-start.2 = (f32[1,16,16,384]{3,1,2,0:T(8,128)S(1)}, f32[1,16,16,384]{3,1,2,0:T(8,128)S(1)}, u32[]{:S(2)}, u32[]{:S(2)}) collective-permute-start(f32[1,16,16,384]{3,1,2,0:T(8,128)S(1)} %get-tuple-element.1802), channel_id=1, source_target_pairs={{0,16},{16,32},{32,48},{48,64},{64,80},{80,96},{96,112},{1,17},{17... | collective-permute-start | bytes 1179656 | tf_op jit(solution)/shard_map/while/body/eval_jaxpr/ppermute | solution.py:14
  594.9 13.5 %collective-permute-start.2 = (f32[1,16,16,384]{3,1,2,0:T(8,128)S(1)}, f32[1,16,16,384]{3,1,2,0:T(8,128)S(1)}, u32[]{:S(2)}, u32[]{:S(2)}) collective-permute-start(f32[1,16,16,384]{3,1,2,0:T(8,128)S(1)} %get-tuple-element.1802), channel_id=1, source_target_pairs={{0,16},{16,32},{32,48},{48,64},{64,80},{80,96},{96,112},{1,17},{17... | collective-permute-start | bytes 1179656 | tf_op jit(solution)/shard_map/while/body/eval_jaxpr/ppermute | solution.py:14
  629.9 18.4 %collective-permute-start.2 = (f32[1,16,16,384]{3,1,2,0:T(8,128)S(1)}, f32[1,16,16,384]{3,1,2,0:T(8,128)S(1)}, u32[]{:S(2)}, u32[]{:S(2)}) collective-permute-start(f32[1,16,16,384]{3,1,2,0:T(8,128)S(1)} %get-tuple-element.1802), channel_id=1, source_target_pairs={{0,16},{16,32},{32,48},{48,64},{64,80},{80,96},{96,112},{1,17},{17... | collective-permute-start | bytes 1179656 | tf_op jit(solution)/shard_map/while/body/eval_jaxpr/ppermute | solution.py:14
  673.4 24.4 %collective-permute-start.2 = (f32[1,16,16,384]{3,1,2,0:T(8,128)S(1)}, f32[1,16,16,384]{3,1,2,0:T(8,128)S(1)}, u32[]{:S(2)}, u32[]{:S(2)}) collective-permute-start(f32[1,16,16,384]{3,1,2,0:T(8,128)S(1)} %get-tuple-element.1802), channel_id=1, source_target_pairs={{0,16},{16,32},{32,48},{48,64},{64,80},{80,96},{96,112},{1,17},{17... | collective-permute-start | bytes 1179656 | tf_op jit(solution)/shard_map/while/body/eval_jaxpr/ppermute | solution.py:14
  705.4 280.6 %while.83 = (s32[]{:T(128)}, f32[1,16,16,384]{3,1,2,0:T(8,128)S(1)}, bf16[6,16,16,384]{3,2,1,0:T(8,128)(2,1)}, bf16[6,16,16,384]{3,2,1,0:T(8,128)(2,1)}, s32[]{:...) while((s32[]{:T(128)}, ...), condition=%wide.region_43.44_spmd, body=%wide.region_31.0_spmd.sunk | while | flops 982010688 | bytes 27228124 | solution.py:252
  724.3 11.8 %collective-permute-done.3 = f32[1,16,16,384]{3,1,2,0:T(8,128)S(1)} collective-permute-done((f32[1,16,16,384]{3,1,2,0:T(8,128)}, f32[1,16,16,384]{3,1,2,0:T(8,128)S(1)}, u32[]{:S(2)}, u32[]{:S(2)}) %collective-permute-start.3) | collective-permute-done | bytes 393248 | tf_op jit(solution)/shard_map/while/body/eval_jaxpr/ppermute | solution.py:14
  755.0 12.6 %collective-permute-done.3 = f32[1,16,16,384]{3,1,2,0:T(8,128)S(1)} collective-permute-done((f32[1,16,16,384]{3,1,2,0:T(8,128)}, f32[1,16,16,384]{3,1,2,0:T(8,128)S(1)}, u32[]{:S(2)}, u32[]{:S(2)}) %collective-permute-start.3) | collective-permute-done | bytes 393248 | tf_op jit(solution)/shard_map/while/body/eval_jaxpr/ppermute | solution.py:14
  786.0 14.2 %collective-permute-done.3 = f32[1,16,16,384]{3,1,2,0:T(8,128)S(1)} collective-permute-done((f32[1,16,16,384]{3,1,2,0:T(8,128)}, f32[1,16,16,384]{3,1,2,0:T(8,128)S(1)}, u32[]{:S(2)}, u32[]{:S(2)}) %collective-permute-start.3) | collective-permute-done | bytes 393248 | tf_op jit(solution)/shard_map/while/body/eval_jaxpr/ppermute | solution.py:14
  803.6 87.8 %collective-permute-done.3 = f32[1,16,16,384]{3,1,2,0:T(8,128)S(1)} collective-permute-done((f32[1,16,16,384]{3,1,2,0:T(8,128)}, f32[1,16,16,384]{3,1,2,0:T(8,128)S(1)}, u32[]{:S(2)}, u32[]{:S(2)}) %collective-permute-start.3) | collective-permute-done | bytes 393248 | tf_op jit(solution)/shard_map/while/body/eval_jaxpr/ppermute | solution.py:14
  952.6 12.6 %collective-permute-done.3 = f32[1,16,16,384]{3,1,2,0:T(8,128)S(1)} collective-permute-done((f32[1,16,16,384]{3,1,2,0:T(8,128)}, f32[1,16,16,384]{3,1,2,0:T(8,128)S(1)}, u32[]{:S(2)}, u32[]{:S(2)}) %collective-permute-start.3) | collective-permute-done | bytes 393248 | tf_op jit(solution)/shard_map/while/body/eval_jaxpr/ppermute | solution.py:14
  1011.1 91.8 %reduce-scatter.2.cloned.1.call-done = f32[1,3,3,72,384]{4,3,2,1,0:T(8,128)} async-done(((f32[1,3,3,1152,384]{4,3,2,1,0:T(8,128)}), f32[1,3,3,72,384]{4,3,2,1,0:T(8,128)}) %reduce-scatter.2.cloned.1.call-update) | async-done | bytes 995344 | tf_op jit(solution)/shard_map/reduce_scatter | solution.py:269
  (954 shorter events, 775.2 us)
Async XLA Ops:
  7.2 1095.7 %reduce-scatter.2.cloned.1.call-start = ((), (), s32[]{:S(2)}) async-start(), calls=%async_computation.1 | async-start | bytes 16920576 | tf_op jit(solution)/shard_map/reduce_scatter | solution.py:269
  104.3 15.2 %collective-permute-start = (f32[1,16,16,384]{3,1,2,0:T(8,128)S(1)}, f32[1,16,16,384]{3,1,2,0:T(8,128)S(1)}, u32[]{:S(2)}, u32[]{:S(2)}) collective-permute-start(f32[1,16,16,384]{3,1,2,0:T(8,128)S(1)} %get-tuple-element.2033), channel_id=1, source_target_pairs={{0,16},{16,32},{32,48},{48,64},{64,80},{80,96},{96,112},{1,17},{17... | collective-permute-start | bytes 1179656 | tf_op jit(solution)/shard_map/while/body/eval_jaxpr/ppermute | solution.py:14
  131.4 14.2 %collective-permute-start = (f32[1,16,16,384]{3,1,2,0:T(8,128)S(1)}, f32[1,16,16,384]{3,1,2,0:T(8,128)S(1)}, u32[]{:S(2)}, u32[]{:S(2)}) collective-permute-start(f32[1,16,16,384]{3,1,2,0:T(8,128)S(1)} %get-tuple-element.2033), channel_id=1, source_target_pairs={{0,16},{16,32},{32,48},{48,64},{64,80},{80,96},{96,112},{1,17},{17... | collective-permute-start | bytes 1179656 | tf_op jit(solution)/shard_map/while/body/eval_jaxpr/ppermute | solution.py:14
  157.6 17.5 %collective-permute-start = (f32[1,16,16,384]{3,1,2,0:T(8,128)S(1)}, f32[1,16,16,384]{3,1,2,0:T(8,128)S(1)}, u32[]{:S(2)}, u32[]{:S(2)}) collective-permute-start(f32[1,16,16,384]{3,1,2,0:T(8,128)S(1)} %get-tuple-element.2033), channel_id=1, source_target_pairs={{0,16},{16,32},{32,48},{48,64},{64,80},{80,96},{96,112},{1,17},{17... | collective-permute-start | bytes 1179656 | tf_op jit(solution)/shard_map/while/body/eval_jaxpr/ppermute | solution.py:14
  190.7 19.3 %collective-permute-start = (f32[1,16,16,384]{3,1,2,0:T(8,128)S(1)}, f32[1,16,16,384]{3,1,2,0:T(8,128)S(1)}, u32[]{:S(2)}, u32[]{:S(2)}) collective-permute-start(f32[1,16,16,384]{3,1,2,0:T(8,128)S(1)} %get-tuple-element.2033), channel_id=1, source_target_pairs={{0,16},{16,32},{32,48},{48,64},{64,80},{80,96},{96,112},{1,17},{17... | collective-permute-start | bytes 1179656 | tf_op jit(solution)/shard_map/while/body/eval_jaxpr/ppermute | solution.py:14
  215.5 14.9 %collective-permute-start.1 = (f32[1,16,16,384]{3,1,2,0:T(8,128)S(1)}, f32[1,16,16,384]{3,1,2,0:T(8,128)S(1)}, u32[]{:S(2)}, u32[]{:S(2)}) collective-permute-start(f32[1,16,16,384]{3,1,2,0:T(8,128)S(1)} %get-tuple-element.2034), channel_id=1, source_target_pairs={{16,0},{32,16},{48,32},{64,48},{80,64},{96,80},{112,96},{17,1},{33... | collective-permute-start | bytes 1179656 | tf_op jit(solution)/shard_map/while/body/eval_jaxpr/ppermute | solution.py:14
  232.3 16.3 %collective-permute-start.1 = (f32[1,16,16,384]{3,1,2,0:T(8,128)S(1)}, f32[1,16,16,384]{3,1,2,0:T(8,128)S(1)}, u32[]{:S(2)}, u32[]{:S(2)}) collective-permute-start(f32[1,16,16,384]{3,1,2,0:T(8,128)S(1)} %get-tuple-element.2034), channel_id=1, source_target_pairs={{16,0},{32,16},{48,32},{64,48},{80,64},{96,80},{112,96},{17,1},{33... | collective-permute-start | bytes 1179656 | tf_op jit(solution)/shard_map/while/body/eval_jaxpr/ppermute | solution.py:14
  250.6 17.4 %collective-permute-start.1 = (f32[1,16,16,384]{3,1,2,0:T(8,128)S(1)}, f32[1,16,16,384]{3,1,2,0:T(8,128)S(1)}, u32[]{:S(2)}, u32[]{:S(2)}) collective-permute-start(f32[1,16,16,384]{3,1,2,0:T(8,128)S(1)} %get-tuple-element.2034), channel_id=1, source_target_pairs={{16,0},{32,16},{48,32},{64,48},{80,64},{96,80},{112,96},{17,1},{33... | collective-permute-start | bytes 1179656 | tf_op jit(solution)/shard_map/while/body/eval_jaxpr/ppermute | solution.py:14
  270.0 19.8 %collective-permute-start.1 = (f32[1,16,16,384]{3,1,2,0:T(8,128)S(1)}, f32[1,16,16,384]{3,1,2,0:T(8,128)S(1)}, u32[]{:S(2)}, u32[]{:S(2)}) collective-permute-start(f32[1,16,16,384]{3,1,2,0:T(8,128)S(1)} %get-tuple-element.2034), channel_id=1, source_target_pairs={{16,0},{32,16},{48,32},{64,48},{80,64},{96,80},{112,96},{17,1},{33... | collective-permute-start | bytes 1179656 | tf_op jit(solution)/shard_map/while/body/eval_jaxpr/ppermute | solution.py:14
  291.8 17.0 %collective-permute-start.1 = (f32[1,16,16,384]{3,1,2,0:T(8,128)S(1)}, f32[1,16,16,384]{3,1,2,0:T(8,128)S(1)}, u32[]{:S(2)}, u32[]{:S(2)}) collective-permute-start(f32[1,16,16,384]{3,1,2,0:T(8,128)S(1)} %get-tuple-element.2034), channel_id=1, source_target_pairs={{16,0},{32,16},{48,32},{64,48},{80,64},{96,80},{112,96},{17,1},{33... | collective-permute-start | bytes 1179656 | tf_op jit(solution)/shard_map/while/body/eval_jaxpr/ppermute | solution.py:14
  322.4 36.6 %collective-permute-start.1 = (f32[1,16,16,384]{3,1,2,0:T(8,128)S(1)}, f32[1,16,16,384]{3,1,2,0:T(8,128)S(1)}, u32[]{:S(2)}, u32[]{:S(2)}) collective-permute-start(f32[1,16,16,384]{3,1,2,0:T(8,128)S(1)} %get-tuple-element.2034), channel_id=1, source_target_pairs={{16,0},{32,16},{48,32},{64,48},{80,64},{96,80},{112,96},{17,1},{33... | collective-permute-start | bytes 1179656 | tf_op jit(solution)/shard_map/while/body/eval_jaxpr/ppermute | solution.py:14
  391.6 14.9 %collective-permute-start.1 = (f32[1,16,16,384]{3,1,2,0:T(8,128)S(1)}, f32[1,16,16,384]{3,1,2,0:T(8,128)S(1)}, u32[]{:S(2)}, u32[]{:S(2)}) collective-permute-start(f32[1,16,16,384]{3,1,2,0:T(8,128)S(1)} %get-tuple-element.2034), channel_id=1, source_target_pairs={{16,0},{32,16},{48,32},{64,48},{80,64},{96,80},{112,96},{17,1},{33... | collective-permute-start | bytes 1179656 | tf_op jit(solution)/shard_map/while/body/eval_jaxpr/ppermute | solution.py:14
  416.0 15.6 %collective-permute-start.1 = (f32[1,16,16,384]{3,1,2,0:T(8,128)S(1)}, f32[1,16,16,384]{3,1,2,0:T(8,128)S(1)}, u32[]{:S(2)}, u32[]{:S(2)}) collective-permute-start(f32[1,16,16,384]{3,1,2,0:T(8,128)S(1)} %get-tuple-element.2034), channel_id=1, source_target_pairs={{16,0},{32,16},{48,32},{64,48},{80,64},{96,80},{112,96},{17,1},{33... | collective-permute-start | bytes 1179656 | tf_op jit(solution)/shard_map/while/body/eval_jaxpr/ppermute | solution.py:14
  558.4 20.3 %collective-permute-start.2 = (f32[1,16,16,384]{3,1,2,0:T(8,128)S(1)}, f32[1,16,16,384]{3,1,2,0:T(8,128)S(1)}, u32[]{:S(2)}, u32[]{:S(2)}) collective-permute-start(f32[1,16,16,384]{3,1,2,0:T(8,128)S(1)} %get-tuple-element.1802), channel_id=1, source_target_pairs={{0,16},{16,32},{32,48},{48,64},{64,80},{80,96},{96,112},{1,17},{17... | collective-permute-start | bytes 1179656 | tf_op jit(solution)/shard_map/while/body/eval_jaxpr/ppermute | solution.py:14
  594.9 18.7 %collective-permute-start.2 = (f32[1,16,16,384]{3,1,2,0:T(8,128)S(1)}, f32[1,16,16,384]{3,1,2,0:T(8,128)S(1)}, u32[]{:S(2)}, u32[]{:S(2)}) collective-permute-start(f32[1,16,16,384]{3,1,2,0:T(8,128)S(1)} %get-tuple-element.1802), channel_id=1, source_target_pairs={{0,16},{16,32},{32,48},{48,64},{64,80},{80,96},{96,112},{1,17},{17... | collective-permute-start | bytes 1179656 | tf_op jit(solution)/shard_map/while/body/eval_jaxpr/ppermute | solution.py:14
  629.9 23.7 %collective-permute-start.2 = (f32[1,16,16,384]{3,1,2,0:T(8,128)S(1)}, f32[1,16,16,384]{3,1,2,0:T(8,128)S(1)}, u32[]{:S(2)}, u32[]{:S(2)}) collective-permute-start(f32[1,16,16,384]{3,1,2,0:T(8,128)S(1)} %get-tuple-element.1802), channel_id=1, source_target_pairs={{0,16},{16,32},{32,48},{48,64},{64,80},{80,96},{96,112},{1,17},{17... | collective-permute-start | bytes 1179656 | tf_op jit(solution)/shard_map/while/body/eval_jaxpr/ppermute | solution.py:14
  673.4 29.7 %collective-permute-start.2 = (f32[1,16,16,384]{3,1,2,0:T(8,128)S(1)}, f32[1,16,16,384]{3,1,2,0:T(8,128)S(1)}, u32[]{:S(2)}, u32[]{:S(2)}) collective-permute-start(f32[1,16,16,384]{3,1,2,0:T(8,128)S(1)} %get-tuple-element.1802), channel_id=1, source_target_pairs={{0,16},{16,32},{32,48},{48,64},{64,80},{80,96},{96,112},{1,17},{17... | collective-permute-start | bytes 1179656 | tf_op jit(solution)/shard_map/while/body/eval_jaxpr/ppermute | solution.py:14
  706.8 14.0 %collective-permute-start.3 = (f32[1,16,16,384]{3,1,2,0:T(8,128)}, f32[1,16,16,384]{3,1,2,0:T(8,128)S(1)}, u32[]{:S(2)}, u32[]{:S(2)}) collective-permute-start(f32[1,16,16,384]{3,1,2,0:T(8,128)} %get-tuple-element.1819), channel_id=1, source_target_pairs={{16,0},{32,16},{48,32},{64,48},{80,64},{96,80},{112,96},{17,1},{33... | collective-permute-start | bytes 1179656 | tf_op jit(solution)/shard_map/while/body/eval_jaxpr/ppermute | solution.py:14
  722.2 14.0 %collective-permute-start.3 = (f32[1,16,16,384]{3,1,2,0:T(8,128)}, f32[1,16,16,384]{3,1,2,0:T(8,128)S(1)}, u32[]{:S(2)}, u32[]{:S(2)}) collective-permute-start(f32[1,16,16,384]{3,1,2,0:T(8,128)} %get-tuple-element.1819), channel_id=1, source_target_pairs={{16,0},{32,16},{48,32},{64,48},{80,64},{96,80},{112,96},{17,1},{33... | collective-permute-start | bytes 1179656 | tf_op jit(solution)/shard_map/while/body/eval_jaxpr/ppermute | solution.py:14
  737.5 14.0 %collective-permute-start.3 = (f32[1,16,16,384]{3,1,2,0:T(8,128)}, f32[1,16,16,384]{3,1,2,0:T(8,128)S(1)}, u32[]{:S(2)}, u32[]{:S(2)}) collective-permute-start(f32[1,16,16,384]{3,1,2,0:T(8,128)} %get-tuple-element.1819), channel_id=1, source_target_pairs={{16,0},{32,16},{48,32},{64,48},{80,64},{96,80},{112,96},{17,1},{33... | collective-permute-start | bytes 1179656 | tf_op jit(solution)/shard_map/while/body/eval_jaxpr/ppermute | solution.py:14
  752.8 14.8 %collective-permute-start.3 = (f32[1,16,16,384]{3,1,2,0:T(8,128)}, f32[1,16,16,384]{3,1,2,0:T(8,128)S(1)}, u32[]{:S(2)}, u32[]{:S(2)}) collective-permute-start(f32[1,16,16,384]{3,1,2,0:T(8,128)} %get-tuple-element.1819), channel_id=1, source_target_pairs={{16,0},{32,16},{48,32},{64,48},{80,64},{96,80},{112,96},{17,1},{33... | collective-permute-start | bytes 1179656 | tf_op jit(solution)/shard_map/while/body/eval_jaxpr/ppermute | solution.py:14
  783.8 16.3 %collective-permute-start.3 = (f32[1,16,16,384]{3,1,2,0:T(8,128)}, f32[1,16,16,384]{3,1,2,0:T(8,128)S(1)}, u32[]{:S(2)}, u32[]{:S(2)}) collective-permute-start(f32[1,16,16,384]{3,1,2,0:T(8,128)} %get-tuple-element.1819), channel_id=1, source_target_pairs={{16,0},{32,16},{48,32},{64,48},{80,64},{96,80},{112,96},{17,1},{33... | collective-permute-start | bytes 1179656 | tf_op jit(solution)/shard_map/while/body/eval_jaxpr/ppermute | solution.py:14
  801.5 90.0 %collective-permute-start.3 = (f32[1,16,16,384]{3,1,2,0:T(8,128)}, f32[1,16,16,384]{3,1,2,0:T(8,128)S(1)}, u32[]{:S(2)}, u32[]{:S(2)}) collective-permute-start(f32[1,16,16,384]{3,1,2,0:T(8,128)} %get-tuple-element.1819), channel_id=1, source_target_pairs={{16,0},{32,16},{48,32},{64,48},{80,64},{96,80},{112,96},{17,1},{33... | collective-permute-start | bytes 1179656 | tf_op jit(solution)/shard_map/while/body/eval_jaxpr/ppermute | solution.py:14
  950.5 14.7 %collective-permute-start.3 = (f32[1,16,16,384]{3,1,2,0:T(8,128)}, f32[1,16,16,384]{3,1,2,0:T(8,128)S(1)}, u32[]{:S(2)}, u32[]{:S(2)}) collective-permute-start(f32[1,16,16,384]{3,1,2,0:T(8,128)} %get-tuple-element.1819), channel_id=1, source_target_pairs={{16,0},{32,16},{48,32},{64,48},{80,64},{96,80},{112,96},{17,1},{33... | collective-permute-start | bytes 1179656 | tf_op jit(solution)/shard_map/while/body/eval_jaxpr/ppermute | solution.py:14
  (74 other events, 346.2 us)
Sparse Core Ops, SparseCore 0:
  1011.2 91.6 reduce-scatter.1

commit v7 on v6

--- a/solution.py
+++ b/solution.py
@@ -12,6 +12,24 @@
     count = lax.axis_size(axis)
     initial, last = (max(0, -steps), min(count, count - steps))
     return lax.ppermute(value, axis, [(source, source + steps) for source in range(initial, last)])
+
+
+def crossing_pairs(steps):
+    sections = lax.axis_size("section")
+    replicas = lax.axis_size("dp")
+    half, flip = (sections // 2, replicas // 2)
+    pairs = []
+    for source in range(max(0, -steps), min(sections, sections - steps)):
+        target = source + steps
+        crosses = (source < half) != (target < half)
+        for replica in range(replicas):
+            other = (replica + flip) % replicas if crosses else replica
+            pairs.append((source * replicas + replica, target * replicas + other))
+    return pairs
+
+
+def passed_across(value, steps):
+    return lax.ppermute(value, ("section", "dp"), crossing_pairs(steps))
 
 
 def embed(stamps_in, channels):
@@ -106,8 +124,15 @@
     channels = clean.shape[3]
     enc_kernel = enc_weight[0]
     dec_kernel = dec_weight[0]
-    narrow_table = modulation(stamps, channels)
-    wide_table = modulation(stamps, 2 * channels)
+    replicas = lax.axis_size("dp")
+    flipped_stamps = lax.ppermute(
+        stamps.astype(jnp.float32),
+        "dp",
+        [(replica, (replica + replicas // 2) % replicas) for replica in range(replicas)],
+    )
+    held_stamps = jnp.where(section_index < sections // 2, stamps.astype(jnp.float32), flipped_stamps)
+    narrow_table = modulation(held_stamps, channels)
+    wide_table = modulation(held_stamps, 2 * channels)
     enc_back_kernel = flipped(enc_kernel)
     dec_back_kernel = flipped(dec_kernel)
     keep_level, spread_level = noise_levels(stamps)
@@ -145,7 +170,7 @@
         )
         enc_inputs = put_row(enc_inputs, source, slot_index)
         skips = put_row(skips, result, slot_index)
-        incoming = passed_along(result, "section", 1)
+        incoming = passed_across(result, 1)
         return (incoming, enc_inputs, skips)
 
     _, enc_inputs, skips = lax.fori_loop(
@@ -166,7 +191,7 @@
         )
         dec_inputs = put_row(dec_inputs, source, slot_index)
         outputs = put_row(outputs, result, slot_index)
-        incoming = passed_along(result, "section", -1)
+        incoming = passed_across(result, -1)
         return (incoming, dec_inputs, outputs)
 
     _, dec_inputs, outputs = lax.fori_loop(
@@ -208,7 +233,7 @@
         up_grads = put_row(up_grads, up_piece, slot_index)
         dec_acts = put_row(dec_acts, acts, slot_index)
         dec_cots = put_row(dec_cots, cots, slot_index)
-        incoming = passed_along(up_piece, "section", 1)
+        incoming = passed_across(up_piece, 1)
         return (incoming, skip_grads, up_grads, dec_acts, dec_cots)
 
     _, skip_grads, up_grads, dec_acts, dec_cots = lax.fori_loop(
@@ -246,7 +271,7 @@
         down_piece, acts, cots = lax.cond(active, encoder_working, encoder_resting)
         enc_acts = put_row(enc_acts, acts, slot_index)
         enc_cots = put_row(enc_cots, cots, slot_index)
-        incoming = passed_along(down_piece, "section", -1)
+        incoming = passed_across(down_piece, -1)
         return (incoming, enc_acts, enc_cots)
 
     _, enc_acts, enc_cots = lax.fori_loop(

time: 1120 us -> 1110 us (level)
    ppermute x44 -> x45, waiting for transfers between devices: 458 us -> 455 us  [the longest x44 455 us: passed_across(): return lax.ppermute(value, ('section', 'dp'), crossing_pairs(steps))]
    ppermute x44 -> x45, starting transfers between devices: 207 us -> 206 us  [the longest x44 204 us: passed_across(): return lax.ppermute(value, ('section', 'dp'), crossing_pairs(steps))]
  transfers between devices with their start and end apart: 45 -> 46, of which waited for: 45 -> 45; matrix products, arithmetic and copies ran while one was open for 5% -> 7% of each run, Pallas kernels for 0% -> 0%
where the time goes in v7:
time: 1110 us
  waiting for transfers between devices  546 us (49%)
  starting transfers between devices  206 us (19%)
  local copies, waits for them, and re-layouts  163 us (15%)
  other arithmetic  99.5 us (9%)
  matrix products  75.1 us (7%)
  between operations  14.2 us (1%)
    ppermute x44, waiting for transfers between devices, passed_across(): return lax.ppermute(value, ('section', 'dp'), crossing_pairs(steps))  455 us
    ppermute x44, starting transfers between devices, passed_across(): return lax.ppermute(value, ('section', 'dp'), crossing_pairs(steps))  204 us
    reduce_scatter x1, waiting for transfers between devices, shards(): share = lax.psum_scatter(both, 'dp', scatter_dimension=3, tiled=True)  90.8 us
    conv_general_dilated x16, matrix products, conv_apply(): lax.conv_general_dilated(activations, weight, window_strides=(1, 1), padd...  60.5 us
    dynamic_update_slice x66, local copies, waits for them, and re-layouts, put_row(): lax.dynamic_update_slice_in_dim(buffer, piece.astype(buffer.dtype), slot_...  54.4 us
    dynamic_update_slice x22, other arithmetic, put_row(): lax.dynamic_update_slice_in_dim(buffer, piece.astype(buffer.dtype), slot_...  31.8 us
    dynamic_slice x22, local copies, waits for them, and re-layouts, pick_row(): return lax.dynamic_slice_in_dim(buffer, slot_index, 1, 0)  22.5 us
  transfers between devices with their start and end apart: 46, of which 45 were waited for; matrix products, arithmetic and copies ran while one was open for 7% of the time, Pallas kernels for 0%

profile of v7, /device:TPU:0, one launch (start us, length us, event | category | flops | bytes accessed | tf_op | source)
XLA Modules:
  0.0 1108.9 jit_solution(3224688017751721620)
XLA Ops:
  37.2 174.8 %while.80 = (s32[]{:T(128)}, f32[1,16,16,384]{3,1,2,0:T(8,128)S(1)}, f32[6,16,16,384]{3,1,2,0:T(8,128)S(1)}, f32[6,16,16,384]{3,1,2,0:T(8,128)}, s32[]{:T(128)},...) while((s32[]{:T(128)}, ...), condition=%wide.region_8.9_spmd, body=%wide.region_0.8_spmd.sunk | while | flops 979749568 | bytes 12841028 | solution.py:176
  160.6 12.4 %collective-permute-start = (f32[1,16,16,384]{3,1,2,0:T(8,128)S(1)}, f32[1,16,16,384]{3,1,2,0:T(8,128)S(1)}, u32[]{:S(2)}, u32[]{:S(2)}) collective-permute-start(f32[1,16,16,384]{3,1,2,0:T(8,128)S(1)} %get-tuple-element.2034), channel_id=1, source_target_pairs={{0,16},{1,17},{2,18},{3,19},{4,20},{5,21},{6,22},{7,23},{8,24},{9,... | collective-permute-start | bytes 1179656 | tf_op jit(solution)/shard_map/while/body/eval_jaxpr/ppermute | solution.py:32
  193.4 13.3 %collective-permute-start = (f32[1,16,16,384]{3,1,2,0:T(8,128)S(1)}, f32[1,16,16,384]{3,1,2,0:T(8,128)S(1)}, u32[]{:S(2)}, u32[]{:S(2)}) collective-permute-start(f32[1,16,16,384]{3,1,2,0:T(8,128)S(1)} %get-tuple-element.2034), channel_id=1, source_target_pairs={{0,16},{1,17},{2,18},{3,19},{4,20},{5,21},{6,22},{7,23},{8,24},{9,... | collective-permute-start | bytes 1179656 | tf_op jit(solution)/shard_map/while/body/eval_jaxpr/ppermute | solution.py:32
  215.5 236.7 %while.81 = (s32[]{:T(128)}, f32[1,16,16,384]{3,1,2,0:T(8,128)S(1)}, f32[6,16,16,384]{3,1,2,0:T(8,128)}, f32[6,16,16,384]{3,1,2,0:T(8,128)}, s32[]{:T(128)}, /*i...) while((s32[]{:T(128)}, ...), condition=%wide.region_17.18_spmd, body=%wide.region_9.0_spmd.sunk | while | flops 1959351552 | bytes 20765760 | solution.py:197
  219.6 12.1 %collective-permute-done.1 = f32[1,16,16,384]{3,1,2,0:T(8,128)S(1)} collective-permute-done((f32[1,16,16,384]{3,1,2,0:T(8,128)S(1)}, f32[1,16,16,384]{3,1,2,0:T(8,128)S(1)}, u32[]{:S(2)}, u32[]{:S(2)}) %collective-permute-start.1) | collective-permute-done | bytes 393248 | tf_op jit(solution)/shard_map/while/body/eval_jaxpr/ppermute | solution.py:32
  235.7 13.4 %collective-permute-done.1 = f32[1,16,16,384]{3,1,2,0:T(8,128)S(1)} collective-permute-done((f32[1,16,16,384]{3,1,2,0:T(8,128)S(1)}, f32[1,16,16,384]{3,1,2,0:T(8,128)S(1)}, u32[]{:S(2)}, u32[]{:S(2)}) %collective-permute-start.1) | collective-permute-done | bytes 393248 | tf_op jit(solution)/shard_map/while/body/eval_jaxpr/ppermute | solution.py:32
  253.2 14.5 %collective-permute-done.1 = f32[1,16,16,384]{3,1,2,0:T(8,128)S(1)} collective-permute-done((f32[1,16,16,384]{3,1,2,0:T(8,128)S(1)}, f32[1,16,16,384]{3,1,2,0:T(8,128)S(1)}, u32[]{:S(2)}, u32[]{:S(2)}) %collective-permute-start.1) | collective-permute-done | bytes 393248 | tf_op jit(solution)/shard_map/while/body/eval_jaxpr/ppermute | solution.py:32
  271.9 17.8 %collective-permute-done.1 = f32[1,16,16,384]{3,1,2,0:T(8,128)S(1)} collective-permute-done((f32[1,16,16,384]{3,1,2,0:T(8,128)S(1)}, f32[1,16,16,384]{3,1,2,0:T(8,128)S(1)}, u32[]{:S(2)}, u32[]{:S(2)}) %collective-permute-start.1) | collective-permute-done | bytes 393248 | tf_op jit(solution)/shard_map/while/body/eval_jaxpr/ppermute | solution.py:32
  293.8 14.5 %collective-permute-done.1 = f32[1,16,16,384]{3,1,2,0:T(8,128)S(1)} collective-permute-done((f32[1,16,16,384]{3,1,2,0:T(8,128)S(1)}, f32[1,16,16,384]{3,1,2,0:T(8,128)S(1)}, u32[]{:S(2)}, u32[]{:S(2)}) %collective-permute-start.1) | collective-permute-done | bytes 393248 | tf_op jit(solution)/shard_map/while/body/eval_jaxpr/ppermute | solution.py:32
  324.0 37.4 %collective-permute-done.1 = f32[1,16,16,384]{3,1,2,0:T(8,128)S(1)} collective-permute-done((f32[1,16,16,384]{3,1,2,0:T(8,128)S(1)}, f32[1,16,16,384]{3,1,2,0:T(8,128)S(1)}, u32[]{:S(2)}, u32[]{:S(2)}) %collective-permute-start.1) | collective-permute-done | bytes 393248 | tf_op jit(solution)/shard_map/while/body/eval_jaxpr/ppermute | solution.py:32
  395.6 11.9 %collective-permute-done.1 = f32[1,16,16,384]{3,1,2,0:T(8,128)S(1)} collective-permute-done((f32[1,16,16,384]{3,1,2,0:T(8,128)S(1)}, f32[1,16,16,384]{3,1,2,0:T(8,128)S(1)}, u32[]{:S(2)}, u32[]{:S(2)}) %collective-permute-start.1) | collective-permute-done | bytes 393248 | tf_op jit(solution)/shard_map/while/body/eval_jaxpr/ppermute | solution.py:32
  419.1 13.9 %collective-permute-done.1 = f32[1,16,16,384]{3,1,2,0:T(8,128)S(1)} collective-permute-done((f32[1,16,16,384]{3,1,2,0:T(8,128)S(1)}, f32[1,16,16,384]{3,1,2,0:T(8,128)S(1)}, u32[]{:S(2)}, u32[]{:S(2)}) %collective-permute-start.1) | collective-permute-done | bytes 393248 | tf_op jit(solution)/shard_map/while/body/eval_jaxpr/ppermute | solution.py:32
  458.2 243.6 %while.82 = (s32[]{:T(128)}, f32[1,16,16,384]{3,1,2,0:T(8,128)S(1)}, f32[6,16,16,384]{3,1,2,0:T(8,128)}, f32[6,16,16,384]{3,1,2,0:T(8,128)}, bf16[6,16,16,768]{3...) while((s32[]{:T(128)}, ...), condition=%wide.region_30.31_spmd, body=%wide.region_18.30_spmd.sunk | while | flops 1967265280 | bytes 31725936 | solution.py:239
  558.8 15.1 %collective-permute-start.2 = (f32[1,16,16,384]{3,1,2,0:T(8,128)S(1)}, f32[1,16,16,384]{3,1,2,0:T(8,128)S(1)}, u32[]{:S(2)}, u32[]{:S(2)}) collective-permute-start(f32[1,16,16,384]{3,1,2,0:T(8,128)S(1)} %get-tuple-element.1803), channel_id=1, source_target_pairs={{0,16},{1,17},{2,18},{3,19},{4,20},{5,21},{6,22},{7,23},{8,24},{9,... | collective-permute-start | bytes 1179656 | tf_op jit(solution)/shard_map/while/body/eval_jaxpr/ppermute | solution.py:32
  595.4 13.5 %collective-permute-start.2 = (f32[1,16,16,384]{3,1,2,0:T(8,128)S(1)}, f32[1,16,16,384]{3,1,2,0:T(8,128)S(1)}, u32[]{:S(2)}, u32[]{:S(2)}) collective-permute-start(f32[1,16,16,384]{3,1,2,0:T(8,128)S(1)} %get-tuple-element.1803), channel_id=1, source_target_pairs={{0,16},{1,17},{2,18},{3,19},{4,20},{5,21},{6,22},{7,23},{8,24},{9,... | collective-permute-start | bytes 1179656 | tf_op jit(solution)/shard_map/while/body/eval_jaxpr/ppermute | solution.py:32
  630.3 17.6 %collective-permute-start.2 = (f32[1,16,16,384]{3,1,2,0:T(8,128)S(1)}, f32[1,16,16,384]{3,1,2,0:T(8,128)S(1)}, u32[]{:S(2)}, u32[]{:S(2)}) collective-permute-start(f32[1,16,16,384]{3,1,2,0:T(8,128)S(1)} %get-tuple-element.1803), channel_id=1, source_target_pairs={{0,16},{1,17},{2,18},{3,19},{4,20},{5,21},{6,22},{7,23},{8,24},{9,... | collective-permute-start | bytes 1179656 | tf_op jit(solution)/shard_map/while/body/eval_jaxpr/ppermute | solution.py:32
  672.7 23.8 %collective-permute-start.2 = (f32[1,16,16,384]{3,1,2,0:T(8,128)S(1)}, f32[1,16,16,384]{3,1,2,0:T(8,128)S(1)}, u32[]{:S(2)}, u32[]{:S(2)}) collective-permute-start(f32[1,16,16,384]{3,1,2,0:T(8,128)S(1)} %get-tuple-element.1803), channel_id=1, source_target_pairs={{0,16},{1,17},{2,18},{3,19},{4,20},{5,21},{6,22},{7,23},{8,24},{9,... | collective-permute-start | bytes 1179656 | tf_op jit(solution)/shard_map/while/body/eval_jaxpr/ppermute | solution.py:32
  704.1 278.4 %while.83 = (s32[]{:T(128)}, f32[1,16,16,384]{3,1,2,0:T(8,128)S(1)}, bf16[6,16,16,384]{3,2,1,0:T(8,128)(2,1)}, bf16[6,16,16,384]{3,2,1,0:T(8,128)(2,1)}, s32[]{:...) while((s32[]{:T(128)}, ...), condition=%wide.region_43.44_spmd, body=%wide.region_31.43_spmd.sunk | while | flops 982010688 | bytes 27228124 | solution.py:277
  737.7 11.6 %collective-permute-done.3 = f32[1,16,16,384]{3,1,2,0:T(8,128)S(1)} collective-permute-done((f32[1,16,16,384]{3,1,2,0:T(8,128)}, f32[1,16,16,384]{3,1,2,0:T(8,128)S(1)}, u32[]{:S(2)}, u32[]{:S(2)}) %collective-permute-start.3) | collective-permute-done | bytes 393248 | tf_op jit(solution)/shard_map/while/body/eval_jaxpr/ppermute | solution.py:32
  752.8 13.7 %collective-permute-done.3 = f32[1,16,16,384]{3,1,2,0:T(8,128)S(1)} collective-permute-done((f32[1,16,16,384]{3,1,2,0:T(8,128)}, f32[1,16,16,384]{3,1,2,0:T(8,128)S(1)}, u32[]{:S(2)}, u32[]{:S(2)}) %collective-permute-start.3) | collective-permute-done | bytes 393248 | tf_op jit(solution)/shard_map/while/body/eval_jaxpr/ppermute | solution.py:32
  784.5 14.5 %collective-permute-done.3 = f32[1,16,16,384]{3,1,2,0:T(8,128)S(1)} collective-permute-done((f32[1,16,16,384]{3,1,2,0:T(8,128)}, f32[1,16,16,384]{3,1,2,0:T(8,128)S(1)}, u32[]{:S(2)}, u32[]{:S(2)}) %collective-permute-start.3) | collective-permute-done | bytes 393248 | tf_op jit(solution)/shard_map/while/body/eval_jaxpr/ppermute | solution.py:32
  802.5 85.2 %collective-permute-done.3 = f32[1,16,16,384]{3,1,2,0:T(8,128)S(1)} collective-permute-done((f32[1,16,16,384]{3,1,2,0:T(8,128)}, f32[1,16,16,384]{3,1,2,0:T(8,128)S(1)}, u32[]{:S(2)}, u32[]{:S(2)}) %collective-permute-start.3) | collective-permute-done | bytes 393248 | tf_op jit(solution)/shard_map/while/body/eval_jaxpr/ppermute | solution.py:32
  924.1 13.6 %collective-permute-done.3 = f32[1,16,16,384]{3,1,2,0:T(8,128)S(1)} collective-permute-done((f32[1,16,16,384]{3,1,2,0:T(8,128)}, f32[1,16,16,384]{3,1,2,0:T(8,128)S(1)}, u32[]{:S(2)}, u32[]{:S(2)}) %collective-permute-start.3) | collective-permute-done | bytes 393248 | tf_op jit(solution)/shard_map/while/body/eval_jaxpr/ppermute | solution.py:32
  1007.6 90.8 %reduce-scatter.2.cloned.1.call-done = f32[1,3,3,72,384]{4,3,2,1,0:T(8,128)} async-done(((f32[1,3,3,1152,384]{4,3,2,1,0:T(8,128)}), f32[1,3,3,72,384]{4,3,2,1,0:T(8,128)}) %reduce-scatter.2.cloned.1.call-update) | async-done | bytes 995344 | tf_op jit(solution)/shard_map/reduce_scatter | solution.py:294
  (958 shorter events, 774.3 us)
Async XLA Ops:
  7.2 1091.2 %reduce-scatter.2.cloned.1.call-start = ((), (), s32[]{:S(2)}) async-start(), calls=%async_computation.1 | async-start | bytes 16920576 | tf_op jit(solution)/shard_map/reduce_scatter | solution.py:294
  7.9 24.8 %collective-permute-start.4 = (f32[4]{0:T(128)S(1)}, f32[4]{0:T(128)S(1)}, u32[]{:S(2)}, u32[]{:S(2)}) collective-permute-start(f32[4]{0:T(128)S(1)} %convert_element_type.108), channel_id=1, source_target_pairs={{0,8},{1,9},{2,10},{3,11},{4,12},{5,13},{6,14},{7,15},{8,0},{9,1},... | collective-permute-start | bytes 56 | tf_op jit(solution)/shard_map/ppermute | solution.py:128
  107.5 15.2 %collective-permute-start = (f32[1,16,16,384]{3,1,2,0:T(8,128)S(1)}, f32[1,16,16,384]{3,1,2,0:T(8,128)S(1)}, u32[]{:S(2)}, u32[]{:S(2)}) collective-permute-start(f32[1,16,16,384]{3,1,2,0:T(8,128)S(1)} %get-tuple-element.2034), channel_id=1, source_target_pairs={{0,16},{1,17},{2,18},{3,19},{4,20},{5,21},{6,22},{7,23},{8,24},{9,... | collective-permute-start | bytes 1179656 | tf_op jit(solution)/shard_map/while/body/eval_jaxpr/ppermute | solution.py:32
  134.6 14.0 %collective-permute-start = (f32[1,16,16,384]{3,1,2,0:T(8,128)S(1)}, f32[1,16,16,384]{3,1,2,0:T(8,128)S(1)}, u32[]{:S(2)}, u32[]{:S(2)}) collective-permute-start(f32[1,16,16,384]{3,1,2,0:T(8,128)S(1)} %get-tuple-element.2034), channel_id=1, source_target_pairs={{0,16},{1,17},{2,18},{3,19},{4,20},{5,21},{6,22},{7,23},{8,24},{9,... | collective-permute-start | bytes 1179656 | tf_op jit(solution)/shard_map/while/body/eval_jaxpr/ppermute | solution.py:32
  160.6 17.6 %collective-permute-start = (f32[1,16,16,384]{3,1,2,0:T(8,128)S(1)}, f32[1,16,16,384]{3,1,2,0:T(8,128)S(1)}, u32[]{:S(2)}, u32[]{:S(2)}) collective-permute-start(f32[1,16,16,384]{3,1,2,0:T(8,128)S(1)} %get-tuple-element.2034), channel_id=1, source_target_pairs={{0,16},{1,17},{2,18},{3,19},{4,20},{5,21},{6,22},{7,23},{8,24},{9,... | collective-permute-start | bytes 1179656 | tf_op jit(solution)/shard_map/while/body/eval_jaxpr/ppermute | solution.py:32
  193.4 18.5 %collective-permute-start = (f32[1,16,16,384]{3,1,2,0:T(8,128)S(1)}, f32[1,16,16,384]{3,1,2,0:T(8,128)S(1)}, u32[]{:S(2)}, u32[]{:S(2)}) collective-permute-start(f32[1,16,16,384]{3,1,2,0:T(8,128)S(1)} %get-tuple-element.2034), channel_id=1, source_target_pairs={{0,16},{1,17},{2,18},{3,19},{4,20},{5,21},{6,22},{7,23},{8,24},{9,... | collective-permute-start | bytes 1179656 | tf_op jit(solution)/shard_map/while/body/eval_jaxpr/ppermute | solution.py:32
  217.5 14.2 %collective-permute-start.1 = (f32[1,16,16,384]{3,1,2,0:T(8,128)S(1)}, f32[1,16,16,384]{3,1,2,0:T(8,128)S(1)}, u32[]{:S(2)}, u32[]{:S(2)}) collective-permute-start(f32[1,16,16,384]{3,1,2,0:T(8,128)S(1)} %get-tuple-element.2035), channel_id=1, source_target_pairs={{16,0},{17,1},{18,2},{19,3},{20,4},{21,5},{22,6},{23,7},{24,8},{25... | collective-permute-start | bytes 1179656 | tf_op jit(solution)/shard_map/while/body/eval_jaxpr/ppermute | solution.py:32
  233.6 15.5 %collective-permute-start.1 = (f32[1,16,16,384]{3,1,2,0:T(8,128)S(1)}, f32[1,16,16,384]{3,1,2,0:T(8,128)S(1)}, u32[]{:S(2)}, u32[]{:S(2)}) collective-permute-start(f32[1,16,16,384]{3,1,2,0:T(8,128)S(1)} %get-tuple-element.2035), channel_id=1, source_target_pairs={{16,0},{17,1},{18,2},{19,3},{20,4},{21,5},{22,6},{23,7},{24,8},{25... | collective-permute-start | bytes 1179656 | tf_op jit(solution)/shard_map/while/body/eval_jaxpr/ppermute | solution.py:32
  251.1 16.6 %collective-permute-start.1 = (f32[1,16,16,384]{3,1,2,0:T(8,128)S(1)}, f32[1,16,16,384]{3,1,2,0:T(8,128)S(1)}, u32[]{:S(2)}, u32[]{:S(2)}) collective-permute-start(f32[1,16,16,384]{3,1,2,0:T(8,128)S(1)} %get-tuple-element.2035), channel_id=1, source_target_pairs={{16,0},{17,1},{18,2},{19,3},{20,4},{21,5},{22,6},{23,7},{24,8},{25... | collective-permute-start | bytes 1179656 | tf_op jit(solution)/shard_map/while/body/eval_jaxpr/ppermute | solution.py:32
  269.8 19.9 %collective-permute-start.1 = (f32[1,16,16,384]{3,1,2,0:T(8,128)S(1)}, f32[1,16,16,384]{3,1,2,0:T(8,128)S(1)}, u32[]{:S(2)}, u32[]{:S(2)}) collective-permute-start(f32[1,16,16,384]{3,1,2,0:T(8,128)S(1)} %get-tuple-element.2035), channel_id=1, source_target_pairs={{16,0},{17,1},{18,2},{19,3},{20,4},{21,5},{22,6},{23,7},{24,8},{25... | collective-permute-start | bytes 1179656 | tf_op jit(solution)/shard_map/while/body/eval_jaxpr/ppermute | solution.py:32
  291.7 16.6 %collective-permute-start.1 = (f32[1,16,16,384]{3,1,2,0:T(8,128)S(1)}, f32[1,16,16,384]{3,1,2,0:T(8,128)S(1)}, u32[]{:S(2)}, u32[]{:S(2)}) collective-permute-start(f32[1,16,16,384]{3,1,2,0:T(8,128)S(1)} %get-tuple-element.2035), channel_id=1, source_target_pairs={{16,0},{17,1},{18,2},{19,3},{20,4},{21,5},{22,6},{23,7},{24,8},{25... | collective-permute-start | bytes 1179656 | tf_op jit(solution)/shard_map/while/body/eval_jaxpr/ppermute | solution.py:32
  321.9 39.5 %collective-permute-start.1 = (f32[1,16,16,384]{3,1,2,0:T(8,128)S(1)}, f32[1,16,16,384]{3,1,2,0:T(8,128)S(1)}, u32[]{:S(2)}, u32[]{:S(2)}) collective-permute-start(f32[1,16,16,384]{3,1,2,0:T(8,128)S(1)} %get-tuple-element.2035), channel_id=1, source_target_pairs={{16,0},{17,1},{18,2},{19,3},{20,4},{21,5},{22,6},{23,7},{24,8},{25... | collective-permute-start | bytes 1179656 | tf_op jit(solution)/shard_map/while/body/eval_jaxpr/ppermute | solution.py:32
  393.5 14.0 %collective-permute-start.1 = (f32[1,16,16,384]{3,1,2,0:T(8,128)S(1)}, f32[1,16,16,384]{3,1,2,0:T(8,128)S(1)}, u32[]{:S(2)}, u32[]{:S(2)}) collective-permute-start(f32[1,16,16,384]{3,1,2,0:T(8,128)S(1)} %get-tuple-element.2035), channel_id=1, source_target_pairs={{16,0},{17,1},{18,2},{19,3},{20,4},{21,5},{22,6},{23,7},{24,8},{25... | collective-permute-start | bytes 1179656 | tf_op jit(solution)/shard_map/while/body/eval_jaxpr/ppermute | solution.py:32
  417.0 16.0 %collective-permute-start.1 = (f32[1,16,16,384]{3,1,2,0:T(8,128)S(1)}, f32[1,16,16,384]{3,1,2,0:T(8,128)S(1)}, u32[]{:S(2)}, u32[]{:S(2)}) collective-permute-start(f32[1,16,16,384]{3,1,2,0:T(8,128)S(1)} %get-tuple-element.2035), channel_id=1, source_target_pairs={{16,0},{17,1},{18,2},{19,3},{20,4},{21,5},{22,6},{23,7},{24,8},{25... | collective-permute-start | bytes 1179656 | tf_op jit(solution)/shard_map/while/body/eval_jaxpr/ppermute | solution.py:32
  558.8 20.3 %collective-permute-start.2 = (f32[1,16,16,384]{3,1,2,0:T(8,128)S(1)}, f32[1,16,16,384]{3,1,2,0:T(8,128)S(1)}, u32[]{:S(2)}, u32[]{:S(2)}) collective-permute-start(f32[1,16,16,384]{3,1,2,0:T(8,128)S(1)} %get-tuple-element.1803), channel_id=1, source_target_pairs={{0,16},{1,17},{2,18},{3,19},{4,20},{5,21},{6,22},{7,23},{8,24},{9,... | collective-permute-start | bytes 1179656 | tf_op jit(solution)/shard_map/while/body/eval_jaxpr/ppermute | solution.py:32
  595.4 18.7 %collective-permute-start.2 = (f32[1,16,16,384]{3,1,2,0:T(8,128)S(1)}, f32[1,16,16,384]{3,1,2,0:T(8,128)S(1)}, u32[]{:S(2)}, u32[]{:S(2)}) collective-permute-start(f32[1,16,16,384]{3,1,2,0:T(8,128)S(1)} %get-tuple-element.1803), channel_id=1, source_target_pairs={{0,16},{1,17},{2,18},{3,19},{4,20},{5,21},{6,22},{7,23},{8,24},{9,... | collective-permute-start | bytes 1179656 | tf_op jit(solution)/shard_map/while/body/eval_jaxpr/ppermute | solution.py:32
  630.3 22.9 %collective-permute-start.2 = (f32[1,16,16,384]{3,1,2,0:T(8,128)S(1)}, f32[1,16,16,384]{3,1,2,0:T(8,128)S(1)}, u32[]{:S(2)}, u32[]{:S(2)}) collective-permute-start(f32[1,16,16,384]{3,1,2,0:T(8,128)S(1)} %get-tuple-element.1803), channel_id=1, source_target_pairs={{0,16},{1,17},{2,18},{3,19},{4,20},{5,21},{6,22},{7,23},{8,24},{9,... | collective-permute-start | bytes 1179656 | tf_op jit(solution)/shard_map/while/body/eval_jaxpr/ppermute | solution.py:32
  672.7 29.0 %collective-permute-start.2 = (f32[1,16,16,384]{3,1,2,0:T(8,128)S(1)}, f32[1,16,16,384]{3,1,2,0:T(8,128)S(1)}, u32[]{:S(2)}, u32[]{:S(2)}) collective-permute-start(f32[1,16,16,384]{3,1,2,0:T(8,128)S(1)} %get-tuple-element.1803), channel_id=1, source_target_pairs={{0,16},{1,17},{2,18},{3,19},{4,20},{5,21},{6,22},{7,23},{8,24},{9,... | collective-permute-start | bytes 1179656 | tf_op jit(solution)/shard_map/while/body/eval_jaxpr/ppermute | solution.py:32
  720.5 13.7 %collective-permute-start.3 = (f32[1,16,16,384]{3,1,2,0:T(8,128)}, f32[1,16,16,384]{3,1,2,0:T(8,128)S(1)}, u32[]{:S(2)}, u32[]{:S(2)}) collective-permute-start(f32[1,16,16,384]{3,1,2,0:T(8,128)} %get-tuple-element.1820), channel_id=1, source_target_pairs={{16,0},{17,1},{18,2},{19,3},{20,4},{21,5},{22,6},{23,7},{24,8},{25... | collective-permute-start | bytes 1179656 | tf_op jit(solution)/shard_map/while/body/eval_jaxpr/ppermute | solution.py:32
  735.6 13.7 %collective-permute-start.3 = (f32[1,16,16,384]{3,1,2,0:T(8,128)}, f32[1,16,16,384]{3,1,2,0:T(8,128)S(1)}, u32[]{:S(2)}, u32[]{:S(2)}) collective-permute-start(f32[1,16,16,384]{3,1,2,0:T(8,128)} %get-tuple-element.1820), channel_id=1, source_target_pairs={{16,0},{17,1},{18,2},{19,3},{20,4},{21,5},{22,6},{23,7},{24,8},{25... | collective-permute-start | bytes 1179656 | tf_op jit(solution)/shard_map/while/body/eval_jaxpr/ppermute | solution.py:32
  750.6 15.8 %collective-permute-start.3 = (f32[1,16,16,384]{3,1,2,0:T(8,128)}, f32[1,16,16,384]{3,1,2,0:T(8,128)S(1)}, u32[]{:S(2)}, u32[]{:S(2)}) collective-permute-start(f32[1,16,16,384]{3,1,2,0:T(8,128)} %get-tuple-element.1820), channel_id=1, source_target_pairs={{16,0},{17,1},{18,2},{19,3},{20,4},{21,5},{22,6},{23,7},{24,8},{25... | collective-permute-start | bytes 1179656 | tf_op jit(solution)/shard_map/while/body/eval_jaxpr/ppermute | solution.py:32
  782.4 16.6 %collective-permute-start.3 = (f32[1,16,16,384]{3,1,2,0:T(8,128)}, f32[1,16,16,384]{3,1,2,0:T(8,128)S(1)}, u32[]{:S(2)}, u32[]{:S(2)}) collective-permute-start(f32[1,16,16,384]{3,1,2,0:T(8,128)} %get-tuple-element.1820), channel_id=1, source_target_pairs={{16,0},{17,1},{18,2},{19,3},{20,4},{21,5},{22,6},{23,7},{24,8},{25... | collective-permute-start | bytes 1179656 | tf_op jit(solution)/shard_map/while/body/eval_jaxpr/ppermute | solution.py:32
  800.4 87.4 %collective-permute-start.3 = (f32[1,16,16,384]{3,1,2,0:T(8,128)}, f32[1,16,16,384]{3,1,2,0:T(8,128)S(1)}, u32[]{:S(2)}, u32[]{:S(2)}) collective-permute-start(f32[1,16,16,384]{3,1,2,0:T(8,128)} %get-tuple-element.1820), channel_id=1, source_target_pairs={{16,0},{17,1},{18,2},{19,3},{20,4},{21,5},{22,6},{23,7},{24,8},{25... | collective-permute-start | bytes 1179656 | tf_op jit(solution)/shard_map/while/body/eval_jaxpr/ppermute | solution.py:32
  922.0 15.7 %collective-permute-start.3 = (f32[1,16,16,384]{3,1,2,0:T(8,128)}, f32[1,16,16,384]{3,1,2,0:T(8,128)S(1)}, u32[]{:S(2)}, u32[]{:S(2)}) collective-permute-start(f32[1,16,16,384]{3,1,2,0:T(8,128)} %get-tuple-element.1820), channel_id=1, source_target_pairs={{16,0},{17,1},{18,2},{19,3},{20,4},{21,5},{22,6},{23,7},{24,8},{25... | collective-permute-start | bytes 1179656 | tf_op jit(solution)/shard_map/while/body/eval_jaxpr/ppermute | solution.py:32
  (76 other events, 360.7 us)
Sparse Core Ops, SparseCore 0:
  1007.7 90.6 reduce-scatter.1

commit v8 on v6

--- a/solution.py
+++ b/solution.py
@@ -51,23 +51,14 @@
 
 
 def conv_weight_grad(activations, cotangent):
-    batch_rows, height, breadth, channels = activations.shape
-    padded = jnp.pad(activations, ((0, 0), (1, 1), (1, 1), (0, 0)))
-    flat_cot = cotangent.astype(jnp.bfloat16).reshape(-1, cotangent.shape[3])
-    kernel_rows = []
-    for row_off in range(3):
-        kernel_cols = []
-        for col_off in range(3):
-            window = padded[:, row_off : row_off + height, col_off : col_off + breadth, :].reshape(
-                -1, channels
-            )
-            kernel_cols.append(
-                lax.dot_general(
-                    window, flat_cot, (((0,), (0,)), ((), ())), preferred_element_type=jnp.float32
-                )
-            )
-        kernel_rows.append(jnp.stack(kernel_cols))
-    return jnp.stack(kernel_rows)
+    return lax.conv_general_dilated(
+        activations,
+        cotangent.astype(jnp.bfloat16),
+        window_strides=(1, 1),
+        padding=((1, 1), (1, 1)),
+        dimension_numbers=("CHWN", "IHWO", "HWNC"),
+        preferred_element_type=jnp.float32,
+    )
 
 
 def modulation(stamps_in, channels):
@@ -178,13 +169,14 @@
         input_grad = pullback(conv_back(cotangent, weight))[0]
         return (input_grad, activated.astype(jnp.bfloat16), cotangent.astype(jnp.bfloat16))
 
+    top_grads = factor * (
+        outputs - jnp.pad(noise.astype(jnp.float32), ((1, 1), (0, 0), (0, 0), (0, 0)))
+    )
+
     def decoder_back_tick(tick_now, carried):
         incoming, skip_grads, up_grads, dec_acts, dec_cots = carried
         active, sample_at, slot_index = locate(tick_now, section_index)
-        top_grad = factor * (
-            pick_row(outputs, slot_index) - pick_row(noise, sample_at).astype(jnp.float32)
-        )
-        flowing = jnp.where(section_index == 0, top_grad, incoming)
+        flowing = jnp.where(section_index == 0, pick_row(top_grads, slot_index), incoming)
         joined = jnp.concatenate(
             [pick_row(dec_inputs, slot_index), pick_row(skips, slot_index)], axis=3
         )

time: 1120 us -> 1150 us (1.027)
  local copies, waits for them, and re-layouts: 163 us -> 186 us
  waiting for transfers between devices: 550 us -> 528 us
    conv_general_dilated x0 -> x2, matrix products: none -> 23.6 us  [conv_weight_grad(): lax.conv_general_dilated(activations, cotangent.astype(jnp.bfloat16), win...]
    dynamic_update_slice x66, local copies, waits for them, and re-layouts: 54.4 us -> 74.4 us  [put_row(): lax.dynamic_update_slice_in_dim(buffer, piece.astype(buffer.dtype), slot_...]
    ppermute x44, waiting for transfers between devices: 458 us -> 440 us  [passed_along(): lax.ppermute(value, axis, [(source, source + steps) for source in range(i...]
    dot_general x18 -> x0, matrix products: 14.6 us -> none  [conv_weight_grad(): lax.dot_general(window, flat_cot, (((0,), (0,)), ((), ())), preferred_ele...]
  transfers between devices with their start and end apart: 45 -> 45, of which waited for: 45 -> 45; matrix products, arithmetic and copies ran while one was open for 5% -> 7% of each run, Pallas kernels for 0% -> 0%
where the time goes in v8:
time: 1150 us; the launch traced here: 1140 us
  waiting for transfers between devices  528 us (46%)
  starting transfers between devices  210 us (18%)
  local copies, waits for them, and re-layouts  186 us (16%)
  other arithmetic  108 us (9%)
  matrix products  84.2 us (7%)
  between operations  14.4 us (1%)
    ppermute x44, waiting for transfers between devices, passed_along(): lax.ppermute(value, axis, [(source, source + steps) for source in range(i...  440 us
    ppermute x44, starting transfers between devices, passed_along(): lax.ppermute(value, axis, [(source, source + steps) for source in range(i...  210 us
    reduce_scatter x1, waiting for transfers between devices, shards(): share = lax.psum_scatter(both, 'dp', scatter_dimension=3, tiled=True)  87.9 us
    dynamic_update_slice x66, local copies, waits for them, and re-layouts, put_row(): lax.dynamic_update_slice_in_dim(buffer, piece.astype(buffer.dtype), slot_...  74.4 us
    conv_general_dilated x16, matrix products, conv_apply(): lax.conv_general_dilated(activations, weight, window_strides=(1, 1), padd...  60.6 us
    dynamic_update_slice x22, other arithmetic, put_row(): lax.dynamic_update_slice_in_dim(buffer, piece.astype(buffer.dtype), slot_...  31.9 us
    conv_general_dilated x2, matrix products, conv_weight_grad(): lax.conv_general_dilated(activations, cotangent.astype(jnp.bfloat16), win...  23.6 us
  transfers between devices with their start and end apart: 45, of which 45 were waited for; matrix products, arithmetic and copies ran while one was open for 7% of the time, Pallas kernels for 0%

profile of v8, /device:TPU:0, one launch (start us, length us, event | category | flops | bytes accessed | tf_op | source)
XLA Modules:
  0.0 1135.7 jit_solution(11333453277527650642)
XLA Ops:
  37.0 174.1 %while.80 = (s32[]{:T(128)}, f32[1,16,16,384]{3,1,2,0:T(8,128)S(1)}, f32[6,16,16,384]{3,1,2,0:T(8,128)S(1)}, f32[6,16,16,384]{3,1,2,0:T(8,128)}, s32[]{:T(128)},...) while((s32[]{:T(128)}, ...), condition=%wide.region_8.9_spmd, body=%wide.region_0.8_spmd.sunk | while | flops 979749568 | bytes 12841028 | solution.py:142
  158.7 12.3 %collective-permute-start = (f32[1,16,16,384]{3,1,2,0:T(8,128)S(1)}, f32[1,16,16,384]{3,1,2,0:T(8,128)S(1)}, u32[]{:S(2)}, u32[]{:S(2)}) collective-permute-start(f32[1,16,16,384]{3,1,2,0:T(8,128)S(1)} %get-tuple-element.1978), channel_id=1, source_target_pairs={{0,16},{16,32},{32,48},{48,64},{64,80},{80,96},{96,112},{1,17},{17... | collective-permute-start | bytes 1179656 | tf_op jit(solution)/shard_map/while/body/eval_jaxpr/ppermute | solution.py:14
  191.8 14.0 %collective-permute-start = (f32[1,16,16,384]{3,1,2,0:T(8,128)S(1)}, f32[1,16,16,384]{3,1,2,0:T(8,128)S(1)}, u32[]{:S(2)}, u32[]{:S(2)}) collective-permute-start(f32[1,16,16,384]{3,1,2,0:T(8,128)S(1)} %get-tuple-element.1978), channel_id=1, source_target_pairs={{0,16},{16,32},{32,48},{48,64},{64,80},{80,96},{96,112},{1,17},{17... | collective-permute-start | bytes 1179656 | tf_op jit(solution)/shard_map/while/body/eval_jaxpr/ppermute | solution.py:14
  214.6 234.1 %while.81 = (s32[]{:T(128)}, f32[1,16,16,384]{3,1,2,0:T(8,128)S(1)}, f32[6,16,16,384]{3,1,2,0:T(8,128)}, f32[6,16,16,384]{3,1,2,0:T(8,128)}, s32[]{:T(128)}, /*i...) while((s32[]{:T(128)}, ...), condition=%wide.region_17.18_spmd, body=%wide.region_9.17_spmd.sunk | while | flops 1959351552 | bytes 20765760 | solution.py:163
  218.8 12.8 %collective-permute-done.1 = f32[1,16,16,384]{3,1,2,0:T(8,128)S(1)} collective-permute-done((f32[1,16,16,384]{3,1,2,0:T(8,128)S(1)}, f32[1,16,16,384]{3,1,2,0:T(8,128)S(1)}, u32[]{:S(2)}, u32[]{:S(2)}) %collective-permute-start.1) | collective-permute-done | bytes 393248 | tf_op jit(solution)/shard_map/while/body/eval_jaxpr/ppermute | solution.py:14
  235.6 14.2 %collective-permute-done.1 = f32[1,16,16,384]{3,1,2,0:T(8,128)S(1)} collective-permute-done((f32[1,16,16,384]{3,1,2,0:T(8,128)S(1)}, f32[1,16,16,384]{3,1,2,0:T(8,128)S(1)}, u32[]{:S(2)}, u32[]{:S(2)}) %collective-permute-start.1) | collective-permute-done | bytes 393248 | tf_op jit(solution)/shard_map/while/body/eval_jaxpr/ppermute | solution.py:14
  253.9 15.3 %collective-permute-done.1 = f32[1,16,16,384]{3,1,2,0:T(8,128)S(1)} collective-permute-done((f32[1,16,16,384]{3,1,2,0:T(8,128)S(1)}, f32[1,16,16,384]{3,1,2,0:T(8,128)S(1)}, u32[]{:S(2)}, u32[]{:S(2)}) %collective-permute-start.1) | collective-permute-done | bytes 393248 | tf_op jit(solution)/shard_map/while/body/eval_jaxpr/ppermute | solution.py:14
  273.3 17.7 %collective-permute-done.1 = f32[1,16,16,384]{3,1,2,0:T(8,128)S(1)} collective-permute-done((f32[1,16,16,384]{3,1,2,0:T(8,128)S(1)}, f32[1,16,16,384]{3,1,2,0:T(8,128)S(1)}, u32[]{:S(2)}, u32[]{:S(2)}) %collective-permute-start.1) | collective-permute-done | bytes 393248 | tf_op jit(solution)/shard_map/while/body/eval_jaxpr/ppermute | solution.py:14
  295.1 14.9 %collective-permute-done.1 = f32[1,16,16,384]{3,1,2,0:T(8,128)S(1)} collective-permute-done((f32[1,16,16,384]{3,1,2,0:T(8,128)S(1)}, f32[1,16,16,384]{3,1,2,0:T(8,128)S(1)}, u32[]{:S(2)}, u32[]{:S(2)}) %collective-permute-start.1) | collective-permute-done | bytes 393248 | tf_op jit(solution)/shard_map/while/body/eval_jaxpr/ppermute | solution.py:14
  325.8 32.2 %collective-permute-done.1 = f32[1,16,16,384]{3,1,2,0:T(8,128)S(1)} collective-permute-done((f32[1,16,16,384]{3,1,2,0:T(8,128)S(1)}, f32[1,16,16,384]{3,1,2,0:T(8,128)S(1)}, u32[]{:S(2)}, u32[]{:S(2)}) %collective-permute-start.1) | collective-permute-done | bytes 393248 | tf_op jit(solution)/shard_map/while/body/eval_jaxpr/ppermute | solution.py:14
  369.3 11.8 %collective-permute-done.1 = f32[1,16,16,384]{3,1,2,0:T(8,128)S(1)} collective-permute-done((f32[1,16,16,384]{3,1,2,0:T(8,128)S(1)}, f32[1,16,16,384]{3,1,2,0:T(8,128)S(1)}, u32[]{:S(2)}, u32[]{:S(2)}) %collective-permute-start.1) | collective-permute-done | bytes 393248 | tf_op jit(solution)/shard_map/while/body/eval_jaxpr/ppermute | solution.py:14
  392.4 13.0 %collective-permute-done.1 = f32[1,16,16,384]{3,1,2,0:T(8,128)S(1)} collective-permute-done((f32[1,16,16,384]{3,1,2,0:T(8,128)S(1)}, f32[1,16,16,384]{3,1,2,0:T(8,128)S(1)}, u32[]{:S(2)}, u32[]{:S(2)}) %collective-permute-start.1) | collective-permute-done | bytes 393248 | tf_op jit(solution)/shard_map/while/body/eval_jaxpr/ppermute | solution.py:14
  416.6 13.3 %collective-permute-done.1 = f32[1,16,16,384]{3,1,2,0:T(8,128)S(1)} collective-permute-done((f32[1,16,16,384]{3,1,2,0:T(8,128)S(1)}, f32[1,16,16,384]{3,1,2,0:T(8,128)S(1)}, u32[]{:S(2)}, u32[]{:S(2)}) %collective-permute-start.1) | collective-permute-done | bytes 393248 | tf_op jit(solution)/shard_map/while/body/eval_jaxpr/ppermute | solution.py:14
  458.6 250.7 %while.82 = (s32[]{:T(128)}, f32[1,16,16,384]{3,1,2,0:T(8,128)S(1)}, f32[6,16,16,384]{3,1,2,0:T(8,128)}, f32[6,16,16,384]{3,1,2,0:T(8,128)}, bf16[6,16,16,768]{3...) while((s32[]{:T(128)}, ...), condition=%wide.region_30.31_spmd, body=%wide.region_18.30_spmd.sunk | while | flops 1966970368 | bytes 30546140 | solution.py:206
  562.8 15.2 %collective-permute-start.2 = (f32[1,16,16,384]{3,1,2,0:T(8,128)S(1)}, f32[1,16,16,384]{3,1,2,0:T(8,128)S(1)}, u32[]{:S(2)}, u32[]{:S(2)}) collective-permute-start(f32[1,16,16,384]{3,1,2,0:T(8,128)S(1)} %get-tuple-element.1753), channel_id=1, source_target_pairs={{0,16},{16,32},{32,48},{48,64},{64,80},{80,96},{96,112},{1,17},{17... | collective-permute-start | bytes 1179656 | tf_op jit(solution)/shard_map/while/body/eval_jaxpr/ppermute | solution.py:14
  599.1 14.1 %collective-permute-start.2 = (f32[1,16,16,384]{3,1,2,0:T(8,128)S(1)}, f32[1,16,16,384]{3,1,2,0:T(8,128)S(1)}, u32[]{:S(2)}, u32[]{:S(2)}) collective-permute-start(f32[1,16,16,384]{3,1,2,0:T(8,128)S(1)} %get-tuple-element.1753), channel_id=1, source_target_pairs={{0,16},{16,32},{32,48},{48,64},{64,80},{80,96},{96,112},{1,17},{17... | collective-permute-start | bytes 1179656 | tf_op jit(solution)/shard_map/while/body/eval_jaxpr/ppermute | solution.py:14
  634.4 18.8 %collective-permute-start.2 = (f32[1,16,16,384]{3,1,2,0:T(8,128)S(1)}, f32[1,16,16,384]{3,1,2,0:T(8,128)S(1)}, u32[]{:S(2)}, u32[]{:S(2)}) collective-permute-start(f32[1,16,16,384]{3,1,2,0:T(8,128)S(1)} %get-tuple-element.1753), channel_id=1, source_target_pairs={{0,16},{16,32},{32,48},{48,64},{64,80},{80,96},{96,112},{1,17},{17... | collective-permute-start | bytes 1179656 | tf_op jit(solution)/shard_map/while/body/eval_jaxpr/ppermute | solution.py:14
  677.9 26.2 %collective-permute-start.2 = (f32[1,16,16,384]{3,1,2,0:T(8,128)S(1)}, f32[1,16,16,384]{3,1,2,0:T(8,128)S(1)}, u32[]{:S(2)}, u32[]{:S(2)}) collective-permute-start(f32[1,16,16,384]{3,1,2,0:T(8,128)S(1)} %get-tuple-element.1753), channel_id=1, source_target_pairs={{0,16},{16,32},{32,48},{48,64},{64,80},{80,96},{96,112},{1,17},{17... | collective-permute-start | bytes 1179656 | tf_op jit(solution)/shard_map/while/body/eval_jaxpr/ppermute | solution.py:14
  711.6 288.5 %while.83 = (s32[]{:T(128)}, f32[1,16,16,384]{3,1,2,0:T(8,128)S(1)}, bf16[6,16,16,384]{3,1,2,0:T(8,128)(2,1)}, bf16[6,16,16,384]{3,1,2,0:T(8,128)(2,1)}, s32[]{:...) while((s32[]{:T(128)}, ...), condition=%wide.region_43.44_spmd, body=%wide.region_31.0_spmd.sunk | while | flops 982010688 | bytes 27228124 | solution.py:244
  796.2 14.3 %collective-permute-done.3 = f32[1,16,16,384]{3,1,2,0:T(8,128)S(1)} collective-permute-done((f32[1,16,16,384]{3,1,2,0:T(8,128)}, f32[1,16,16,384]{3,1,2,0:T(8,128)S(1)}, u32[]{:S(2)}, u32[]{:S(2)}) %collective-permute-start.3) | collective-permute-done | bytes 393248 | tf_op jit(solution)/shard_map/while/body/eval_jaxpr/ppermute | solution.py:14
  815.5 85.1 %collective-permute-done.3 = f32[1,16,16,384]{3,1,2,0:T(8,128)S(1)} collective-permute-done((f32[1,16,16,384]{3,1,2,0:T(8,128)}, f32[1,16,16,384]{3,1,2,0:T(8,128)S(1)}, u32[]{:S(2)}, u32[]{:S(2)}) %collective-permute-start.3) | collective-permute-done | bytes 393248 | tf_op jit(solution)/shard_map/while/body/eval_jaxpr/ppermute | solution.py:14
  939.6 15.7 %collective-permute-done.3 = f32[1,16,16,384]{3,1,2,0:T(8,128)S(1)} collective-permute-done((f32[1,16,16,384]{3,1,2,0:T(8,128)}, f32[1,16,16,384]{3,1,2,0:T(8,128)S(1)}, u32[]{:S(2)}, u32[]{:S(2)}) %collective-permute-start.3) | collective-permute-done | bytes 393248 | tf_op jit(solution)/shard_map/while/body/eval_jaxpr/ppermute | solution.py:14
  1014.0 14.7 %fusion.59 = f32[3,3,768,384]{3,2,1,0:T(8,128)S(1)} fusion(bf16[6,16,16,768]{3,0,2,1:T(8,128)(2,1)S(1)} %copy.35, bf16[6,16,16,384]{3,0,2,1:T(8,128)(2,1)S(1)} %copy.36), kind=kOutput, calls=%fused_computation.133 | convolution fusion | flops 4992270336 | bytes 12976128 | tf_op jit(solution)/shard_map/conv_general_dilated | solution.py:54
  1037.1 87.9 %reduce-scatter.2.cloned.1.call-done = f32[1,3,3,72,384]{4,3,2,1,0:T(8,128)} async-done(((f32[1,3,3,1152,384]{4,3,2,1,0:T(8,128)}), f32[1,3,3,72,384]{4,3,2,1,0:T(8,128)}) %reduce-scatter.2.cloned.1.call-update) | async-done | bytes 995344 | tf_op jit(solution)/shard_map/reduce_scatter | solution.py:261
  (920 shorter events, 812.6 us)
Async XLA Ops:
  7.2 1117.8 %reduce-scatter.2.cloned.1.call-start = ((), (), s32[]{:S(2)}) async-start(), calls=%async_computation.1 | async-start | bytes 16920576 | tf_op jit(solution)/shard_map/reduce_scatter | solution.py:261
  105.5 15.2 %collective-permute-start = (f32[1,16,16,384]{3,1,2,0:T(8,128)S(1)}, f32[1,16,16,384]{3,1,2,0:T(8,128)S(1)}, u32[]{:S(2)}, u32[]{:S(2)}) collective-permute-start(f32[1,16,16,384]{3,1,2,0:T(8,128)S(1)} %get-tuple-element.1978), channel_id=1, source_target_pairs={{0,16},{16,32},{32,48},{48,64},{64,80},{80,96},{96,112},{1,17},{17... | collective-permute-start | bytes 1179656 | tf_op jit(solution)/shard_map/while/body/eval_jaxpr/ppermute | solution.py:14
  132.6 14.2 %collective-permute-start = (f32[1,16,16,384]{3,1,2,0:T(8,128)S(1)}, f32[1,16,16,384]{3,1,2,0:T(8,128)S(1)}, u32[]{:S(2)}, u32[]{:S(2)}) collective-permute-start(f32[1,16,16,384]{3,1,2,0:T(8,128)S(1)} %get-tuple-element.1978), channel_id=1, source_target_pairs={{0,16},{16,32},{32,48},{48,64},{64,80},{80,96},{96,112},{1,17},{17... | collective-permute-start | bytes 1179656 | tf_op jit(solution)/shard_map/while/body/eval_jaxpr/ppermute | solution.py:14
  158.7 17.5 %collective-permute-start = (f32[1,16,16,384]{3,1,2,0:T(8,128)S(1)}, f32[1,16,16,384]{3,1,2,0:T(8,128)S(1)}, u32[]{:S(2)}, u32[]{:S(2)}) collective-permute-start(f32[1,16,16,384]{3,1,2,0:T(8,128)S(1)} %get-tuple-element.1978), channel_id=1, source_target_pairs={{0,16},{16,32},{32,48},{48,64},{64,80},{80,96},{96,112},{1,17},{17... | collective-permute-start | bytes 1179656 | tf_op jit(solution)/shard_map/while/body/eval_jaxpr/ppermute | solution.py:14
  191.8 19.3 %collective-permute-start = (f32[1,16,16,384]{3,1,2,0:T(8,128)S(1)}, f32[1,16,16,384]{3,1,2,0:T(8,128)S(1)}, u32[]{:S(2)}, u32[]{:S(2)}) collective-permute-start(f32[1,16,16,384]{3,1,2,0:T(8,128)S(1)} %get-tuple-element.1978), channel_id=1, source_target_pairs={{0,16},{16,32},{32,48},{48,64},{64,80},{80,96},{96,112},{1,17},{17... | collective-permute-start | bytes 1179656 | tf_op jit(solution)/shard_map/while/body/eval_jaxpr/ppermute | solution.py:14
  216.7 14.9 %collective-permute-start.1 = (f32[1,16,16,384]{3,1,2,0:T(8,128)S(1)}, f32[1,16,16,384]{3,1,2,0:T(8,128)S(1)}, u32[]{:S(2)}, u32[]{:S(2)}) collective-permute-start(f32[1,16,16,384]{3,1,2,0:T(8,128)S(1)} %get-tuple-element.1979), channel_id=1, source_target_pairs={{16,0},{32,16},{48,32},{64,48},{80,64},{96,80},{112,96},{17,1},{33... | collective-permute-start | bytes 1179656 | tf_op jit(solution)/shard_map/while/body/eval_jaxpr/ppermute | solution.py:14
  233.5 16.3 %collective-permute-start.1 = (f32[1,16,16,384]{3,1,2,0:T(8,128)S(1)}, f32[1,16,16,384]{3,1,2,0:T(8,128)S(1)}, u32[]{:S(2)}, u32[]{:S(2)}) collective-permute-start(f32[1,16,16,384]{3,1,2,0:T(8,128)S(1)} %get-tuple-element.1979), channel_id=1, source_target_pairs={{16,0},{32,16},{48,32},{64,48},{80,64},{96,80},{112,96},{17,1},{33... | collective-permute-start | bytes 1179656 | tf_op jit(solution)/shard_map/while/body/eval_jaxpr/ppermute | solution.py:14
  251.8 17.4 %collective-permute-start.1 = (f32[1,16,16,384]{3,1,2,0:T(8,128)S(1)}, f32[1,16,16,384]{3,1,2,0:T(8,128)S(1)}, u32[]{:S(2)}, u32[]{:S(2)}) collective-permute-start(f32[1,16,16,384]{3,1,2,0:T(8,128)S(1)} %get-tuple-element.1979), channel_id=1, source_target_pairs={{16,0},{32,16},{48,32},{64,48},{80,64},{96,80},{112,96},{17,1},{33... | collective-permute-start | bytes 1179656 | tf_op jit(solution)/shard_map/while/body/eval_jaxpr/ppermute | solution.py:14
  271.2 19.8 %collective-permute-start.1 = (f32[1,16,16,384]{3,1,2,0:T(8,128)S(1)}, f32[1,16,16,384]{3,1,2,0:T(8,128)S(1)}, u32[]{:S(2)}, u32[]{:S(2)}) collective-permute-start(f32[1,16,16,384]{3,1,2,0:T(8,128)S(1)} %get-tuple-element.1979), channel_id=1, source_target_pairs={{16,0},{32,16},{48,32},{64,48},{80,64},{96,80},{112,96},{17,1},{33... | collective-permute-start | bytes 1179656 | tf_op jit(solution)/shard_map/while/body/eval_jaxpr/ppermute | solution.py:14
  293.0 17.0 %collective-permute-start.1 = (f32[1,16,16,384]{3,1,2,0:T(8,128)S(1)}, f32[1,16,16,384]{3,1,2,0:T(8,128)S(1)}, u32[]{:S(2)}, u32[]{:S(2)}) collective-permute-start(f32[1,16,16,384]{3,1,2,0:T(8,128)S(1)} %get-tuple-element.1979), channel_id=1, source_target_pairs={{16,0},{32,16},{48,32},{64,48},{80,64},{96,80},{112,96},{17,1},{33... | collective-permute-start | bytes 1179656 | tf_op jit(solution)/shard_map/while/body/eval_jaxpr/ppermute | solution.py:14
  323.7 34.3 %collective-permute-start.1 = (f32[1,16,16,384]{3,1,2,0:T(8,128)S(1)}, f32[1,16,16,384]{3,1,2,0:T(8,128)S(1)}, u32[]{:S(2)}, u32[]{:S(2)}) collective-permute-start(f32[1,16,16,384]{3,1,2,0:T(8,128)S(1)} %get-tuple-element.1979), channel_id=1, source_target_pairs={{16,0},{32,16},{48,32},{64,48},{80,64},{96,80},{112,96},{17,1},{33... | collective-permute-start | bytes 1179656 | tf_op jit(solution)/shard_map/while/body/eval_jaxpr/ppermute | solution.py:14
  367.2 13.9 %collective-permute-start.1 = (f32[1,16,16,384]{3,1,2,0:T(8,128)S(1)}, f32[1,16,16,384]{3,1,2,0:T(8,128)S(1)}, u32[]{:S(2)}, u32[]{:S(2)}) collective-permute-start(f32[1,16,16,384]{3,1,2,0:T(8,128)S(1)} %get-tuple-element.1979), channel_id=1, source_target_pairs={{16,0},{32,16},{48,32},{64,48},{80,64},{96,80},{112,96},{17,1},{33... | collective-permute-start | bytes 1179656 | tf_op jit(solution)/shard_map/while/body/eval_jaxpr/ppermute | solution.py:14
  390.3 15.1 %collective-permute-start.1 = (f32[1,16,16,384]{3,1,2,0:T(8,128)S(1)}, f32[1,16,16,384]{3,1,2,0:T(8,128)S(1)}, u32[]{:S(2)}, u32[]{:S(2)}) collective-permute-start(f32[1,16,16,384]{3,1,2,0:T(8,128)S(1)} %get-tuple-element.1979), channel_id=1, source_target_pairs={{16,0},{32,16},{48,32},{64,48},{80,64},{96,80},{112,96},{17,1},{33... | collective-permute-start | bytes 1179656 | tf_op jit(solution)/shard_map/while/body/eval_jaxpr/ppermute | solution.py:14
  414.5 15.3 %collective-permute-start.1 = (f32[1,16,16,384]{3,1,2,0:T(8,128)S(1)}, f32[1,16,16,384]{3,1,2,0:T(8,128)S(1)}, u32[]{:S(2)}, u32[]{:S(2)}) collective-permute-start(f32[1,16,16,384]{3,1,2,0:T(8,128)S(1)} %get-tuple-element.1979), channel_id=1, source_target_pairs={{16,0},{32,16},{48,32},{64,48},{80,64},{96,80},{112,96},{17,1},{33... | collective-permute-start | bytes 1179656 | tf_op jit(solution)/shard_map/while/body/eval_jaxpr/ppermute | solution.py:14
  562.8 20.5 %collective-permute-start.2 = (f32[1,16,16,384]{3,1,2,0:T(8,128)S(1)}, f32[1,16,16,384]{3,1,2,0:T(8,128)S(1)}, u32[]{:S(2)}, u32[]{:S(2)}) collective-permute-start(f32[1,16,16,384]{3,1,2,0:T(8,128)S(1)} %get-tuple-element.1753), channel_id=1, source_target_pairs={{0,16},{16,32},{32,48},{48,64},{64,80},{80,96},{96,112},{1,17},{17... | collective-permute-start | bytes 1179656 | tf_op jit(solution)/shard_map/while/body/eval_jaxpr/ppermute | solution.py:14
  599.1 19.4 %collective-permute-start.2 = (f32[1,16,16,384]{3,1,2,0:T(8,128)S(1)}, f32[1,16,16,384]{3,1,2,0:T(8,128)S(1)}, u32[]{:S(2)}, u32[]{:S(2)}) collective-permute-start(f32[1,16,16,384]{3,1,2,0:T(8,128)S(1)} %get-tuple-element.1753), channel_id=1, source_target_pairs={{0,16},{16,32},{32,48},{48,64},{64,80},{80,96},{96,112},{1,17},{17... | collective-permute-start | bytes 1179656 | tf_op jit(solution)/shard_map/while/body/eval_jaxpr/ppermute | solution.py:14
  634.4 24.1 %collective-permute-start.2 = (f32[1,16,16,384]{3,1,2,0:T(8,128)S(1)}, f32[1,16,16,384]{3,1,2,0:T(8,128)S(1)}, u32[]{:S(2)}, u32[]{:S(2)}) collective-permute-start(f32[1,16,16,384]{3,1,2,0:T(8,128)S(1)} %get-tuple-element.1753), channel_id=1, source_target_pairs={{0,16},{16,32},{32,48},{48,64},{64,80},{80,96},{96,112},{1,17},{17... | collective-permute-start | bytes 1179656 | tf_op jit(solution)/shard_map/while/body/eval_jaxpr/ppermute | solution.py:14
  677.9 31.4 %collective-permute-start.2 = (f32[1,16,16,384]{3,1,2,0:T(8,128)S(1)}, f32[1,16,16,384]{3,1,2,0:T(8,128)S(1)}, u32[]{:S(2)}, u32[]{:S(2)}) collective-permute-start(f32[1,16,16,384]{3,1,2,0:T(8,128)S(1)} %get-tuple-element.1753), channel_id=1, source_target_pairs={{0,16},{16,32},{32,48},{48,64},{64,80},{80,96},{96,112},{1,17},{17... | collective-permute-start | bytes 1179656 | tf_op jit(solution)/shard_map/while/body/eval_jaxpr/ppermute | solution.py:14
  713.6 14.1 %collective-permute-start.3 = (f32[1,16,16,384]{3,1,2,0:T(8,128)}, f32[1,16,16,384]{3,1,2,0:T(8,128)S(1)}, u32[]{:S(2)}, u32[]{:S(2)}) collective-permute-start(f32[1,16,16,384]{3,1,2,0:T(8,128)} %get-tuple-element.1770), channel_id=1, source_target_pairs={{16,0},{32,16},{48,32},{64,48},{80,64},{96,80},{112,96},{17,1},{33... | collective-permute-start | bytes 1179656 | tf_op jit(solution)/shard_map/while/body/eval_jaxpr/ppermute | solution.py:14
  729.7 14.0 %collective-permute-start.3 = (f32[1,16,16,384]{3,1,2,0:T(8,128)}, f32[1,16,16,384]{3,1,2,0:T(8,128)S(1)}, u32[]{:S(2)}, u32[]{:S(2)}) collective-permute-start(f32[1,16,16,384]{3,1,2,0:T(8,128)} %get-tuple-element.1770), channel_id=1, source_target_pairs={{16,0},{32,16},{48,32},{64,48},{80,64},{96,80},{112,96},{17,1},{33... | collective-permute-start | bytes 1179656 | tf_op jit(solution)/shard_map/while/body/eval_jaxpr/ppermute | solution.py:14
  761.5 14.3 %collective-permute-start.3 = (f32[1,16,16,384]{3,1,2,0:T(8,128)}, f32[1,16,16,384]{3,1,2,0:T(8,128)S(1)}, u32[]{:S(2)}, u32[]{:S(2)}) collective-permute-start(f32[1,16,16,384]{3,1,2,0:T(8,128)} %get-tuple-element.1770), channel_id=1, source_target_pairs={{16,0},{32,16},{48,32},{64,48},{80,64},{96,80},{112,96},{17,1},{33... | collective-permute-start | bytes 1179656 | tf_op jit(solution)/shard_map/while/body/eval_jaxpr/ppermute | solution.py:14
  793.2 17.3 %collective-permute-start.3 = (f32[1,16,16,384]{3,1,2,0:T(8,128)}, f32[1,16,16,384]{3,1,2,0:T(8,128)S(1)}, u32[]{:S(2)}, u32[]{:S(2)}) collective-permute-start(f32[1,16,16,384]{3,1,2,0:T(8,128)} %get-tuple-element.1770), channel_id=1, source_target_pairs={{16,0},{32,16},{48,32},{64,48},{80,64},{96,80},{112,96},{17,1},{33... | collective-permute-start | bytes 1179656 | tf_op jit(solution)/shard_map/while/body/eval_jaxpr/ppermute | solution.py:14
  812.5 88.1 %collective-permute-start.3 = (f32[1,16,16,384]{3,1,2,0:T(8,128)}, f32[1,16,16,384]{3,1,2,0:T(8,128)S(1)}, u32[]{:S(2)}, u32[]{:S(2)}) collective-permute-start(f32[1,16,16,384]{3,1,2,0:T(8,128)} %get-tuple-element.1770), channel_id=1, source_target_pairs={{16,0},{32,16},{48,32},{64,48},{80,64},{96,80},{112,96},{17,1},{33... | collective-permute-start | bytes 1179656 | tf_op jit(solution)/shard_map/while/body/eval_jaxpr/ppermute | solution.py:14
  936.6 18.7 %collective-permute-start.3 = (f32[1,16,16,384]{3,1,2,0:T(8,128)}, f32[1,16,16,384]{3,1,2,0:T(8,128)S(1)}, u32[]{:S(2)}, u32[]{:S(2)}) collective-permute-start(f32[1,16,16,384]{3,1,2,0:T(8,128)} %get-tuple-element.1770), channel_id=1, source_target_pairs={{16,0},{32,16},{48,32},{64,48},{80,64},{96,80},{112,96},{17,1},{33... | collective-permute-start | bytes 1179656 | tf_op jit(solution)/shard_map/while/body/eval_jaxpr/ppermute | solution.py:14
  (69 other events, 360.8 us)
Sparse Core Ops, SparseCore 0:
  1037.2 87.7 reduce-scatter.1

commit v9 on v6

--- a/solution.py
+++ b/solution.py
@@ -178,13 +178,14 @@
         input_grad = pullback(conv_back(cotangent, weight))[0]
         return (input_grad, activated.astype(jnp.bfloat16), cotangent.astype(jnp.bfloat16))
 
+    top_grads = factor * (
+        outputs - jnp.pad(noise.astype(jnp.float32), ((1, 1), (0, 0), (0, 0), (0, 0)))
+    )
+
     def decoder_back_tick(tick_now, carried):
         incoming, skip_grads, up_grads, dec_acts, dec_cots = carried
         active, sample_at, slot_index = locate(tick_now, section_index)
-        top_grad = factor * (
-            pick_row(outputs, slot_index) - pick_row(noise, sample_at).astype(jnp.float32)
-        )
-        flowing = jnp.where(section_index == 0, top_grad, incoming)
+        flowing = jnp.where(section_index == 0, pick_row(top_grads, slot_index), incoming)
         joined = jnp.concatenate(
             [pick_row(dec_inputs, slot_index), pick_row(skips, slot_index)], axis=3
         )

time: 1120 us -> 1120 us (level)
  local copies, waits for them, and re-layouts: 163 us -> 175 us
    dynamic_update_slice x66, local copies, waits for them, and re-layouts: 54.4 us -> 65.8 us  [put_row(): lax.dynamic_update_slice_in_dim(buffer, piece.astype(buffer.dtype), slot_...]
  transfers between devices with their start and end apart: 45 -> 45, of which waited for: 45 -> 45; matrix products, arithmetic and copies ran while one was open for 5% -> 6% of each run, Pallas kernels for 0% -> 0%
where the time goes in v9:
time: 1120 us
  waiting for transfers between devices  539 us (48%)
  starting transfers between devices  207 us (18%)
  local copies, waits for them, and re-layouts  175 us (16%)
  other arithmetic  103 us (9%)
  matrix products  75.1 us (7%)
  between operations  14.3 us (1%)
    ppermute x44, waiting for transfers between devices, passed_along(): lax.ppermute(value, axis, [(source, source + steps) for source in range(i...  448 us
    ppermute x44, starting transfers between devices, passed_along(): lax.ppermute(value, axis, [(source, source + steps) for source in range(i...  207 us
    reduce_scatter x1, waiting for transfers between devices, shards(): share = lax.psum_scatter(both, 'dp', scatter_dimension=3, tiled=True)  91.1 us
    dynamic_update_slice x66, local copies, waits for them, and re-layouts, put_row(): lax.dynamic_update_slice_in_dim(buffer, piece.astype(buffer.dtype), slot_...  65.8 us
    conv_general_dilated x16, matrix products, conv_apply(): lax.conv_general_dilated(activations, weight, window_strides=(1, 1), padd...  60.5 us
    dynamic_update_slice x22, other arithmetic, put_row(): lax.dynamic_update_slice_in_dim(buffer, piece.astype(buffer.dtype), slot_...  31.9 us
    dynamic_slice x22, local copies, waits for them, and re-layouts, pick_row(): return lax.dynamic_slice_in_dim(buffer, slot_index, 1, 0)  22.5 us
  transfers between devices with their start and end apart: 45, of which 45 were waited for; matrix products, arithmetic and copies ran while one was open for 6% of the time, Pallas kernels for 0%

profile of v9, /device:TPU:0, one launch (start us, length us, event | category | flops | bytes accessed | tf_op | source)
XLA Modules:
  0.0 1119.2 jit_solution(9081128195313762524)
XLA Ops:
  37.0 174.1 %while.80 = (s32[]{:T(128)}, f32[1,16,16,384]{3,1,2,0:T(8,128)S(1)}, f32[6,16,16,384]{3,1,2,0:T(8,128)S(1)}, f32[6,16,16,384]{3,1,2,0:T(8,128)}, s32[]{:T(128)},...) while((s32[]{:T(128)}, ...), condition=%wide.region_8.9_spmd, body=%wide.region_0.8_spmd.sunk | while | flops 979749568 | bytes 12841028 | solution.py:151
  158.7 12.3 %collective-permute-start = (f32[1,16,16,384]{3,1,2,0:T(8,128)S(1)}, f32[1,16,16,384]{3,1,2,0:T(8,128)S(1)}, u32[]{:S(2)}, u32[]{:S(2)}) collective-permute-start(f32[1,16,16,384]{3,1,2,0:T(8,128)S(1)} %get-tuple-element.1978), channel_id=1, source_target_pairs={{0,16},{16,32},{32,48},{48,64},{64,80},{80,96},{96,112},{1,17},{17... | collective-permute-start | bytes 1179656 | tf_op jit(solution)/shard_map/while/body/eval_jaxpr/ppermute | solution.py:14
  191.8 14.0 %collective-permute-start = (f32[1,16,16,384]{3,1,2,0:T(8,128)S(1)}, f32[1,16,16,384]{3,1,2,0:T(8,128)S(1)}, u32[]{:S(2)}, u32[]{:S(2)}) collective-permute-start(f32[1,16,16,384]{3,1,2,0:T(8,128)S(1)} %get-tuple-element.1978), channel_id=1, source_target_pairs={{0,16},{16,32},{32,48},{48,64},{64,80},{80,96},{96,112},{1,17},{17... | collective-permute-start | bytes 1179656 | tf_op jit(solution)/shard_map/while/body/eval_jaxpr/ppermute | solution.py:14
  214.6 237.2 %while.81 = (s32[]{:T(128)}, f32[1,16,16,384]{3,1,2,0:T(8,128)S(1)}, f32[6,16,16,384]{3,1,2,0:T(8,128)}, f32[6,16,16,384]{3,1,2,0:T(8,128)}, s32[]{:T(128)}, /*i...) while((s32[]{:T(128)}, ...), condition=%wide.region_17.18_spmd, body=%wide.region_9.17_spmd.sunk | while | flops 1959351552 | bytes 20765760 | solution.py:172
  218.8 12.8 %collective-permute-done.1 = f32[1,16,16,384]{3,1,2,0:T(8,128)S(1)} collective-permute-done((f32[1,16,16,384]{3,1,2,0:T(8,128)S(1)}, f32[1,16,16,384]{3,1,2,0:T(8,128)S(1)}, u32[]{:S(2)}, u32[]{:S(2)}) %collective-permute-start.1) | collective-permute-done | bytes 393248 | tf_op jit(solution)/shard_map/while/body/eval_jaxpr/ppermute | solution.py:14
  235.6 14.2 %collective-permute-done.1 = f32[1,16,16,384]{3,1,2,0:T(8,128)S(1)} collective-permute-done((f32[1,16,16,384]{3,1,2,0:T(8,128)S(1)}, f32[1,16,16,384]{3,1,2,0:T(8,128)S(1)}, u32[]{:S(2)}, u32[]{:S(2)}) %collective-permute-start.1) | collective-permute-done | bytes 393248 | tf_op jit(solution)/shard_map/while/body/eval_jaxpr/ppermute | solution.py:14
  253.9 15.3 %collective-permute-done.1 = f32[1,16,16,384]{3,1,2,0:T(8,128)S(1)} collective-permute-done((f32[1,16,16,384]{3,1,2,0:T(8,128)S(1)}, f32[1,16,16,384]{3,1,2,0:T(8,128)S(1)}, u32[]{:S(2)}, u32[]{:S(2)}) %collective-permute-start.1) | collective-permute-done | bytes 393248 | tf_op jit(solution)/shard_map/while/body/eval_jaxpr/ppermute | solution.py:14
  273.3 17.7 %collective-permute-done.1 = f32[1,16,16,384]{3,1,2,0:T(8,128)S(1)} collective-permute-done((f32[1,16,16,384]{3,1,2,0:T(8,128)S(1)}, f32[1,16,16,384]{3,1,2,0:T(8,128)S(1)}, u32[]{:S(2)}, u32[]{:S(2)}) %collective-permute-start.1) | collective-permute-done | bytes 393248 | tf_op jit(solution)/shard_map/while/body/eval_jaxpr/ppermute | solution.py:14
  295.1 14.9 %collective-permute-done.1 = f32[1,16,16,384]{3,1,2,0:T(8,128)S(1)} collective-permute-done((f32[1,16,16,384]{3,1,2,0:T(8,128)S(1)}, f32[1,16,16,384]{3,1,2,0:T(8,128)S(1)}, u32[]{:S(2)}, u32[]{:S(2)}) %collective-permute-start.1) | collective-permute-done | bytes 393248 | tf_op jit(solution)/shard_map/while/body/eval_jaxpr/ppermute | solution.py:14
  325.8 34.3 %collective-permute-done.1 = f32[1,16,16,384]{3,1,2,0:T(8,128)S(1)} collective-permute-done((f32[1,16,16,384]{3,1,2,0:T(8,128)S(1)}, f32[1,16,16,384]{3,1,2,0:T(8,128)S(1)}, u32[]{:S(2)}, u32[]{:S(2)}) %collective-permute-start.1) | collective-permute-done | bytes 393248 | tf_op jit(solution)/shard_map/while/body/eval_jaxpr/ppermute | solution.py:14
  394.8 12.8 %collective-permute-done.1 = f32[1,16,16,384]{3,1,2,0:T(8,128)S(1)} collective-permute-done((f32[1,16,16,384]{3,1,2,0:T(8,128)S(1)}, f32[1,16,16,384]{3,1,2,0:T(8,128)S(1)}, u32[]{:S(2)}, u32[]{:S(2)}) %collective-permute-start.1) | collective-permute-done | bytes 393248 | tf_op jit(solution)/shard_map/while/body/eval_jaxpr/ppermute | solution.py:14
  419.2 13.5 %collective-permute-done.1 = f32[1,16,16,384]{3,1,2,0:T(8,128)S(1)} collective-permute-done((f32[1,16,16,384]{3,1,2,0:T(8,128)S(1)}, f32[1,16,16,384]{3,1,2,0:T(8,128)S(1)}, u32[]{:S(2)}, u32[]{:S(2)}) %collective-permute-start.1) | collective-permute-done | bytes 393248 | tf_op jit(solution)/shard_map/while/body/eval_jaxpr/ppermute | solution.py:14
  461.7 244.7 %while.82 = (s32[]{:T(128)}, f32[1,16,16,384]{3,1,2,0:T(8,128)S(1)}, f32[6,16,16,384]{3,1,2,0:T(8,128)}, f32[6,16,16,384]{3,1,2,0:T(8,128)}, bf16[6,16,16,768]{3...) while((s32[]{:T(128)}, ...), condition=%wide.region_30.31_spmd, body=%wide.region_18.30_spmd.sunk | while | flops 1966970368 | bytes 30546264 | solution.py:215
  562.9 15.3 %collective-permute-start.2 = (f32[1,16,16,384]{3,1,2,0:T(8,128)S(1)}, f32[1,16,16,384]{3,1,2,0:T(8,128)S(1)}, u32[]{:S(2)}, u32[]{:S(2)}) collective-permute-start(f32[1,16,16,384]{3,1,2,0:T(8,128)S(1)} %get-tuple-element.1753), channel_id=1, source_target_pairs={{0,16},{16,32},{32,48},{48,64},{64,80},{80,96},{96,112},{1,17},{17... | collective-permute-start | bytes 1179656 | tf_op jit(solution)/shard_map/while/body/eval_jaxpr/ppermute | solution.py:14
  599.2 13.6 %collective-permute-start.2 = (f32[1,16,16,384]{3,1,2,0:T(8,128)S(1)}, f32[1,16,16,384]{3,1,2,0:T(8,128)S(1)}, u32[]{:S(2)}, u32[]{:S(2)}) collective-permute-start(f32[1,16,16,384]{3,1,2,0:T(8,128)S(1)} %get-tuple-element.1753), channel_id=1, source_target_pairs={{0,16},{16,32},{32,48},{48,64},{64,80},{80,96},{96,112},{1,17},{17... | collective-permute-start | bytes 1179656 | tf_op jit(solution)/shard_map/while/body/eval_jaxpr/ppermute | solution.py:14
  633.9 18.6 %collective-permute-start.2 = (f32[1,16,16,384]{3,1,2,0:T(8,128)S(1)}, f32[1,16,16,384]{3,1,2,0:T(8,128)S(1)}, u32[]{:S(2)}, u32[]{:S(2)}) collective-permute-start(f32[1,16,16,384]{3,1,2,0:T(8,128)S(1)} %get-tuple-element.1753), channel_id=1, source_target_pairs={{0,16},{16,32},{32,48},{48,64},{64,80},{80,96},{96,112},{1,17},{17... | collective-permute-start | bytes 1179656 | tf_op jit(solution)/shard_map/while/body/eval_jaxpr/ppermute | solution.py:14
  677.1 24.1 %collective-permute-start.2 = (f32[1,16,16,384]{3,1,2,0:T(8,128)S(1)}, f32[1,16,16,384]{3,1,2,0:T(8,128)S(1)}, u32[]{:S(2)}, u32[]{:S(2)}) collective-permute-start(f32[1,16,16,384]{3,1,2,0:T(8,128)S(1)} %get-tuple-element.1753), channel_id=1, source_target_pairs={{0,16},{16,32},{32,48},{48,64},{64,80},{80,96},{96,112},{1,17},{17... | collective-permute-start | bytes 1179656 | tf_op jit(solution)/shard_map/while/body/eval_jaxpr/ppermute | solution.py:14
  708.8 283.8 %while.83 = (s32[]{:T(128)}, f32[1,16,16,384]{3,1,2,0:T(8,128)S(1)}, bf16[6,16,16,384]{3,2,1,0:T(8,128)(2,1)}, bf16[6,16,16,384]{3,2,1,0:T(8,128)(2,1)}, s32[]{:...) while((s32[]{:T(128)}, ...), condition=%wide.region_43.44_spmd, body=%wide.region_31.43_spmd.sunk | while | flops 982010688 | bytes 27228124 | solution.py:253
  727.8 11.8 %collective-permute-done.3 = f32[1,16,16,384]{3,1,2,0:T(8,128)S(1)} collective-permute-done((f32[1,16,16,384]{3,1,2,0:T(8,128)}, f32[1,16,16,384]{3,1,2,0:T(8,128)S(1)}, u32[]{:S(2)}, u32[]{:S(2)}) %collective-permute-start.3) | collective-permute-done | bytes 393248 | tf_op jit(solution)/shard_map/while/body/eval_jaxpr/ppermute | solution.py:14
  758.5 13.3 %collective-permute-done.3 = f32[1,16,16,384]{3,1,2,0:T(8,128)S(1)} collective-permute-done((f32[1,16,16,384]{3,1,2,0:T(8,128)}, f32[1,16,16,384]{3,1,2,0:T(8,128)S(1)}, u32[]{:S(2)}, u32[]{:S(2)}) %collective-permute-start.3) | collective-permute-done | bytes 393248 | tf_op jit(solution)/shard_map/while/body/eval_jaxpr/ppermute | solution.py:14
  790.3 15.0 %collective-permute-done.3 = f32[1,16,16,384]{3,1,2,0:T(8,128)S(1)} collective-permute-done((f32[1,16,16,384]{3,1,2,0:T(8,128)}, f32[1,16,16,384]{3,1,2,0:T(8,128)S(1)}, u32[]{:S(2)}, u32[]{:S(2)}) %collective-permute-start.3) | collective-permute-done | bytes 393248 | tf_op jit(solution)/shard_map/while/body/eval_jaxpr/ppermute | solution.py:14
  808.8 87.3 %collective-permute-done.3 = f32[1,16,16,384]{3,1,2,0:T(8,128)S(1)} collective-permute-done((f32[1,16,16,384]{3,1,2,0:T(8,128)}, f32[1,16,16,384]{3,1,2,0:T(8,128)S(1)}, u32[]{:S(2)}, u32[]{:S(2)}) %collective-permute-start.3) | collective-permute-done | bytes 393248 | tf_op jit(solution)/shard_map/while/body/eval_jaxpr/ppermute | solution.py:14
  933.1 14.3 %collective-permute-done.3 = f32[1,16,16,384]{3,1,2,0:T(8,128)S(1)} collective-permute-done((f32[1,16,16,384]{3,1,2,0:T(8,128)}, f32[1,16,16,384]{3,1,2,0:T(8,128)S(1)}, u32[]{:S(2)}, u32[]{:S(2)}) %collective-permute-start.3) | collective-permute-done | bytes 393248 | tf_op jit(solution)/shard_map/while/body/eval_jaxpr/ppermute | solution.py:14
  1017.6 91.1 %reduce-scatter.2.cloned.1.call-done = f32[1,3,3,72,384]{4,3,2,1,0:T(8,128)} async-done(((f32[1,3,3,1152,384]{4,3,2,1,0:T(8,128)}), f32[1,3,3,72,384]{4,3,2,1,0:T(8,128)}) %reduce-scatter.2.cloned.1.call-update) | async-done | bytes 995344 | tf_op jit(solution)/shard_map/reduce_scatter | solution.py:270
  (944 shorter events, 788.3 us)
Async XLA Ops:
  7.2 1101.5 %reduce-scatter.2.cloned.1.call-start = ((), (), s32[]{:S(2)}) async-start(), calls=%async_computation.1 | async-start | bytes 16920576 | tf_op jit(solution)/shard_map/reduce_scatter | solution.py:270
  105.5 15.2 %collective-permute-start = (f32[1,16,16,384]{3,1,2,0:T(8,128)S(1)}, f32[1,16,16,384]{3,1,2,0:T(8,128)S(1)}, u32[]{:S(2)}, u32[]{:S(2)}) collective-permute-start(f32[1,16,16,384]{3,1,2,0:T(8,128)S(1)} %get-tuple-element.1978), channel_id=1, source_target_pairs={{0,16},{16,32},{32,48},{48,64},{64,80},{80,96},{96,112},{1,17},{17... | collective-permute-start | bytes 1179656 | tf_op jit(solution)/shard_map/while/body/eval_jaxpr/ppermute | solution.py:14
  132.6 14.2 %collective-permute-start = (f32[1,16,16,384]{3,1,2,0:T(8,128)S(1)}, f32[1,16,16,384]{3,1,2,0:T(8,128)S(1)}, u32[]{:S(2)}, u32[]{:S(2)}) collective-permute-start(f32[1,16,16,384]{3,1,2,0:T(8,128)S(1)} %get-tuple-element.1978), channel_id=1, source_target_pairs={{0,16},{16,32},{32,48},{48,64},{64,80},{80,96},{96,112},{1,17},{17... | collective-permute-start | bytes 1179656 | tf_op jit(solution)/shard_map/while/body/eval_jaxpr/ppermute | solution.py:14
  158.7 17.5 %collective-permute-start = (f32[1,16,16,384]{3,1,2,0:T(8,128)S(1)}, f32[1,16,16,384]{3,1,2,0:T(8,128)S(1)}, u32[]{:S(2)}, u32[]{:S(2)}) collective-permute-start(f32[1,16,16,384]{3,1,2,0:T(8,128)S(1)} %get-tuple-element.1978), channel_id=1, source_target_pairs={{0,16},{16,32},{32,48},{48,64},{64,80},{80,96},{96,112},{1,17},{17... | collective-permute-start | bytes 1179656 | tf_op jit(solution)/shard_map/while/body/eval_jaxpr/ppermute | solution.py:14
  191.8 19.3 %collective-permute-start = (f32[1,16,16,384]{3,1,2,0:T(8,128)S(1)}, f32[1,16,16,384]{3,1,2,0:T(8,128)S(1)}, u32[]{:S(2)}, u32[]{:S(2)}) collective-permute-start(f32[1,16,16,384]{3,1,2,0:T(8,128)S(1)} %get-tuple-element.1978), channel_id=1, source_target_pairs={{0,16},{16,32},{32,48},{48,64},{64,80},{80,96},{96,112},{1,17},{17... | collective-permute-start | bytes 1179656 | tf_op jit(solution)/shard_map/while/body/eval_jaxpr/ppermute | solution.py:14
  216.7 14.9 %collective-permute-start.1 = (f32[1,16,16,384]{3,1,2,0:T(8,128)S(1)}, f32[1,16,16,384]{3,1,2,0:T(8,128)S(1)}, u32[]{:S(2)}, u32[]{:S(2)}) collective-permute-start(f32[1,16,16,384]{3,1,2,0:T(8,128)S(1)} %get-tuple-element.1979), channel_id=1, source_target_pairs={{16,0},{32,16},{48,32},{64,48},{80,64},{96,80},{112,96},{17,1},{33... | collective-permute-start | bytes 1179656 | tf_op jit(solution)/shard_map/while/body/eval_jaxpr/ppermute | solution.py:14
  233.5 16.3 %collective-permute-start.1 = (f32[1,16,16,384]{3,1,2,0:T(8,128)S(1)}, f32[1,16,16,384]{3,1,2,0:T(8,128)S(1)}, u32[]{:S(2)}, u32[]{:S(2)}) collective-permute-start(f32[1,16,16,384]{3,1,2,0:T(8,128)S(1)} %get-tuple-element.1979), channel_id=1, source_target_pairs={{16,0},{32,16},{48,32},{64,48},{80,64},{96,80},{112,96},{17,1},{33... | collective-permute-start | bytes 1179656 | tf_op jit(solution)/shard_map/while/body/eval_jaxpr/ppermute | solution.py:14
  251.8 17.4 %collective-permute-start.1 = (f32[1,16,16,384]{3,1,2,0:T(8,128)S(1)}, f32[1,16,16,384]{3,1,2,0:T(8,128)S(1)}, u32[]{:S(2)}, u32[]{:S(2)}) collective-permute-start(f32[1,16,16,384]{3,1,2,0:T(8,128)S(1)} %get-tuple-element.1979), channel_id=1, source_target_pairs={{16,0},{32,16},{48,32},{64,48},{80,64},{96,80},{112,96},{17,1},{33... | collective-permute-start | bytes 1179656 | tf_op jit(solution)/shard_map/while/body/eval_jaxpr/ppermute | solution.py:14
  271.2 19.8 %collective-permute-start.1 = (f32[1,16,16,384]{3,1,2,0:T(8,128)S(1)}, f32[1,16,16,384]{3,1,2,0:T(8,128)S(1)}, u32[]{:S(2)}, u32[]{:S(2)}) collective-permute-start(f32[1,16,16,384]{3,1,2,0:T(8,128)S(1)} %get-tuple-element.1979), channel_id=1, source_target_pairs={{16,0},{32,16},{48,32},{64,48},{80,64},{96,80},{112,96},{17,1},{33... | collective-permute-start | bytes 1179656 | tf_op jit(solution)/shard_map/while/body/eval_jaxpr/ppermute | solution.py:14
  293.0 17.0 %collective-permute-start.1 = (f32[1,16,16,384]{3,1,2,0:T(8,128)S(1)}, f32[1,16,16,384]{3,1,2,0:T(8,128)S(1)}, u32[]{:S(2)}, u32[]{:S(2)}) collective-permute-start(f32[1,16,16,384]{3,1,2,0:T(8,128)S(1)} %get-tuple-element.1979), channel_id=1, source_target_pairs={{16,0},{32,16},{48,32},{64,48},{80,64},{96,80},{112,96},{17,1},{33... | collective-permute-start | bytes 1179656 | tf_op jit(solution)/shard_map/while/body/eval_jaxpr/ppermute | solution.py:14
  323.7 36.4 %collective-permute-start.1 = (f32[1,16,16,384]{3,1,2,0:T(8,128)S(1)}, f32[1,16,16,384]{3,1,2,0:T(8,128)S(1)}, u32[]{:S(2)}, u32[]{:S(2)}) collective-permute-start(f32[1,16,16,384]{3,1,2,0:T(8,128)S(1)} %get-tuple-element.1979), channel_id=1, source_target_pairs={{16,0},{32,16},{48,32},{64,48},{80,64},{96,80},{112,96},{17,1},{33... | collective-permute-start | bytes 1179656 | tf_op jit(solution)/shard_map/while/body/eval_jaxpr/ppermute | solution.py:14
  392.7 14.9 %collective-permute-start.1 = (f32[1,16,16,384]{3,1,2,0:T(8,128)S(1)}, f32[1,16,16,384]{3,1,2,0:T(8,128)S(1)}, u32[]{:S(2)}, u32[]{:S(2)}) collective-permute-start(f32[1,16,16,384]{3,1,2,0:T(8,128)S(1)} %get-tuple-element.1979), channel_id=1, source_target_pairs={{16,0},{32,16},{48,32},{64,48},{80,64},{96,80},{112,96},{17,1},{33... | collective-permute-start | bytes 1179656 | tf_op jit(solution)/shard_map/while/body/eval_jaxpr/ppermute | solution.py:14
  417.1 15.6 %collective-permute-start.1 = (f32[1,16,16,384]{3,1,2,0:T(8,128)S(1)}, f32[1,16,16,384]{3,1,2,0:T(8,128)S(1)}, u32[]{:S(2)}, u32[]{:S(2)}) collective-permute-start(f32[1,16,16,384]{3,1,2,0:T(8,128)S(1)} %get-tuple-element.1979), channel_id=1, source_target_pairs={{16,0},{32,16},{48,32},{64,48},{80,64},{96,80},{112,96},{17,1},{33... | collective-permute-start | bytes 1179656 | tf_op jit(solution)/shard_map/while/body/eval_jaxpr/ppermute | solution.py:14
  562.9 20.5 %collective-permute-start.2 = (f32[1,16,16,384]{3,1,2,0:T(8,128)S(1)}, f32[1,16,16,384]{3,1,2,0:T(8,128)S(1)}, u32[]{:S(2)}, u32[]{:S(2)}) collective-permute-start(f32[1,16,16,384]{3,1,2,0:T(8,128)S(1)} %get-tuple-element.1753), channel_id=1, source_target_pairs={{0,16},{16,32},{32,48},{48,64},{64,80},{80,96},{96,112},{1,17},{17... | collective-permute-start | bytes 1179656 | tf_op jit(solution)/shard_map/while/body/eval_jaxpr/ppermute | solution.py:14
  599.2 18.9 %collective-permute-start.2 = (f32[1,16,16,384]{3,1,2,0:T(8,128)S(1)}, f32[1,16,16,384]{3,1,2,0:T(8,128)S(1)}, u32[]{:S(2)}, u32[]{:S(2)}) collective-permute-start(f32[1,16,16,384]{3,1,2,0:T(8,128)S(1)} %get-tuple-element.1753), channel_id=1, source_target_pairs={{0,16},{16,32},{32,48},{48,64},{64,80},{80,96},{96,112},{1,17},{17... | collective-permute-start | bytes 1179656 | tf_op jit(solution)/shard_map/while/body/eval_jaxpr/ppermute | solution.py:14
  633.9 23.9 %collective-permute-start.2 = (f32[1,16,16,384]{3,1,2,0:T(8,128)S(1)}, f32[1,16,16,384]{3,1,2,0:T(8,128)S(1)}, u32[]{:S(2)}, u32[]{:S(2)}) collective-permute-start(f32[1,16,16,384]{3,1,2,0:T(8,128)S(1)} %get-tuple-element.1753), channel_id=1, source_target_pairs={{0,16},{16,32},{32,48},{48,64},{64,80},{80,96},{96,112},{1,17},{17... | collective-permute-start | bytes 1179656 | tf_op jit(solution)/shard_map/while/body/eval_jaxpr/ppermute | solution.py:14
  677.1 29.4 %collective-permute-start.2 = (f32[1,16,16,384]{3,1,2,0:T(8,128)S(1)}, f32[1,16,16,384]{3,1,2,0:T(8,128)S(1)}, u32[]{:S(2)}, u32[]{:S(2)}) collective-permute-start(f32[1,16,16,384]{3,1,2,0:T(8,128)S(1)} %get-tuple-element.1753), channel_id=1, source_target_pairs={{0,16},{16,32},{32,48},{48,64},{64,80},{80,96},{96,112},{1,17},{17... | collective-permute-start | bytes 1179656 | tf_op jit(solution)/shard_map/while/body/eval_jaxpr/ppermute | solution.py:14
  710.3 14.0 %collective-permute-start.3 = (f32[1,16,16,384]{3,1,2,0:T(8,128)}, f32[1,16,16,384]{3,1,2,0:T(8,128)S(1)}, u32[]{:S(2)}, u32[]{:S(2)}) collective-permute-start(f32[1,16,16,384]{3,1,2,0:T(8,128)} %get-tuple-element.1770), channel_id=1, source_target_pairs={{16,0},{32,16},{48,32},{64,48},{80,64},{96,80},{112,96},{17,1},{33... | collective-permute-start | bytes 1179656 | tf_op jit(solution)/shard_map/while/body/eval_jaxpr/ppermute | solution.py:14
  725.6 14.0 %collective-permute-start.3 = (f32[1,16,16,384]{3,1,2,0:T(8,128)}, f32[1,16,16,384]{3,1,2,0:T(8,128)S(1)}, u32[]{:S(2)}, u32[]{:S(2)}) collective-permute-start(f32[1,16,16,384]{3,1,2,0:T(8,128)} %get-tuple-element.1770), channel_id=1, source_target_pairs={{16,0},{32,16},{48,32},{64,48},{80,64},{96,80},{112,96},{17,1},{33... | collective-permute-start | bytes 1179656 | tf_op jit(solution)/shard_map/while/body/eval_jaxpr/ppermute | solution.py:14
  741.0 14.0 %collective-permute-start.3 = (f32[1,16,16,384]{3,1,2,0:T(8,128)}, f32[1,16,16,384]{3,1,2,0:T(8,128)S(1)}, u32[]{:S(2)}, u32[]{:S(2)}) collective-permute-start(f32[1,16,16,384]{3,1,2,0:T(8,128)} %get-tuple-element.1770), channel_id=1, source_target_pairs={{16,0},{32,16},{48,32},{64,48},{80,64},{96,80},{112,96},{17,1},{33... | collective-permute-start | bytes 1179656 | tf_op jit(solution)/shard_map/while/body/eval_jaxpr/ppermute | solution.py:14
  756.4 15.4 %collective-permute-start.3 = (f32[1,16,16,384]{3,1,2,0:T(8,128)}, f32[1,16,16,384]{3,1,2,0:T(8,128)S(1)}, u32[]{:S(2)}, u32[]{:S(2)}) collective-permute-start(f32[1,16,16,384]{3,1,2,0:T(8,128)} %get-tuple-element.1770), channel_id=1, source_target_pairs={{16,0},{32,16},{48,32},{64,48},{80,64},{96,80},{112,96},{17,1},{33... | collective-permute-start | bytes 1179656 | tf_op jit(solution)/shard_map/while/body/eval_jaxpr/ppermute | solution.py:14
  788.2 17.1 %collective-permute-start.3 = (f32[1,16,16,384]{3,1,2,0:T(8,128)}, f32[1,16,16,384]{3,1,2,0:T(8,128)S(1)}, u32[]{:S(2)}, u32[]{:S(2)}) collective-permute-start(f32[1,16,16,384]{3,1,2,0:T(8,128)} %get-tuple-element.1770), channel_id=1, source_target_pairs={{16,0},{32,16},{48,32},{64,48},{80,64},{96,80},{112,96},{17,1},{33... | collective-permute-start | bytes 1179656 | tf_op jit(solution)/shard_map/while/body/eval_jaxpr/ppermute | solution.py:14
  806.7 89.4 %collective-permute-start.3 = (f32[1,16,16,384]{3,1,2,0:T(8,128)}, f32[1,16,16,384]{3,1,2,0:T(8,128)S(1)}, u32[]{:S(2)}, u32[]{:S(2)}) collective-permute-start(f32[1,16,16,384]{3,1,2,0:T(8,128)} %get-tuple-element.1770), channel_id=1, source_target_pairs={{16,0},{32,16},{48,32},{64,48},{80,64},{96,80},{112,96},{17,1},{33... | collective-permute-start | bytes 1179656 | tf_op jit(solution)/shard_map/while/body/eval_jaxpr/ppermute | solution.py:14
  931.0 16.5 %collective-permute-start.3 = (f32[1,16,16,384]{3,1,2,0:T(8,128)}, f32[1,16,16,384]{3,1,2,0:T(8,128)S(1)}, u32[]{:S(2)}, u32[]{:S(2)}) collective-permute-start(f32[1,16,16,384]{3,1,2,0:T(8,128)} %get-tuple-element.1770), channel_id=1, source_target_pairs={{16,0},{32,16},{48,32},{64,48},{80,64},{96,80},{112,96},{17,1},{33... | collective-permute-start | bytes 1179656 | tf_op jit(solution)/shard_map/while/body/eval_jaxpr/ppermute | solution.py:14
  (74 other events, 347.3 us)
Sparse Core Ops, SparseCore 0:
  1017.7 90.9 reduce-scatter.1

commit v10 on v6

--- a/solution.py
+++ b/solution.py
@@ -11,7 +11,10 @@
 def passed_along(value, axis, steps):
     count = lax.axis_size(axis)
     initial, last = (max(0, -steps), min(count, count - steps))
-    return lax.ppermute(value, axis, [(source, source + steps) for source in range(initial, last)])
+    pairs = [(source, source + steps) for source in range(initial, last)]
+    half = value.shape[1] // 2
+    pieces = [value[:, :half], value[:, half:]]
+    return jnp.concatenate([lax.ppermute(piece, axis, pairs) for piece in pieces], axis=1)
 
 
 def embed(stamps_in, channels):

time: 1120 us -> 1150 us (1.027)
  starting transfers between devices: 207 us -> 312 us
  waiting for transfers between devices: 550 us -> 449 us
  other arithmetic: 100 us -> 112 us
    ppermute x44 -> x88, starting transfers between devices: 207 us -> 312 us  [passed_along(): lax.ppermute(piece, axis, pairs)]
    ppermute x44 -> x88, waiting for transfers between devices: 458 us -> 359 us  [passed_along(): lax.ppermute(piece, axis, pairs)]
    slice x0 -> x44, local copies, waits for them, and re-layouts: none -> 12.5 us  [passed_along(): pieces = [value[:, :half], value[:, half:]]]
  transfers between devices with their start and end apart: 45 -> 89, of which waited for: 45 -> 74; matrix products, arithmetic and copies ran while one was open for 5% -> 5% of each run, Pallas kernels for 0% -> 0%
where the time goes in v10:
time: 1150 us; the launch traced here: 1140 us
  waiting for transfers between devices  449 us (39%)
  starting transfers between devices  312 us (27%)
  local copies, waits for them, and re-layouts  169 us (15%)
  other arithmetic  112 us (10%)
  matrix products  75.2 us (7%)
  between operations  14.3 us (1%)
    ppermute x88, waiting for transfers between devices, passed_along(): lax.ppermute(piece, axis, pairs)  359 us
    ppermute x88, starting transfers between devices, passed_along(): lax.ppermute(piece, axis, pairs)  312 us
    reduce_scatter x1, waiting for transfers between devices, shards(): share = lax.psum_scatter(both, 'dp', scatter_dimension=3, tiled=True)  90.3 us
    conv_general_dilated x16, matrix products, conv_apply(): lax.conv_general_dilated(activations, weight, window_strides=(1, 1), padd...  60.6 us
    dynamic_update_slice x66, local copies, waits for them, and re-layouts, put_row(): lax.dynamic_update_slice_in_dim(buffer, piece.astype(buffer.dtype), slot_...  54.3 us
    dynamic_update_slice x22, other arithmetic, put_row(): lax.dynamic_update_slice_in_dim(buffer, piece.astype(buffer.dtype), slot_...  31.9 us
  transfers between devices with their start and end apart: 89, of which 74 were waited for; matrix products, arithmetic and copies ran while one was open for 5% of the time, Pallas kernels for 0%

profile of v10, /device:TPU:0, one launch (start us, length us, event | category | flops | bytes accessed | tf_op | source)
XLA Modules:
  0.0 1139.7 jit_solution(7775324693024042185)
XLA Ops:
  35.8 199.5 %while.80 = (s32[]{:T(128)}, f32[1,16,16,384]{3,1,2,0:T(8,128)S(1)}, f32[6,16,16,384]{3,1,2,0:T(8,128)S(1)}, f32[6,16,16,384]{3,1,2,0:T(8,128)}, s32[]{:T(128)},...) while((s32[]{:T(128)}, ...), condition=%wide.region_8.9_spmd, body=%wide.region_0.8_spmd.sunk | while | flops 979847872 | bytes 14413932 | solution.py:154
  109.1 10.0 collective-permute-start
  161.2 10.0 collective-permute-start
  188.3 12.3 %collective-permute-start.1 = (f32[1,8,16,384]{3,1,2,0:T(8,128)S(1)}, f32[1,8,16,384]{3,1,2,0:T(8,128)}, u32[]{:S(2)}, u32[]{:S(2)}) collective-permute-start(f32[1,8,16,384]{3,1,2,0:T(8,128)S(1)} %get-tuple-element.1792), channel_id=1, source_target_pairs={{0,16},{16,32},{32,48},{48,64},{64,80},{80,96},{96,112},{1,17},{17... | collective-permute-start | bytes 589832 | tf_op jit(solution)/shard_map/while/body/eval_jaxpr/ppermute | solution.py:17
  238.8 225.7 %while.81 = (s32[]{:T(128)}, f32[1,16,16,384]{3,1,2,0:T(8,128)S(1)}, f32[6,16,16,384]{3,1,2,0:T(8,128)}, f32[6,16,16,384]{3,1,2,0:T(8,128)}, s32[]{:T(128)}, /*i...) while((s32[]{:T(128)}, ...), condition=%wide.region_17.18_spmd, body=%wide.region_9.17_spmd.sunk | while | flops 1959449856 | bytes 22338664 | solution.py:175
  293.0 10.5 collective-permute-done.2
  340.4 29.4 %collective-permute-done.2 = f32[1,8,16,384]{3,1,2,0:T(8,128)S(1)} collective-permute-done((f32[1,8,16,384]{3,1,2,0:T(8,128)S(1)}, f32[1,8,16,384]{3,1,2,0:T(8,128)S(1)}, u32[]{:S(2)}, u32[]{:S(2)}) %collective-permute-start.2) | collective-permute-done | bytes 196640 | tf_op jit(solution)/shard_map/while/body/eval_jaxpr/ppermute | solution.py:17
  470.5 265.8 %while.82 = (s32[]{:T(128)}, f32[1,16,16,384]{3,1,2,0:T(8,128)S(1)}, f32[6,16,16,384]{3,1,2,0:T(8,128)}, f32[6,16,16,384]{3,1,2,0:T(8,128)}, bf16[6,16,16,768]{3...) while((s32[]{:T(128)}, ...), condition=%wide.region_30.31_spmd, body=%wide.region_18.30_spmd.sunk | while | flops 1967363584 | bytes 33298840 | solution.py:217
  473.9 10.8 conditional.10
  498.2 10.8 conditional.10
  524.7 10.8 conditional.10
  550.5 10.8 conditional.10
  575.8 15.1 %collective-permute-start.4 = (f32[1,8,16,384]{3,1,2,0:T(8,128)S(1)}, f32[1,8,16,384]{3,1,2,0:T(8,128)S(1)}, u32[]{:S(2)}, u32[]{:S(2)}) collective-permute-start(f32[1,8,16,384]{3,1,2,0:T(8,128)S(1)} %get-tuple-element.1823), channel_id=1, source_target_pairs={{0,16},{16,32},{32,48},{48,64},{64,80},{80,96},{96,112},{1,17},{17... | collective-permute-start | bytes 589832 | tf_op jit(solution)/shard_map/while/body/eval_jaxpr/ppermute | solution.py:17
  604.7 14.2 %collective-permute-start.5 = (f32[1,8,16,384]{3,1,2,0:T(8,128)S(1)}, f32[1,8,16,384]{3,1,2,0:T(8,128)S(1)}, u32[]{:S(2)}, u32[]{:S(2)}) collective-permute-start(f32[1,8,16,384]{3,1,2,0:T(8,128)S(1)} %get-tuple-element.1824), channel_id=1, source_target_pairs={{0,16},{16,32},{32,48},{48,64},{64,80},{80,96},{96,112},{1,17},{17... | collective-permute-start | bytes 589832 | tf_op jit(solution)/shard_map/while/body/eval_jaxpr/ppermute | solution.py:17
  643.0 15.1 %collective-permute-start.4 = (f32[1,8,16,384]{3,1,2,0:T(8,128)S(1)}, f32[1,8,16,384]{3,1,2,0:T(8,128)S(1)}, u32[]{:S(2)}, u32[]{:S(2)}) collective-permute-start(f32[1,8,16,384]{3,1,2,0:T(8,128)S(1)} %get-tuple-element.1823), channel_id=1, source_target_pairs={{0,16},{16,32},{32,48},{48,64},{64,80},{80,96},{96,112},{1,17},{17... | collective-permute-start | bytes 589832 | tf_op jit(solution)/shard_map/while/body/eval_jaxpr/ppermute | solution.py:17
  674.8 16.4 %collective-permute-start.5 = (f32[1,8,16,384]{3,1,2,0:T(8,128)S(1)}, f32[1,8,16,384]{3,1,2,0:T(8,128)S(1)}, u32[]{:S(2)}, u32[]{:S(2)}) collective-permute-start(f32[1,8,16,384]{3,1,2,0:T(8,128)S(1)} %get-tuple-element.1824), channel_id=1, source_target_pairs={{0,16},{16,32},{32,48},{48,64},{64,80},{80,96},{96,112},{1,17},{17... | collective-permute-start | bytes 589832 | tf_op jit(solution)/shard_map/while/body/eval_jaxpr/ppermute | solution.py:17
  715.2 9.9 collective-permute-start.4
  738.7 275.1 %while.83 = (s32[]{:T(128)}, f32[1,16,16,384]{3,1,2,0:T(8,128)S(1)}, bf16[6,16,16,384]{3,2,1,0:T(8,128)(2,1)}, bf16[6,16,16,384]{3,2,1,0:T(8,128)(2,1)}, s32[]{:...) while((s32[]{:T(128)}, ...), condition=%wide.region_43.44_spmd, body=%wide.region_31.0_spmd.sunk | while | flops 982108992 | bytes 28800936 | solution.py:255
  829.4 87.2 %collective-permute-done.6 = f32[1,8,16,384]{3,1,2,0:T(8,128)S(1)} collective-permute-done((f32[1,8,16,384]{3,1,2,0:T(8,128)S(1)}, f32[1,8,16,384]{3,1,2,0:T(8,128)S(1)}, u32[]{:S(2)}, u32[]{:S(2)}) %collective-permute-start.6) | collective-permute-done | bytes 196640 | tf_op jit(solution)/shard_map/while/body/eval_jaxpr/ppermute | solution.py:17
  919.1 10.5 conditional.11
  944.6 10.5 conditional.11
  966.6 10.5 conditional.11
  992.3 10.5 conditional.11
  1038.9 90.3 %reduce-scatter.2.cloned.1.call-done = f32[1,3,3,72,384]{4,3,2,1,0:T(8,128)} async-done(((f32[1,3,3,1152,384]{4,3,2,1,0:T(8,128)}), f32[1,3,3,72,384]{4,3,2,1,0:T(8,128)}) %reduce-scatter.2.cloned.1.call-update) | async-done | bytes 995344 | tf_op jit(solution)/shard_map/reduce_scatter | solution.py:272
  (1122 shorter events, 857.8 us)
Async XLA Ops:
  7.2 1122.0 %reduce-scatter.2.cloned.1.call-start = ((), (), s32[]{:S(2)}) async-start(), calls=%async_computation.1 | async-start | bytes 16920576 | tf_op jit(solution)/shard_map/reduce_scatter | solution.py:272
  109.1 13.7 %collective-permute-start = (f32[1,8,16,384]{3,1,2,0:T(8,128)S(1)}, f32[1,8,16,384]{3,1,2,0:T(8,128)S(1)}, u32[]{:S(2)}, u32[]{:S(2)}) collective-permute-start(f32[1,8,16,384]{3,1,2,0:T(8,128)S(1)} %get-tuple-element.1791), channel_id=1, source_target_pairs={{0,16},{16,32},{32,48},{48,64},{64,80},{80,96},{96,112},{1,17},{17... | collective-permute-start | bytes 589832 | tf_op jit(solution)/shard_map/while/body/eval_jaxpr/ppermute | solution.py:17
  126.6 15.1 %collective-permute-start = (f32[1,8,16,384]{3,1,2,0:T(8,128)S(1)}, f32[1,8,16,384]{3,1,2,0:T(8,128)S(1)}, u32[]{:S(2)}, u32[]{:S(2)}) collective-permute-start(f32[1,8,16,384]{3,1,2,0:T(8,128)S(1)} %get-tuple-element.1791), channel_id=1, source_target_pairs={{0,16},{16,32},{32,48},{48,64},{64,80},{80,96},{96,112},{1,17},{17... | collective-permute-start | bytes 589832 | tf_op jit(solution)/shard_map/while/body/eval_jaxpr/ppermute | solution.py:17
  161.2 17.3 %collective-permute-start = (f32[1,8,16,384]{3,1,2,0:T(8,128)S(1)}, f32[1,8,16,384]{3,1,2,0:T(8,128)S(1)}, u32[]{:S(2)}, u32[]{:S(2)}) collective-permute-start(f32[1,8,16,384]{3,1,2,0:T(8,128)S(1)} %get-tuple-element.1791), channel_id=1, source_target_pairs={{0,16},{16,32},{32,48},{48,64},{64,80},{80,96},{96,112},{1,17},{17... | collective-permute-start | bytes 589832 | tf_op jit(solution)/shard_map/while/body/eval_jaxpr/ppermute | solution.py:17
  183.8 17.6 %collective-permute-start = (f32[1,8,16,384]{3,1,2,0:T(8,128)S(1)}, f32[1,8,16,384]{3,1,2,0:T(8,128)S(1)}, u32[]{:S(2)}, u32[]{:S(2)}) collective-permute-start(f32[1,8,16,384]{3,1,2,0:T(8,128)S(1)} %get-tuple-element.1791), channel_id=1, source_target_pairs={{0,16},{16,32},{32,48},{48,64},{64,80},{80,96},{96,112},{1,17},{17... | collective-permute-start | bytes 589832 | tf_op jit(solution)/shard_map/while/body/eval_jaxpr/ppermute | solution.py:17
  188.3 16.8 %collective-permute-start.1 = (f32[1,8,16,384]{3,1,2,0:T(8,128)S(1)}, f32[1,8,16,384]{3,1,2,0:T(8,128)}, u32[]{:S(2)}, u32[]{:S(2)}) collective-permute-start(f32[1,8,16,384]{3,1,2,0:T(8,128)S(1)} %get-tuple-element.1792), channel_id=1, source_target_pairs={{0,16},{16,32},{32,48},{48,64},{64,80},{80,96},{96,112},{1,17},{17... | collective-permute-start | bytes 589832 | tf_op jit(solution)/shard_map/while/body/eval_jaxpr/ppermute | solution.py:17
  273.5 14.0 %collective-permute-start.3 = (f32[1,8,16,384]{3,1,2,0:T(8,128)S(1)}, f32[1,8,16,384]{3,1,2,0:T(8,128)S(1)}, u32[]{:S(2)}, u32[]{:S(2)}) collective-permute-start(f32[1,8,16,384]{3,1,2,0:T(8,128)S(1)} %get-tuple-element.1806), channel_id=1, source_target_pairs={{16,0},{32,16},{48,32},{64,48},{80,64},{96,80},{112,96},{17,1},{33... | collective-permute-start | bytes 589832 | tf_op jit(solution)/shard_map/while/body/eval_jaxpr/ppermute | solution.py:17
  289.6 13.9 %collective-permute-start.2 = (f32[1,8,16,384]{3,1,2,0:T(8,128)S(1)}, f32[1,8,16,384]{3,1,2,0:T(8,128)S(1)}, u32[]{:S(2)}, u32[]{:S(2)}) collective-permute-start(f32[1,8,16,384]{3,1,2,0:T(8,128)S(1)} %get-tuple-element.1805), channel_id=1, source_target_pairs={{16,0},{32,16},{48,32},{64,48},{80,64},{96,80},{112,96},{17,1},{33... | collective-permute-start | bytes 589832 | tf_op jit(solution)/shard_map/while/body/eval_jaxpr/ppermute | solution.py:17
  290.9 15.6 %collective-permute-start.3 = (f32[1,8,16,384]{3,1,2,0:T(8,128)S(1)}, f32[1,8,16,384]{3,1,2,0:T(8,128)S(1)}, u32[]{:S(2)}, u32[]{:S(2)}) collective-permute-start(f32[1,8,16,384]{3,1,2,0:T(8,128)S(1)} %get-tuple-element.1806), channel_id=1, source_target_pairs={{16,0},{32,16},{48,32},{64,48},{80,64},{96,80},{112,96},{17,1},{33... | collective-permute-start | bytes 589832 | tf_op jit(solution)/shard_map/while/body/eval_jaxpr/ppermute | solution.py:17
  337.0 32.8 %collective-permute-start.2 = (f32[1,8,16,384]{3,1,2,0:T(8,128)S(1)}, f32[1,8,16,384]{3,1,2,0:T(8,128)S(1)}, u32[]{:S(2)}, u32[]{:S(2)}) collective-permute-start(f32[1,8,16,384]{3,1,2,0:T(8,128)S(1)} %get-tuple-element.1805), channel_id=1, source_target_pairs={{16,0},{32,16},{48,32},{64,48},{80,64},{96,80},{112,96},{17,1},{33... | collective-permute-start | bytes 589832 | tf_op jit(solution)/shard_map/while/body/eval_jaxpr/ppermute | solution.py:17
  338.3 33.6 %collective-permute-start.3 = (f32[1,8,16,384]{3,1,2,0:T(8,128)S(1)}, f32[1,8,16,384]{3,1,2,0:T(8,128)S(1)}, u32[]{:S(2)}, u32[]{:S(2)}) collective-permute-start(f32[1,8,16,384]{3,1,2,0:T(8,128)S(1)} %get-tuple-element.1806), channel_id=1, source_target_pairs={{16,0},{32,16},{48,32},{64,48},{80,64},{96,80},{112,96},{17,1},{33... | collective-permute-start | bytes 589832 | tf_op jit(solution)/shard_map/while/body/eval_jaxpr/ppermute | solution.py:17
  406.4 13.9 %collective-permute-start.3 = (f32[1,8,16,384]{3,1,2,0:T(8,128)S(1)}, f32[1,8,16,384]{3,1,2,0:T(8,128)S(1)}, u32[]{:S(2)}, u32[]{:S(2)}) collective-permute-start(f32[1,8,16,384]{3,1,2,0:T(8,128)S(1)} %get-tuple-element.1806), channel_id=1, source_target_pairs={{16,0},{32,16},{48,32},{64,48},{80,64},{96,80},{112,96},{17,1},{33... | collective-permute-start | bytes 589832 | tf_op jit(solution)/shard_map/while/body/eval_jaxpr/ppermute | solution.py:17
  431.3 13.9 %collective-permute-start.3 = (f32[1,8,16,384]{3,1,2,0:T(8,128)S(1)}, f32[1,8,16,384]{3,1,2,0:T(8,128)S(1)}, u32[]{:S(2)}, u32[]{:S(2)}) collective-permute-start(f32[1,8,16,384]{3,1,2,0:T(8,128)S(1)} %get-tuple-element.1806), channel_id=1, source_target_pairs={{16,0},{32,16},{48,32},{64,48},{80,64},{96,80},{112,96},{17,1},{33... | collective-permute-start | bytes 589832 | tf_op jit(solution)/shard_map/while/body/eval_jaxpr/ppermute | solution.py:17
  575.8 20.1 %collective-permute-start.4 = (f32[1,8,16,384]{3,1,2,0:T(8,128)S(1)}, f32[1,8,16,384]{3,1,2,0:T(8,128)S(1)}, u32[]{:S(2)}, u32[]{:S(2)}) collective-permute-start(f32[1,8,16,384]{3,1,2,0:T(8,128)S(1)} %get-tuple-element.1823), channel_id=1, source_target_pairs={{0,16},{16,32},{32,48},{48,64},{64,80},{80,96},{96,112},{1,17},{17... | collective-permute-start | bytes 589832 | tf_op jit(solution)/shard_map/while/body/eval_jaxpr/ppermute | solution.py:17
  600.3 21.1 %collective-permute-start.4 = (f32[1,8,16,384]{3,1,2,0:T(8,128)S(1)}, f32[1,8,16,384]{3,1,2,0:T(8,128)S(1)}, u32[]{:S(2)}, u32[]{:S(2)}) collective-permute-start(f32[1,8,16,384]{3,1,2,0:T(8,128)S(1)} %get-tuple-element.1823), channel_id=1, source_target_pairs={{0,16},{16,32},{32,48},{48,64},{64,80},{80,96},{96,112},{1,17},{17... | collective-permute-start | bytes 589832 | tf_op jit(solution)/shard_map/while/body/eval_jaxpr/ppermute | solution.py:17
  604.7 17.3 %collective-permute-start.5 = (f32[1,8,16,384]{3,1,2,0:T(8,128)S(1)}, f32[1,8,16,384]{3,1,2,0:T(8,128)S(1)}, u32[]{:S(2)}, u32[]{:S(2)}) collective-permute-start(f32[1,8,16,384]{3,1,2,0:T(8,128)S(1)} %get-tuple-element.1824), channel_id=1, source_target_pairs={{0,16},{16,32},{32,48},{48,64},{64,80},{80,96},{96,112},{1,17},{17... | collective-permute-start | bytes 589832 | tf_op jit(solution)/shard_map/while/body/eval_jaxpr/ppermute | solution.py:17
  625.4 13.6 %collective-permute-start.4 = (f32[1,8,16,384]{3,1,2,0:T(8,128)S(1)}, f32[1,8,16,384]{3,1,2,0:T(8,128)S(1)}, u32[]{:S(2)}, u32[]{:S(2)}) collective-permute-start(f32[1,8,16,384]{3,1,2,0:T(8,128)S(1)} %get-tuple-element.1823), channel_id=1, source_target_pairs={{0,16},{16,32},{32,48},{48,64},{64,80},{80,96},{96,112},{1,17},{17... | collective-permute-start | bytes 589832 | tf_op jit(solution)/shard_map/while/body/eval_jaxpr/ppermute | solution.py:17
  643.0 23.4 %collective-permute-start.4 = (f32[1,8,16,384]{3,1,2,0:T(8,128)S(1)}, f32[1,8,16,384]{3,1,2,0:T(8,128)S(1)}, u32[]{:S(2)}, u32[]{:S(2)}) collective-permute-start(f32[1,8,16,384]{3,1,2,0:T(8,128)S(1)} %get-tuple-element.1823), channel_id=1, source_target_pairs={{0,16},{16,32},{32,48},{48,64},{64,80},{80,96},{96,112},{1,17},{17... | collective-permute-start | bytes 589832 | tf_op jit(solution)/shard_map/while/body/eval_jaxpr/ppermute | solution.py:17
  670.4 23.3 %collective-permute-start.4 = (f32[1,8,16,384]{3,1,2,0:T(8,128)S(1)}, f32[1,8,16,384]{3,1,2,0:T(8,128)S(1)}, u32[]{:S(2)}, u32[]{:S(2)}) collective-permute-start(f32[1,8,16,384]{3,1,2,0:T(8,128)S(1)} %get-tuple-element.1823), channel_id=1, source_target_pairs={{0,16},{16,32},{32,48},{48,64},{64,80},{80,96},{96,112},{1,17},{17... | collective-permute-start | bytes 589832 | tf_op jit(solution)/shard_map/while/body/eval_jaxpr/ppermute | solution.py:17
  674.8 19.6 %collective-permute-start.5 = (f32[1,8,16,384]{3,1,2,0:T(8,128)S(1)}, f32[1,8,16,384]{3,1,2,0:T(8,128)S(1)}, u32[]{:S(2)}, u32[]{:S(2)}) collective-permute-start(f32[1,8,16,384]{3,1,2,0:T(8,128)S(1)} %get-tuple-element.1824), channel_id=1, source_target_pairs={{0,16},{16,32},{32,48},{48,64},{64,80},{80,96},{96,112},{1,17},{17... | collective-permute-start | bytes 589832 | tf_op jit(solution)/shard_map/while/body/eval_jaxpr/ppermute | solution.py:17
  715.2 20.5 %collective-permute-start.4 = (f32[1,8,16,384]{3,1,2,0:T(8,128)S(1)}, f32[1,8,16,384]{3,1,2,0:T(8,128)S(1)}, u32[]{:S(2)}, u32[]{:S(2)}) collective-permute-start(f32[1,8,16,384]{3,1,2,0:T(8,128)S(1)} %get-tuple-element.1823), channel_id=1, source_target_pairs={{0,16},{16,32},{32,48},{48,64},{64,80},{80,96},{96,112},{1,17},{17... | collective-permute-start | bytes 589832 | tf_op jit(solution)/shard_map/while/body/eval_jaxpr/ppermute | solution.py:17
  755.4 13.9 %collective-permute-start.7 = (f32[1,8,16,384]{3,1,2,0:T(8,128)S(1)}, f32[1,8,16,384]{3,1,2,0:T(8,128)S(1)}, u32[]{:S(2)}, u32[]{:S(2)}) collective-permute-start(f32[1,8,16,384]{3,1,2,0:T(8,128)S(1)} %get-tuple-element.1843), channel_id=1, source_target_pairs={{16,0},{32,16},{48,32},{64,48},{80,64},{96,80},{112,96},{17,1},{33... | collective-permute-start | bytes 589832 | tf_op jit(solution)/shard_map/while/body/eval_jaxpr/ppermute | solution.py:17
  825.9 90.6 %collective-permute-start.6 = (f32[1,8,16,384]{3,1,2,0:T(8,128)S(1)}, f32[1,8,16,384]{3,1,2,0:T(8,128)S(1)}, u32[]{:S(2)}, u32[]{:S(2)}) collective-permute-start(f32[1,8,16,384]{3,1,2,0:T(8,128)S(1)} %get-tuple-element.1842), channel_id=1, source_target_pairs={{16,0},{32,16},{48,32},{64,48},{80,64},{96,80},{112,96},{17,1},{33... | collective-permute-start | bytes 589832 | tf_op jit(solution)/shard_map/while/body/eval_jaxpr/ppermute | solution.py:17
  827.2 91.8 %collective-permute-start.7 = (f32[1,8,16,384]{3,1,2,0:T(8,128)S(1)}, f32[1,8,16,384]{3,1,2,0:T(8,128)S(1)}, u32[]{:S(2)}, u32[]{:S(2)}) collective-permute-start(f32[1,8,16,384]{3,1,2,0:T(8,128)S(1)} %get-tuple-element.1843), channel_id=1, source_target_pairs={{16,0},{32,16},{48,32},{64,48},{80,64},{96,80},{112,96},{17,1},{33... | collective-permute-start | bytes 589832 | tf_op jit(solution)/shard_map/while/body/eval_jaxpr/ppermute | solution.py:17
  (114 other events, 724.0 us)
Sparse Core Ops, SparseCore 0:
  1039.0 90.1 reduce-scatter.1

commit v11 on v7

--- a/solution.py
+++ b/solution.py
@@ -189,13 +189,13 @@
             lambda: block_forward(joined, source, dec_kernel, stamp_one),
             lambda: blank_piece,
         )
-        dec_inputs = put_row(dec_inputs, source, slot_index)
+        dec_inputs = put_row(dec_inputs, joined, slot_index)
         outputs = put_row(outputs, result, slot_index)
         incoming = passed_across(result, -1)
         return (incoming, dec_inputs, outputs)
 
     _, dec_inputs, outputs = lax.fori_loop(
-        0, ticks_total, decoder_tick, (blank_piece, padded(row_shape), padded(row_shape))
+        0, ticks_total, decoder_tick, (blank_piece, padded(wide_shape), padded(row_shape))
     )
 
     def input_backward(inputs, weight, stamp_one, cotangent):
@@ -210,9 +210,7 @@
             pick_row(outputs, slot_index) - pick_row(noise, sample_at).astype(jnp.float32)
         )
         flowing = jnp.where(section_index == 0, top_grad, incoming)
-        joined = jnp.concatenate(
-            [pick_row(dec_inputs, slot_index), pick_row(skips, slot_index)], axis=3
-        )
+        joined = pick_row(dec_inputs, slot_index)
         stamp_one = chosen_row(wide_table, sample_at)
 
         def decoder_working():

time: 1110 us -> 1320 us (1.19)
  local copies, waits for them, and re-layouts: 163 us -> 234 us
  other arithmetic: 99.5 us -> 160 us
  waiting for transfers between devices: 546 us -> 590 us
  starting transfers between devices: 206 us -> 231 us
    ppermute x44, waiting for transfers between devices: 455 us -> 499 us  [passed_across(): return lax.ppermute(value, ('section', 'dp'), crossing_pairs(steps))]
    dynamic_update_slice x66, local copies, waits for them, and re-layouts: 54.4 us -> 89.5 us  [put_row(): lax.dynamic_update_slice_in_dim(buffer, piece.astype(buffer.dtype), slot_...]
    ppermute x44, starting transfers between devices: 204 us -> 229 us  [passed_across(): return lax.ppermute(value, ('section', 'dp'), crossing_pairs(steps))]
    dynamic_slice x22 -> x0, local copies, waits for them, and re-layouts: 22.5 us -> none  [pick_row(): return lax.dynamic_slice_in_dim(buffer, slot_index, 1, 0)]
    broadcast_in_dim x39, local copies, waits for them, and re-layouts: 6.28 us -> 22.8 us  [shards(): blank_piece = jnp.zeros((1,) + clean.shape[1:], jnp.float32)]
  transfers between devices with their start and end apart: 46 -> 46, of which waited for: 45 -> 45; matrix products, arithmetic and copies ran while one was open for 7% -> 9% of each run, Pallas kernels for 0% -> 0%
where the time goes in v11:
time: 1320 us; the launch traced here: 1310 us
  waiting for transfers between devices  590 us (45%)
  local copies, waits for them, and re-layouts  234 us (18%)
  starting transfers between devices  231 us (18%)
  other arithmetic  160 us (12%)
  matrix products  75.1 us (6%)
  between operations  14.2 us (1%)
    ppermute x44, waiting for transfers between devices, passed_across(): return lax.ppermute(value, ('section', 'dp'), crossing_pairs(steps))  499 us
    ppermute x44, starting transfers between devices, passed_across(): return lax.ppermute(value, ('section', 'dp'), crossing_pairs(steps))  229 us
    reduce_scatter x1, waiting for transfers between devices, shards(): share = lax.psum_scatter(both, 'dp', scatter_dimension=3, tiled=True)  91 us
    dynamic_update_slice x66, local copies, waits for them, and re-layouts, put_row(): lax.dynamic_update_slice_in_dim(buffer, piece.astype(buffer.dtype), slot_...  89.5 us
    conv_general_dilated x16, matrix products, conv_apply(): lax.conv_general_dilated(activations, weight, window_strides=(1, 1), padd...  60.5 us
  transfers between devices with their start and end apart: 46, of which 45 were waited for; matrix products, arithmetic and copies ran while one was open for 9% of the time, Pallas kernels for 0%

profile of v11, /device:TPU:0, one launch (start us, length us, event | category | flops | bytes accessed | tf_op | source)
XLA Modules:
  0.0 1308.8 jit_solution(13597244554530671484)
XLA Ops:
  38.5 180.0 %while.80 = (s32[]{:T(128)}, f32[1,16,16,384]{3,1,2,0:T(8,128)S(1)}, f32[6,16,16,384]{3,1,2,0:T(8,128)S(1)}, f32[6,16,16,384]{3,1,2,0:T(8,128)}, s32[]{:T(128)},...) while((s32[]{:T(128)}, ...), condition=%wide.region_8.9_spmd, body=%wide.region_0.8_spmd.sunk | while | flops 979749568 | bytes 12841028 | solution.py:176
  223.6 337.0 %while.81 = (s32[]{:T(128)}, f32[1,16,16,384]{3,1,2,0:T(8,128)}, f32[6,16,16,768]{3,1,2,0:T(8,128)}, f32[6,16,16,384]{3,1,2,0:T(8,128)}, s32[]{:T(128)}, /*index...) while((s32[]{:T(128)}, f32[1,16,16,384]{3,1,2,0:T(8,128)}, ...), condition=%wide.region_17.18_spmd, body=%wide.region_9.0_spmd.sunk | while | flops 1959351552 | bytes 21158468 | solution.py:197
  280.5 16.6 %collective-permute-done.1 = f32[1,16,16,384]{3,1,2,0:T(8,128)} collective-permute-done((f32[1,16,16,384]{3,1,2,0:T(8,128)S(1)}, f32[1,16,16,384]{3,1,2,0:T(8,128)}, u32[]{:S(2)}, u32[]{:S(2)}) %collective-permute-start.1) | collective-permute-done | bytes 393248 | tf_op jit(solution)/shard_map/while/body/eval_jaxpr/ppermute | solution.py:32
  302.0 15.8 %collective-permute-done.1 = f32[1,16,16,384]{3,1,2,0:T(8,128)} collective-permute-done((f32[1,16,16,384]{3,1,2,0:T(8,128)S(1)}, f32[1,16,16,384]{3,1,2,0:T(8,128)}, u32[]{:S(2)}, u32[]{:S(2)}) %collective-permute-start.1) | collective-permute-done | bytes 393248 | tf_op jit(solution)/shard_map/while/body/eval_jaxpr/ppermute | solution.py:32
  335.5 99.5 %collective-permute-done.1 = f32[1,16,16,384]{3,1,2,0:T(8,128)} collective-permute-done((f32[1,16,16,384]{3,1,2,0:T(8,128)S(1)}, f32[1,16,16,384]{3,1,2,0:T(8,128)}, u32[]{:S(2)}, u32[]{:S(2)}) %collective-permute-start.1) | collective-permute-done | bytes 393248 | tf_op jit(solution)/shard_map/while/body/eval_jaxpr/ppermute | solution.py:32
  437.8 16.3 %conditional.9 = (f32[1,16,16,384]{3,1,2,0:T(8,128)S(1)}) conditional(s32[]{:T(128)} %convert_element_type.136, () %tuple.242, (f32[1,16,16,768]{3,1,2,0:T(8,128)S(1)}, s32[]{:T(128)}, s32[4,1]{0,1:T(1,128)}, f32[4,768]{1,0:T(4,128)}, bf16[3,3,768,384]{3,2,1,0:T(8,128)(2,1)}, /*index=5*/f32[1,16,16,384]{3,1,2,0:T(8,128)S(1)}) %tuple.243), branch_computations={%region_10.10_spmd, %region_11.16_spmd} | conditional | flops 1959056640 | bytes 14866654 | solution.py:187
  469.9 16.3 %conditional.9 = (f32[1,16,16,384]{3,1,2,0:T(8,128)S(1)}) conditional(s32[]{:T(128)} %convert_element_type.136, () %tuple.242, (f32[1,16,16,768]{3,1,2,0:T(8,128)S(1)}, s32[]{:T(128)}, s32[4,1]{0,1:T(1,128)}, f32[4,768]{1,0:T(4,128)}, bf16[3,3,768,384]{3,2,1,0:T(8,128)(2,1)}, /*index=5*/f32[1,16,16,384]{3,1,2,0:T(8,128)S(1)}) %tuple.243), branch_computations={%region_10.10_spmd, %region_11.16_spmd} | conditional | flops 1959056640 | bytes 14866654 | solution.py:187
  502.3 16.3 %conditional.9 = (f32[1,16,16,384]{3,1,2,0:T(8,128)S(1)}) conditional(s32[]{:T(128)} %convert_element_type.136, () %tuple.242, (f32[1,16,16,768]{3,1,2,0:T(8,128)S(1)}, s32[]{:T(128)}, s32[4,1]{0,1:T(1,128)}, f32[4,768]{1,0:T(4,128)}, bf16[3,3,768,384]{3,2,1,0:T(8,128)(2,1)}, /*index=5*/f32[1,16,16,384]{3,1,2,0:T(8,128)S(1)}) %tuple.243), branch_computations={%region_10.10_spmd, %region_11.16_spmd} | conditional | flops 1959056640 | bytes 14866654 | solution.py:187
  534.6 16.3 %conditional.9 = (f32[1,16,16,384]{3,1,2,0:T(8,128)S(1)}) conditional(s32[]{:T(128)} %convert_element_type.136, () %tuple.242, (f32[1,16,16,768]{3,1,2,0:T(8,128)S(1)}, s32[]{:T(128)}, s32[4,1]{0,1:T(1,128)}, f32[4,768]{1,0:T(4,128)}, bf16[3,3,768,384]{3,2,1,0:T(8,128)(2,1)}, /*index=5*/f32[1,16,16,384]{3,1,2,0:T(8,128)S(1)}) %tuple.243), branch_computations={%region_10.10_spmd, %region_11.16_spmd} | conditional | flops 1959056640 | bytes 14866654 | solution.py:187
  566.6 312.7 %while.82 = (s32[]{:T(128)}, f32[1,16,16,384]{3,1,2,0:T(8,128)S(1)}, f32[6,16,16,384]{3,1,2,0:T(8,128)}, f32[6,16,16,384]{3,1,2,0:T(8,128)}, bf16[6,16,16,768]{3...) while((s32[]{:T(128)}, ...), condition=%wide.region_30.31_spmd, body=%wide.region_18.30_spmd.sunk | while | flops 1962350080 | bytes 29409768 | solution.py:237
  568.3 22.2 %conditional.10 = (f32[1,16,16,384]{3,1,2,0:T(8,128)}, f32[1,16,16,384]{3,1,2,0:T(8,128)}, bf16[1,16,16,768]{3,1,2,0:T(8,128)(2,1)}, bf16[1,16,16,384]{3,1,2,0:T(8,128)(2,1)S(1)}) conditional(s32[]{:T(128)} %convert_element_type.138, () %tuple.246, (pred[]{:T(512)}, f32[6,16,16,384]{3,1,2,0:T(8,128)}, s32[]{:T(128)}, ...), branch_computations={%region_19.19_spmd, %region_20.29_spmd} | conditional | flops 1962251776 | bytes 24492588 | solution.py:229
  598.9 22.2 %conditional.10 = (f32[1,16,16,384]{3,1,2,0:T(8,128)}, f32[1,16,16,384]{3,1,2,0:T(8,128)}, bf16[1,16,16,768]{3,1,2,0:T(8,128)(2,1)}, bf16[1,16,16,384]{3,1,2,0:T(8,128)(2,1)S(1)}) conditional(s32[]{:T(128)} %convert_element_type.138, () %tuple.246, (pred[]{:T(512)}, f32[6,16,16,384]{3,1,2,0:T(8,128)}, s32[]{:T(128)}, ...), branch_computations={%region_19.19_spmd, %region_20.29_spmd} | conditional | flops 1962251776 | bytes 24492588 | solution.py:229
  632.4 22.2 %conditional.10 = (f32[1,16,16,384]{3,1,2,0:T(8,128)}, f32[1,16,16,384]{3,1,2,0:T(8,128)}, bf16[1,16,16,768]{3,1,2,0:T(8,128)(2,1)}, bf16[1,16,16,384]{3,1,2,0:T(8,128)(2,1)S(1)}) conditional(s32[]{:T(128)} %convert_element_type.138, () %tuple.246, (pred[]{:T(512)}, f32[6,16,16,384]{3,1,2,0:T(8,128)}, s32[]{:T(128)}, ...), branch_computations={%region_19.19_spmd, %region_20.29_spmd} | conditional | flops 1962251776 | bytes 24492588 | solution.py:229
  665.9 22.2 %conditional.10 = (f32[1,16,16,384]{3,1,2,0:T(8,128)}, f32[1,16,16,384]{3,1,2,0:T(8,128)}, bf16[1,16,16,768]{3,1,2,0:T(8,128)(2,1)}, bf16[1,16,16,384]{3,1,2,0:T(8,128)(2,1)S(1)}) conditional(s32[]{:T(128)} %convert_element_type.138, () %tuple.246, (pred[]{:T(512)}, f32[6,16,16,384]{3,1,2,0:T(8,128)}, s32[]{:T(128)}, ...), branch_computations={%region_19.19_spmd, %region_20.29_spmd} | conditional | flops 1962251776 | bytes 24492588 | solution.py:229
  701.8 24.1 %collective-permute-start.2 = (f32[1,16,16,384]{3,1,2,0:T(8,128)}, f32[1,16,16,384]{3,1,2,0:T(8,128)S(1)}, u32[]{:S(2)}, u32[]{:S(2)}) collective-permute-start(f32[1,16,16,384]{3,1,2,0:T(8,128)} %get-tuple-element.1781), channel_id=1, source_target_pairs={{0,16},{1,17},{2,18},{3,19},{4,20},{5,21},{6,22},{7,23},{8,24},{9,... | collective-permute-start | bytes 1179656 | tf_op jit(solution)/shard_map/while/body/eval_jaxpr/ppermute | solution.py:32
  749.6 21.1 %collective-permute-start.2 = (f32[1,16,16,384]{3,1,2,0:T(8,128)}, f32[1,16,16,384]{3,1,2,0:T(8,128)S(1)}, u32[]{:S(2)}, u32[]{:S(2)}) collective-permute-start(f32[1,16,16,384]{3,1,2,0:T(8,128)} %get-tuple-element.1781), channel_id=1, source_target_pairs={{0,16},{1,17},{2,18},{3,19},{4,20},{5,21},{6,22},{7,23},{8,24},{9,... | collective-permute-start | bytes 1179656 | tf_op jit(solution)/shard_map/while/body/eval_jaxpr/ppermute | solution.py:32
  793.9 26.0 %collective-permute-start.2 = (f32[1,16,16,384]{3,1,2,0:T(8,128)}, f32[1,16,16,384]{3,1,2,0:T(8,128)S(1)}, u32[]{:S(2)}, u32[]{:S(2)}) collective-permute-start(f32[1,16,16,384]{3,1,2,0:T(8,128)} %get-tuple-element.1781), channel_id=1, source_target_pairs={{0,16},{1,17},{2,18},{3,19},{4,20},{5,21},{6,22},{7,23},{8,24},{9,... | collective-permute-start | bytes 1179656 | tf_op jit(solution)/shard_map/while/body/eval_jaxpr/ppermute | solution.py:32
  846.3 27.4 %collective-permute-start.2 = (f32[1,16,16,384]{3,1,2,0:T(8,128)}, f32[1,16,16,384]{3,1,2,0:T(8,128)S(1)}, u32[]{:S(2)}, u32[]{:S(2)}) collective-permute-start(f32[1,16,16,384]{3,1,2,0:T(8,128)} %get-tuple-element.1781), channel_id=1, source_target_pairs={{0,16},{1,17},{2,18},{3,19},{4,20},{5,21},{6,22},{7,23},{8,24},{9,... | collective-permute-start | bytes 1179656 | tf_op jit(solution)/shard_map/while/body/eval_jaxpr/ppermute | solution.py:32
  881.6 300.6 %while.83 = (s32[]{:T(128)}, f32[1,16,16,384]{3,1,2,0:T(8,128)S(1)}, bf16[6,16,16,384]{3,2,1,0:T(8,128)(2,1)}, bf16[6,16,16,384]{3,2,1,0:T(8,128)(2,1)}, s32[]{:...) while((s32[]{:T(128)}, ...), condition=%wide.region_43.44_spmd, body=%wide.region_31.43_spmd.sunk | while | flops 982010688 | bytes 27228124 | solution.py:275
  903.0 19.4 %collective-permute-done.3 = f32[1,16,16,384]{3,1,2,0:T(8,128)S(1)} collective-permute-done((f32[1,16,16,384]{3,1,2,0:T(8,128)}, f32[1,16,16,384]{3,1,2,0:T(8,128)S(1)}, u32[]{:S(2)}, u32[]{:S(2)}) %collective-permute-start.3) | collective-permute-done | bytes 393248 | tf_op jit(solution)/shard_map/while/body/eval_jaxpr/ppermute | solution.py:32
  943.5 20.4 %collective-permute-done.3 = f32[1,16,16,384]{3,1,2,0:T(8,128)S(1)} collective-permute-done((f32[1,16,16,384]{3,1,2,0:T(8,128)}, f32[1,16,16,384]{3,1,2,0:T(8,128)S(1)}, u32[]{:S(2)}, u32[]{:S(2)}) %collective-permute-start.3) | collective-permute-done | bytes 393248 | tf_op jit(solution)/shard_map/while/body/eval_jaxpr/ppermute | solution.py:32
  983.4 24.6 %collective-permute-done.3 = f32[1,16,16,384]{3,1,2,0:T(8,128)S(1)} collective-permute-done((f32[1,16,16,384]{3,1,2,0:T(8,128)}, f32[1,16,16,384]{3,1,2,0:T(8,128)S(1)}, u32[]{:S(2)}, u32[]{:S(2)}) %collective-permute-start.3) | collective-permute-done | bytes 393248 | tf_op jit(solution)/shard_map/while/body/eval_jaxpr/ppermute | solution.py:32
  1011.6 74.4 %collective-permute-done.3 = f32[1,16,16,384]{3,1,2,0:T(8,128)S(1)} collective-permute-done((f32[1,16,16,384]{3,1,2,0:T(8,128)}, f32[1,16,16,384]{3,1,2,0:T(8,128)S(1)}, u32[]{:S(2)}, u32[]{:S(2)}) %collective-permute-start.3) | collective-permute-done | bytes 393248 | tf_op jit(solution)/shard_map/while/body/eval_jaxpr/ppermute | solution.py:32
  1207.2 91.0 %reduce-scatter.2.cloned.1.call-done = f32[1,3,3,72,384]{4,3,2,1,0:T(8,128)} async-done(((f32[1,3,3,1152,384]{4,3,2,1,0:T(8,128)}), f32[1,3,3,72,384]{4,3,2,1,0:T(8,128)}) %reduce-scatter.2.cloned.1.call-update) | async-done | bytes 995344 | tf_op jit(solution)/shard_map/reduce_scatter | solution.py:292
  (939 shorter events, 923.3 us)
Async XLA Ops:
  7.2 1291.1 %reduce-scatter.2.cloned.1.call-start = ((), (), s32[]{:S(2)}) async-start(), calls=%async_computation.1 | async-start | bytes 16920576 | tf_op jit(solution)/shard_map/reduce_scatter | solution.py:292
  7.9 26.2 %collective-permute-start.4 = (f32[4]{0:T(128)S(1)}, f32[4]{0:T(128)S(1)}, u32[]{:S(2)}, u32[]{:S(2)}) collective-permute-start(f32[4]{0:T(128)S(1)} %convert_element_type.108), channel_id=1, source_target_pairs={{0,8},{1,9},{2,10},{3,11},{4,12},{5,13},{6,14},{7,15},{8,0},{9,1},... | collective-permute-start | bytes 56 | tf_op jit(solution)/shard_map/ppermute | solution.py:128
  110.6 14.7 %collective-permute-start = (f32[1,16,16,384]{3,1,2,0:T(8,128)}, f32[1,16,16,384]{3,1,2,0:T(8,128)S(1)}, u32[]{:S(2)}, u32[]{:S(2)}) collective-permute-start(f32[1,16,16,384]{3,1,2,0:T(8,128)} %get-tuple-element.2009), channel_id=1, source_target_pairs={{0,16},{1,17},{2,18},{3,19},{4,20},{5,21},{6,22},{7,23},{8,24},{9,... | collective-permute-start | bytes 1179656 | tf_op jit(solution)/shard_map/while/body/eval_jaxpr/ppermute | solution.py:32
  165.7 17.7 %collective-permute-start = (f32[1,16,16,384]{3,1,2,0:T(8,128)}, f32[1,16,16,384]{3,1,2,0:T(8,128)S(1)}, u32[]{:S(2)}, u32[]{:S(2)}) collective-permute-start(f32[1,16,16,384]{3,1,2,0:T(8,128)} %get-tuple-element.2009), channel_id=1, source_target_pairs={{0,16},{1,17},{2,18},{3,19},{4,20},{5,21},{6,22},{7,23},{8,24},{9,... | collective-permute-start | bytes 1179656 | tf_op jit(solution)/shard_map/while/body/eval_jaxpr/ppermute | solution.py:32
  200.4 18.0 %collective-permute-start = (f32[1,16,16,384]{3,1,2,0:T(8,128)}, f32[1,16,16,384]{3,1,2,0:T(8,128)S(1)}, u32[]{:S(2)}, u32[]{:S(2)}) collective-permute-start(f32[1,16,16,384]{3,1,2,0:T(8,128)} %get-tuple-element.2009), channel_id=1, source_target_pairs={{0,16},{1,17},{2,18},{3,19},{4,20},{5,21},{6,22},{7,23},{8,24},{9,... | collective-permute-start | bytes 1179656 | tf_op jit(solution)/shard_map/while/body/eval_jaxpr/ppermute | solution.py:32
  226.5 13.5 %collective-permute-start.1 = (f32[1,16,16,384]{3,1,2,0:T(8,128)S(1)}, f32[1,16,16,384]{3,1,2,0:T(8,128)}, u32[]{:S(2)}, u32[]{:S(2)}) collective-permute-start(f32[1,16,16,384]{3,1,2,0:T(8,128)S(1)} %get-tuple-element.2010), channel_id=1, source_target_pairs={{16,0},{17,1},{18,2},{19,3},{20,4},{21,5},{22,6},{23,7},{24,8},{25... | collective-permute-start | bytes 1179656 | tf_op jit(solution)/shard_map/while/body/eval_jaxpr/ppermute | solution.py:32
  242.8 14.2 %collective-permute-start.1 = (f32[1,16,16,384]{3,1,2,0:T(8,128)S(1)}, f32[1,16,16,384]{3,1,2,0:T(8,128)}, u32[]{:S(2)}, u32[]{:S(2)}) collective-permute-start(f32[1,16,16,384]{3,1,2,0:T(8,128)S(1)} %get-tuple-element.2010), channel_id=1, source_target_pairs={{16,0},{17,1},{18,2},{19,3},{20,4},{21,5},{22,6},{23,7},{24,8},{25... | collective-permute-start | bytes 1179656 | tf_op jit(solution)/shard_map/while/body/eval_jaxpr/ppermute | solution.py:32
  259.9 15.6 %collective-permute-start.1 = (f32[1,16,16,384]{3,1,2,0:T(8,128)S(1)}, f32[1,16,16,384]{3,1,2,0:T(8,128)}, u32[]{:S(2)}, u32[]{:S(2)}) collective-permute-start(f32[1,16,16,384]{3,1,2,0:T(8,128)S(1)} %get-tuple-element.2010), channel_id=1, source_target_pairs={{16,0},{17,1},{18,2},{19,3},{20,4},{21,5},{22,6},{23,7},{24,8},{25... | collective-permute-start | bytes 1179656 | tf_op jit(solution)/shard_map/while/body/eval_jaxpr/ppermute | solution.py:32
  278.4 18.7 %collective-permute-start.1 = (f32[1,16,16,384]{3,1,2,0:T(8,128)S(1)}, f32[1,16,16,384]{3,1,2,0:T(8,128)}, u32[]{:S(2)}, u32[]{:S(2)}) collective-permute-start(f32[1,16,16,384]{3,1,2,0:T(8,128)S(1)} %get-tuple-element.2010), channel_id=1, source_target_pairs={{16,0},{17,1},{18,2},{19,3},{20,4},{21,5},{22,6},{23,7},{24,8},{25... | collective-permute-start | bytes 1179656 | tf_op jit(solution)/shard_map/while/body/eval_jaxpr/ppermute | solution.py:32
  299.9 17.9 %collective-permute-start.1 = (f32[1,16,16,384]{3,1,2,0:T(8,128)S(1)}, f32[1,16,16,384]{3,1,2,0:T(8,128)}, u32[]{:S(2)}, u32[]{:S(2)}) collective-permute-start(f32[1,16,16,384]{3,1,2,0:T(8,128)S(1)} %get-tuple-element.2010), channel_id=1, source_target_pairs={{16,0},{17,1},{18,2},{19,3},{20,4},{21,5},{22,6},{23,7},{24,8},{25... | collective-permute-start | bytes 1179656 | tf_op jit(solution)/shard_map/while/body/eval_jaxpr/ppermute | solution.py:32
  333.4 101.6 %collective-permute-start.1 = (f32[1,16,16,384]{3,1,2,0:T(8,128)S(1)}, f32[1,16,16,384]{3,1,2,0:T(8,128)}, u32[]{:S(2)}, u32[]{:S(2)}) collective-permute-start(f32[1,16,16,384]{3,1,2,0:T(8,128)S(1)} %get-tuple-element.2010), channel_id=1, source_target_pairs={{16,0},{17,1},{18,2},{19,3},{20,4},{21,5},{22,6},{23,7},{24,8},{25... | collective-permute-start | bytes 1179656 | tf_op jit(solution)/shard_map/while/body/eval_jaxpr/ppermute | solution.py:32
  701.8 29.7 %collective-permute-start.2 = (f32[1,16,16,384]{3,1,2,0:T(8,128)}, f32[1,16,16,384]{3,1,2,0:T(8,128)S(1)}, u32[]{:S(2)}, u32[]{:S(2)}) collective-permute-start(f32[1,16,16,384]{3,1,2,0:T(8,128)} %get-tuple-element.1781), channel_id=1, source_target_pairs={{0,16},{1,17},{2,18},{3,19},{4,20},{5,21},{6,22},{7,23},{8,24},{9,... | collective-permute-start | bytes 1179656 | tf_op jit(solution)/shard_map/while/body/eval_jaxpr/ppermute | solution.py:32
  749.6 26.7 %collective-permute-start.2 = (f32[1,16,16,384]{3,1,2,0:T(8,128)}, f32[1,16,16,384]{3,1,2,0:T(8,128)S(1)}, u32[]{:S(2)}, u32[]{:S(2)}) collective-permute-start(f32[1,16,16,384]{3,1,2,0:T(8,128)} %get-tuple-element.1781), channel_id=1, source_target_pairs={{0,16},{1,17},{2,18},{3,19},{4,20},{5,21},{6,22},{7,23},{8,24},{9,... | collective-permute-start | bytes 1179656 | tf_op jit(solution)/shard_map/while/body/eval_jaxpr/ppermute | solution.py:32
  793.9 31.6 %collective-permute-start.2 = (f32[1,16,16,384]{3,1,2,0:T(8,128)}, f32[1,16,16,384]{3,1,2,0:T(8,128)S(1)}, u32[]{:S(2)}, u32[]{:S(2)}) collective-permute-start(f32[1,16,16,384]{3,1,2,0:T(8,128)} %get-tuple-element.1781), channel_id=1, source_target_pairs={{0,16},{1,17},{2,18},{3,19},{4,20},{5,21},{6,22},{7,23},{8,24},{9,... | collective-permute-start | bytes 1179656 | tf_op jit(solution)/shard_map/while/body/eval_jaxpr/ppermute | solution.py:32
  846.3 33.0 %collective-permute-start.2 = (f32[1,16,16,384]{3,1,2,0:T(8,128)}, f32[1,16,16,384]{3,1,2,0:T(8,128)S(1)}, u32[]{:S(2)}, u32[]{:S(2)}) collective-permute-start(f32[1,16,16,384]{3,1,2,0:T(8,128)} %get-tuple-element.1781), channel_id=1, source_target_pairs={{0,16},{1,17},{2,18},{3,19},{4,20},{5,21},{6,22},{7,23},{8,24},{9,... | collective-permute-start | bytes 1179656 | tf_op jit(solution)/shard_map/while/body/eval_jaxpr/ppermute | solution.py:32
  883.0 16.4 %collective-permute-start.3 = (f32[1,16,16,384]{3,1,2,0:T(8,128)}, f32[1,16,16,384]{3,1,2,0:T(8,128)S(1)}, u32[]{:S(2)}, u32[]{:S(2)}) collective-permute-start(f32[1,16,16,384]{3,1,2,0:T(8,128)} %get-tuple-element.1798), channel_id=1, source_target_pairs={{16,0},{17,1},{18,2},{19,3},{20,4},{21,5},{22,6},{23,7},{24,8},{25... | collective-permute-start | bytes 1179656 | tf_op jit(solution)/shard_map/while/body/eval_jaxpr/ppermute | solution.py:32
  900.8 21.5 %collective-permute-start.3 = (f32[1,16,16,384]{3,1,2,0:T(8,128)}, f32[1,16,16,384]{3,1,2,0:T(8,128)S(1)}, u32[]{:S(2)}, u32[]{:S(2)}) collective-permute-start(f32[1,16,16,384]{3,1,2,0:T(8,128)} %get-tuple-element.1798), channel_id=1, source_target_pairs={{16,0},{17,1},{18,2},{19,3},{20,4},{21,5},{22,6},{23,7},{24,8},{25... | collective-permute-start | bytes 1179656 | tf_op jit(solution)/shard_map/while/body/eval_jaxpr/ppermute | solution.py:32
  923.7 16.3 %collective-permute-start.3 = (f32[1,16,16,384]{3,1,2,0:T(8,128)}, f32[1,16,16,384]{3,1,2,0:T(8,128)S(1)}, u32[]{:S(2)}, u32[]{:S(2)}) collective-permute-start(f32[1,16,16,384]{3,1,2,0:T(8,128)} %get-tuple-element.1798), channel_id=1, source_target_pairs={{16,0},{17,1},{18,2},{19,3},{20,4},{21,5},{22,6},{23,7},{24,8},{25... | collective-permute-start | bytes 1179656 | tf_op jit(solution)/shard_map/while/body/eval_jaxpr/ppermute | solution.py:32
  941.4 22.6 %collective-permute-start.3 = (f32[1,16,16,384]{3,1,2,0:T(8,128)}, f32[1,16,16,384]{3,1,2,0:T(8,128)S(1)}, u32[]{:S(2)}, u32[]{:S(2)}) collective-permute-start(f32[1,16,16,384]{3,1,2,0:T(8,128)} %get-tuple-element.1798), channel_id=1, source_target_pairs={{16,0},{17,1},{18,2},{19,3},{20,4},{21,5},{22,6},{23,7},{24,8},{25... | collective-permute-start | bytes 1179656 | tf_op jit(solution)/shard_map/while/body/eval_jaxpr/ppermute | solution.py:32
  965.3 14.6 %collective-permute-start.3 = (f32[1,16,16,384]{3,1,2,0:T(8,128)}, f32[1,16,16,384]{3,1,2,0:T(8,128)S(1)}, u32[]{:S(2)}, u32[]{:S(2)}) collective-permute-start(f32[1,16,16,384]{3,1,2,0:T(8,128)} %get-tuple-element.1798), channel_id=1, source_target_pairs={{16,0},{17,1},{18,2},{19,3},{20,4},{21,5},{22,6},{23,7},{24,8},{25... | collective-permute-start | bytes 1179656 | tf_op jit(solution)/shard_map/while/body/eval_jaxpr/ppermute | solution.py:32
  981.3 26.8 %collective-permute-start.3 = (f32[1,16,16,384]{3,1,2,0:T(8,128)}, f32[1,16,16,384]{3,1,2,0:T(8,128)S(1)}, u32[]{:S(2)}, u32[]{:S(2)}) collective-permute-start(f32[1,16,16,384]{3,1,2,0:T(8,128)} %get-tuple-element.1798), channel_id=1, source_target_pairs={{16,0},{17,1},{18,2},{19,3},{20,4},{21,5},{22,6},{23,7},{24,8},{25... | collective-permute-start | bytes 1179656 | tf_op jit(solution)/shard_map/while/body/eval_jaxpr/ppermute | solution.py:32
  1009.4 76.5 %collective-permute-start.3 = (f32[1,16,16,384]{3,1,2,0:T(8,128)}, f32[1,16,16,384]{3,1,2,0:T(8,128)S(1)}, u32[]{:S(2)}, u32[]{:S(2)}) collective-permute-start(f32[1,16,16,384]{3,1,2,0:T(8,128)} %get-tuple-element.1798), channel_id=1, source_target_pairs={{16,0},{17,1},{18,2},{19,3},{20,4},{21,5},{22,6},{23,7},{24,8},{25... | collective-permute-start | bytes 1179656 | tf_op jit(solution)/shard_map/while/body/eval_jaxpr/ppermute | solution.py:32
  1121.2 14.0 %collective-permute-start.3 = (f32[1,16,16,384]{3,1,2,0:T(8,128)}, f32[1,16,16,384]{3,1,2,0:T(8,128)S(1)}, u32[]{:S(2)}, u32[]{:S(2)}) collective-permute-start(f32[1,16,16,384]{3,1,2,0:T(8,128)} %get-tuple-element.1798), channel_id=1, source_target_pairs={{16,0},{17,1},{18,2},{19,3},{20,4},{21,5},{22,6},{23,7},{24,8},{25... | collective-permute-start | bytes 1179656 | tf_op jit(solution)/shard_map/while/body/eval_jaxpr/ppermute | solution.py:32
  1146.2 15.1 %collective-permute-start.3 = (f32[1,16,16,384]{3,1,2,0:T(8,128)}, f32[1,16,16,384]{3,1,2,0:T(8,128)S(1)}, u32[]{:S(2)}, u32[]{:S(2)}) collective-permute-start(f32[1,16,16,384]{3,1,2,0:T(8,128)} %get-tuple-element.1798), channel_id=1, source_target_pairs={{16,0},{17,1},{18,2},{19,3},{20,4},{21,5},{22,6},{23,7},{24,8},{25... | collective-permute-start | bytes 1179656 | tf_op jit(solution)/shard_map/while/body/eval_jaxpr/ppermute | solution.py:32
  (83 other events, 363.0 us)
Sparse Core Ops, SparseCore 0:
  1207.4 90.8 reduce-scatter.1

commit v12 on v7

--- a/solution.py
+++ b/solution.py
@@ -204,7 +204,7 @@
         return (input_grad, activated.astype(jnp.bfloat16), cotangent.astype(jnp.bfloat16))
 
     def decoder_back_tick(tick_now, carried):
-        incoming, skip_grads, up_grads, dec_acts, dec_cots = carried
+        incoming, skip_grads, dec_acts, dec_cots = carried
         active, sample_at, slot_index = locate(tick_now, section_index)
         top_grad = factor * (
             pick_row(outputs, slot_index) - pick_row(noise, sample_at).astype(jnp.float32)
@@ -229,21 +229,20 @@
             )
 
         up_piece, skip_grad, acts, cots = lax.cond(active, decoder_working, decoder_resting)
-        skip_grads = put_row(skip_grads, skip_grad, slot_index)
-        up_grads = put_row(up_grads, up_piece, slot_index)
+        kept = jnp.where(section_index == last_section, up_piece + skip_grad, skip_grad)
+        skip_grads = put_row(skip_grads, kept, slot_index)
         dec_acts = put_row(dec_acts, acts, slot_index)
         dec_cots = put_row(dec_cots, cots, slot_index)
         incoming = passed_across(up_piece, 1)
-        return (incoming, skip_grads, up_grads, dec_acts, dec_cots)
-
-    _, skip_grads, up_grads, dec_acts, dec_cots = lax.fori_loop(
+        return (incoming, skip_grads, dec_acts, dec_cots)
+
+    _, skip_grads, dec_acts, dec_cots = lax.fori_loop(
         0,
         ticks_total,
         decoder_back_tick,
         (
             blank_piece,
             padded(row_shape),
-            padded(row_shape),
             padded(wide_shape, jnp.bfloat16),
             padded(row_shape, jnp.bfloat16),
         ),
@@ -253,10 +252,8 @@
     def encoder_back_tick(tick_now, carried):
         incoming, enc_acts, enc_cots = carried
         active, sample_at, slot_index = locate(tick_now, last_section - section_index)
-        arriving = jnp.where(
-            section_index == last_section, pick_row(up_grads, slot_index), incoming
-        )
-        merged = arriving + pick_row(skip_grads, slot_index)
+        skip_row = pick_row(skip_grads, slot_index)
+        merged = jnp.where(section_index == last_section, skip_row, incoming + skip_row)
         block_input = pick_row(enc_inputs, slot_index)
         stamp_one = chosen_row(narrow_table, sample_at)
 

time: 1110 us -> 1170 us (1.054)
  waiting for transfers between devices: 546 us -> 591 us
  other arithmetic: 99.5 us -> 127 us
  local copies, waits for them, and re-layouts: 163 us -> 146 us
    ppermute x44, waiting for transfers between devices: 455 us -> 499 us  [passed_across(): return lax.ppermute(value, ('section', 'dp'), crossing_pairs(steps))]
    dynamic_update_slice x66 -> x55, local copies, waits for them, and re-layouts: 54.4 us -> 44 us  [put_row(): lax.dynamic_update_slice_in_dim(buffer, piece.astype(buffer.dtype), slot_...]
    dynamic_update_slice x22 -> x33, other arithmetic: 31.8 us -> 40.7 us  [put_row(): lax.dynamic_update_slice_in_dim(buffer, piece.astype(buffer.dtype), slot_...]
where the time goes in v12:
time: 1170 us; the launch traced here: 1160 us
  waiting for transfers between devices  591 us (51%)
  starting transfers between devices  203 us (17%)
  local copies, waits for them, and re-layouts  146 us (12%)
  other arithmetic  127 us (11%)
  matrix products  75.1 us (6%)
  between operations  14.2 us (1%)
    ppermute x44, waiting for transfers between devices, passed_across(): return lax.ppermute(value, ('section', 'dp'), crossing_pairs(steps))  499 us
    ppermute x44, starting transfers between devices, passed_across(): return lax.ppermute(value, ('section', 'dp'), crossing_pairs(steps))  201 us
    reduce_scatter x1, waiting for transfers between devices, shards(): share = lax.psum_scatter(both, 'dp', scatter_dimension=3, tiled=True)  92.6 us
    conv_general_dilated x16, matrix products, conv_apply(): lax.conv_general_dilated(activations, weight, window_strides=(1, 1), padd...  60.5 us
    dynamic_update_slice x55, local copies, waits for them, and re-layouts, put_row(): lax.dynamic_update_slice_in_dim(buffer, piece.astype(buffer.dtype), slot_...  44 us
    dynamic_update_slice x33, other arithmetic, put_row(): lax.dynamic_update_slice_in_dim(buffer, piece.astype(buffer.dtype), slot_...  40.7 us
  transfers between devices with their start and end apart: 46, of which 45 were waited for; matrix products, arithmetic and copies ran while one was open for 7% of the time, Pallas kernels for 0%

profile of v12, /device:TPU:0, one launch (start us, length us, event | category | flops | bytes accessed | tf_op | source)
XLA Modules:
  0.0 1161.7 jit_solution(4944211921833816562)
XLA Ops:
  37.0 174.8 %while.78 = (s32[]{:T(128)}, f32[1,16,16,384]{3,1,2,0:T(8,128)S(1)}, f32[6,16,16,384]{3,1,2,0:T(8,128)S(1)}, f32[6,16,16,384]{3,1,2,0:T(8,128)}, s32[]{:T(128)},...) while((s32[]{:T(128)}, ...), condition=%wide.region_8.9_spmd, body=%wide.region_0.8_spmd.sunk | while | flops 979749568 | bytes 12841028 | solution.py:176
  160.6 12.1 %collective-permute-start = (f32[1,16,16,384]{3,1,2,0:T(8,128)S(1)}, f32[1,16,16,384]{3,1,2,0:T(8,128)S(1)}, u32[]{:S(2)}, u32[]{:S(2)}) collective-permute-start(f32[1,16,16,384]{3,1,2,0:T(8,128)S(1)} %get-tuple-element.1969), channel_id=1, source_target_pairs={{0,16},{1,17},{2,18},{3,19},{4,20},{5,21},{6,22},{7,23},{8,24},{9,... | collective-permute-start | bytes 1179656 | tf_op jit(solution)/shard_map/while/body/eval_jaxpr/ppermute | solution.py:32
  193.3 13.3 %collective-permute-start = (f32[1,16,16,384]{3,1,2,0:T(8,128)S(1)}, f32[1,16,16,384]{3,1,2,0:T(8,128)S(1)}, u32[]{:S(2)}, u32[]{:S(2)}) collective-permute-start(f32[1,16,16,384]{3,1,2,0:T(8,128)S(1)} %get-tuple-element.1969), channel_id=1, source_target_pairs={{0,16},{1,17},{2,18},{3,19},{4,20},{5,21},{6,22},{7,23},{8,24},{9,... | collective-permute-start | bytes 1179656 | tf_op jit(solution)/shard_map/while/body/eval_jaxpr/ppermute | solution.py:32
  215.2 236.7 %while.79 = (s32[]{:T(128)}, f32[1,16,16,384]{3,1,2,0:T(8,128)S(1)}, f32[6,16,16,384]{3,1,2,0:T(8,128)}, f32[6,16,16,384]{3,1,2,0:T(8,128)}, s32[]{:T(128)}, /*i...) while((s32[]{:T(128)}, ...), condition=%wide.region_17.18_spmd, body=%wide.region_9.0_spmd.sunk | while | flops 1959351552 | bytes 20765760 | solution.py:197
  235.5 13.5 %collective-permute-done.1 = f32[1,16,16,384]{3,1,2,0:T(8,128)S(1)} collective-permute-done((f32[1,16,16,384]{3,1,2,0:T(8,128)S(1)}, f32[1,16,16,384]{3,1,2,0:T(8,128)S(1)}, u32[]{:S(2)}, u32[]{:S(2)}) %collective-permute-start.1) | collective-permute-done | bytes 393248 | tf_op jit(solution)/shard_map/while/body/eval_jaxpr/ppermute | solution.py:32
  253.0 14.6 %collective-permute-done.1 = f32[1,16,16,384]{3,1,2,0:T(8,128)S(1)} collective-permute-done((f32[1,16,16,384]{3,1,2,0:T(8,128)S(1)}, f32[1,16,16,384]{3,1,2,0:T(8,128)S(1)}, u32[]{:S(2)}, u32[]{:S(2)}) %collective-permute-start.1) | collective-permute-done | bytes 393248 | tf_op jit(solution)/shard_map/while/body/eval_jaxpr/ppermute | solution.py:32
  271.6 17.9 %collective-permute-done.1 = f32[1,16,16,384]{3,1,2,0:T(8,128)S(1)} collective-permute-done((f32[1,16,16,384]{3,1,2,0:T(8,128)S(1)}, f32[1,16,16,384]{3,1,2,0:T(8,128)S(1)}, u32[]{:S(2)}, u32[]{:S(2)}) %collective-permute-start.1) | collective-permute-done | bytes 393248 | tf_op jit(solution)/shard_map/while/body/eval_jaxpr/ppermute | solution.py:32
  293.5 14.5 %collective-permute-done.1 = f32[1,16,16,384]{3,1,2,0:T(8,128)S(1)} collective-permute-done((f32[1,16,16,384]{3,1,2,0:T(8,128)S(1)}, f32[1,16,16,384]{3,1,2,0:T(8,128)S(1)}, u32[]{:S(2)}, u32[]{:S(2)}) %collective-permute-start.1) | collective-permute-done | bytes 393248 | tf_op jit(solution)/shard_map/while/body/eval_jaxpr/ppermute | solution.py:32
  323.7 37.6 %collective-permute-done.1 = f32[1,16,16,384]{3,1,2,0:T(8,128)S(1)} collective-permute-done((f32[1,16,16,384]{3,1,2,0:T(8,128)S(1)}, f32[1,16,16,384]{3,1,2,0:T(8,128)S(1)}, u32[]{:S(2)}, u32[]{:S(2)}) %collective-permute-start.1) | collective-permute-done | bytes 393248 | tf_op jit(solution)/shard_map/while/body/eval_jaxpr/ppermute | solution.py:32
  418.7 14.0 %collective-permute-done.1 = f32[1,16,16,384]{3,1,2,0:T(8,128)S(1)} collective-permute-done((f32[1,16,16,384]{3,1,2,0:T(8,128)S(1)}, f32[1,16,16,384]{3,1,2,0:T(8,128)S(1)}, u32[]{:S(2)}, u32[]{:S(2)}) %collective-permute-start.1) | collective-permute-done | bytes 393248 | tf_op jit(solution)/shard_map/while/body/eval_jaxpr/ppermute | solution.py:32
  456.3 234.8 %while.80 = (s32[]{:T(128)}, f32[1,16,16,384]{3,1,2,0:T(8,128)S(1)}, f32[6,16,16,384]{3,1,2,0:T(8,128)}, bf16[6,16,16,768]{3,2,1,0:T(8,128)(2,1)}, bf16[6,16,16,...) while((s32[]{:T(128)}, ...), condition=%wide.region_30.31_spmd, body=%wide.region_18.30_spmd.sunk | while | flops 1967461888 | bytes 32906120 | solution.py:239
  553.8 15.8 %collective-permute-start.2 = (f32[1,16,16,384]{3,1,2,0:T(8,128)S(1)}, f32[1,16,16,384]{3,1,2,0:T(8,128)S(1)}, u32[]{:S(2)}, u32[]{:S(2)}) collective-permute-start(f32[1,16,16,384]{3,1,2,0:T(8,128)S(1)} %get-tuple-element.1744), channel_id=1, source_target_pairs={{0,16},{1,17},{2,18},{3,19},{4,20},{5,21},{6,22},{7,23},{8,24},{9,... | collective-permute-start | bytes 1179656 | tf_op jit(solution)/shard_map/while/body/eval_jaxpr/ppermute | solution.py:32
  623.4 17.8 %collective-permute-start.2 = (f32[1,16,16,384]{3,1,2,0:T(8,128)S(1)}, f32[1,16,16,384]{3,1,2,0:T(8,128)S(1)}, u32[]{:S(2)}, u32[]{:S(2)}) collective-permute-start(f32[1,16,16,384]{3,1,2,0:T(8,128)S(1)} %get-tuple-element.1744), channel_id=1, source_target_pairs={{0,16},{1,17},{2,18},{3,19},{4,20},{5,21},{6,22},{7,23},{8,24},{9,... | collective-permute-start | bytes 1179656 | tf_op jit(solution)/shard_map/while/body/eval_jaxpr/ppermute | solution.py:32
  664.2 21.6 %collective-permute-start.2 = (f32[1,16,16,384]{3,1,2,0:T(8,128)S(1)}, f32[1,16,16,384]{3,1,2,0:T(8,128)S(1)}, u32[]{:S(2)}, u32[]{:S(2)}) collective-permute-start(f32[1,16,16,384]{3,1,2,0:T(8,128)S(1)} %get-tuple-element.1744), channel_id=1, source_target_pairs={{0,16},{1,17},{2,18},{3,19},{4,20},{5,21},{6,22},{7,23},{8,24},{9,... | collective-permute-start | bytes 1179656 | tf_op jit(solution)/shard_map/while/body/eval_jaxpr/ppermute | solution.py:32
  693.4 340.2 %while.81 = (s32[]{:T(128)}, f32[1,16,16,384]{3,1,2,0:T(8,128)S(1)}, bf16[6,16,16,384]{3,2,1,0:T(8,128)(2,1)}, bf16[6,16,16,384]{3,2,1,0:T(8,128)(2,1)}, s32[]{:...) while((s32[]{:T(128)}, ...), condition=%wide.region_43.44_spmd, body=%wide.region_31.43_spmd.sunk | while | flops 982207296 | bytes 26847144 | solution.py:274
  710.9 21.3 %collective-permute-done.3 = f32[1,16,16,384]{3,1,2,0:T(8,128)S(1)} collective-permute-done((f32[1,16,16,384]{3,1,2,0:T(8,128)}, f32[1,16,16,384]{3,1,2,0:T(8,128)S(1)}, u32[]{:S(2)}, u32[]{:S(2)}) %collective-permute-start.3) | collective-permute-done | bytes 393248 | tf_op jit(solution)/shard_map/while/body/eval_jaxpr/ppermute | solution.py:32
  774.5 17.1 %collective-permute-done.3 = f32[1,16,16,384]{3,1,2,0:T(8,128)S(1)} collective-permute-done((f32[1,16,16,384]{3,1,2,0:T(8,128)}, f32[1,16,16,384]{3,1,2,0:T(8,128)S(1)}, u32[]{:S(2)}, u32[]{:S(2)}) %collective-permute-start.3) | collective-permute-done | bytes 393248 | tf_op jit(solution)/shard_map/while/body/eval_jaxpr/ppermute | solution.py:32
  794.6 118.8 %collective-permute-done.3 = f32[1,16,16,384]{3,1,2,0:T(8,128)S(1)} collective-permute-done((f32[1,16,16,384]{3,1,2,0:T(8,128)}, f32[1,16,16,384]{3,1,2,0:T(8,128)S(1)}, u32[]{:S(2)}, u32[]{:S(2)}) %collective-permute-start.3) | collective-permute-done | bytes 393248 | tf_op jit(solution)/shard_map/while/body/eval_jaxpr/ppermute | solution.py:32
  913.5 17.1 %conditional.11 = (f32[1,16,16,384]{3,1,2,0:T(8,128)}, bf16[1,16,16,384]{3,1,2,0:T(8,128)(2,1)S(1)}, bf16[1,16,16,384]{3,1,2,0:T(8,128)(2,1)S(1)}) conditional(s32[]{:T(128)} %convert_element_type.139, () %tuple.248, (pred[]{:T(512)}, f32[6,16,16,384]{3,1,2,0:T(8,128)}, s32[]{:T(128)}, f32[1,16,16,384]{3,1,2,0:T(8,128)S(1)}, ...), branch_computations={%region_32.32_spmd, %region_33.42_spmd} | conditional | flops 982207296 | bytes 24486960 | solution.py:268
  943.8 17.1 %conditional.11 = (f32[1,16,16,384]{3,1,2,0:T(8,128)}, bf16[1,16,16,384]{3,1,2,0:T(8,128)(2,1)S(1)}, bf16[1,16,16,384]{3,1,2,0:T(8,128)(2,1)S(1)}) conditional(s32[]{:T(128)} %convert_element_type.139, () %tuple.248, (pred[]{:T(512)}, f32[6,16,16,384]{3,1,2,0:T(8,128)}, s32[]{:T(128)}, f32[1,16,16,384]{3,1,2,0:T(8,128)S(1)}, ...), branch_computations={%region_32.32_spmd, %region_33.42_spmd} | conditional | flops 982207296 | bytes 24486960 | solution.py:268
  974.1 17.1 %conditional.11 = (f32[1,16,16,384]{3,1,2,0:T(8,128)}, bf16[1,16,16,384]{3,1,2,0:T(8,128)(2,1)S(1)}, bf16[1,16,16,384]{3,1,2,0:T(8,128)(2,1)S(1)}) conditional(s32[]{:T(128)} %convert_element_type.139, () %tuple.248, (pred[]{:T(512)}, f32[6,16,16,384]{3,1,2,0:T(8,128)}, s32[]{:T(128)}, f32[1,16,16,384]{3,1,2,0:T(8,128)S(1)}, ...), branch_computations={%region_32.32_spmd, %region_33.42_spmd} | conditional | flops 982207296 | bytes 24486960 | solution.py:268
  993.3 13.2 %collective-permute-done.3 = f32[1,16,16,384]{3,1,2,0:T(8,128)S(1)} collective-permute-done((f32[1,16,16,384]{3,1,2,0:T(8,128)}, f32[1,16,16,384]{3,1,2,0:T(8,128)S(1)}, u32[]{:S(2)}, u32[]{:S(2)}) %collective-permute-start.3) | collective-permute-done | bytes 393248 | tf_op jit(solution)/shard_map/while/body/eval_jaxpr/ppermute | solution.py:32
  1006.6 17.1 %conditional.11 = (f32[1,16,16,384]{3,1,2,0:T(8,128)}, bf16[1,16,16,384]{3,1,2,0:T(8,128)(2,1)S(1)}, bf16[1,16,16,384]{3,1,2,0:T(8,128)(2,1)S(1)}) conditional(s32[]{:T(128)} %convert_element_type.139, () %tuple.248, (pred[]{:T(512)}, f32[6,16,16,384]{3,1,2,0:T(8,128)}, s32[]{:T(128)}, f32[1,16,16,384]{3,1,2,0:T(8,128)S(1)}, ...), branch_computations={%region_32.32_spmd, %region_33.42_spmd} | conditional | flops 982207296 | bytes 24486960 | solution.py:268
  1058.6 92.6 %reduce-scatter.2.cloned.1.call-done = f32[1,3,3,72,384]{4,3,2,1,0:T(8,128)} async-done(((f32[1,3,3,1152,384]{4,3,2,1,0:T(8,128)}), f32[1,3,3,72,384]{4,3,2,1,0:T(8,128)}) %reduce-scatter.2.cloned.1.call-update) | async-done | bytes 995344 | tf_op jit(solution)/shard_map/reduce_scatter | solution.py:291
  (960 shorter events, 793.6 us)
Async XLA Ops:
  7.2 1144.0 %reduce-scatter.2.cloned.1.call-start = ((), (), s32[]{:S(2)}) async-start(), calls=%async_computation.1 | async-start | bytes 16920576 | tf_op jit(solution)/shard_map/reduce_scatter | solution.py:291
  7.9 24.7 %collective-permute-start.4 = (f32[4]{0:T(128)S(1)}, f32[4]{0:T(128)S(1)}, u32[]{:S(2)}, u32[]{:S(2)}) collective-permute-start(f32[4]{0:T(128)S(1)} %convert_element_type.108), channel_id=1, source_target_pairs={{0,8},{1,9},{2,10},{3,11},{4,12},{5,13},{6,14},{7,15},{8,0},{9,1},... | collective-permute-start | bytes 56 | tf_op jit(solution)/shard_map/ppermute | solution.py:128
  107.4 15.2 %collective-permute-start = (f32[1,16,16,384]{3,1,2,0:T(8,128)S(1)}, f32[1,16,16,384]{3,1,2,0:T(8,128)S(1)}, u32[]{:S(2)}, u32[]{:S(2)}) collective-permute-start(f32[1,16,16,384]{3,1,2,0:T(8,128)S(1)} %get-tuple-element.1969), channel_id=1, source_target_pairs={{0,16},{1,17},{2,18},{3,19},{4,20},{5,21},{6,22},{7,23},{8,24},{9,... | collective-permute-start | bytes 1179656 | tf_op jit(solution)/shard_map/while/body/eval_jaxpr/ppermute | solution.py:32
  134.5 14.2 %collective-permute-start = (f32[1,16,16,384]{3,1,2,0:T(8,128)S(1)}, f32[1,16,16,384]{3,1,2,0:T(8,128)S(1)}, u32[]{:S(2)}, u32[]{:S(2)}) collective-permute-start(f32[1,16,16,384]{3,1,2,0:T(8,128)S(1)} %get-tuple-element.1969), channel_id=1, source_target_pairs={{0,16},{1,17},{2,18},{3,19},{4,20},{5,21},{6,22},{7,23},{8,24},{9,... | collective-permute-start | bytes 1179656 | tf_op jit(solution)/shard_map/while/body/eval_jaxpr/ppermute | solution.py:32
  160.6 17.4 %collective-permute-start = (f32[1,16,16,384]{3,1,2,0:T(8,128)S(1)}, f32[1,16,16,384]{3,1,2,0:T(8,128)S(1)}, u32[]{:S(2)}, u32[]{:S(2)}) collective-permute-start(f32[1,16,16,384]{3,1,2,0:T(8,128)S(1)} %get-tuple-element.1969), channel_id=1, source_target_pairs={{0,16},{1,17},{2,18},{3,19},{4,20},{5,21},{6,22},{7,23},{8,24},{9,... | collective-permute-start | bytes 1179656 | tf_op jit(solution)/shard_map/while/body/eval_jaxpr/ppermute | solution.py:32
  193.3 18.5 %collective-permute-start = (f32[1,16,16,384]{3,1,2,0:T(8,128)S(1)}, f32[1,16,16,384]{3,1,2,0:T(8,128)S(1)}, u32[]{:S(2)}, u32[]{:S(2)}) collective-permute-start(f32[1,16,16,384]{3,1,2,0:T(8,128)S(1)} %get-tuple-element.1969), channel_id=1, source_target_pairs={{0,16},{1,17},{2,18},{3,19},{4,20},{5,21},{6,22},{7,23},{8,24},{9,... | collective-permute-start | bytes 1179656 | tf_op jit(solution)/shard_map/while/body/eval_jaxpr/ppermute | solution.py:32
  217.2 14.2 %collective-permute-start.1 = (f32[1,16,16,384]{3,1,2,0:T(8,128)S(1)}, f32[1,16,16,384]{3,1,2,0:T(8,128)S(1)}, u32[]{:S(2)}, u32[]{:S(2)}) collective-permute-start(f32[1,16,16,384]{3,1,2,0:T(8,128)S(1)} %get-tuple-element.1970), channel_id=1, source_target_pairs={{16,0},{17,1},{18,2},{19,3},{20,4},{21,5},{22,6},{23,7},{24,8},{25... | collective-permute-start | bytes 1179656 | tf_op jit(solution)/shard_map/while/body/eval_jaxpr/ppermute | solution.py:32
  233.4 15.5 %collective-permute-start.1 = (f32[1,16,16,384]{3,1,2,0:T(8,128)S(1)}, f32[1,16,16,384]{3,1,2,0:T(8,128)S(1)}, u32[]{:S(2)}, u32[]{:S(2)}) collective-permute-start(f32[1,16,16,384]{3,1,2,0:T(8,128)S(1)} %get-tuple-element.1970), channel_id=1, source_target_pairs={{16,0},{17,1},{18,2},{19,3},{20,4},{21,5},{22,6},{23,7},{24,8},{25... | collective-permute-start | bytes 1179656 | tf_op jit(solution)/shard_map/while/body/eval_jaxpr/ppermute | solution.py:32
  250.9 16.6 %collective-permute-start.1 = (f32[1,16,16,384]{3,1,2,0:T(8,128)S(1)}, f32[1,16,16,384]{3,1,2,0:T(8,128)S(1)}, u32[]{:S(2)}, u32[]{:S(2)}) collective-permute-start(f32[1,16,16,384]{3,1,2,0:T(8,128)S(1)} %get-tuple-element.1970), channel_id=1, source_target_pairs={{16,0},{17,1},{18,2},{19,3},{20,4},{21,5},{22,6},{23,7},{24,8},{25... | collective-permute-start | bytes 1179656 | tf_op jit(solution)/shard_map/while/body/eval_jaxpr/ppermute | solution.py:32
  269.5 19.9 %collective-permute-start.1 = (f32[1,16,16,384]{3,1,2,0:T(8,128)S(1)}, f32[1,16,16,384]{3,1,2,0:T(8,128)S(1)}, u32[]{:S(2)}, u32[]{:S(2)}) collective-permute-start(f32[1,16,16,384]{3,1,2,0:T(8,128)S(1)} %get-tuple-element.1970), channel_id=1, source_target_pairs={{16,0},{17,1},{18,2},{19,3},{20,4},{21,5},{22,6},{23,7},{24,8},{25... | collective-permute-start | bytes 1179656 | tf_op jit(solution)/shard_map/while/body/eval_jaxpr/ppermute | solution.py:32
  291.4 16.6 %collective-permute-start.1 = (f32[1,16,16,384]{3,1,2,0:T(8,128)S(1)}, f32[1,16,16,384]{3,1,2,0:T(8,128)S(1)}, u32[]{:S(2)}, u32[]{:S(2)}) collective-permute-start(f32[1,16,16,384]{3,1,2,0:T(8,128)S(1)} %get-tuple-element.1970), channel_id=1, source_target_pairs={{16,0},{17,1},{18,2},{19,3},{20,4},{21,5},{22,6},{23,7},{24,8},{25... | collective-permute-start | bytes 1179656 | tf_op jit(solution)/shard_map/while/body/eval_jaxpr/ppermute | solution.py:32
  321.7 39.7 %collective-permute-start.1 = (f32[1,16,16,384]{3,1,2,0:T(8,128)S(1)}, f32[1,16,16,384]{3,1,2,0:T(8,128)S(1)}, u32[]{:S(2)}, u32[]{:S(2)}) collective-permute-start(f32[1,16,16,384]{3,1,2,0:T(8,128)S(1)} %get-tuple-element.1970), channel_id=1, source_target_pairs={{16,0},{17,1},{18,2},{19,3},{20,4},{21,5},{22,6},{23,7},{24,8},{25... | collective-permute-start | bytes 1179656 | tf_op jit(solution)/shard_map/while/body/eval_jaxpr/ppermute | solution.py:32
  393.2 13.9 %collective-permute-start.1 = (f32[1,16,16,384]{3,1,2,0:T(8,128)S(1)}, f32[1,16,16,384]{3,1,2,0:T(8,128)S(1)}, u32[]{:S(2)}, u32[]{:S(2)}) collective-permute-start(f32[1,16,16,384]{3,1,2,0:T(8,128)S(1)} %get-tuple-element.1970), channel_id=1, source_target_pairs={{16,0},{17,1},{18,2},{19,3},{20,4},{21,5},{22,6},{23,7},{24,8},{25... | collective-permute-start | bytes 1179656 | tf_op jit(solution)/shard_map/while/body/eval_jaxpr/ppermute | solution.py:32
  416.6 16.1 %collective-permute-start.1 = (f32[1,16,16,384]{3,1,2,0:T(8,128)S(1)}, f32[1,16,16,384]{3,1,2,0:T(8,128)S(1)}, u32[]{:S(2)}, u32[]{:S(2)}) collective-permute-start(f32[1,16,16,384]{3,1,2,0:T(8,128)S(1)} %get-tuple-element.1970), channel_id=1, source_target_pairs={{16,0},{17,1},{18,2},{19,3},{20,4},{21,5},{22,6},{23,7},{24,8},{25... | collective-permute-start | bytes 1179656 | tf_op jit(solution)/shard_map/while/body/eval_jaxpr/ppermute | solution.py:32
  553.8 21.5 %collective-permute-start.2 = (f32[1,16,16,384]{3,1,2,0:T(8,128)S(1)}, f32[1,16,16,384]{3,1,2,0:T(8,128)S(1)}, u32[]{:S(2)}, u32[]{:S(2)}) collective-permute-start(f32[1,16,16,384]{3,1,2,0:T(8,128)S(1)} %get-tuple-element.1744), channel_id=1, source_target_pairs={{0,16},{1,17},{2,18},{3,19},{4,20},{5,21},{6,22},{7,23},{8,24},{9,... | collective-permute-start | bytes 1179656 | tf_op jit(solution)/shard_map/while/body/eval_jaxpr/ppermute | solution.py:32
  591.3 17.7 %collective-permute-start.2 = (f32[1,16,16,384]{3,1,2,0:T(8,128)S(1)}, f32[1,16,16,384]{3,1,2,0:T(8,128)S(1)}, u32[]{:S(2)}, u32[]{:S(2)}) collective-permute-start(f32[1,16,16,384]{3,1,2,0:T(8,128)S(1)} %get-tuple-element.1744), channel_id=1, source_target_pairs={{0,16},{1,17},{2,18},{3,19},{4,20},{5,21},{6,22},{7,23},{8,24},{9,... | collective-permute-start | bytes 1179656 | tf_op jit(solution)/shard_map/while/body/eval_jaxpr/ppermute | solution.py:32
  623.4 23.0 %collective-permute-start.2 = (f32[1,16,16,384]{3,1,2,0:T(8,128)S(1)}, f32[1,16,16,384]{3,1,2,0:T(8,128)S(1)}, u32[]{:S(2)}, u32[]{:S(2)}) collective-permute-start(f32[1,16,16,384]{3,1,2,0:T(8,128)S(1)} %get-tuple-element.1744), channel_id=1, source_target_pairs={{0,16},{1,17},{2,18},{3,19},{4,20},{5,21},{6,22},{7,23},{8,24},{9,... | collective-permute-start | bytes 1179656 | tf_op jit(solution)/shard_map/while/body/eval_jaxpr/ppermute | solution.py:32
  664.2 26.9 %collective-permute-start.2 = (f32[1,16,16,384]{3,1,2,0:T(8,128)S(1)}, f32[1,16,16,384]{3,1,2,0:T(8,128)S(1)}, u32[]{:S(2)}, u32[]{:S(2)}) collective-permute-start(f32[1,16,16,384]{3,1,2,0:T(8,128)S(1)} %get-tuple-element.1744), channel_id=1, source_target_pairs={{0,16},{1,17},{2,18},{3,19},{4,20},{5,21},{6,22},{7,23},{8,24},{9,... | collective-permute-start | bytes 1179656 | tf_op jit(solution)/shard_map/while/body/eval_jaxpr/ppermute | solution.py:32
  694.3 13.7 %collective-permute-start.3 = (f32[1,16,16,384]{3,1,2,0:T(8,128)}, f32[1,16,16,384]{3,1,2,0:T(8,128)S(1)}, u32[]{:S(2)}, u32[]{:S(2)}) collective-permute-start(f32[1,16,16,384]{3,1,2,0:T(8,128)} %get-tuple-element.1758), channel_id=1, source_target_pairs={{16,0},{17,1},{18,2},{19,3},{20,4},{21,5},{22,6},{23,7},{24,8},{25... | collective-permute-start | bytes 1179656 | tf_op jit(solution)/shard_map/while/body/eval_jaxpr/ppermute | solution.py:32
  708.8 23.4 %collective-permute-start.3 = (f32[1,16,16,384]{3,1,2,0:T(8,128)}, f32[1,16,16,384]{3,1,2,0:T(8,128)S(1)}, u32[]{:S(2)}, u32[]{:S(2)}) collective-permute-start(f32[1,16,16,384]{3,1,2,0:T(8,128)} %get-tuple-element.1758), channel_id=1, source_target_pairs={{16,0},{17,1},{18,2},{19,3},{20,4},{21,5},{22,6},{23,7},{24,8},{25... | collective-permute-start | bytes 1179656 | tf_op jit(solution)/shard_map/while/body/eval_jaxpr/ppermute | solution.py:32
  758.4 13.2 %collective-permute-start.3 = (f32[1,16,16,384]{3,1,2,0:T(8,128)}, f32[1,16,16,384]{3,1,2,0:T(8,128)S(1)}, u32[]{:S(2)}, u32[]{:S(2)}) collective-permute-start(f32[1,16,16,384]{3,1,2,0:T(8,128)} %get-tuple-element.1758), channel_id=1, source_target_pairs={{16,0},{17,1},{18,2},{19,3},{20,4},{21,5},{22,6},{23,7},{24,8},{25... | collective-permute-start | bytes 1179656 | tf_op jit(solution)/shard_map/while/body/eval_jaxpr/ppermute | solution.py:32
  772.4 19.3 %collective-permute-start.3 = (f32[1,16,16,384]{3,1,2,0:T(8,128)}, f32[1,16,16,384]{3,1,2,0:T(8,128)S(1)}, u32[]{:S(2)}, u32[]{:S(2)}) collective-permute-start(f32[1,16,16,384]{3,1,2,0:T(8,128)} %get-tuple-element.1758), channel_id=1, source_target_pairs={{16,0},{17,1},{18,2},{19,3},{20,4},{21,5},{22,6},{23,7},{24,8},{25... | collective-permute-start | bytes 1179656 | tf_op jit(solution)/shard_map/while/body/eval_jaxpr/ppermute | solution.py:32
  792.5 120.9 %collective-permute-start.3 = (f32[1,16,16,384]{3,1,2,0:T(8,128)}, f32[1,16,16,384]{3,1,2,0:T(8,128)S(1)}, u32[]{:S(2)}, u32[]{:S(2)}) collective-permute-start(f32[1,16,16,384]{3,1,2,0:T(8,128)} %get-tuple-element.1758), channel_id=1, source_target_pairs={{16,0},{17,1},{18,2},{19,3},{20,4},{21,5},{22,6},{23,7},{24,8},{25... | collective-permute-start | bytes 1179656 | tf_op jit(solution)/shard_map/while/body/eval_jaxpr/ppermute | solution.py:32
  991.2 15.3 %collective-permute-start.3 = (f32[1,16,16,384]{3,1,2,0:T(8,128)}, f32[1,16,16,384]{3,1,2,0:T(8,128)S(1)}, u32[]{:S(2)}, u32[]{:S(2)}) collective-permute-start(f32[1,16,16,384]{3,1,2,0:T(8,128)} %get-tuple-element.1758), channel_id=1, source_target_pairs={{16,0},{17,1},{18,2},{19,3},{20,4},{21,5},{22,6},{23,7},{24,8},{25... | collective-permute-start | bytes 1179656 | tf_op jit(solution)/shard_map/while/body/eval_jaxpr/ppermute | solution.py:32
  (83 other events, 398.4 us)
Sparse Core Ops, SparseCore 0:
  1058.7 92.4 reduce-scatter.1

commit v13 on v7

--- a/solution.py
+++ b/solution.py
@@ -72,20 +72,19 @@
     batch_rows, height, breadth, channels = activations.shape
     padded = jnp.pad(activations, ((0, 0), (1, 1), (1, 1), (0, 0)))
     flat_cot = cotangent.astype(jnp.bfloat16).reshape(-1, cotangent.shape[3])
-    kernel_rows = []
-    for row_off in range(3):
-        kernel_cols = []
-        for col_off in range(3):
-            window = padded[:, row_off : row_off + height, col_off : col_off + breadth, :].reshape(
-                -1, channels
-            )
-            kernel_cols.append(
-                lax.dot_general(
-                    window, flat_cot, (((0,), (0,)), ((), ())), preferred_element_type=jnp.float32
-                )
-            )
-        kernel_rows.append(jnp.stack(kernel_cols))
-    return jnp.stack(kernel_rows)
+
+    def one_tap(tap, kernel):
+        row_off, col_off = (tap // 3, tap % 3)
+        window = lax.dynamic_slice(
+            padded, (0, row_off, col_off, 0), (batch_rows, height, breadth, channels)
+        ).reshape(-1, channels)
+        product = lax.dot_general(
+            window, flat_cot, (((0,), (0,)), ((), ())), preferred_element_type=jnp.float32
+        )
+        return lax.dynamic_update_slice(kernel, product[None, None], (row_off, col_off, 0, 0))
+
+    kernel = jnp.zeros((3, 3, channels, cotangent.shape[3]), jnp.float32)
+    return lax.fori_loop(0, 9, one_tap, kernel)
 
 
 def modulation(stamps_in, channels):

time: 1110 us -> 1170 us (1.054)
  local copies, waits for them, and re-layouts: 163 us -> 202 us
  matrix products: 75.1 us -> 104 us
  waiting for transfers between devices: 546 us -> 526 us
    dot_general x18, matrix products: 14.6 us -> 43.9 us  [one_tap(): lax.dot_general(window, flat_cot, (((0,), (0,)), ((), ())), preferred_ele...]
    ppermute x44, waiting for transfers between devices: 455 us -> 435 us  [passed_across(): return lax.ppermute(value, ('section', 'dp'), crossing_pairs(steps))]
    dynamic_slice x0 -> x18, local copies, waits for them, and re-layouts: none -> 19.9 us  [one_tap(): lax.dynamic_slice(padded, (0, row_off, col_off, 0), (batch_rows, height,...]
    dynamic_update_slice x66 -> x77, local copies, waits for them, and re-layouts: 54.4 us -> 70.8 us  [put_row(): lax.dynamic_update_slice_in_dim(buffer, piece.astype(buffer.dtype), slot_...]
  transfers between devices with their start and end apart: 46 -> 46, of which waited for: 45 -> 45; matrix products, arithmetic and copies ran while one was open for 7% -> 8% of each run, Pallas kernels for 0% -> 0%
where the time goes in v13:
time: 1170 us; the launch traced here: 1160 us
  waiting for transfers between devices  526 us (45%)
  starting transfers between devices  202 us (17%)
  local copies, waits for them, and re-layouts  202 us (17%)
  other arithmetic  107 us (9%)
  matrix products  104 us (9%)
  between operations  14.2 us (1%)
    ppermute x44, waiting for transfers between devices, passed_across(): return lax.ppermute(value, ('section', 'dp'), crossing_pairs(steps))  435 us
    ppermute x44, starting transfers between devices, passed_across(): return lax.ppermute(value, ('section', 'dp'), crossing_pairs(steps))  200 us
    reduce_scatter x1, waiting for transfers between devices, shards(): share = lax.psum_scatter(both, 'dp', scatter_dimension=3, tiled=True)  90.8 us
    dynamic_update_slice x77, local copies, waits for them, and re-layouts, put_row(): lax.dynamic_update_slice_in_dim(buffer, piece.astype(buffer.dtype), slot_...  70.8 us
    conv_general_dilated x16, matrix products, conv_apply(): lax.conv_general_dilated(activations, weight, window_strides=(1, 1), padd...  60.5 us
    dot_general x18, matrix products, one_tap(): lax.dot_general(window, flat_cot, (((0,), (0,)), ((), ())), preferred_ele...  43.9 us
    dynamic_update_slice x22, other arithmetic, put_row(): lax.dynamic_update_slice_in_dim(buffer, piece.astype(buffer.dtype), slot_...  31.8 us
  transfers between devices with their start and end apart: 46, of which 45 were waited for; matrix products, arithmetic and copies ran while one was open for 8% of the time, Pallas kernels for 0%

profile of v13, /device:TPU:0, one launch (start us, length us, event | category | flops | bytes accessed | tf_op | source)
XLA Modules:
  0.0 1161.1 jit_solution(13584778656864845921)
XLA Ops:
  37.2 174.8 %while.110 = (s32[]{:T(128)}, f32[1,16,16,384]{3,1,2,0:T(8,128)S(1)}, f32[6,16,16,384]{3,1,2,0:T(8,128)S(1)}, f32[6,16,16,384]{3,1,2,0:T(8,128)}, s32[]{:T(128)}...) while((s32[]{:T(128)}, ...), condition=%wide.region_8.9_spmd, body=%wide.region_0.8_spmd.sunk | while | flops 979749568 | bytes 12841028 | solution.py:175
  160.6 12.4 %collective-permute-start = (f32[1,16,16,384]{3,1,2,0:T(8,128)S(1)}, f32[1,16,16,384]{3,1,2,0:T(8,128)S(1)}, u32[]{:S(2)}, u32[]{:S(2)}) collective-permute-start(f32[1,16,16,384]{3,1,2,0:T(8,128)S(1)} %get-tuple-element.2376), channel_id=1, source_target_pairs={{0,16},{1,17},{2,18},{3,19},{4,20},{5,21},{6,22},{7,23},{8,24},{9,... | collective-permute-start | bytes 1179656 | tf_op jit(solution)/shard_map/while/body/eval_jaxpr/ppermute | solution.py:32
  193.4 13.3 %collective-permute-start = (f32[1,16,16,384]{3,1,2,0:T(8,128)S(1)}, f32[1,16,16,384]{3,1,2,0:T(8,128)S(1)}, u32[]{:S(2)}, u32[]{:S(2)}) collective-permute-start(f32[1,16,16,384]{3,1,2,0:T(8,128)S(1)} %get-tuple-element.2376), channel_id=1, source_target_pairs={{0,16},{1,17},{2,18},{3,19},{4,20},{5,21},{6,22},{7,23},{8,24},{9,... | collective-permute-start | bytes 1179656 | tf_op jit(solution)/shard_map/while/body/eval_jaxpr/ppermute | solution.py:32
  215.5 233.6 %while.111 = (s32[]{:T(128)}, f32[1,16,16,384]{3,1,2,0:T(8,128)S(1)}, f32[6,16,16,384]{3,1,2,0:T(8,128)}, f32[6,16,16,384]{3,1,2,0:T(8,128)}, s32[]{:T(128)}, /*...) while((s32[]{:T(128)}, ...), condition=%wide.region_17.18_spmd, body=%wide.region_9.0_spmd.sunk | while | flops 1959351552 | bytes 20765760 | solution.py:196
  219.6 12.1 %collective-permute-done.1 = f32[1,16,16,384]{3,1,2,0:T(8,128)S(1)} collective-permute-done((f32[1,16,16,384]{3,1,2,0:T(8,128)S(1)}, f32[1,16,16,384]{3,1,2,0:T(8,128)S(1)}, u32[]{:S(2)}, u32[]{:S(2)}) %collective-permute-start.1) | collective-permute-done | bytes 393248 | tf_op jit(solution)/shard_map/while/body/eval_jaxpr/ppermute | solution.py:32
  235.7 13.4 %collective-permute-done.1 = f32[1,16,16,384]{3,1,2,0:T(8,128)S(1)} collective-permute-done((f32[1,16,16,384]{3,1,2,0:T(8,128)S(1)}, f32[1,16,16,384]{3,1,2,0:T(8,128)S(1)}, u32[]{:S(2)}, u32[]{:S(2)}) %collective-permute-start.1) | collective-permute-done | bytes 393248 | tf_op jit(solution)/shard_map/while/body/eval_jaxpr/ppermute | solution.py:32
  253.2 14.5 %collective-permute-done.1 = f32[1,16,16,384]{3,1,2,0:T(8,128)S(1)} collective-permute-done((f32[1,16,16,384]{3,1,2,0:T(8,128)S(1)}, f32[1,16,16,384]{3,1,2,0:T(8,128)S(1)}, u32[]{:S(2)}, u32[]{:S(2)}) %collective-permute-start.1) | collective-permute-done | bytes 393248 | tf_op jit(solution)/shard_map/while/body/eval_jaxpr/ppermute | solution.py:32
  271.8 17.8 %collective-permute-done.1 = f32[1,16,16,384]{3,1,2,0:T(8,128)S(1)} collective-permute-done((f32[1,16,16,384]{3,1,2,0:T(8,128)S(1)}, f32[1,16,16,384]{3,1,2,0:T(8,128)S(1)}, u32[]{:S(2)}, u32[]{:S(2)}) %collective-permute-start.1) | collective-permute-done | bytes 393248 | tf_op jit(solution)/shard_map/while/body/eval_jaxpr/ppermute | solution.py:32
  293.8 14.5 %collective-permute-done.1 = f32[1,16,16,384]{3,1,2,0:T(8,128)S(1)} collective-permute-done((f32[1,16,16,384]{3,1,2,0:T(8,128)S(1)}, f32[1,16,16,384]{3,1,2,0:T(8,128)S(1)}, u32[]{:S(2)}, u32[]{:S(2)}) %collective-permute-start.1) | collective-permute-done | bytes 393248 | tf_op jit(solution)/shard_map/while/body/eval_jaxpr/ppermute | solution.py:32
  324.0 35.3 %collective-permute-done.1 = f32[1,16,16,384]{3,1,2,0:T(8,128)S(1)} collective-permute-done((f32[1,16,16,384]{3,1,2,0:T(8,128)S(1)}, f32[1,16,16,384]{3,1,2,0:T(8,128)S(1)}, u32[]{:S(2)}, u32[]{:S(2)}) %collective-permute-start.1) | collective-permute-done | bytes 393248 | tf_op jit(solution)/shard_map/while/body/eval_jaxpr/ppermute | solution.py:32
  392.9 12.3 %collective-permute-done.1 = f32[1,16,16,384]{3,1,2,0:T(8,128)S(1)} collective-permute-done((f32[1,16,16,384]{3,1,2,0:T(8,128)S(1)}, f32[1,16,16,384]{3,1,2,0:T(8,128)S(1)}, u32[]{:S(2)}, u32[]{:S(2)}) %collective-permute-start.1) | collective-permute-done | bytes 393248 | tf_op jit(solution)/shard_map/while/body/eval_jaxpr/ppermute | solution.py:32
  416.5 13.7 %collective-permute-done.1 = f32[1,16,16,384]{3,1,2,0:T(8,128)S(1)} collective-permute-done((f32[1,16,16,384]{3,1,2,0:T(8,128)S(1)}, f32[1,16,16,384]{3,1,2,0:T(8,128)S(1)}, u32[]{:S(2)}, u32[]{:S(2)}) %collective-permute-start.1) | collective-permute-done | bytes 393248 | tf_op jit(solution)/shard_map/while/body/eval_jaxpr/ppermute | solution.py:32
  455.1 234.9 %while.112 = (s32[]{:T(128)}, f32[1,16,16,384]{3,1,2,0:T(8,128)S(1)}, f32[6,16,16,384]{3,1,2,0:T(8,128)}, f32[6,16,16,384]{3,1,2,0:T(8,128)}, bf16[6,16,16,768]{...) while((s32[]{:T(128)}, ...), condition=%wide.region_30.31_spmd, body=%wide.region_18.30_spmd.sunk | while | flops 1967265280 | bytes 31725936 | solution.py:238
  551.4 14.3 %collective-permute-start.2 = (f32[1,16,16,384]{3,1,2,0:T(8,128)S(1)}, f32[1,16,16,384]{3,1,2,0:T(8,128)S(1)}, u32[]{:S(2)}, u32[]{:S(2)}) collective-permute-start(f32[1,16,16,384]{3,1,2,0:T(8,128)S(1)} %get-tuple-element.2085), channel_id=1, source_target_pairs={{0,16},{1,17},{2,18},{3,19},{4,20},{5,21},{6,22},{7,23},{8,24},{9,... | collective-permute-start | bytes 1179656 | tf_op jit(solution)/shard_map/while/body/eval_jaxpr/ppermute | solution.py:32
  587.6 11.9 %collective-permute-start.2 = (f32[1,16,16,384]{3,1,2,0:T(8,128)S(1)}, f32[1,16,16,384]{3,1,2,0:T(8,128)S(1)}, u32[]{:S(2)}, u32[]{:S(2)}) collective-permute-start(f32[1,16,16,384]{3,1,2,0:T(8,128)S(1)} %get-tuple-element.2085), channel_id=1, source_target_pairs={{0,16},{1,17},{2,18},{3,19},{4,20},{5,21},{6,22},{7,23},{8,24},{9,... | collective-permute-start | bytes 1179656 | tf_op jit(solution)/shard_map/while/body/eval_jaxpr/ppermute | solution.py:32
  621.0 16.8 %collective-permute-start.2 = (f32[1,16,16,384]{3,1,2,0:T(8,128)S(1)}, f32[1,16,16,384]{3,1,2,0:T(8,128)S(1)}, u32[]{:S(2)}, u32[]{:S(2)}) collective-permute-start(f32[1,16,16,384]{3,1,2,0:T(8,128)S(1)} %get-tuple-element.2085), channel_id=1, source_target_pairs={{0,16},{1,17},{2,18},{3,19},{4,20},{5,21},{6,22},{7,23},{8,24},{9,... | collective-permute-start | bytes 1179656 | tf_op jit(solution)/shard_map/while/body/eval_jaxpr/ppermute | solution.py:32
  662.6 22.2 %collective-permute-start.2 = (f32[1,16,16,384]{3,1,2,0:T(8,128)S(1)}, f32[1,16,16,384]{3,1,2,0:T(8,128)S(1)}, u32[]{:S(2)}, u32[]{:S(2)}) collective-permute-start(f32[1,16,16,384]{3,1,2,0:T(8,128)S(1)} %get-tuple-element.2085), channel_id=1, source_target_pairs={{0,16},{1,17},{2,18},{3,19},{4,20},{5,21},{6,22},{7,23},{8,24},{9,... | collective-permute-start | bytes 1179656 | tf_op jit(solution)/shard_map/while/body/eval_jaxpr/ppermute | solution.py:32
  692.4 278.3 %while.113 = (s32[]{:T(128)}, f32[1,16,16,384]{3,1,2,0:T(8,128)S(1)}, bf16[6,16,16,384]{3,2,1,0:T(8,128)(2,1)}, bf16[6,16,16,384]{3,1,2,0:T(8,128)(2,1)}, s32[]{...) while((s32[]{:T(128)}, ...), condition=%wide.region_43.44_spmd, body=%wide.region_31.43_spmd.sunk | while | flops 982010688 | bytes 27228544 | solution.py:276
  773.9 13.1 %collective-permute-done.3 = f32[1,16,16,384]{3,1,2,0:T(8,128)S(1)} collective-permute-done((f32[1,16,16,384]{3,1,2,0:T(8,128)}, f32[1,16,16,384]{3,1,2,0:T(8,128)S(1)}, u32[]{:S(2)}, u32[]{:S(2)}) %collective-permute-start.3) | collective-permute-done | bytes 393248 | tf_op jit(solution)/shard_map/while/body/eval_jaxpr/ppermute | solution.py:32
  792.2 81.6 %collective-permute-done.3 = f32[1,16,16,384]{3,1,2,0:T(8,128)S(1)} collective-permute-done((f32[1,16,16,384]{3,1,2,0:T(8,128)}, f32[1,16,16,384]{3,1,2,0:T(8,128)S(1)}, u32[]{:S(2)}, u32[]{:S(2)}) %collective-permute-start.3) | collective-permute-done | bytes 393248 | tf_op jit(solution)/shard_map/while/body/eval_jaxpr/ppermute | solution.py:32
  912.3 14.3 %collective-permute-done.3 = f32[1,16,16,384]{3,1,2,0:T(8,128)S(1)} collective-permute-done((f32[1,16,16,384]{3,1,2,0:T(8,128)}, f32[1,16,16,384]{3,1,2,0:T(8,128)S(1)}, u32[]{:S(2)}, u32[]{:S(2)}) %collective-permute-start.3) | collective-permute-done | bytes 393248 | tf_op jit(solution)/shard_map/while/body/eval_jaxpr/ppermute | solution.py:32
  976.7 16.1 %while.114 = (s32[]{:T(128)}, f32[3,3,384,384]{3,2,1,0:T(8,128)}, bf16[4,18,18,384]{3,2,1,0:T(8,128)(2,1)S(1)}, bf16[1024,384]{1,0:T(8,128)(2,1)S(1)}, s32[]{:T(...) while((s32[]{:T(128)}, f32[3,3,384,384]{3,2,1,0:T(8,128)}, ...), condition=%wide.region_45.46_spmd, body=%wide.region_44.45_spmd.sunk | while | flops 301989920 | bytes 3735894 | solution.py:87
  1000.7 48.0 %while.115 = (s32[]{:T(128)}, f32[3,3,768,384]{3,2,1,0:T(8,128)}, bf16[4,18,18,768]{3,2,1,0:T(8,128)(2,1)S(1)}, bf16[1024,384]{1,0:T(8,128)(2,1)S(1)}, s32[]{:T(...) while((s32[]{:T(128)}, f32[3,3,768,384]{3,2,1,0:T(8,128)}, ...), condition=%wide.region_47.48_spmd, body=%wide.region_46.47_spmd.sunk | while | flops 603979776 | bytes 6685014 | solution.py:87
  1059.7 90.8 %reduce-scatter.2.cloned.1.call-done = f32[1,3,3,72,384]{4,3,2,1,0:T(8,128)} async-done(((f32[1,3,3,1152,384]{4,3,2,1,0:T(8,128)}), f32[1,3,3,72,384]{4,3,2,1,0:T(8,128)}) %reduce-scatter.2.cloned.1.call-update) | async-done | bytes 995344 | tf_op jit(solution)/shard_map/reduce_scatter | solution.py:293
  (983 shorter events, 865.4 us)
Async XLA Ops:
  7.2 1143.3 %reduce-scatter.2.cloned.1.call-start = ((), (), s32[]{:S(2)}) async-start(), calls=%async_computation.1 | async-start | bytes 16920576 | tf_op jit(solution)/shard_map/reduce_scatter | solution.py:293
  7.9 24.8 %collective-permute-start.4 = (f32[4]{0:T(128)S(1)}, f32[4]{0:T(128)S(1)}, u32[]{:S(2)}, u32[]{:S(2)}) collective-permute-start(f32[4]{0:T(128)S(1)} %convert_element_type.108), channel_id=1, source_target_pairs={{0,8},{1,9},{2,10},{3,11},{4,12},{5,13},{6,14},{7,15},{8,0},{9,1},... | collective-permute-start | bytes 56 | tf_op jit(solution)/shard_map/ppermute | solution.py:127
  107.5 15.2 %collective-permute-start = (f32[1,16,16,384]{3,1,2,0:T(8,128)S(1)}, f32[1,16,16,384]{3,1,2,0:T(8,128)S(1)}, u32[]{:S(2)}, u32[]{:S(2)}) collective-permute-start(f32[1,16,16,384]{3,1,2,0:T(8,128)S(1)} %get-tuple-element.2376), channel_id=1, source_target_pairs={{0,16},{1,17},{2,18},{3,19},{4,20},{5,21},{6,22},{7,23},{8,24},{9,... | collective-permute-start | bytes 1179656 | tf_op jit(solution)/shard_map/while/body/eval_jaxpr/ppermute | solution.py:32
  134.6 14.0 %collective-permute-start = (f32[1,16,16,384]{3,1,2,0:T(8,128)S(1)}, f32[1,16,16,384]{3,1,2,0:T(8,128)S(1)}, u32[]{:S(2)}, u32[]{:S(2)}) collective-permute-start(f32[1,16,16,384]{3,1,2,0:T(8,128)S(1)} %get-tuple-element.2376), channel_id=1, source_target_pairs={{0,16},{1,17},{2,18},{3,19},{4,20},{5,21},{6,22},{7,23},{8,24},{9,... | collective-permute-start | bytes 1179656 | tf_op jit(solution)/shard_map/while/body/eval_jaxpr/ppermute | solution.py:32
  160.6 17.6 %collective-permute-start = (f32[1,16,16,384]{3,1,2,0:T(8,128)S(1)}, f32[1,16,16,384]{3,1,2,0:T(8,128)S(1)}, u32[]{:S(2)}, u32[]{:S(2)}) collective-permute-start(f32[1,16,16,384]{3,1,2,0:T(8,128)S(1)} %get-tuple-element.2376), channel_id=1, source_target_pairs={{0,16},{1,17},{2,18},{3,19},{4,20},{5,21},{6,22},{7,23},{8,24},{9,... | collective-permute-start | bytes 1179656 | tf_op jit(solution)/shard_map/while/body/eval_jaxpr/ppermute | solution.py:32
  193.4 18.5 %collective-permute-start = (f32[1,16,16,384]{3,1,2,0:T(8,128)S(1)}, f32[1,16,16,384]{3,1,2,0:T(8,128)S(1)}, u32[]{:S(2)}, u32[]{:S(2)}) collective-permute-start(f32[1,16,16,384]{3,1,2,0:T(8,128)S(1)} %get-tuple-element.2376), channel_id=1, source_target_pairs={{0,16},{1,17},{2,18},{3,19},{4,20},{5,21},{6,22},{7,23},{8,24},{9,... | collective-permute-start | bytes 1179656 | tf_op jit(solution)/shard_map/while/body/eval_jaxpr/ppermute | solution.py:32
  217.5 14.2 %collective-permute-start.1 = (f32[1,16,16,384]{3,1,2,0:T(8,128)S(1)}, f32[1,16,16,384]{3,1,2,0:T(8,128)S(1)}, u32[]{:S(2)}, u32[]{:S(2)}) collective-permute-start(f32[1,16,16,384]{3,1,2,0:T(8,128)S(1)} %get-tuple-element.2377), channel_id=1, source_target_pairs={{16,0},{17,1},{18,2},{19,3},{20,4},{21,5},{22,6},{23,7},{24,8},{25... | collective-permute-start | bytes 1179656 | tf_op jit(solution)/shard_map/while/body/eval_jaxpr/ppermute | solution.py:32
  233.6 15.5 %collective-permute-start.1 = (f32[1,16,16,384]{3,1,2,0:T(8,128)S(1)}, f32[1,16,16,384]{3,1,2,0:T(8,128)S(1)}, u32[]{:S(2)}, u32[]{:S(2)}) collective-permute-start(f32[1,16,16,384]{3,1,2,0:T(8,128)S(1)} %get-tuple-element.2377), channel_id=1, source_target_pairs={{16,0},{17,1},{18,2},{19,3},{20,4},{21,5},{22,6},{23,7},{24,8},{25... | collective-permute-start | bytes 1179656 | tf_op jit(solution)/shard_map/while/body/eval_jaxpr/ppermute | solution.py:32
  251.1 16.6 %collective-permute-start.1 = (f32[1,16,16,384]{3,1,2,0:T(8,128)S(1)}, f32[1,16,16,384]{3,1,2,0:T(8,128)S(1)}, u32[]{:S(2)}, u32[]{:S(2)}) collective-permute-start(f32[1,16,16,384]{3,1,2,0:T(8,128)S(1)} %get-tuple-element.2377), channel_id=1, source_target_pairs={{16,0},{17,1},{18,2},{19,3},{20,4},{21,5},{22,6},{23,7},{24,8},{25... | collective-permute-start | bytes 1179656 | tf_op jit(solution)/shard_map/while/body/eval_jaxpr/ppermute | solution.py:32
  269.7 19.9 %collective-permute-start.1 = (f32[1,16,16,384]{3,1,2,0:T(8,128)S(1)}, f32[1,16,16,384]{3,1,2,0:T(8,128)S(1)}, u32[]{:S(2)}, u32[]{:S(2)}) collective-permute-start(f32[1,16,16,384]{3,1,2,0:T(8,128)S(1)} %get-tuple-element.2377), channel_id=1, source_target_pairs={{16,0},{17,1},{18,2},{19,3},{20,4},{21,5},{22,6},{23,7},{24,8},{25... | collective-permute-start | bytes 1179656 | tf_op jit(solution)/shard_map/while/body/eval_jaxpr/ppermute | solution.py:32
  291.7 16.6 %collective-permute-start.1 = (f32[1,16,16,384]{3,1,2,0:T(8,128)S(1)}, f32[1,16,16,384]{3,1,2,0:T(8,128)S(1)}, u32[]{:S(2)}, u32[]{:S(2)}) collective-permute-start(f32[1,16,16,384]{3,1,2,0:T(8,128)S(1)} %get-tuple-element.2377), channel_id=1, source_target_pairs={{16,0},{17,1},{18,2},{19,3},{20,4},{21,5},{22,6},{23,7},{24,8},{25... | collective-permute-start | bytes 1179656 | tf_op jit(solution)/shard_map/while/body/eval_jaxpr/ppermute | solution.py:32
  321.9 37.4 %collective-permute-start.1 = (f32[1,16,16,384]{3,1,2,0:T(8,128)S(1)}, f32[1,16,16,384]{3,1,2,0:T(8,128)S(1)}, u32[]{:S(2)}, u32[]{:S(2)}) collective-permute-start(f32[1,16,16,384]{3,1,2,0:T(8,128)S(1)} %get-tuple-element.2377), channel_id=1, source_target_pairs={{16,0},{17,1},{18,2},{19,3},{20,4},{21,5},{22,6},{23,7},{24,8},{25... | collective-permute-start | bytes 1179656 | tf_op jit(solution)/shard_map/while/body/eval_jaxpr/ppermute | solution.py:32
  390.9 14.4 %collective-permute-start.1 = (f32[1,16,16,384]{3,1,2,0:T(8,128)S(1)}, f32[1,16,16,384]{3,1,2,0:T(8,128)S(1)}, u32[]{:S(2)}, u32[]{:S(2)}) collective-permute-start(f32[1,16,16,384]{3,1,2,0:T(8,128)S(1)} %get-tuple-element.2377), channel_id=1, source_target_pairs={{16,0},{17,1},{18,2},{19,3},{20,4},{21,5},{22,6},{23,7},{24,8},{25... | collective-permute-start | bytes 1179656 | tf_op jit(solution)/shard_map/while/body/eval_jaxpr/ppermute | solution.py:32
  414.4 15.7 %collective-permute-start.1 = (f32[1,16,16,384]{3,1,2,0:T(8,128)S(1)}, f32[1,16,16,384]{3,1,2,0:T(8,128)S(1)}, u32[]{:S(2)}, u32[]{:S(2)}) collective-permute-start(f32[1,16,16,384]{3,1,2,0:T(8,128)S(1)} %get-tuple-element.2377), channel_id=1, source_target_pairs={{16,0},{17,1},{18,2},{19,3},{20,4},{21,5},{22,6},{23,7},{24,8},{25... | collective-permute-start | bytes 1179656 | tf_op jit(solution)/shard_map/while/body/eval_jaxpr/ppermute | solution.py:32
  551.4 19.5 %collective-permute-start.2 = (f32[1,16,16,384]{3,1,2,0:T(8,128)S(1)}, f32[1,16,16,384]{3,1,2,0:T(8,128)S(1)}, u32[]{:S(2)}, u32[]{:S(2)}) collective-permute-start(f32[1,16,16,384]{3,1,2,0:T(8,128)S(1)} %get-tuple-element.2085), channel_id=1, source_target_pairs={{0,16},{1,17},{2,18},{3,19},{4,20},{5,21},{6,22},{7,23},{8,24},{9,... | collective-permute-start | bytes 1179656 | tf_op jit(solution)/shard_map/while/body/eval_jaxpr/ppermute | solution.py:32
  587.6 17.1 %collective-permute-start.2 = (f32[1,16,16,384]{3,1,2,0:T(8,128)S(1)}, f32[1,16,16,384]{3,1,2,0:T(8,128)S(1)}, u32[]{:S(2)}, u32[]{:S(2)}) collective-permute-start(f32[1,16,16,384]{3,1,2,0:T(8,128)S(1)} %get-tuple-element.2085), channel_id=1, source_target_pairs={{0,16},{1,17},{2,18},{3,19},{4,20},{5,21},{6,22},{7,23},{8,24},{9,... | collective-permute-start | bytes 1179656 | tf_op jit(solution)/shard_map/while/body/eval_jaxpr/ppermute | solution.py:32
  621.0 22.1 %collective-permute-start.2 = (f32[1,16,16,384]{3,1,2,0:T(8,128)S(1)}, f32[1,16,16,384]{3,1,2,0:T(8,128)S(1)}, u32[]{:S(2)}, u32[]{:S(2)}) collective-permute-start(f32[1,16,16,384]{3,1,2,0:T(8,128)S(1)} %get-tuple-element.2085), channel_id=1, source_target_pairs={{0,16},{1,17},{2,18},{3,19},{4,20},{5,21},{6,22},{7,23},{8,24},{9,... | collective-permute-start | bytes 1179656 | tf_op jit(solution)/shard_map/while/body/eval_jaxpr/ppermute | solution.py:32
  662.6 27.5 %collective-permute-start.2 = (f32[1,16,16,384]{3,1,2,0:T(8,128)S(1)}, f32[1,16,16,384]{3,1,2,0:T(8,128)S(1)}, u32[]{:S(2)}, u32[]{:S(2)}) collective-permute-start(f32[1,16,16,384]{3,1,2,0:T(8,128)S(1)} %get-tuple-element.2085), channel_id=1, source_target_pairs={{0,16},{1,17},{2,18},{3,19},{4,20},{5,21},{6,22},{7,23},{8,24},{9,... | collective-permute-start | bytes 1179656 | tf_op jit(solution)/shard_map/while/body/eval_jaxpr/ppermute | solution.py:32
  709.1 13.7 %collective-permute-start.3 = (f32[1,16,16,384]{3,1,2,0:T(8,128)}, f32[1,16,16,384]{3,1,2,0:T(8,128)S(1)}, u32[]{:S(2)}, u32[]{:S(2)}) collective-permute-start(f32[1,16,16,384]{3,1,2,0:T(8,128)} %get-tuple-element.2102), channel_id=1, source_target_pairs={{16,0},{17,1},{18,2},{19,3},{20,4},{21,5},{22,6},{23,7},{24,8},{25... | collective-permute-start | bytes 1179656 | tf_op jit(solution)/shard_map/while/body/eval_jaxpr/ppermute | solution.py:32
  724.3 13.7 %collective-permute-start.3 = (f32[1,16,16,384]{3,1,2,0:T(8,128)}, f32[1,16,16,384]{3,1,2,0:T(8,128)S(1)}, u32[]{:S(2)}, u32[]{:S(2)}) collective-permute-start(f32[1,16,16,384]{3,1,2,0:T(8,128)} %get-tuple-element.2102), channel_id=1, source_target_pairs={{16,0},{17,1},{18,2},{19,3},{20,4},{21,5},{22,6},{23,7},{24,8},{25... | collective-permute-start | bytes 1179656 | tf_op jit(solution)/shard_map/while/body/eval_jaxpr/ppermute | solution.py:32
  739.4 14.6 %collective-permute-start.3 = (f32[1,16,16,384]{3,1,2,0:T(8,128)}, f32[1,16,16,384]{3,1,2,0:T(8,128)S(1)}, u32[]{:S(2)}, u32[]{:S(2)}) collective-permute-start(f32[1,16,16,384]{3,1,2,0:T(8,128)} %get-tuple-element.2102), channel_id=1, source_target_pairs={{16,0},{17,1},{18,2},{19,3},{20,4},{21,5},{22,6},{23,7},{24,8},{25... | collective-permute-start | bytes 1179656 | tf_op jit(solution)/shard_map/while/body/eval_jaxpr/ppermute | solution.py:32
  770.3 16.8 %collective-permute-start.3 = (f32[1,16,16,384]{3,1,2,0:T(8,128)}, f32[1,16,16,384]{3,1,2,0:T(8,128)S(1)}, u32[]{:S(2)}, u32[]{:S(2)}) collective-permute-start(f32[1,16,16,384]{3,1,2,0:T(8,128)} %get-tuple-element.2102), channel_id=1, source_target_pairs={{16,0},{17,1},{18,2},{19,3},{20,4},{21,5},{22,6},{23,7},{24,8},{25... | collective-permute-start | bytes 1179656 | tf_op jit(solution)/shard_map/while/body/eval_jaxpr/ppermute | solution.py:32
  788.5 85.3 %collective-permute-start.3 = (f32[1,16,16,384]{3,1,2,0:T(8,128)}, f32[1,16,16,384]{3,1,2,0:T(8,128)S(1)}, u32[]{:S(2)}, u32[]{:S(2)}) collective-permute-start(f32[1,16,16,384]{3,1,2,0:T(8,128)} %get-tuple-element.2102), channel_id=1, source_target_pairs={{16,0},{17,1},{18,2},{19,3},{20,4},{21,5},{22,6},{23,7},{24,8},{25... | collective-permute-start | bytes 1179656 | tf_op jit(solution)/shard_map/while/body/eval_jaxpr/ppermute | solution.py:32
  908.7 18.0 %collective-permute-start.3 = (f32[1,16,16,384]{3,1,2,0:T(8,128)}, f32[1,16,16,384]{3,1,2,0:T(8,128)S(1)}, u32[]{:S(2)}, u32[]{:S(2)}) collective-permute-start(f32[1,16,16,384]{3,1,2,0:T(8,128)} %get-tuple-element.2102), channel_id=1, source_target_pairs={{16,0},{17,1},{18,2},{19,3},{20,4},{21,5},{22,6},{23,7},{24,8},{25... | collective-permute-start | bytes 1179656 | tf_op jit(solution)/shard_map/while/body/eval_jaxpr/ppermute | solution.py:32
  (69 other events, 363.6 us)
Sparse Core Ops, SparseCore 0:
  1059.9 90.6 reduce-scatter.1
